TPU v7x, 256 devices: a whole 4x4x8 slice. The times are simulated.
256 devices in a mesh: seq: 32 (over y, x, core), seg: 8 (over z).
Axes of the slice: x: 4, y: 4, z: 8, core: 2. Of those that a mesh axis runs over, the one named last changes fastest.
Arguments:
- query_rows: bfloat16 [8, 8192, 4, 128], P('seg', 'seq'), may hold values from -6 to 6
- key_rows: bfloat16 [8, 8192, 2, 4, 128], P('seg', 'seq'), may hold values from -6 to 6
- value_rows: bfloat16 [8, 8192, 2, 4, 128], P('seg', 'seq'), may hold values from -6 to 6
- out_gain: float32 [4, 128], replicated, may hold values from 0.5 to 1.5
- initial_state: float32 [4, 128, 128], replicated, may hold values from -24 to 24
Outputs:
- normed_out: bfloat16 [8, 8192, 4, 128], P('seg', 'seq')
All inputs are finite; a program needn't handle non-finite values.
Results may differ from a plain program's by a relative error of at most 0.004.
Values sent between devices are 32-bit elements; how exact they have to be, the bound alone decides.
No kernel may reach another device: no remote copies, remote signals or barrier semaphores. Data moves between devices by JAX's collectives and lax.ppermute only.
A program may use at most 128 MiB of HBM per device.

v0:
```python
import jax
import jax.numpy as jnp
from jax import lax
from jax.sharding import PartitionSpec as P

DK = 128
DV = 128
HEADS = 4
REFL = 2
GROUP = 128


highest = lax.Precision.HIGHEST


def carried_in(part, axis, combine, identity):
    place = lax.axis_index(axis)
    gathered = lax.all_gather(part, axis)
    state = jnp.zeros_like(part) + jnp.asarray(identity, part.dtype)

    def one(step, state):
        return combine(state, lax.dynamic_index_in_dim(gathered, step, 0, False))

    return lax.fori_loop(0, place, one, state)


def from_root(block, axis, owner):
    block = jnp.where(lax.axis_index(axis) == owner, block, jnp.zeros_like(block))
    return lax.psum(block, axis)


def unit_keys(raw):
    raw = raw.astype(jnp.float32)
    return raw * lax.rsqrt(jnp.sum(raw * raw, axis=-1, keepdims=True) + 1e-06)


def solve_single(matrix, target):
    return jax.scipy.linalg.solve_triangular(matrix, target, lower=True, unit_diagonal=True)


def block_factors(query, keyed, valued):
    steps = keyed.shape[-2]
    tokens = query.shape[-2]
    key_gram = jnp.einsum("...id,...jd->...ij", keyed, keyed, precision=highest)
    lower_unit = jnp.eye(steps, dtype=jnp.float32) + jnp.tril(2.0 * key_gram, -1)
    target = jnp.concatenate([2.0 * keyed, 2.0 * valued], axis=-1)
    flat_lower = lower_unit.reshape(-1, steps, steps)
    flat_target = target.reshape(-1, steps, target.shape[-1])
    solved = jax.vmap(solve_single)(flat_lower, flat_target).reshape(target.shape)
    weights = solved[..., : keyed.shape[-1]]
    updates = solved[..., keyed.shape[-1] :]
    visible = jnp.arange(steps)[None, :] <= REFL * jnp.arange(tokens)[:, None] + (REFL - 1)
    scores = jnp.where(
        visible, jnp.einsum("...td,...ld->...tl", query, keyed, precision=highest), 0.0
    )
    return (weights, updates, scores)


def compose(first_pair, second_pair):
    second_trans = second_pair[..., :DK]
    moved = jnp.einsum("...de,...ef->...df", second_trans, first_pair, precision=highest)
    added = jnp.concatenate([jnp.zeros_like(second_trans), second_pair[..., DK:]], axis=-1)
    return moved + added


def identity_pair():
    eye_part = jnp.broadcast_to(jnp.eye(DK, dtype=jnp.float32), (HEADS, DK, DK))
    return jnp.concatenate([eye_part, jnp.zeros((HEADS, DK, DV), jnp.float32)], axis=-1)


def apply_pair(pair, state):
    return jnp.einsum("hde,hef->hdf", pair[..., :DK], state, precision=highest) + pair[..., DK:]


def per_device(query_rows, key_rows, value_rows, out_gain, initial_state):
    tokens = query_rows.shape[1]
    nblock = tokens // GROUP
    query = (
        query_rows[0].astype(jnp.float32).reshape(nblock, GROUP, HEADS, DK).transpose(0, 2, 1, 3)
    )
    keyed = unit_keys(key_rows[0]).reshape(nblock, GROUP * REFL, HEADS, DK).transpose(0, 2, 1, 3)
    valued = (
        value_rows[0]
        .astype(jnp.float32)
        .reshape(nblock, GROUP * REFL, HEADS, DV)
        .transpose(0, 2, 1, 3)
    )
    weights, updates, scores = block_factors(query, keyed, valued)
    trans_block = jnp.eye(DK, dtype=jnp.float32) - jnp.einsum(
        "chld,chle->chde", keyed, weights, precision=highest
    )
    state_block = jnp.einsum("chld,chle->chde", keyed, updates, precision=highest)
    block_pairs = jnp.concatenate([trans_block, state_block], axis=-1)
    project = query - jnp.einsum("chtl,chld->chtd", scores, weights, precision=highest)
    local_read = jnp.einsum("chtl,chle->chte", scores, updates, precision=highest)

    def accumulate(carry, piece):
        return (compose(carry, piece), carry)

    own_pair, before = lax.scan(accumulate, identity_pair(), block_pairs)
    reach = jnp.einsum("chtd,chde->chte", project, before[..., :DK], precision=highest)
    base_read = (
        jnp.einsum("chtd,chde->chte", project, before[..., DK:], precision=highest) + local_read
    )
    seq_before = carried_in(own_pair, "seq", compose, identity_pair())
    closing = compose(seq_before, own_pair)
    seg_total = from_root(closing, "seq", lax.axis_size("seq") - 1)
    seg_before = carried_in(seg_total, "seg", compose, identity_pair())
    entry_state = apply_pair(seg_before, initial_state)
    incoming = apply_pair(seq_before, entry_state)
    reads = jnp.einsum("chtd,hde->chte", reach, incoming, precision=highest) + base_read
    reads = reads.transpose(0, 2, 1, 3).reshape(1, tokens, HEADS, DV)
    scale = lax.rsqrt(jnp.mean(reads * reads, axis=-1, keepdims=True) + 1e-06)
    return (reads * scale * out_gain).astype(jnp.bfloat16)


def solution(mesh):
    return jax.shard_map(
        per_device,
        mesh=mesh,
        in_specs=(
            P("seg", "seq", None, None),
            P("seg", "seq", None, None, None),
            P("seg", "seq", None, None, None),
            P(),
            P(),
        ),
        out_specs=P("seg", "seq", None, None),
        check_vma=False,
    )
```

profile of v0, /device:TPU:1, one launch (start us, length us, event | category | flops | bytes accessed | tf_op | source)
XLA Modules:
  0.0 516.8 jit_solution(4025722564114510679)
XLA Ops:
  6.5 0.7 fusion.40
  7.3 1.8 multiply_reduce_fusion
  9.1 1.1 convert.5
  10.5 0.2 convert_multiply_fusion
  10.7 1.0 copy.130
  11.9 1.3 bitcast_multiply_fusion
  13.2 2.3 select_add_fusion
  15.5 0.3 fusion.3
  15.9 6.1 %while.36 = (s32[]{:T(128)}, f32[8,256,256]{2,1,0:T(8,128)S(1)}, s32[2,2]{1,0:T(2,128)S(1)}, f32[2,8,128,128]{3,2,0,1:T(8,128)}, s32[]{:T(128)}) while((s32[]{:T(128)}, f32[8,256,256]{2,1,0:T(8,128)S(1)}, s32[2,2]{1,0:T(2,128)S(1)}, f32[2,8,128,128]{3,2,0,1:T(8,128)}, s32[]{:T(128)}) %tuple.63), condition=%wide.while_cond, body=%wide.while_body.sunk | while | flops 2 | bytes 1049709 | solution.py:38
  16.0 0.6 fusion.72
  16.6 2.4 bitcast_dynamic-update-slice_fusion.5
  19.0 0.6 fusion.72
  19.6 2.4 bitcast_dynamic-update-slice_fusion.5
  22.0 158.6 %custom-call.4 = f32[8,2,128,128]{2,3,1,0:T(8,128)} custom-call(f32[8,2,128,128]{3,2,1,0:T(8,128)} %bitcast.115), custom_call_target="InvertDiagBlocksLowerTriangular" | custom-call | tf_op jit(solution)/shard_map/vmap(jit(_solve_triangular))/triangular_solve | solution.py:38
  180.6 1.8 pad_maximum_fusion
  182.4 1.1 fusion.10
  183.5 1.0 convolution_subtract_fusion
  184.6 1.1 fusion.24
  185.7 0.2 pad_maximum_fusion.1
  186.0 2.2 fusion.15
  188.2 2.2 convolution_subtract_fusion.2
  190.5 0.8 copy.142
  191.3 1.1 pad_maximum_fusion.2
  192.3 7.3 %while.33 = (s32[]{:T(128)}, f32[4,128,256]{2,1,0:T(8,128)}, f32[2,4,128,256]{3,2,1,0:T(8,128)}, f32[2,4,128,256]{2,3,1,0:T(8,128)}, s32[]{:T(128)}) while((s32[]{:T(128)}, f32[4,128,256]{2,1,0:T(8,128)}, f32[2,4,128,256]{3,2,1,0:T(8,128)}, f32[2,4,128,256]{2,3,1,0:T(8,128)}, s32[]{:T(128)}) %tuple.66), condition=%wide.region_2.3_spmd, body=%wide.region_1.2_spmd.sunk | while | flops 201457664 | bytes 10485865 | solution.py:100
  192.3 1.1 copy.166
  193.5 0.9 bitcast_dynamic-update-slice_fusion.4
  194.6 1.4 convolution_add_fusion.10
  196.0 1.1 copy.166
  197.1 0.8 bitcast_dynamic-update-slice_fusion.4
  198.2 1.4 convolution_add_fusion.10
  199.7 1.0 slice.67
  200.7 80.8 %all-gather.6.cloned.1.call-done = f32[128,128,256]{2,1,0:T(8,128)} async-done(((f32[4,128,256]{2,1,0:T(8,128)}), f32[128,128,256]{2,1,0:T(8,128)}) %all-gather.6.cloned.1.call-update) | async-done | bytes 16777232 | tf_op jit(solution)/shard_map/all_gather | solution.py:18
  281.5 2.0 while.34
  281.6 1.1 dynamic-slice_bitcast_fusion.4
  282.7 0.6 convolution_add_fusion.11
  283.5 2.4 fusion.8
  286.0 165.0 %all-reduce.7.cloned.1.call-done = f32[1,4,128,256]{3,2,1,0:T(8,128)} async-done(((f32[1,4,128,256]{3,2,1,0:T(8,128)}), f32[1,4,128,256]{3,2,1,0:T(8,128)}) %all-reduce.7.cloned.1.call-update) | async-done | bytes 524304 | tf_op jit(solution)/shard_map/psum | solution.py:29
  451.1 0.7 fusion.4
  451.8 0.8 copy-done.2
  452.6 1.9 convolution_subtract_fusion.1
  454.5 1.7 fusion.25
  456.2 1.7 fusion.21
  457.8 1.9 fusion.5
  459.7 47.7 %all-gather.4.cloned.1.call-done = f32[8,4,128,256]{3,2,1,0:T(8,128)} async-done(((f32[1,4,128,256]{3,2,1,0:T(8,128)}), f32[8,4,128,256]{3,2,1,0:T(8,128)}) %all-gather.4.cloned.1.call-update) | async-done | bytes 4194320 | tf_op jit(solution)/shard_map/all_gather | solution.py:18
  507.4 0.4 convolution_add_fusion.6
  507.8 0.4 fusion.9
  508.2 0.8 multiply_reduce_fusion.1
  509.1 1.1 fusion.28
  (53 shorter events, 1.6 us)
Async XLA Ops:
  6.5 500.9 %copy-start = (f32[4,128,128]{2,1,0:T(8,128)S(1)}, f32[4,128,128]{2,1,0:T(8,128)}, u32[]{:S(2)}) copy-start(f32[4,128,128]{2,1,0:T(8,128)} %param.15) | copy-start | bytes 786436
  6.5 4.0 copy-start.7
  6.5 275.0 %all-gather.6.cloned.1.call-start = ((), (), s32[]{:S(2)}) async-start(), calls=%async_computation.2 | async-start | bytes 17301504 | tf_op jit(solution)/shard_map/all_gather | solution.py:18
  13.2 2.3 copy-start.5
  180.6 1.9 copy-start.4
  185.9 4.5 copy-start.1
  192.3 2.0 copy-start.3
  196.0 2.0 copy-start.3
  199.6 251.4 %all-reduce.7.cloned.1.call-start = ((), (), s32[]{:S(2)}) async-start(), calls=%async_computation | async-start | bytes 1048576 | tf_op jit(solution)/shard_map/psum | solution.py:29
  283.5 167.6 %copy-start.6 = (bf16[1,256,4,128]{3,2,1,0:T(4,128)(2,1)S(1)}, bf16[1,256,4,128]{3,2,1,0:T(4,128)(2,1)}, u32[]{:S(2)}) copy-start(bf16[1,256,4,128]{3,2,1,0:T(4,128)(2,1)} %param.11) | copy-start | bytes 786436
  285.9 221.5 %all-gather.4.cloned.1.call-start = ((), (), s32[]{:S(2)}) async-start(), calls=%async_computation.1 | async-start | bytes 4718592 | tf_op jit(solution)/shard_map/all_gather | solution.py:18
  451.0 1.6 copy-start.2
  507.4 1.7 copy-start.8
Sparse Core Ops, SparseCore 0:
  199.8 81.7 all-gather.5
  286.0 164.9 all-reduce.6
  452.9 54.4 all-gather.3
where the time goes:
time: 526 us; the launch traced here: 517 us
  waiting for transfers between devices  294 us (56%)
  other arithmetic  169 us (32%)
  matrix products  25 us (5%)
  local copies, waits for them, and re-layouts  15.7 us (3%)
  between operations  13.4 us (3%)
    psum x1, waiting for transfers between devices, from_root(): return lax.psum(block, axis)  165 us
    another operation x7, other arithmetic, solve_single(): jax.scipy.linalg.solve_triangular(matrix, target, lower=True, unit_diagon...  160 us
    all_gather x2, waiting for transfers between devices, carried_in(): gathered = lax.all_gather(part, axis)  128 us
  transfers between devices with their start and end apart: 3, of which 3 were waited for; matrix products, arithmetic and copies ran while one was open for 2% of the time, Pallas kernels for 0%

commit v1 on v0

v1 whole, which is shorter than its diff:
```python
import jax
import jax.numpy as jnp
from jax import lax
from jax.experimental import pallas as pl
from jax.experimental.pallas import tpu as pltpu
from jax.sharding import PartitionSpec as P

D = 128
HEADS = 4
REFL = 2
BLK = 128
XS = 4
YS = 4
CS = 2
HALF = D // CS
MSG = D + HALF

f32 = jnp.float32
bf16 = jnp.bfloat16


def split(x):
    high = x.astype(bf16)
    low = (x - high.astype(f32)).astype(bf16)
    return high, low


def dot_nn(a, b):
    return lax.dot_general(a, b, (((1,), (0,)), ((), ())), preferred_element_type=f32)


def dot_nt(a, b):
    return lax.dot_general(a, b, (((1,), (1,)), ((), ())), preferred_element_type=f32)


def wide(x):
    high, low = split(x)
    return jnp.concatenate([high, low], axis=1)


def tall_wide(x):
    row = wide(x)
    return jnp.concatenate([row, row], axis=0)


def mm_pre(left_wide, right_tall):
    out = dot_nn(left_wide, right_tall)
    n = out.shape[1] // 2
    return out[:, :n] + out[:, n:]


def mm(a, b):
    return mm_pre(wide(a), tall_wide(b))


def mm_nt(a, b):
    ah, al = split(a)
    bh, bl = split(b)
    return dot_nt(ah, bh) + dot_nt(ah, bl) + dot_nt(al, bh)


def iota2(shape, dim):
    return lax.broadcasted_iota(jnp.int32, shape, dim)


def factor_kernel(r_ref, v_ref, m_ref, z_ref, p_ref):
    heads = r_ref.shape[0]
    nblk = r_ref.shape[1] // BLK
    row = iota2((BLK, BLK), 0)
    col = iota2((BLK, BLK), 1)
    eye = row == col
    chains = [(h, b) for h in range(heads) for b in range(nblk)]
    rs, rts, vts, uppers, invs, ccols, crows = [], [], [], [], [], [], []
    for h, b in chains:
        r = r_ref[h, b * BLK : (b + 1) * BLK, :]
        v = v_ref[h, b * BLK : (b + 1) * BLK, :]
        rt = r.T
        gram = dot_nn(r, rt)
        diag = jnp.where(eye, gram, 0.0)
        ccol = lax.rsqrt(jnp.sum(diag, axis=1, keepdims=True) + 1e-06)
        crow = lax.rsqrt(jnp.sum(diag, axis=0, keepdims=True) + 1e-06)
        upper = jnp.where(row < col, 2.0 * ccol * crow * gram, 0.0)
        pair = ((row >> 1) == (col >> 1)) & (row < col)
        inv = jnp.where(eye, 1.0, 0.0) - jnp.where(pair, upper, 0.0)
        rs.append(r)
        rts.append(rt)
        vts.append(v.T)
        uppers.append(upper)
        invs.append(inv)
        ccols.append(ccol)
        crows.append(crow)
    for level in range(1, 7):
        off = ((row >> (level + 1)) == (col >> (level + 1))) & (
            (row >> level) < (col >> level)
        )
        talls = [tall_wide(inv) for inv in invs]
        mids = [
            mm_pre(wide(jnp.where(off, upper, 0.0)), tall) for upper, tall in zip(uppers, talls)
        ]
        invs = [inv - mm(inv, mid) for inv, mid in zip(invs, mids)]
    pairs = []
    base = jnp.where(iota2((2 * D, D), 0) == iota2((2 * D, D), 1), 1.0, 0.0)
    sign = jnp.where(iota2((2 * D, D), 0) < D, -1.0, 1.0)
    for i, (h, b) in enumerate(chains):
        wh, wl = split(2.0 * ccols[i] * invs[i])
        uh, ul = split(2.0 * invs[i])
        wt = dot_nn(jnp.concatenate([rts[i], rts[i]], axis=1), jnp.concatenate([wh, wl], axis=0))
        ut = dot_nn(jnp.concatenate([vts[i], vts[i]], axis=1), jnp.concatenate([uh, ul], axis=0))
        z = jnp.concatenate([wt, ut], axis=0) * crows[i]
        z_ref[h, b] = z
        rr = jnp.concatenate([rs[i], rs[i]], axis=0)
        pairs.append(base + sign * dot_nn(wide(z), rr))
    for h in range(heads):
        own = pairs[h * nblk : (h + 1) * nblk]
        for b in range(nblk - 1):
            p_ref[h, b] = own[b]
        while len(own) > 1:
            own = [compose(own[i], own[i + 1]) for i in range(0, len(own), 2)]
        m_ref[h] = own[0]


def compose(first, second):
    moved = mm(first, second[:D])
    keep = jnp.concatenate([jnp.zeros((D, D), f32), second[D:]], axis=0)
    return moved + keep


def factor_call(r, v, group):
    heads, steps, _ = r.shape
    nblk = steps // BLK
    return pl.pallas_call(
        factor_kernel,
        grid=(heads // group,),
        in_specs=[pl.BlockSpec((group, steps, D), lambda i: (i, 0, 0))] * 2,
        out_specs=[
            pl.BlockSpec((group, 2 * D, D), lambda i: (i, 0, 0)),
            pl.BlockSpec((group, nblk, 2 * D, D), lambda i: (i, 0, 0, 0)),
            pl.BlockSpec((group, nblk - 1, 2 * D, D), lambda i: (i, 0, 0, 0)),
        ],
        out_shape=[
            jax.ShapeDtypeStruct((heads, 2 * D, D), f32),
            jax.ShapeDtypeStruct((heads, nblk, 2 * D, D), f32),
            jax.ShapeDtypeStruct((heads, nblk - 1, 2 * D, D), f32),
        ],
        compiler_params=pltpu.CompilerParams(vmem_limit_bytes=48 << 20),
        name="factor",
    )(r, v)


def chip_kernel(pos_ref, own_ref, sib_ref, *out_refs):
    x = pos_ref[0]
    core = pos_ref[2]
    half = pl.ds(pl.multiple_of(D + core * HALF, HALF), HALF)
    both = [own_ref, sib_ref]
    for k in range(XS):
        head = lax.rem(x + k, HEADS)

        def run(first, second, k=k, head=head):
            rows = jnp.concatenate([first[head, :D, :], first[head, half, :]], axis=0)
            moved = mm(rows, second[head, :D, :])
            out_refs[k][:D, :] = moved[:D]
            out_refs[k][D:, :] = moved[D:] + second[head, half, :]

        @pl.when(core == 0)
        def _():
            run(both[0], both[1])

        @pl.when(core == 1)
        def _():
            run(both[1], both[0])


def ordered_load(slots, place, scratch):
    n = len(slots)
    for k in range(n):
        scratch[lax.rem(place + n - k, n)] = slots[k][...]


def msg_compose(rows, second):
    moved = mm(rows, second[:D])
    return jnp.concatenate([moved[:D], moved[D:] + second[D:]], axis=0)


def row_kernel(pos_ref, s0, s1, s2, s3, total_ref, pre_ref, scratch):
    ordered_load([s0, s1, s2, s3], pos_ref[0], scratch)
    p1 = scratch[0]
    tail = msg_compose(scratch[2], scratch[3])
    p2 = msg_compose(p1, scratch[1])
    total_ref[...] = msg_compose(p2, tail)
    pre_ref[0] = p1
    pre_ref[1] = p2
    pre_ref[2] = msg_compose(p2, scratch[2])


def column_kernel(pos_ref, s0, s1, s2, s3, total_ref, pre_ref, scratch, hold):
    y = pos_ref[1]
    ordered_load([s0, s1, s2, s3], y, scratch)
    p1 = scratch[0]
    tail = msg_compose(scratch[2], scratch[3])
    p2 = msg_compose(p1, scratch[1])
    total_ref[...] = msg_compose(p2, tail)
    hold[0] = jnp.where(iota2((MSG, D), 0) == iota2((MSG, D), 1), 1.0, 0.0)
    hold[1] = p1
    hold[2] = p2
    hold[3] = msg_compose(p2, scratch[2])
    pre_ref[...] = hold[y]


def window_kernel(pos_ref, own, s1, s2, s3, init_ref, win_ref, state_ref, incl_ref):
    g = pos_ref[3]
    rows = jnp.concatenate(
        [jnp.where(iota2((MSG, D), 0) == iota2((MSG, D), 1), 1.0, 0.0), init_ref[...]], axis=0
    )
    for k, ref in ((3, s3), (2, s2), (1, s1)):
        b = ref[D:, :]
        moved = mm(rows, ref[:D, :])
        moved = jnp.concatenate([moved[:D], moved[D : D + HALF] + b, moved[D + HALF :] + b], axis=0)
        rows = jnp.where(g >= k, moved, rows)
    win_ref[...] = rows[:MSG]
    state = rows[MSG:]
    state_ref[...] = state
    incl_ref[...] = mm(state, own[:D, :]) + own[D:, :]


def entry_kernel(pos_ref, win_ref, state_ref, early_ref, ypre_ref, xpre_ref, *refs):
    outs, scratch = refs[:-1], refs[-1]
    x = pos_ref[0]
    g = pos_ref[3]
    late = mm(early_ref[...], win_ref[:D, :]) + win_ref[D:, :]
    state = jnp.where(g >= 4, late, state_ref[...])
    state = mm(state, ypre_ref[:D, :]) + ypre_ref[D:, :]
    scratch[0] = state
    left = wide(state)
    for i in range(XS - 1):
        scratch[i + 1] = mm_pre(left, tall_wide(xpre_ref[i, :D, :])) + xpre_ref[i, D:, :]
    for k in range(XS):
        outs[k][...] = scratch[lax.rem(x + k, XS)]


def reach_kernel(q_ref, r_ref, z_ref, p_ref, pre_ref, reach_ref, base_ref):
    tokens = q_ref.shape[1]
    nblk = z_ref.shape[1]
    span = tokens // nblk
    prefix = pre_ref[0]
    visible = iota2((span, BLK), 1) <= REFL * iota2((span, BLK), 0) + (REFL - 1)
    for b in range(nblk):
        q = q_ref[0, b * span : (b + 1) * span, :]
        scores = jnp.where(visible, dot_nt(q, r_ref[0, b * BLK : (b + 1) * BLK, :]), 0.0)
        sz = mm_nt(scores, z_ref[0, b])
        project = q.astype(f32) - sz[:, :D]
        moved = mm_nt(project, prefix)
        reach_ref[0, b * span : (b + 1) * span, :] = moved[:, :D]
        base_ref[0, b * span : (b + 1) * span, :] = moved[:, D:] + sz[:, D:]
        if b + 1 < nblk:
            prefix = compose(prefix, p_ref[0, b])


def read_kernel(reach_ref, base_ref, state_ref, gain_ref, out_ref):
    for h in range(HEADS):
        read = mm_nt(reach_ref[h], state_ref[h]) + base_ref[h]
        scale = lax.rsqrt(jnp.mean(read * read, axis=-1, keepdims=True) + 1e-06)
        out_ref[h] = (read * scale * gain_ref[h : h + 1, :]).astype(bf16)


def full(*shape):
    return pl.BlockSpec(shape, lambda: (0,) * len(shape))


def small_call(kernel, name, pos, arrays, outs, scratch=()):
    return pl.pallas_call(
        kernel,
        in_specs=[pl.BlockSpec(memory_space=pltpu.SMEM)]
        + [pl.BlockSpec(memory_space=pltpu.VMEM)] * len(arrays),
        out_specs=[pl.BlockSpec(memory_space=pltpu.VMEM)] * len(outs),
        out_shape=[jax.ShapeDtypeStruct(s, f32) for s in outs],
        scratch_shapes=[pltpu.VMEM(s, f32) for s in scratch],
        name=name,
    )(pos, *arrays)


def seq_perm(move):
    pairs = []
    for y in range(YS):
        for x in range(XS):
            for c in range(CS):
                ny, nx, nc = move(y, x, c)
                pairs.append(((y * XS + x) * CS + c, (ny * XS + nx) * CS + nc))
    return pairs


def per_device(query_rows, key_rows, value_rows, out_gain, initial_state):
    tokens = query_rows.shape[1]
    steps = tokens * REFL
    nblk = steps // BLK
    place = lax.axis_index("seq")
    seg = lax.axis_index("seg")
    core = place % CS
    x = (place // CS) % XS
    y = place // (CS * XS)
    pos = jnp.stack([x, y, core, seg]).astype(jnp.int32)

    swap = seq_perm(lambda y, x, c: (y, x, 1 - c))
    along_x = [seq_perm(lambda y, x, c, k=k: (y, (x + k) % XS, c)) for k in range(1, XS)]
    along_y = [seq_perm(lambda y, x, c, k=k: ((y + k) % YS, x, c)) for k in range(1, YS)]
    segs = 8
    along_z = [[(i, (i + k) % segs) for i in range(segs)] for k in range(1, 4)]
    jump = [(i, (i + 4) % segs) for i in range(segs)]

    r = key_rows[0].reshape(steps, HEADS, D).transpose(1, 0, 2)
    v = value_rows[0].reshape(steps, HEADS, D).transpose(1, 0, 2)
    q = query_rows[0].transpose(1, 0, 2)
    pair, z, parts = factor_call(r, v, 1)
    sib = lax.ppermute(pair, "seq", swap)
    slots = small_call(chip_kernel, "chip", pos, [pair, sib], [(MSG, D)] * XS)
    slots = [slots[0]] + [
        lax.ppermute(s, "seq", p) for s, p in zip(slots[1:], along_x)
    ]
    total, xpre = small_call(
        row_kernel, "row", pos, slots, [(MSG, D), (XS - 1, MSG, D)], [(XS, MSG, D)]
    )
    slots = [total] + [lax.ppermute(total, "seq", p) for p in along_y]
    total, ypre = small_call(
        column_kernel, "column", pos, slots, [(MSG, D), (MSG, D)], [(YS, MSG, D), (YS, MSG, D)]
    )
    slots = [total] + [lax.ppermute(total, "seg", p) for p in along_z]
    start = lax.dynamic_index_in_dim(initial_state, x, 0, False).T
    start = lax.dynamic_slice_in_dim(start, core * HALF, HALF, 0)
    win, state, incl = small_call(
        window_kernel, "window", pos, slots + [start], [(MSG, D), (HALF, D), (HALF, D)]
    )
    early = lax.ppermute(incl, "seg", jump)
    slots = small_call(
        entry_kernel,
        "entry",
        pos,
        [win, state, early, ypre, xpre],
        [(HALF, D)] * XS,
        [(XS, HALF, D)],
    )
    slots = [slots[0]] + [lax.ppermute(s, "seq", p) for s, p in zip(slots[1:], along_x)]

    eye_pair = jnp.concatenate([jnp.eye(D, dtype=f32), jnp.zeros((D, D), f32)], axis=0)
    before = jnp.where(core == 1, sib, jnp.broadcast_to(eye_pair, sib.shape))
    reach, base = pl.pallas_call(
        reach_kernel,
        grid=(HEADS,),
        in_specs=[
            pl.BlockSpec((1, tokens, D), lambda i: (i, 0, 0)),
            pl.BlockSpec((1, steps, D), lambda i: (i, 0, 0)),
            pl.BlockSpec((1, nblk, 2 * D, D), lambda i: (i, 0, 0, 0)),
            pl.BlockSpec((1, nblk - 1, 2 * D, D), lambda i: (i, 0, 0, 0)),
            pl.BlockSpec((1, 2 * D, D), lambda i: (i, 0, 0)),
        ],
        out_specs=[pl.BlockSpec((1, tokens, D), lambda i: (i, 0, 0))] * 2,
        out_shape=[jax.ShapeDtypeStruct((HEADS, tokens, D), f32)] * 2,
        name="reach",
    )(q, r, z, parts, before)

    mine = jnp.stack(slots)
    other = lax.ppermute(mine, "seq", swap)
    low = jnp.where(core == 0, mine, other)
    high = jnp.where(core == 0, other, mine)
    states = jnp.concatenate([low, high], axis=1)
    order = (x - jnp.arange(HEADS)) % HEADS
    states = jnp.take(states, order, axis=0)
    out = pl.pallas_call(
        read_kernel,
        out_shape=jax.ShapeDtypeStruct((HEADS, tokens, D), bf16),
        name="read",
    )(reach, base, states, out_gain)
    return out.transpose(1, 0, 2)[None]


def solution(mesh):
    return jax.shard_map(
        per_device,
        mesh=mesh,
        in_specs=(
            P("seg", "seq", None, None),
            P("seg", "seq", None, None, None),
            P("seg", "seq", None, None, None),
            P(),
            P(),
        ),
        out_specs=P("seg", "seq", None, None),
        check_vma=False,
    )
```

time: 526 us -> 109 us (0.21); the launches traced: 517 us -> 108 us
  waiting for transfers between devices: 294 us -> 20.3 us
  other arithmetic: 169 us -> 3.06 us
  Pallas kernels: 0 us -> 37.1 us
  starting transfers between devices: 0.09 us -> 34.6 us
  matrix products: 25 us -> 0 us
  between operations: 13.4 us -> 0.14 us
    psum x1 -> x0, waiting for transfers between devices: 165 us -> none  [from_root(): return lax.psum(block, axis)]
    another operation x7 -> x2, other arithmetic: 160 us -> 1.35 us  [the longest x1 0.77 us: per_device(): mine = jnp.stack(slots)]
    all_gather x2 -> x0, waiting for transfers between devices: 128 us -> none  [carried_in(): gathered = lax.all_gather(part, axis)]
    pallas_call x0 -> x8, Pallas kernels: none -> 37.1 us  [the longest x1 13.9 us: factor_call(): pl.pallas_call(factor_kernel, grid=(heads // group,), in_specs=[pl.BlockS...]
    ppermute x0 -> x15, starting transfers between devices: none -> 34.6 us  [the longest x3 8.96 us: per_device(): slots = [total] + [lax.ppermute(total, 'seg', p) for p in along_z]]
    dot_general x15 -> x0, matrix products: 21.7 us -> none  [the longest x4 5.74 us: compose(): jnp.einsum('...de,...ef->...df', second_trans, first_pair, precision=high...]
    ppermute x0 -> x15, waiting for transfers between devices: none -> 20.3 us  [the longest x3 8.13 us: per_device(): slots = [total] + [lax.ppermute(total, 'seg', p) for p in along_z]]
    unnamed x18 -> x41, local copies, waits for them, and re-layouts: 1.71 us -> 10 us
  transfers between devices with their start and end apart: 3 -> 15, of which waited for: 3 -> 13; matrix products, arithmetic and copies ran while one was open for 2% -> 3% of each run, Pallas kernels for 0% -> 9%
where the time goes in v1:
time: 109 us; the launch traced here: 108 us
  Pallas kernels  37.1 us (34%)
  starting transfers between devices  34.6 us (32%)
  waiting for transfers between devices  20.3 us (19%)
  local copies, waits for them, and re-layouts  13.2 us (12%)
  other arithmetic  3.06 us (3%)
    pallas_call x1, Pallas kernels, factor_call(): pl.pallas_call(factor_kernel, grid=(heads // group,), in_specs=[pl.BlockS...  13.9 us
    pallas_call x5, Pallas kernels, small_call(): pl.pallas_call(kernel, in_specs=[pl.BlockSpec(memory_space=pltpu.SMEM)] +...  11.5 us
    unnamed x41, local copies, waits for them, and re-layouts  10 us
    pallas_call x1, Pallas kernels, per_device(): pl.pallas_call(reach_kernel, grid=(HEADS,), in_specs=[pl.BlockSpec((1, to...  9.3 us
    ppermute x3, starting transfers between devices, per_device(): slots = [total] + [lax.ppermute(total, 'seg', p) for p in along_z]  8.96 us
    ppermute x3, waiting for transfers between devices, per_device(): slots = [total] + [lax.ppermute(total, 'seg', p) for p in along_z]  8.13 us
    ppermute x1, starting transfers between devices, per_device(): other = lax.ppermute(mine, 'seq', swap)  7.52 us
    ppermute x6, waiting for transfers between devices, per_device(): lax.ppermute(s, 'seq', p)  6.72 us
  transfers between devices with their start and end apart: 15, of which 13 were waited for; matrix products, arithmetic and copies ran while one was open for 3% of the time, Pallas kernels for 9%

profile of v1, /device:TPU:1, one launch (start us, length us, event | category | flops | bytes accessed | tf_op | source)
XLA Modules:
  0.0 108.4 jit_solution(972501858065467406)
XLA Ops:
  0.0 1.5 %copy.7 = bf16[1,256,2,4,128]{4,2,1,3,0:T(2,128)(2,1)S(1)} copy(bf16[1,256,2,4,128]{4,3,2,1,0:T(4,128)(2,1)} %param.6) | data formatting | bytes 1048576 | tf_op args[1]
  1.5 1.6 %copy.8 = bf16[1,256,2,4,128]{4,2,1,3,0:T(2,128)(2,1)S(1)} copy(bf16[1,256,2,4,128]{4,3,2,1,0:T(4,128)(2,1)} %param.7) | data formatting | bytes 1048576 | tf_op args[2]
  3.2 13.9 %factor.1 = (f32[4,256,128]{2,1,0:T(8,128)S(1)}, f32[4,4,256,128]{3,2,1,0:T(8,128)S(1)}, f32[4,3,256,128]{3,2,1,0:T(8,128)S(1)}) custom-call(bf16[4,512,128]{2,1,0:T(8,128)(2,1)S(1)} %bitcast.27, bf16[4,512,128]{2,1,0:T(8,128)(2,1)S(1)} %bitcast.29), custom_call_target="tpu_custom_call" | custom-call | tf_op jit(solution)/shard_map/factor/pallas_call | solution.py:131
  17.0 1.3 %copy-done.2 = f32[4,4,256,128]{3,2,1,0:T(8,128)} copy-done((f32[4,4,256,128]{3,2,1,0:T(8,128)}, f32[4,4,256,128]{3,2,1,0:T(8,128)S(1)}, u32[]{:S(2)}) %copy-start.2) | copy-done | bytes 2097176
  18.4 1.2 %copy-done.3 = f32[4,3,256,128]{3,2,1,0:T(8,128)} copy-done((f32[4,3,256,128]{3,2,1,0:T(8,128)}, f32[4,3,256,128]{3,2,1,0:T(8,128)S(1)}, u32[]{:S(2)}) %copy-start.3) | copy-done | bytes 1572888
  19.5 3.2 %collective-permute-start = (f32[4,256,128]{2,1,0:T(8,128)S(1)}, f32[4,256,128]{2,1,0:T(8,128)S(1)}, u32[]{:S(2)}, u32[]{:S(2)}) collective-permute-start(f32[4,256,128]{2,1,0:T(8,128)S(1)} %get-tuple-element.27.own_ref), channel_id=1, source_target_pairs={{0,8},{8,0},{16,24},{24,16},{32,40},{40,32},{48,56},{56,48},{64,72... | collective-permute-start | bytes 1572872 | tf_op jit(solution)/shard_map/ppermute | solution.py:313
  22.9 0.7 copy.9
  23.5 0.6 pad_add_fusion.pos_ref
  24.3 0.8 copy-done.5
  25.1 2.7 %chip.1 = (f32[192,128]{1,0:T(8,128)}, f32[192,128]{1,0:T(8,128)}, f32[192,128]{1,0:T(8,128)}, f32[192,128]{1,0:T(8,128)}) custom-call(s32[4]{0:T(128)} %pad_add_fusion.pos_ref, f32[4,256,128]{2,1,0:T(8,128)} %copy-done.4, f32[4,256,128]{2,1,0:T(8,128)} %copy-done.5), custom_call_target="tpu_custom_call" | custom-call | tf_op jit(solution)/shard_map/chip/pallas_call | solution.py:270
  27.8 1.9 %collective-permute-start.2 = (f32[192,128]{1,0:T(8,128)}, f32[192,128]{1,0:T(8,128)S(1)}, u32[]{:S(2)}, u32[]{:S(2)}) collective-permute-start(f32[192,128]{1,0:T(8,128)} %get-tuple-element.32), channel_id=1, source_target_pairs={{0,32},{8,40},{16,48},{24,56},{32,0},{40,8},{48,16},{56,24},{64,96... | collective-permute-start | bytes 294920 | tf_op jit(solution)/shard_map/ppermute | solution.py:316
  29.7 1.2 %collective-permute-start.3 = (f32[192,128]{1,0:T(8,128)}, f32[192,128]{1,0:T(8,128)S(1)}, u32[]{:S(2)}, u32[]{:S(2)}) collective-permute-start(f32[192,128]{1,0:T(8,128)} %get-tuple-element.33), channel_id=1, source_target_pairs={{0,48},{8,56},{16,0},{24,8},{32,16},{40,24},{48,32},{56,40},{64,11... | collective-permute-start | bytes 294920 | tf_op jit(solution)/shard_map/ppermute | solution.py:316
  30.9 3.3 %collective-permute-done.1.s1 = f32[192,128]{1,0:T(8,128)S(1)} collective-permute-done((f32[192,128]{1,0:T(8,128)}, f32[192,128]{1,0:T(8,128)S(1)}, u32[]{:S(2)}, u32[]{:S(2)}) %collective-permute-start.1) | collective-permute-done | bytes 98336 | tf_op jit(solution)/shard_map/ppermute | solution.py:316
  34.2 0.4 collective-permute-done.2.s2
  34.6 1.0 collective-permute-done.3.s3
  35.6 0.6 copy-done.12
  36.2 2.2 %row.1 = (f32[192,128]{1,0:T(8,128)}, f32[3,192,128]{2,1,0:T(8,128)}) custom-call(s32[4]{0:T(128)} %pad_add_fusion.pos_ref, f32[192,128]{1,0:T(8,128)} %get-tuple-element.30.s0, f32[192,128]{1,0:T(8,128)} %copy-done.9, f32[192,128]{1,0:T(8,128)} %copy-done.10, f32[192,128]{1,0:T(8,128)} %copy-done.12), custom_call_target="tpu_custom_call" | custom-call | tf_op jit(solution)/shard_map/row/pallas_call | solution.py:270
  38.8 2.6 %collective-permute-start.5 = (f32[192,128]{1,0:T(8,128)}, f32[192,128]{1,0:T(8,128)S(1)}, u32[]{:S(2)}, u32[]{:S(2)}) collective-permute-start(f32[192,128]{1,0:T(8,128)} %get-tuple-element.34.s0), channel_id=1, source_target_pairs={{0,128},{8,136},{16,144},{24,152},{32,160},{40,168},{48,176},{56,1... | collective-permute-start | bytes 294920 | tf_op jit(solution)/shard_map/ppermute | solution.py:321
  41.4 1.1 collective-permute-start.6
  42.5 0.9 collective-permute-done.4.s1
  43.3 1.7 %collective-permute-done.5.s2 = f32[192,128]{1,0:T(8,128)S(1)} collective-permute-done((f32[192,128]{1,0:T(8,128)}, f32[192,128]{1,0:T(8,128)S(1)}, u32[]{:S(2)}, u32[]{:S(2)}) %collective-permute-start.5) | collective-permute-done | bytes 98336 | tf_op jit(solution)/shard_map/ppermute | solution.py:321
  45.0 0.3 collective-permute-done.6.s3
  45.7 0.6 copy-done.14
  46.3 2.1 %column.1 = (f32[192,128]{1,0:T(8,128)}, f32[192,128]{1,0:T(8,128)}) custom-call(s32[4]{0:T(128)} %pad_add_fusion.pos_ref, f32[192,128]{1,0:T(8,128)} %get-tuple-element.34.s0, f32[192,128]{1,0:T(8,128)} %copy-done.11, f32[192,128]{1,0:T(8,128)} %copy-done.13, f32[192,128]{1,0:T(8,128)} %copy-done.14), custom_call_target="tpu_custom_call" | custom-call | tf_op jit(solution)/shard_map/column/pallas_call | solution.py:270
  48.4 2.2 %collective-permute-start.7 = (f32[192,128]{1,0:T(8,128)}, f32[192,128]{1,0:T(8,128)S(1)}, u32[]{:S(2)}, u32[]{:S(2)}) collective-permute-start(f32[192,128]{1,0:T(8,128)} %get-tuple-element.35.own), channel_id=1, source_target_pairs={{0,1},{1,2},{2,3},{3,4},{4,5},{5,6},{6,7},{7,0},{8,9},{9,10},{10,1... | collective-permute-start | bytes 294920 | tf_op jit(solution)/shard_map/ppermute | solution.py:325
  50.6 3.0 %collective-permute-start.8 = (f32[192,128]{1,0:T(8,128)}, f32[192,128]{1,0:T(8,128)S(1)}, u32[]{:S(2)}, u32[]{:S(2)}) collective-permute-start(f32[192,128]{1,0:T(8,128)} %get-tuple-element.35.own), channel_id=1, source_target_pairs={{0,2},{1,3},{2,4},{3,5},{4,6},{5,7},{6,0},{7,1},{8,10},{9,11},{10,... | collective-permute-start | bytes 294920 | tf_op jit(solution)/shard_map/ppermute | solution.py:325
  53.6 3.8 %collective-permute-start.9 = (f32[192,128]{1,0:T(8,128)}, f32[192,128]{1,0:T(8,128)S(1)}, u32[]{:S(2)}, u32[]{:S(2)}) collective-permute-start(f32[192,128]{1,0:T(8,128)} %get-tuple-element.35.own), channel_id=1, source_target_pairs={{0,3},{1,4},{2,5},{3,6},{4,7},{5,0},{6,1},{7,2},{8,11},{9,12},{10,... | collective-permute-start | bytes 294920 | tf_op jit(solution)/shard_map/ppermute | solution.py:325
  57.4 2.7 %collective-permute-done.8.s2 = f32[192,128]{1,0:T(8,128)S(1)} collective-permute-done((f32[192,128]{1,0:T(8,128)}, f32[192,128]{1,0:T(8,128)S(1)}, u32[]{:S(2)}, u32[]{:S(2)}) %collective-permute-start.8) | collective-permute-done | bytes 98336 | tf_op jit(solution)/shard_map/ppermute | solution.py:325
  60.1 5.4 %collective-permute-done.9.s3 = f32[192,128]{1,0:T(8,128)S(1)} collective-permute-done((f32[192,128]{1,0:T(8,128)}, f32[192,128]{1,0:T(8,128)S(1)}, u32[]{:S(2)}, u32[]{:S(2)}) %collective-permute-start.9) | collective-permute-done | bytes 98336 | tf_op jit(solution)/shard_map/ppermute | solution.py:325
  65.5 0.6 copy-done.17
  66.2 2.2 %window.1 = (f32[192,128]{1,0:T(8,128)}, f32[64,128]{1,0:T(8,128)}, f32[64,128]{1,0:T(8,128)}) custom-call(s32[4]{0:T(128)} %pad_add_fusion.pos_ref, f32[192,128]{1,0:T(8,128)} %get-tuple-element.35.own, f32[192,128]{1,0:T(8,128)} %copy-done.15, f32[192,128]{1,0:T(8,128)} %copy-done.16, f32[192,128]{1,0:T(8,128)} %copy-done.17, f32[64,128]{1,0:T(8,128)} %bitcast.32), custom_call_target="tpu_custom_call" | custom-call | tf_op jit(solution)/shard_map/window/pallas_call | solution.py:270
  68.4 4.5 %collective-permute-start.10 = (f32[64,128]{1,0:T(8,128)}, f32[64,128]{1,0:T(8,128)S(1)}, u32[]{:S(2)}, u32[]{:S(2)}) collective-permute-start(f32[64,128]{1,0:T(8,128)} %get-tuple-element.38), channel_id=1, source_target_pairs={{0,4},{1,5},{2,6},{3,7},{4,0},{5,1},{6,2},{7,3},{8,12},{9,13},{10,... | collective-permute-start | bytes 98312 | tf_op jit(solution)/shard_map/ppermute | solution.py:331
  72.9 2.4 %collective-permute-done.10.early_ref = f32[64,128]{1,0:T(8,128)S(1)} collective-permute-done((f32[64,128]{1,0:T(8,128)}, f32[64,128]{1,0:T(8,128)S(1)}, u32[]{:S(2)}, u32[]{:S(2)}) %collective-permute-start.10) | collective-permute-done | bytes 32800 | tf_op jit(solution)/shard_map/ppermute | solution.py:331
  75.3 0.6 copy-done.18
  75.9 2.2 %entry.1 = (f32[64,128]{1,0:T(8,128)}, f32[64,128]{1,0:T(8,128)}, f32[64,128]{1,0:T(8,128)}, f32[64,128]{1,0:T(8,128)}) custom-call(s32[4]{0:T(128)} %pad_add_fusion.pos_ref, f32[192,128]{1,0:T(8,128)} %get-tuple-element.36.win_ref, f32[64,128]{1,0:T(8,128)} %get-tuple-element.37.state_ref, f32[64,128]{1,0:T(8,128)} %copy-done.18, ...), custom_call_target="tpu_custom_call" | custom-call | tf_op jit(solution)/shard_map/entry/pallas_call | solution.py:270
  78.1 0.8 collective-permute-start.11
  79.0 2.3 %collective-permute-start.12 = (f32[64,128]{1,0:T(8,128)}, f32[64,128]{1,0:T(8,128)S(1)}, u32[]{:S(2)}, u32[]{:S(2)}) collective-permute-start(f32[64,128]{1,0:T(8,128)} %get-tuple-element.43), channel_id=1, source_target_pairs={{0,32},{8,40},{16,48},{24,56},{32,0},{40,8},{48,16},{56,24},{64,96... | collective-permute-start | bytes 98312 | tf_op jit(solution)/shard_map/ppermute | solution.py:340
  81.5 0.7 copy.12
  82.3 1.1 %collective-permute-done.12 = f32[64,128]{1,0:T(8,128)S(1)} collective-permute-done((f32[64,128]{1,0:T(8,128)}, f32[64,128]{1,0:T(8,128)S(1)}, u32[]{:S(2)}, u32[]{:S(2)}) %collective-permute-start.12) | collective-permute-done | bytes 32800 | tf_op jit(solution)/shard_map/ppermute | solution.py:340
  83.4 0.8 collective-permute-done.13
  84.2 0.8 pad_maximum_fusion.1
  85.0 7.5 %collective-permute-start.14 = (f32[4,64,128]{2,1,0:T(8,128)S(1)}, f32[4,64,128]{2,1,0:T(8,128)S(1)}, u32[]{:S(2)}, u32[]{:S(2)}) collective-permute-start(f32[4,64,128]{2,1,0:T(8,128)S(1)} %pad_maximum_fusion.1), channel_id=1, source_target_pairs={{0,8},{8,0},{16,24},{24,16},{32,40},{40,32},{48,56},{56,48},{64,72... | collective-permute-start | bytes 393224 | tf_op jit(solution)/shard_map/ppermute | solution.py:360
  92.5 0.8 broadcast_select_fusion.pre_ref
  93.4 9.3 %reach.1 = (f32[4,256,128]{2,1,0:T(8,128)}, f32[4,256,128]{2,1,0:T(8,128)}) custom-call(bf16[4,256,128]{2,1,0:T(8,128)(2,1)} %bitcast.30, bf16[4,512,128]{2,1,0:T(8,128)(2,1)} %bitcast.28, f32[4,4,256,128]{3,2,1,0:T(8,128)} %copy-done.2, f32[4,3,256,128]{3,2,1,0:T(8,128)} %copy-done.3, f32[4,256,128]{2,1,0:T(8,128)} %broadcast_select_fusion.pre_ref), custom_call_target="tpu_custom_call" | custom-call | tf_op jit(solution)/shard_map/reach/pallas_call | solution.py:344
  102.7 0.6 gather_fusion
  103.3 0.8 broadcast_select_fusion.1.state_ref
  104.1 2.5 %read.1 = bf16[4,256,128]{2,1,0:T(8,128)(2,1)} custom-call(f32[4,256,128]{2,1,0:T(8,128)} %get-tuple-element.28.reach_ref, f32[4,256,128]{2,1,0:T(8,128)} %get-tuple-element.29.base_ref, f32[4,128,128]{2,1,0:T(8,128)} %broadcast_select_fusion.1.state_ref, f32[4,128]{1,0:T(4,128)} %gain_ref.1), custom_call_target="tpu_custom_call" | custom-call | tf_op jit(solution)/shard_map/read/pallas_call | solution.py:366
  106.6 1.9 %copy.10 = bf16[1,256,4,128]{3,2,1,0:T(4,128)(2,1)} copy(bf16[1,256,4,128]{3,1,2,0:T(8,128)(2,1)} %bitcast.31) | data formatting | bytes 524288 | tf_op jit(solution)/shard_map/broadcast_in_dim | solution.py:371
  (46 shorter events, 1.3 us)
Async XLA Ops:
  0.0 22.8 %copy-start = (f32[4,128,128]{2,1,0:T(8,128)S(1)}, f32[4,128,128]{2,1,0:T(8,128)}, u32[]{:S(2)}) copy-start(f32[4,128,128]{2,1,0:T(8,128)} %param.9) | copy-start | bytes 786436
  1.5 46.9 %copy-start.1 = (bf16[1,256,2,4,128]{4,2,1,3,0:T(2,128)(2,1)}, bf16[1,256,2,4,128]{4,2,1,3,0:T(2,128)(2,1)S(1)}, u32[]{:S(2)}) copy-start(bf16[1,256,2,4,128]{4,2,1,3,0:T(2,128)(2,1)S(1)} %copy.7) | copy-start | bytes 1572868
  3.1 78.3 %copy-start.7 = (bf16[1,256,4,128]{3,2,1,0:T(4,128)(2,1)S(1)}, bf16[1,256,4,128]{3,2,1,0:T(4,128)(2,1)}, u32[]{:S(2)}) copy-start(bf16[1,256,4,128]{3,2,1,0:T(4,128)(2,1)} %param.5) | copy-start | bytes 786436
  17.0 1.4 %copy-start.2 = (f32[4,4,256,128]{3,2,1,0:T(8,128)}, f32[4,4,256,128]{3,2,1,0:T(8,128)S(1)}, u32[]{:S(2)}) copy-start(f32[4,4,256,128]{3,2,1,0:T(8,128)S(1)} %get-tuple-element.25.z_ref) | copy-start | bytes 6291460
  18.4 1.2 %copy-start.3 = (f32[4,3,256,128]{3,2,1,0:T(8,128)}, f32[4,3,256,128]{3,2,1,0:T(8,128)S(1)}, u32[]{:S(2)}) copy-start(f32[4,3,256,128]{3,2,1,0:T(8,128)S(1)} %get-tuple-element.26.p_ref) | copy-start | bytes 4718596
  19.5 4.8 %copy-start.4 = (f32[4,256,128]{2,1,0:T(8,128)}, f32[4,256,128]{2,1,0:T(8,128)S(1)}, u32[]{:S(2)}) copy-start(f32[4,256,128]{2,1,0:T(8,128)S(1)} %get-tuple-element.27.own_ref) | copy-start | bytes 1572868
  19.5 4.8 %collective-permute-start = (f32[4,256,128]{2,1,0:T(8,128)S(1)}, f32[4,256,128]{2,1,0:T(8,128)S(1)}, u32[]{:S(2)}, u32[]{:S(2)}) collective-permute-start(f32[4,256,128]{2,1,0:T(8,128)S(1)} %get-tuple-element.27.own_ref), channel_id=1, source_target_pairs={{0,8},{8,0},{16,24},{24,16},{32,40},{40,32},{48,56},{56,48},{64,72... | collective-permute-start | bytes 1572872 | tf_op jit(solution)/shard_map/ppermute | solution.py:313
  24.3 0.8 copy-start.5
  27.8 64.7 %copy-start.6 = (f32[4,256,128]{2,1,0:T(8,128)S(1)}, f32[4,256,128]{2,1,0:T(8,128)}, u32[]{:S(2)}) copy-start(f32[4,256,128]{2,1,0:T(8,128)} %copy-done.5) | copy-start | bytes 1572868
  27.8 6.4 %collective-permute-start.1 = (f32[192,128]{1,0:T(8,128)}, f32[192,128]{1,0:T(8,128)S(1)}, u32[]{:S(2)}, u32[]{:S(2)}) collective-permute-start(f32[192,128]{1,0:T(8,128)} %get-tuple-element.31), channel_id=1, source_target_pairs={{0,16},{8,24},{16,32},{24,40},{32,48},{40,56},{48,0},{56,8},{64,80... | collective-permute-start | bytes 294920 | tf_op jit(solution)/shard_map/ppermute | solution.py:316
  27.8 6.8 %collective-permute-start.2 = (f32[192,128]{1,0:T(8,128)}, f32[192,128]{1,0:T(8,128)S(1)}, u32[]{:S(2)}, u32[]{:S(2)}) collective-permute-start(f32[192,128]{1,0:T(8,128)} %get-tuple-element.32), channel_id=1, source_target_pairs={{0,32},{8,40},{16,48},{24,56},{32,0},{40,8},{48,16},{56,24},{64,96... | collective-permute-start | bytes 294920 | tf_op jit(solution)/shard_map/ppermute | solution.py:316
  29.7 5.9 %collective-permute-start.3 = (f32[192,128]{1,0:T(8,128)}, f32[192,128]{1,0:T(8,128)S(1)}, u32[]{:S(2)}, u32[]{:S(2)}) collective-permute-start(f32[192,128]{1,0:T(8,128)} %get-tuple-element.33), channel_id=1, source_target_pairs={{0,48},{8,56},{16,0},{24,8},{32,16},{40,24},{48,32},{56,40},{64,11... | collective-permute-start | bytes 294920 | tf_op jit(solution)/shard_map/ppermute | solution.py:316
  34.2 1.4 %copy-start.9 = (f32[192,128]{1,0:T(8,128)}, f32[192,128]{1,0:T(8,128)S(1)}, u32[]{:S(2)}) copy-start(f32[192,128]{1,0:T(8,128)S(1)} %collective-permute-done.1.s1) | copy-start | bytes 294916
  34.6 1.0 copy-start.10
  35.6 0.6 copy-start.12
  38.4 4.9 %collective-permute-start.4 = (f32[192,128]{1,0:T(8,128)}, f32[192,128]{1,0:T(8,128)S(1)}, u32[]{:S(2)}, u32[]{:S(2)}) collective-permute-start(f32[192,128]{1,0:T(8,128)} %get-tuple-element.34.s0), channel_id=1, source_target_pairs={{0,64},{8,72},{16,80},{24,88},{32,96},{40,104},{48,112},{56,120},{... | collective-permute-start | bytes 294920 | tf_op jit(solution)/shard_map/ppermute | solution.py:321
  38.8 6.3 %collective-permute-start.5 = (f32[192,128]{1,0:T(8,128)}, f32[192,128]{1,0:T(8,128)S(1)}, u32[]{:S(2)}, u32[]{:S(2)}) collective-permute-start(f32[192,128]{1,0:T(8,128)} %get-tuple-element.34.s0), channel_id=1, source_target_pairs={{0,128},{8,136},{16,144},{24,152},{32,160},{40,168},{48,176},{56,1... | collective-permute-start | bytes 294920 | tf_op jit(solution)/shard_map/ppermute | solution.py:321
  41.4 4.0 %collective-permute-start.6 = (f32[192,128]{1,0:T(8,128)}, f32[192,128]{1,0:T(8,128)S(1)}, u32[]{:S(2)}, u32[]{:S(2)}) collective-permute-start(f32[192,128]{1,0:T(8,128)} %get-tuple-element.34.s0), channel_id=1, source_target_pairs={{0,192},{8,200},{16,208},{24,216},{32,224},{40,232},{48,240},{56,2... | collective-permute-start | bytes 294920 | tf_op jit(solution)/shard_map/ppermute | solution.py:321
  43.3 2.0 %copy-start.11 = (f32[192,128]{1,0:T(8,128)}, f32[192,128]{1,0:T(8,128)S(1)}, u32[]{:S(2)}) copy-start(f32[192,128]{1,0:T(8,128)S(1)} %collective-permute-done.4.s1) | copy-start | bytes 294916
  45.0 0.6 copy-start.13
  45.7 0.6 copy-start.14
  48.4 9.0 %collective-permute-start.7 = (f32[192,128]{1,0:T(8,128)}, f32[192,128]{1,0:T(8,128)S(1)}, u32[]{:S(2)}, u32[]{:S(2)}) collective-permute-start(f32[192,128]{1,0:T(8,128)} %get-tuple-element.35.own), channel_id=1, source_target_pairs={{0,1},{1,2},{2,3},{3,4},{4,5},{5,6},{6,7},{7,0},{8,9},{9,10},{10,1... | collective-permute-start | bytes 294920 | tf_op jit(solution)/shard_map/ppermute | solution.py:325
  50.6 9.5 %collective-permute-start.8 = (f32[192,128]{1,0:T(8,128)}, f32[192,128]{1,0:T(8,128)S(1)}, u32[]{:S(2)}, u32[]{:S(2)}) collective-permute-start(f32[192,128]{1,0:T(8,128)} %get-tuple-element.35.own), channel_id=1, source_target_pairs={{0,2},{1,3},{2,4},{3,5},{4,6},{5,7},{6,0},{7,1},{8,10},{9,11},{10,... | collective-permute-start | bytes 294920 | tf_op jit(solution)/shard_map/ppermute | solution.py:325
  53.6 11.9 %collective-permute-start.9 = (f32[192,128]{1,0:T(8,128)}, f32[192,128]{1,0:T(8,128)S(1)}, u32[]{:S(2)}, u32[]{:S(2)}) collective-permute-start(f32[192,128]{1,0:T(8,128)} %get-tuple-element.35.own), channel_id=1, source_target_pairs={{0,3},{1,4},{2,5},{3,6},{4,7},{5,0},{6,1},{7,2},{8,11},{9,12},{10,... | collective-permute-start | bytes 294920 | tf_op jit(solution)/shard_map/ppermute | solution.py:325
  57.4 8.1 %copy-start.15 = (f32[192,128]{1,0:T(8,128)}, f32[192,128]{1,0:T(8,128)S(1)}, u32[]{:S(2)}) copy-start(f32[192,128]{1,0:T(8,128)S(1)} %collective-permute-done.7.s1) | copy-start | bytes 294916
  60.1 5.4 %copy-start.16 = (f32[192,128]{1,0:T(8,128)}, f32[192,128]{1,0:T(8,128)S(1)}, u32[]{:S(2)}) copy-start(f32[192,128]{1,0:T(8,128)S(1)} %collective-permute-done.8.s2) | copy-start | bytes 294916
  65.5 0.6 copy-start.17
  68.4 6.9 %collective-permute-start.10 = (f32[64,128]{1,0:T(8,128)}, f32[64,128]{1,0:T(8,128)S(1)}, u32[]{:S(2)}, u32[]{:S(2)}) collective-permute-start(f32[64,128]{1,0:T(8,128)} %get-tuple-element.38), channel_id=1, source_target_pairs={{0,4},{1,5},{2,6},{3,7},{4,0},{5,1},{6,2},{7,3},{8,12},{9,13},{10,... | collective-permute-start | bytes 98312 | tf_op jit(solution)/shard_map/ppermute | solution.py:331
  75.3 0.6 copy-start.18
  78.1 4.2 %collective-permute-start.11 = (f32[64,128]{1,0:T(8,128)}, f32[64,128]{1,0:T(8,128)S(1)}, u32[]{:S(2)}, u32[]{:S(2)}) collective-permute-start(f32[64,128]{1,0:T(8,128)} %get-tuple-element.42), channel_id=1, source_target_pairs={{0,16},{8,24},{16,32},{24,40},{32,48},{40,56},{48,0},{56,8},{64,80... | collective-permute-start | bytes 98312 | tf_op jit(solution)/shard_map/ppermute | solution.py:340
  79.0 4.5 %collective-permute-start.12 = (f32[64,128]{1,0:T(8,128)}, f32[64,128]{1,0:T(8,128)S(1)}, u32[]{:S(2)}, u32[]{:S(2)}) collective-permute-start(f32[64,128]{1,0:T(8,128)} %get-tuple-element.43), channel_id=1, source_target_pairs={{0,32},{8,40},{16,48},{24,56},{32,0},{40,8},{48,16},{56,24},{64,96... | collective-permute-start | bytes 98312 | tf_op jit(solution)/shard_map/ppermute | solution.py:340
  81.3 3.0 %collective-permute-start.13 = (f32[64,128]{1,0:T(8,128)}, f32[64,128]{1,0:T(8,128)S(1)}, u32[]{:S(2)}, u32[]{:S(2)}) collective-permute-start(f32[64,128]{1,0:T(8,128)} %get-tuple-element.44), channel_id=1, source_target_pairs={{0,48},{8,56},{16,0},{24,8},{32,16},{40,24},{48,32},{56,40},{64,11... | collective-permute-start | bytes 98312 | tf_op jit(solution)/shard_map/ppermute | solution.py:340
  85.0 17.6 %collective-permute-start.14 = (f32[4,64,128]{2,1,0:T(8,128)S(1)}, f32[4,64,128]{2,1,0:T(8,128)S(1)}, u32[]{:S(2)}, u32[]{:S(2)}) collective-permute-start(f32[4,64,128]{2,1,0:T(8,128)S(1)} %pad_maximum_fusion.1), channel_id=1, source_target_pairs={{0,8},{8,0},{16,24},{24,16},{32,40},{40,32},{48,56},{56,48},{64,72... | collective-permute-start | bytes 393224 | tf_op jit(solution)/shard_map/ppermute | solution.py:360
  93.4 9.3 %copy-start.8 = (f32[64,128]{1,0:T(8,128)S(1)}, f32[64,128]{1,0:T(8,128)}, u32[]{:S(2)}) copy-start(f32[64,128]{1,0:T(8,128)} %get-tuple-element.41) | copy-start | bytes 98308

commit v2 on v1

v2 whole, which is shorter than its diff:
```python
import functools

import jax
import jax.numpy as jnp
from jax import lax
from jax.experimental import pallas as pl
from jax.experimental.pallas import tpu as pltpu
from jax.sharding import PartitionSpec as P

D = 128
HEADS = 4
REFL = 2
BLK = 128
XS = 4
YS = 4
CS = 2
HALF = D // CS
MSG = D + HALF

f32 = jnp.float32
bf16 = jnp.bfloat16


def split(x):
    high = x.astype(bf16)
    low = (x - high.astype(f32)).astype(bf16)
    return high, low


def dot_nn(a, b):
    return lax.dot_general(a, b, (((1,), (0,)), ((), ())), preferred_element_type=f32)


def dot_nt(a, b):
    return lax.dot_general(a, b, (((1,), (1,)), ((), ())), preferred_element_type=f32)


def wide(x):
    high, low = split(x)
    return jnp.concatenate([high, low], axis=1)


def tall_wide(x):
    row = wide(x)
    return jnp.concatenate([row, row], axis=0)


def mm_pre(left_wide, right_tall):
    out = dot_nn(left_wide, right_tall)
    n = out.shape[1] // 2
    return out[:, :n] + out[:, n:]


def mm(a, b):
    return mm_pre(wide(a), tall_wide(b))


def mm_nt(a, b):
    ah, al = split(a)
    bh, bl = split(b)
    return dot_nt(ah, bh) + dot_nt(ah, bl) + dot_nt(al, bh)


def iota2(shape, dim):
    return lax.broadcasted_iota(jnp.int32, shape, dim)


def factor_kernel(k_ref, v_ref, m_ref, z_ref, p_ref, r_ref, keys, values):
    keys[...] = k_ref[...].astype(f32)
    values[...] = v_ref[...].astype(f32)
    nblk = r_ref.shape[1] // BLK
    row = iota2((BLK, BLK), 0)
    col = iota2((BLK, BLK), 1)
    eye = row == col
    chains = [(h, b) for h in range(HEADS) for b in range(nblk)]
    rs, rts, vts, uppers, invs, ccols, crows = [], [], [], [], [], [], []
    for h, b in chains:
        rows = pl.ds(h + HEADS * BLK * b, BLK, stride=HEADS)
        r = keys[rows, :].astype(bf16)
        v = values[rows, :].astype(bf16)
        r_ref[h, b * BLK : (b + 1) * BLK, :] = r
        rt = r.T
        gram = dot_nn(r, rt)
        diag = jnp.where(eye, gram, 0.0)
        ccol = lax.rsqrt(jnp.sum(diag, axis=1, keepdims=True) + 1e-06)
        crow = lax.rsqrt(jnp.sum(diag, axis=0, keepdims=True) + 1e-06)
        upper = jnp.where(row < col, 2.0 * ccol * crow * gram, 0.0)
        pair = ((row >> 1) == (col >> 1)) & (row < col)
        inv = jnp.where(eye, 1.0, 0.0) - jnp.where(pair, upper, 0.0)
        rs.append(r)
        rts.append(rt)
        vts.append(v.T)
        uppers.append(upper)
        invs.append(inv)
        ccols.append(ccol)
        crows.append(crow)
    for level in range(1, 7):
        off = ((row >> (level + 1)) == (col >> (level + 1))) & (
            (row >> level) < (col >> level)
        )
        talls = [tall_wide(inv) for inv in invs]
        mids = [
            mm_pre(wide(jnp.where(off, upper, 0.0)), tall) for upper, tall in zip(uppers, talls)
        ]
        invs = [inv - mm(inv, mid) for inv, mid in zip(invs, mids)]
    pairs = []
    base = jnp.where(iota2((2 * D, D), 0) == iota2((2 * D, D), 1), 1.0, 0.0)
    sign = jnp.where(iota2((2 * D, D), 0) < D, -1.0, 1.0)
    for i, (h, b) in enumerate(chains):
        wh, wl = split(2.0 * ccols[i] * invs[i])
        uh, ul = split(2.0 * invs[i])
        wt = dot_nn(jnp.concatenate([rts[i], rts[i]], axis=1), jnp.concatenate([wh, wl], axis=0))
        ut = dot_nn(jnp.concatenate([vts[i], vts[i]], axis=1), jnp.concatenate([uh, ul], axis=0))
        z = jnp.concatenate([wt, ut], axis=0) * crows[i]
        z_ref[h, b] = z
        rr = jnp.concatenate([rs[i], rs[i]], axis=0)
        pairs.append(base + sign * dot_nn(wide(z), rr))
    for h in range(HEADS):
        own = pairs[h * nblk : (h + 1) * nblk]
        for b in range(nblk - 1):
            p_ref[h, b] = own[b]
        while len(own) > 1:
            own = [compose(own[i], own[i + 1]) for i in range(0, len(own), 2)]
        m_ref[h] = own[0]


def compose(first, second):
    moved = mm(first, second[:D])
    keep = jnp.concatenate([jnp.zeros((D, D), f32), second[D:]], axis=0)
    return moved + keep


def whole(*arrays):
    return [pl.BlockSpec(memory_space=pltpu.VMEM)] * len(arrays)


def factor_call(k, v):
    steps = k.shape[0] // HEADS
    nblk = steps // BLK
    return pl.pallas_call(
        factor_kernel,
        in_specs=whole(k, v),
        out_specs=[pl.BlockSpec(memory_space=pltpu.VMEM)] * 4,
        out_shape=[
            jax.ShapeDtypeStruct((HEADS, 2 * D, D), f32),
            jax.ShapeDtypeStruct((HEADS, nblk, 2 * D, D), f32),
            jax.ShapeDtypeStruct((HEADS, nblk - 1, 2 * D, D), f32),
            jax.ShapeDtypeStruct((HEADS, steps, D), bf16),
        ],
        scratch_shapes=[pltpu.VMEM((HEADS * steps, D), f32)] * 2,
        compiler_params=pltpu.CompilerParams(vmem_limit_bytes=40 << 20),
        name="factor",
    )(k, v)


def chip_kernel(pos_ref, own_ref, sib_ref, *out_refs):
    x = pos_ref[0]
    core = pos_ref[2]
    half = pl.ds(pl.multiple_of(D + core * HALF, HALF), HALF)
    lower = core == 0
    for k in range(XS):
        head = lax.rem(x + k, HEADS)
        own_t, sib_t = own_ref[head, :D, :], sib_ref[head, :D, :]
        own_s, sib_s = own_ref[head, half, :], sib_ref[head, half, :]
        rows = jnp.concatenate(
            [jnp.where(lower, own_t, sib_t), jnp.where(lower, own_s, sib_s)], axis=0
        )
        moved = mm(rows, jnp.where(lower, sib_t, own_t))
        out_refs[k][:D, :] = moved[:D]
        out_refs[k][D:, :] = moved[D:] + jnp.where(lower, sib_s, own_s)


def ordered_load(slots, place, scratch):
    n = len(slots)
    for k in range(n):
        scratch[lax.rem(place + n - k, n)] = slots[k][...]


def msg_compose(rows, second):
    moved = mm(rows, second[:D])
    return jnp.concatenate([moved[:D], moved[D:] + second[D:]], axis=0)


def advance(state, second):
    return mm(state, second[:D]) + second[D:]


def prefix_totals(slots, place, total_ref, pre_ref, scratch):
    ordered_load(slots, place, scratch)
    first = scratch[0]
    tail = msg_compose(scratch[2], scratch[3])
    second = msg_compose(first, scratch[1])
    total_ref[...] = msg_compose(second, tail)
    pre_ref[0] = first
    pre_ref[1] = second
    pre_ref[2] = msg_compose(second, scratch[2])


def row_kernel(pos_ref, s0, s1, s2, s3, total_ref, pre_ref, scratch):
    prefix_totals([s0, s1, s2, s3], pos_ref[0], total_ref, pre_ref, scratch)


def column_kernel(pos_ref, s0, s1, s2, s3, total_ref, pre_ref, scratch):
    prefix_totals([s0, s1, s2, s3], pos_ref[1], total_ref, pre_ref, scratch)


def path_kernel(pos_ref, ypre_ref, xpre_ref, init_ref, after_ref, path_ref, start_ref, hold):
    x = pos_ref[0]
    y = pos_ref[1]
    core = pos_ref[2]
    here = ypre_ref[lax.max(y, 1) - 1]
    here = jnp.where(
        y == 0, jnp.where(iota2((MSG, D), 0) == iota2((MSG, D), 1), 1.0, 0.0), here
    )
    path_ref[0] = here
    left = wide(here)
    for i in range(XS - 1):
        moved = mm_pre(left, tall_wide(xpre_ref[i, :D, :]))
        path_ref[i + 1, :D, :] = moved[:D]
        path_ref[i + 1, D:, :] = moved[D:] + xpre_ref[i, D:, :]
    hold[...] = init_ref[x].T
    start_ref[...] = hold[pl.ds(pl.multiple_of(core * HALF, HALF), HALF), :]


def early_states(g, s2, s3, start):
    state = jnp.where(g >= 3, advance(start, s3), start)
    return jnp.where(g >= 2, advance(state, s2), state)


def lead_kernel(pos_ref, own, s1, s2, s3, start_ref, lead_ref):
    g = pos_ref[3]
    state = early_states(g, s2[...], s3[...], start_ref[...])
    step = jnp.where(g >= 1, msg_compose(s1[...], own[...]), own[...])
    lead_ref[...] = advance(state, step)


def fuse_kernel(pos_ref, s1, s2, s3, start_ref, path_ref, after_ref, fuse_ref, state_ref):
    g = pos_ref[3]
    state = early_states(g, s2[...], s3[...], start_ref[...])
    state_ref[...] = jnp.where(g >= 1, advance(state, s1[...]), state)
    window = msg_compose(msg_compose(s3[...], s2[...]), s1[...])
    left = wide(window)
    for i in range(XS):
        path = path_ref[i]
        moved = mm_pre(left, tall_wide(path[:D]))
        moved = jnp.concatenate([moved[:D], moved[D:] + path[D:]], axis=0)
        fuse_ref[i] = jnp.where(g >= 4, moved, path)


def entry_kernel(pos_ref, state_ref, early_ref, fuse_ref, after_ref, o0, o1, o2, o3, scratch):
    x = pos_ref[0]
    state = jnp.where(pos_ref[3] >= 4, early_ref[...], state_ref[...])
    left = wide(state)
    for i in range(XS):
        scratch[i] = mm_pre(left, tall_wide(fuse_ref[i, :D, :])) + fuse_ref[i, D:, :]
    for k, out in enumerate((o0, o1, o2, o3)):
        out[...] = scratch[lax.rem(x + k, XS)]


def reach_kernel(pos_ref, q_ref, r_ref, z_ref, p_ref, sib_ref, after_ref, reach_ref, base_ref, rows, *, head):
    tokens = reach_ref.shape[1]
    nblk = z_ref.shape[1]
    span = tokens // nblk
    group = reach_ref.shape[0]
    rows[...] = q_ref[...].astype(f32)
    visible = iota2((span, BLK), 1) <= REFL * iota2((span, BLK), 0) + (REFL - 1)
    base = jnp.where(iota2((2 * D, D), 0) == iota2((2 * D, D), 1), 1.0, 0.0)
    prefixes = [jnp.where(pos_ref[2] == 1, sib_ref[h], base) for h in range(group)]
    for b in range(nblk):
        for h in range(group):
            part = slice(b * span, (b + 1) * span)
            q = rows[pl.ds(head + h + HEADS * span * b, span, stride=HEADS), :]
            scores = dot_nt(q.astype(bf16), r_ref[h, b * BLK : (b + 1) * BLK, :])
            sz = mm_nt(jnp.where(visible, scores, 0.0), z_ref[h, b])
            project = q - sz[:, :D]
            moved = mm_nt(project, prefixes[h])
            reach_ref[h, part, :] = moved[:, :D]
            base_ref[h, part, :] = moved[:, D:] + sz[:, D:]
            if b + 1 < nblk:
                prefixes[h] = compose(prefixes[h], p_ref[h, b])


def reach_call(pos, q, r, z, p, sib, after, head, group):
    tokens = q.shape[0] // HEADS
    place = head // group

    def spec(array):
        rest = array.shape[1:]
        return pl.BlockSpec((group, *rest), lambda i: (place,) + (0,) * len(rest))

    return pl.pallas_call(
        functools.partial(reach_kernel, head=head),
        grid=(1,),
        in_specs=[
            pl.BlockSpec(memory_space=pltpu.SMEM),
            pl.BlockSpec(q.shape, lambda i: (0, 0)),
            spec(r),
            spec(z),
            spec(p),
            spec(sib),
            pl.BlockSpec(memory_space=pl.ANY),
        ],
        out_specs=[pl.BlockSpec((group, tokens, D), lambda i: (0, 0, 0))] * 2,
        out_shape=[jax.ShapeDtypeStruct((group, tokens, D), f32)] * 2,
        scratch_shapes=[pltpu.VMEM(q.shape, f32)],
        compiler_params=pltpu.CompilerParams(vmem_limit_bytes=16 << 20),
        cost_estimate=pl.CostEstimate(flops=400_000_000 * group, bytes_accessed=3_000_000 * group, transcendentals=0),
        name="reach",
    )(pos, q, r, z, p, sib, after)


def read_kernel(pos_ref, ra, ba, rb, bb, mine_ref, other_ref, gain_ref, out_ref, rows):
    x = pos_ref[0]
    lower = pos_ref[2] == 0
    tokens = ra.shape[1]
    group = ra.shape[0]
    for h in range(HEADS):
        reach, base = (ra, ba) if h < group else (rb, bb)
        slot = lax.rem(x + HEADS - h, HEADS)
        mine, other = mine_ref[slot], other_ref[slot]
        state = jnp.concatenate(
            [jnp.where(lower, mine, other), jnp.where(lower, other, mine)], axis=0
        )
        read = mm_nt(reach[h % group], state) + base[h % group]
        scale = lax.rsqrt(jnp.mean(read * read, axis=-1, keepdims=True) + 1e-06)
        rows[pl.ds(h, tokens, stride=HEADS), :] = read * scale * gain_ref[h : h + 1, :]
    out_ref[...] = rows[...].astype(bf16)


def small_call(kernel, name, pos, arrays, outs, scratch=(), after=None, limit=4, out_dtype=f32):
    extra = [] if after is None else [after]
    return pl.pallas_call(
        kernel,
        in_specs=[pl.BlockSpec(memory_space=pltpu.SMEM)]
        + whole(*arrays)
        + [pl.BlockSpec(memory_space=pl.ANY)] * len(extra),
        out_specs=whole(*outs),
        out_shape=[jax.ShapeDtypeStruct(s, out_dtype) for s in outs],
        scratch_shapes=[pltpu.VMEM(s, f32) for s in scratch],
        compiler_params=pltpu.CompilerParams(vmem_limit_bytes=limit << 20),
        name=name,
    )(pos, *arrays, *extra)


def seq_perm(move):
    pairs = []
    for y in range(YS):
        for x in range(XS):
            for c in range(CS):
                ny, nx, nc = move(y, x, c)
                pairs.append(((y * XS + x) * CS + c, (ny * XS + nx) * CS + nc))
    return pairs


def per_device(query_rows, key_rows, value_rows, out_gain, initial_state):
    tokens = query_rows.shape[1]
    steps = tokens * REFL
    place = lax.axis_index("seq")
    seg = lax.axis_index("seg")
    core = place % CS
    x = (place // CS) % XS
    y = place // (CS * XS)
    pos = jnp.stack([x, y, core, seg]).astype(jnp.int32)

    swap = seq_perm(lambda y, x, c: (y, x, 1 - c))
    along_x = [seq_perm(lambda y, x, c, k=k: (y, (x + k) % XS, c)) for k in range(1, XS)]
    along_y = [seq_perm(lambda y, x, c, k=k: ((y + k) % YS, x, c)) for k in range(1, YS)]
    segs = 8
    along_z = [[(i, (i + k) % segs) for i in range(segs)] for k in range(1, 4)]
    jump = [(i, (i + 4) % segs) for i in range(segs)]

    keys = key_rows.reshape(steps * HEADS, D)
    values = value_rows.reshape(steps * HEADS, D)
    query = query_rows.reshape(tokens * HEADS, D)
    pair, z, parts, r = factor_call(keys, values)
    sib = lax.ppermute(pair, "seq", swap)
    slots = small_call(chip_kernel, "chip", pos, [pair, sib], [(MSG, D)] * XS)
    slots = [slots[0]] + [lax.ppermute(s, "seq", p) for s, p in zip(slots[1:], along_x)]
    total, xpre = small_call(
        row_kernel, "row", pos, slots, [(MSG, D), (XS - 1, MSG, D)], [(XS, MSG, D)]
    )
    slots = [total] + [lax.ppermute(total, "seq", p) for p in along_y]
    total, ypre = small_call(
        column_kernel, "column", pos, slots, [(MSG, D), (YS - 1, MSG, D)], [(YS, MSG, D)]
    )
    slots = [lax.ppermute(total, "seg", p) for p in along_z]
    path, start = small_call(
        path_kernel,
        "path",
        pos,
        [ypre, xpre, initial_state],
        [(XS, MSG, D), (HALF, D)],
        [(D, D)],
        after=total,
    )
    reach_a, base_a = reach_call(pos, query, r, z, parts, sib, path, 0, 2)
    (lead,) = small_call(
        lead_kernel, "lead", pos, [total, *slots, start], [(HALF, D)]
    )
    early = lax.ppermute(lead, "seg", jump)
    fused, state = small_call(
        fuse_kernel, "fuse", pos, [*slots, start, path], [(XS, MSG, D), (HALF, D)], after=lead
    )
    reach_b, base_b = reach_call(pos, query, r, z, parts, sib, lead, 2, 2)
    slots = small_call(
        entry_kernel,
        "entry",
        pos,
        [state, early, fused],
        [(HALF, D)] * XS,
        [(XS, HALF, D)],
        after=reach_b,
    )
    slots = [slots[0]] + [lax.ppermute(s, "seq", p) for s, p in zip(slots[1:], along_x)]
    mine = jnp.stack(slots)
    other = lax.ppermute(mine, "seq", swap)
    (out,) = small_call(
        read_kernel,
        "read",
        pos,
        [reach_a, base_a, reach_b, base_b, mine, other, out_gain],
        [(tokens * HEADS, D)],
        [(tokens * HEADS, D)],
        limit=8,
        out_dtype=bf16,
    )
    return out.reshape(1, tokens, HEADS, D)


def solution(mesh):
    return jax.shard_map(
        per_device,
        mesh=mesh,
        in_specs=(
            P("seg", "seq", None, None),
            P("seg", "seq", None, None, None),
            P("seg", "seq", None, None, None),
            P(),
            P(),
        ),
        out_specs=P("seg", "seq", None, None),
        check_vma=False,
    )
```

time: 109 us -> 80.2 us (0.74)
  Pallas kernels: 37.1 us -> 24.3 us
  local copies, waits for them, and re-layouts: 13.2 us -> 4.24 us
  starting transfers between devices: 34.6 us -> 29 us
  other arithmetic: 3.06 us -> 0.09 us
  waiting for transfers between devices: 20.3 us -> 22.2 us
    pallas_call x3, Pallas kernels: 25.6 us -> 15.5 us  [the longest x2 7.75 us: reach_call(): pl.pallas_call(functools.partial(reach_kernel, head=head), grid=(1,), in_...]
    unnamed x41 -> x14, local copies, waits for them, and re-layouts: 10 us -> 4.24 us
    ppermute x1, starting transfers between devices: 7.52 us -> 3.69 us  [per_device(): other = lax.ppermute(mine, 'seq', swap)]
    pallas_call x5 -> x8, Pallas kernels: 11.5 us -> 8.8 us  [small_call(): pl.pallas_call(kernel, in_specs=[pl.BlockSpec(memory_space=pltpu.SMEM)] +...]
    ppermute x3, waiting for transfers between devices: 2.89 us -> 5.36 us  [per_device(): slots = [total] + [lax.ppermute(total, 'seq', p) for p in along_y]]
    broadcast_in_dim x1 -> x0, local copies, waits for them, and re-layouts: 1.86 us -> none  [per_device(): return out.transpose(1, 0, 2)[None]]
    ppermute x4, waiting for transfers between devices: 10.5 us -> 8.69 us  [the longest x3 8.69 us: per_device(): slots = [lax.ppermute(total, 'seg', p) for p in along_z]]
    select_n x4 -> x0, other arithmetic: 1.65 us -> none  [the longest x1 0.82 us: per_device(): before = jnp.where(core == 1, sib, jnp.broadcast_to(eye_pair, sib.shape))]
  transfers between devices with their start and end apart: 15 -> 15, of which waited for: 13 -> 12; matrix products, arithmetic and copies ran while one was open for 3% -> 0% of each run, Pallas kernels for 9% -> 12%
where the time goes in v2:
time: 80.2 us; the launch traced here: 79.9 us
  starting transfers between devices  29 us (36%)
  Pallas kernels  24.3 us (30%)
  waiting for transfers between devices  22.2 us (28%)
  local copies, waits for them, and re-layouts  4.24 us (5%)
    pallas_call x8, Pallas kernels, small_call(): pl.pallas_call(kernel, in_specs=[pl.BlockSpec(memory_space=pltpu.SMEM)] +...  8.8 us
    ppermute x3, waiting for transfers between devices, per_device(): slots = [lax.ppermute(total, 'seg', p) for p in along_z]  8.69 us
    ppermute x3, starting transfers between devices, per_device(): slots = [lax.ppermute(total, 'seg', p) for p in along_z]  8.45 us
    pallas_call x2, Pallas kernels, reach_call(): pl.pallas_call(functools.partial(reach_kernel, head=head), grid=(1,), in_...  7.75 us
    pallas_call x1, Pallas kernels, factor_call(): pl.pallas_call(factor_kernel, in_specs=whole(k, v), out_specs=[pl.BlockSp...  7.72 us
    ppermute x6, waiting for transfers between devices, per_device(): lax.ppermute(s, 'seq', p)  6.42 us
    ppermute x6, starting transfers between devices, per_device(): lax.ppermute(s, 'seq', p)  6.19 us
    ppermute x3, waiting for transfers between devices, per_device(): slots = [total] + [lax.ppermute(total, 'seq', p) for p in along_y]  5.36 us
  transfers between devices with their start and end apart: 15, of which 12 were waited for; matrix products, arithmetic and copies ran while one was open for 0% of the time, Pallas kernels for 12%

profile of v2, /device:TPU:1, one launch (start us, length us, event | category | flops | bytes accessed | tf_op | source)
XLA Modules:
  0.0 79.9 jit_solution(9507114097467416270)
XLA Ops:
  0.0 1.0 %copy-done.3 = bf16[1,256,2,4,128]{4,3,2,1,0:T(4,128)(2,1)S(1)} copy-done((bf16[1,256,2,4,128]{4,3,2,1,0:T(4,128)(2,1)S(1)}, bf16[1,256,2,4,128]{4,3,2,1,0:T(4,128)(2,1)}, u32[]{:S(2)}) %copy-start.3) | copy-done | bytes 524312
  1.0 1.0 %copy-done.4 = bf16[1,256,2,4,128]{4,3,2,1,0:T(4,128)(2,1)S(1)} copy-done((bf16[1,256,2,4,128]{4,3,2,1,0:T(4,128)(2,1)S(1)}, bf16[1,256,2,4,128]{4,3,2,1,0:T(4,128)(2,1)}, u32[]{:S(2)}) %copy-start.4) | copy-done | bytes 524312
  2.1 7.7 %factor.1 = (f32[4,256,128]{2,1,0:T(8,128)}, f32[4,4,256,128]{3,2,1,0:T(8,128)S(1)}, f32[4,3,256,128]{3,2,1,0:T(8,128)S(1)}, bf16[4,512,128]{2,1,0:T(8,128)(2,1)S(1)}) custom-call(bf16[2048,128]{1,0:T(8,128)(2,1)S(1)} %bitcast.14, bf16[2048,128]{1,0:T(8,128)(2,1)S(1)} %bitcast.15), custom_call_target="tpu_custom_call" | custom-call | tf_op jit(solution)/shard_map/factor/pallas_call | solution.py:140
  9.8 1.2 %copy-done = f32[4,3,256,128]{3,2,1,0:T(8,128)} copy-done((f32[4,3,256,128]{3,2,1,0:T(8,128)}, f32[4,3,256,128]{3,2,1,0:T(8,128)S(1)}, u32[]{:S(2)}) %copy-start) | copy-done | bytes 1572888
  11.0 3.2 %collective-permute-start = (f32[4,256,128]{2,1,0:T(8,128)}, f32[4,256,128]{2,1,0:T(8,128)S(1)}, u32[]{:S(2)}, u32[]{:S(2)}) collective-permute-start(f32[4,256,128]{2,1,0:T(8,128)} %get-tuple-element.32.own_ref), channel_id=1, source_target_pairs={{0,8},{8,0},{16,24},{24,16},{32,40},{40,32},{48,56},{56,48},{64,72... | collective-permute-start | bytes 1572872 | tf_op jit(solution)/shard_map/ppermute | solution.py:376
  14.2 0.1 pad_add_fusion.pos_ref
  14.3 1.7 %collective-permute-done.sib_ref = f32[4,256,128]{2,1,0:T(8,128)S(1)} collective-permute-done((f32[4,256,128]{2,1,0:T(8,128)}, f32[4,256,128]{2,1,0:T(8,128)S(1)}, u32[]{:S(2)}, u32[]{:S(2)}) %collective-permute-start) | collective-permute-done | bytes 524320 | tf_op jit(solution)/shard_map/ppermute | solution.py:376
  16.0 1.3 %chip.1 = (f32[192,128]{1,0:T(8,128)S(1)}, f32[192,128]{1,0:T(8,128)S(1)}, f32[192,128]{1,0:T(8,128)S(1)}, f32[192,128]{1,0:T(8,128)S(1)}) custom-call(s32[4]{0:T(128)S(1)} %pad_add_fusion.pos_ref, f32[4,256,128]{2,1,0:T(8,128)} %get-tuple-element.32.own_ref, f32[4,256,128]{2,1,0:T(8,128)S(1)} %collective-permute-done.sib_ref), custom_call_target="tpu_custom_call" | custom-call | tf_op jit(solution)/shard_map/chip/pallas_call | solution.py:332
  17.3 0.1 collective-permute-start.1
  17.4 1.9 %collective-permute-start.2 = (f32[192,128]{1,0:T(8,128)S(1)}, f32[192,128]{1,0:T(8,128)S(1)}, u32[]{:S(2)}, u32[]{:S(2)}) collective-permute-start(f32[192,128]{1,0:T(8,128)S(1)} %get-tuple-element.35), channel_id=1, source_target_pairs={{0,32},{8,40},{16,48},{24,56},{32,0},{40,8},{48,16},{56,24},{64,96... | collective-permute-start | bytes 294920 | tf_op jit(solution)/shard_map/ppermute | solution.py:378
  19.3 1.2 %collective-permute-start.3 = (f32[192,128]{1,0:T(8,128)S(1)}, f32[192,128]{1,0:T(8,128)S(1)}, u32[]{:S(2)}, u32[]{:S(2)}) collective-permute-start(f32[192,128]{1,0:T(8,128)S(1)} %get-tuple-element.36), channel_id=1, source_target_pairs={{0,48},{8,56},{16,0},{24,8},{32,16},{40,24},{48,32},{56,40},{64,11... | collective-permute-start | bytes 294920 | tf_op jit(solution)/shard_map/ppermute | solution.py:378
  20.5 3.1 %collective-permute-done.1.s1 = f32[192,128]{1,0:T(8,128)S(1)} collective-permute-done((f32[192,128]{1,0:T(8,128)S(1)}, f32[192,128]{1,0:T(8,128)S(1)}, u32[]{:S(2)}, u32[]{:S(2)}) %collective-permute-start.1) | collective-permute-done | bytes 98336 | tf_op jit(solution)/shard_map/ppermute | solution.py:378
  23.6 0.4 collective-permute-done.2.s2
  24.0 1.0 %collective-permute-done.3.s3 = f32[192,128]{1,0:T(8,128)S(1)} collective-permute-done((f32[192,128]{1,0:T(8,128)S(1)}, f32[192,128]{1,0:T(8,128)S(1)}, u32[]{:S(2)}, u32[]{:S(2)}) %collective-permute-start.3) | collective-permute-done | bytes 98336 | tf_op jit(solution)/shard_map/ppermute | solution.py:378
  25.0 1.0 %row.1 = (f32[192,128]{1,0:T(8,128)S(1)}, f32[3,192,128]{2,1,0:T(8,128)S(1)}) custom-call(s32[4]{0:T(128)S(1)} %pad_add_fusion.pos_ref, f32[192,128]{1,0:T(8,128)S(1)} %get-tuple-element.33.s0, f32[192,128]{1,0:T(8,128)S(1)} %collective-permute-done.1.s1, f32[192,128]{1,0:T(8,128)S(1)} %collective-permute-done.2.s2, f32[192,128]{1,0:T(8,128)S(1)} %collective-permute-done.3.s3), custom_call_target="tpu_custom_call" | custom-call | tf_op jit(solution)/shard_map/row/pallas_call | solution.py:332
  26.0 1.8 %collective-permute-start.6 = (f32[192,128]{1,0:T(8,128)S(1)}, f32[192,128]{1,0:T(8,128)S(1)}, u32[]{:S(2)}, u32[]{:S(2)}) collective-permute-start(f32[192,128]{1,0:T(8,128)S(1)} %get-tuple-element.37.s0), channel_id=1, source_target_pairs={{0,192},{8,200},{16,208},{24,216},{32,224},{40,232},{48,240},{56,2... | collective-permute-start | bytes 294920 | tf_op jit(solution)/shard_map/ppermute | solution.py:382
  27.8 0.4 collective-permute-start.5
  28.1 0.7 collective-permute-start.4
  28.8 0.7 collective-permute-done.6.s3
  29.5 3.3 %collective-permute-done.5.s2 = f32[192,128]{1,0:T(8,128)S(1)} collective-permute-done((f32[192,128]{1,0:T(8,128)S(1)}, f32[192,128]{1,0:T(8,128)S(1)}, u32[]{:S(2)}, u32[]{:S(2)}) %collective-permute-start.5) | collective-permute-done | bytes 98336 | tf_op jit(solution)/shard_map/ppermute | solution.py:382
  32.8 1.3 %collective-permute-done.4.s1 = f32[192,128]{1,0:T(8,128)S(1)} collective-permute-done((f32[192,128]{1,0:T(8,128)S(1)}, f32[192,128]{1,0:T(8,128)S(1)}, u32[]{:S(2)}, u32[]{:S(2)}) %collective-permute-start.4) | collective-permute-done | bytes 98336 | tf_op jit(solution)/shard_map/ppermute | solution.py:382
  34.2 1.0 %column.1 = (f32[192,128]{1,0:T(8,128)S(1)}, f32[3,192,128]{2,1,0:T(8,128)S(1)}) custom-call(s32[4]{0:T(128)S(1)} %pad_add_fusion.pos_ref, f32[192,128]{1,0:T(8,128)S(1)} %get-tuple-element.37.s0, f32[192,128]{1,0:T(8,128)S(1)} %collective-permute-done.4.s1, f32[192,128]{1,0:T(8,128)S(1)} %collective-permute-done.5.s2, f32[192,128]{1,0:T(8,128)S(1)} %collective-permute-done.6.s3), custom_call_target="tpu_custom_call" | custom-call | tf_op jit(solution)/shard_map/column/pallas_call | solution.py:332
  35.1 4.4 %collective-permute-start.9 = (f32[192,128]{1,0:T(8,128)S(1)}, f32[192,128]{1,0:T(8,128)S(1)}, u32[]{:S(2)}, u32[]{:S(2)}) collective-permute-start(f32[192,128]{1,0:T(8,128)S(1)} %get-tuple-element.40.after_ref.own), channel_id=1, source_target_pairs={{0,3},{1,4},{2,5},{3,6},{4,7},{5,0},{6,1},{7,2},{8,11},{9,12},{10,... | collective-permute-start | bytes 294920 | tf_op jit(solution)/shard_map/ppermute | solution.py:386
  39.6 3.3 %collective-permute-start.8 = (f32[192,128]{1,0:T(8,128)S(1)}, f32[192,128]{1,0:T(8,128)S(1)}, u32[]{:S(2)}, u32[]{:S(2)}) collective-permute-start(f32[192,128]{1,0:T(8,128)S(1)} %get-tuple-element.40.after_ref.own), channel_id=1, source_target_pairs={{0,2},{1,3},{2,4},{3,5},{4,6},{5,7},{6,0},{7,1},{8,10},{9,11},{10,... | collective-permute-start | bytes 294920 | tf_op jit(solution)/shard_map/ppermute | solution.py:386
  42.9 0.7 collective-permute-start.7
  43.6 0.9 %copy-done.5 = f32[4,128,128]{2,1,0:T(8,128)S(1)} copy-done((f32[4,128,128]{2,1,0:T(8,128)S(1)}, f32[4,128,128]{2,1,0:T(8,128)}, u32[]{:S(2)}) %copy-start.5) | copy-done | bytes 262168
  44.5 0.8 path.1
  45.3 0.0 collective-permute-done.9.s3
  45.3 5.6 %collective-permute-done.8.s2 = f32[192,128]{1,0:T(8,128)S(1)} collective-permute-done((f32[192,128]{1,0:T(8,128)S(1)}, f32[192,128]{1,0:T(8,128)S(1)}, u32[]{:S(2)}, u32[]{:S(2)}) %collective-permute-start.8) | collective-permute-done | bytes 98336 | tf_op jit(solution)/shard_map/ppermute | solution.py:386
  51.0 3.1 %collective-permute-done.7.s1 = f32[192,128]{1,0:T(8,128)S(1)} collective-permute-done((f32[192,128]{1,0:T(8,128)S(1)}, f32[192,128]{1,0:T(8,128)S(1)}, u32[]{:S(2)}, u32[]{:S(2)}) %collective-permute-start.7) | collective-permute-done | bytes 98336 | tf_op jit(solution)/shard_map/ppermute | solution.py:386
  54.0 0.9 %lead.1.after_ref = f32[64,128]{1,0:T(8,128)S(1)} custom-call(s32[4]{0:T(128)S(1)} %pad_add_fusion.pos_ref, f32[192,128]{1,0:T(8,128)S(1)} %get-tuple-element.40.after_ref.own, f32[192,128]{1,0:T(8,128)S(1)} %collective-permute-done.7.s1, f32[192,128]{1,0:T(8,128)S(1)} %collective-permute-done.8.s2, f32[192,128]{1,0:T(8,128)S(1)} %collective-permute-done.9.s3, ...), custom_call_target="tpu_custom_call" | custom-call | tf_op jit(solution)/shard_map/lead/pallas_call | solution.py:332
  55.0 4.6 %collective-permute-start.10 = (f32[64,128]{1,0:T(8,128)S(1)}, f32[64,128]{1,0:T(8,128)S(1)}, u32[]{:S(2)}, u32[]{:S(2)}) collective-permute-start(f32[64,128]{1,0:T(8,128)S(1)} %lead.1.after_ref), channel_id=1, source_target_pairs={{0,4},{1,5},{2,6},{3,7},{4,0},{5,1},{6,2},{7,3},{8,12},{9,13},{10,... | collective-permute-start | bytes 98312 | tf_op jit(solution)/shard_map/ppermute | solution.py:400
  59.6 3.9 %reach.3 = (f32[2,256,128]{2,1,0:T(8,128)S(1)}, f32[2,256,128]{2,1,0:T(8,128)S(1)}) custom-call(s32[4]{0:T(128)S(1)} %pad_add_fusion.pos_ref, bf16[1024,128]{1,0:T(8,128)(2,1)S(1)} %bitcast.12, bf16[4,512,128]{2,1,0:T(8,128)(2,1)S(1)} %get-tuple-element.29.r_ref, f32[4,4,256,128]{3,2,1,0:T(8,128)S(1)} %get-tuple-element.30.z_ref, ...), custom_call_target="tpu_custom_call" | custom-call | flops 800000000 | bytes 6000000 | tf_op jit(solution)/shard_map/reach/pallas_call | solution.py:291
  63.5 1.2 %fuse.1 = (f32[4,192,128]{2,1,0:T(8,128)S(1)}, f32[64,128]{1,0:T(8,128)S(1)}) custom-call(s32[4]{0:T(128)S(1)} %pad_add_fusion.pos_ref, f32[192,128]{1,0:T(8,128)S(1)} %collective-permute-done.7.s1, f32[192,128]{1,0:T(8,128)S(1)} %collective-permute-done.8.s2, f32[192,128]{1,0:T(8,128)S(1)} %collective-permute-done.9.s3, ...), custom_call_target="tpu_custom_call" | custom-call | tf_op jit(solution)/shard_map/fuse/pallas_call | solution.py:332
  64.7 0.0 collective-permute-done.10.early_ref
  64.8 0.8 entry.1
  65.5 0.1 collective-permute-start.11
  65.6 1.8 %collective-permute-start.12 = (f32[64,128]{1,0:T(8,128)S(1)}, f32[64,128]{1,0:T(8,128)S(1)}, u32[]{:S(2)}, u32[]{:S(2)}) collective-permute-start(f32[64,128]{1,0:T(8,128)S(1)} %get-tuple-element.51), channel_id=1, source_target_pairs={{0,32},{8,40},{16,48},{24,56},{32,0},{40,8},{48,16},{56,24},{64,96... | collective-permute-start | bytes 98312 | tf_op jit(solution)/shard_map/ppermute | solution.py:414
  67.4 1.2 %collective-permute-start.13 = (f32[64,128]{1,0:T(8,128)S(1)}, f32[64,128]{1,0:T(8,128)S(1)}, u32[]{:S(2)}, u32[]{:S(2)}) collective-permute-start(f32[64,128]{1,0:T(8,128)S(1)} %get-tuple-element.52), channel_id=1, source_target_pairs={{0,48},{8,56},{16,0},{24,8},{32,16},{40,24},{48,32},{56,40},{64,11... | collective-permute-start | bytes 98312 | tf_op jit(solution)/shard_map/ppermute | solution.py:414
  68.6 1.0 %collective-permute-done.11 = f32[64,128]{1,0:T(8,128)S(1)} collective-permute-done((f32[64,128]{1,0:T(8,128)S(1)}, f32[64,128]{1,0:T(8,128)S(1)}, u32[]{:S(2)}, u32[]{:S(2)}) %collective-permute-start.11) | collective-permute-done | bytes 32800 | tf_op jit(solution)/shard_map/ppermute | solution.py:414
  69.6 0.4 collective-permute-done.12
  70.0 0.5 collective-permute-done.13
  70.5 0.0 copy-start.6
  70.5 3.7 %collective-permute-start.14 = (f32[4,64,128]{2,1,0:T(8,128)S(1)}, f32[4,64,128]{2,1,0:T(8,128)S(1)}, u32[]{:S(2)}, u32[]{:S(2)}) collective-permute-start(f32[4,64,128]{2,1,0:T(8,128)S(1)} %pad_maximum_fusion.mine_ref), channel_id=1, source_target_pairs={{0,8},{8,0},{16,24},{24,16},{32,40},{40,32},{48,56},{56,48},{64,72... | collective-permute-start | bytes 393224 | tf_op jit(solution)/shard_map/ppermute | solution.py:416
  74.2 3.9 %reach.2 = (f32[2,256,128]{2,1,0:T(8,128)S(1)}, f32[2,256,128]{2,1,0:T(8,128)S(1)}) custom-call(s32[4]{0:T(128)S(1)} %pad_add_fusion.pos_ref, bf16[1024,128]{1,0:T(8,128)(2,1)S(1)} %bitcast.13, bf16[4,512,128]{2,1,0:T(8,128)(2,1)S(1)} %get-tuple-element.29.r_ref, f32[4,4,256,128]{3,2,1,0:T(8,128)S(1)} %get-tuple-element.30.z_ref, ...), custom_call_target="tpu_custom_call" | custom-call | flops 800000000 | bytes 6000000 | tf_op jit(solution)/shard_map/reach/pallas_call | solution.py:291
  78.1 0.0 collective-permute-done.14.other_ref
  78.1 0.0 copy-done.6
  78.1 1.8 %read.1 = bf16[1024,128]{1,0:T(8,128)(2,1)} custom-call(s32[4]{0:T(128)S(1)} %pad_add_fusion.pos_ref, f32[2,256,128]{2,1,0:T(8,128)S(1)} %get-tuple-element.42.ra, f32[2,256,128]{2,1,0:T(8,128)S(1)} %get-tuple-element.43.ba, f32[2,256,128]{2,1,0:T(8,128)S(1)} %get-tuple-element.45.after_ref.rb, f32[2,256,128]{2,1,0:T(8,128)S(1)} %get-tuple-element.46.bb, ...), custom_call_target="tpu_custom_call" | custom-call | tf_op jit(solution)/shard_map/read/pallas_call | solution.py:332
  (9 shorter events, 0.0 us)
Async XLA Ops:
  0.0 1.0 %copy-start.3 = (bf16[1,256,2,4,128]{4,3,2,1,0:T(4,128)(2,1)S(1)}, bf16[1,256,2,4,128]{4,3,2,1,0:T(4,128)(2,1)}, u32[]{:S(2)}) copy-start(bf16[1,256,2,4,128]{4,3,2,1,0:T(4,128)(2,1)} %param.6) | copy-start | bytes 1572868
  1.0 1.0 %copy-start.4 = (bf16[1,256,2,4,128]{4,3,2,1,0:T(4,128)(2,1)S(1)}, bf16[1,256,2,4,128]{4,3,2,1,0:T(4,128)(2,1)}, u32[]{:S(2)}) copy-start(bf16[1,256,2,4,128]{4,3,2,1,0:T(4,128)(2,1)} %param.7) | copy-start | bytes 1572868
  2.1 57.5 %copy-start.2 = (bf16[1,256,4,128]{3,2,1,0:T(4,128)(2,1)S(1)}, bf16[1,256,4,128]{3,2,1,0:T(4,128)(2,1)}, u32[]{:S(2)}) copy-start(bf16[1,256,4,128]{3,2,1,0:T(4,128)(2,1)} %param.5) | copy-start | bytes 786436
  9.8 1.2 %copy-start = (f32[4,3,256,128]{3,2,1,0:T(8,128)}, f32[4,3,256,128]{3,2,1,0:T(8,128)S(1)}, u32[]{:S(2)}) copy-start(f32[4,3,256,128]{3,2,1,0:T(8,128)S(1)} %get-tuple-element.31.p_ref) | copy-start | bytes 4718596
  11.0 5.0 %collective-permute-start = (f32[4,256,128]{2,1,0:T(8,128)}, f32[4,256,128]{2,1,0:T(8,128)S(1)}, u32[]{:S(2)}, u32[]{:S(2)}) collective-permute-start(f32[4,256,128]{2,1,0:T(8,128)} %get-tuple-element.32.own_ref), channel_id=1, source_target_pairs={{0,8},{8,0},{16,24},{24,16},{32,40},{40,32},{48,56},{56,48},{64,72... | collective-permute-start | bytes 1572872 | tf_op jit(solution)/shard_map/ppermute | solution.py:376
  14.2 45.4 %copy-start.1 = (f32[4,3,256,128]{3,2,1,0:T(8,128)S(1)}, f32[4,3,256,128]{3,2,1,0:T(8,128)}, u32[]{:S(2)}) copy-start(f32[4,3,256,128]{3,2,1,0:T(8,128)} %copy-done) | copy-start | bytes 4718596
  17.3 6.2 %collective-permute-start.1 = (f32[192,128]{1,0:T(8,128)S(1)}, f32[192,128]{1,0:T(8,128)S(1)}, u32[]{:S(2)}, u32[]{:S(2)}) collective-permute-start(f32[192,128]{1,0:T(8,128)S(1)} %get-tuple-element.34), channel_id=1, source_target_pairs={{0,16},{8,24},{16,32},{24,40},{32,48},{40,56},{48,0},{56,8},{64,80... | collective-permute-start | bytes 294920 | tf_op jit(solution)/shard_map/ppermute | solution.py:378
  17.4 6.6 %collective-permute-start.2 = (f32[192,128]{1,0:T(8,128)S(1)}, f32[192,128]{1,0:T(8,128)S(1)}, u32[]{:S(2)}, u32[]{:S(2)}) collective-permute-start(f32[192,128]{1,0:T(8,128)S(1)} %get-tuple-element.35), channel_id=1, source_target_pairs={{0,32},{8,40},{16,48},{24,56},{32,0},{40,8},{48,16},{56,24},{64,96... | collective-permute-start | bytes 294920 | tf_op jit(solution)/shard_map/ppermute | solution.py:378
  19.3 5.6 %collective-permute-start.3 = (f32[192,128]{1,0:T(8,128)S(1)}, f32[192,128]{1,0:T(8,128)S(1)}, u32[]{:S(2)}, u32[]{:S(2)}) collective-permute-start(f32[192,128]{1,0:T(8,128)S(1)} %get-tuple-element.36), channel_id=1, source_target_pairs={{0,48},{8,56},{16,0},{24,8},{32,16},{40,24},{48,32},{56,40},{64,11... | collective-permute-start | bytes 294920 | tf_op jit(solution)/shard_map/ppermute | solution.py:378
  26.0 3.5 %collective-permute-start.6 = (f32[192,128]{1,0:T(8,128)S(1)}, f32[192,128]{1,0:T(8,128)S(1)}, u32[]{:S(2)}, u32[]{:S(2)}) collective-permute-start(f32[192,128]{1,0:T(8,128)S(1)} %get-tuple-element.37.s0), channel_id=1, source_target_pairs={{0,192},{8,200},{16,208},{24,216},{32,224},{40,232},{48,240},{56,2... | collective-permute-start | bytes 294920 | tf_op jit(solution)/shard_map/ppermute | solution.py:382
  27.8 5.1 %collective-permute-start.5 = (f32[192,128]{1,0:T(8,128)S(1)}, f32[192,128]{1,0:T(8,128)S(1)}, u32[]{:S(2)}, u32[]{:S(2)}) collective-permute-start(f32[192,128]{1,0:T(8,128)S(1)} %get-tuple-element.37.s0), channel_id=1, source_target_pairs={{0,128},{8,136},{16,144},{24,152},{32,160},{40,168},{48,176},{56,1... | collective-permute-start | bytes 294920 | tf_op jit(solution)/shard_map/ppermute | solution.py:382
  28.1 6.1 %collective-permute-start.4 = (f32[192,128]{1,0:T(8,128)S(1)}, f32[192,128]{1,0:T(8,128)S(1)}, u32[]{:S(2)}, u32[]{:S(2)}) collective-permute-start(f32[192,128]{1,0:T(8,128)S(1)} %get-tuple-element.37.s0), channel_id=1, source_target_pairs={{0,64},{8,72},{16,80},{24,88},{32,96},{40,104},{48,112},{56,120},{... | collective-permute-start | bytes 294920 | tf_op jit(solution)/shard_map/ppermute | solution.py:382
  35.1 10.2 %collective-permute-start.9 = (f32[192,128]{1,0:T(8,128)S(1)}, f32[192,128]{1,0:T(8,128)S(1)}, u32[]{:S(2)}, u32[]{:S(2)}) collective-permute-start(f32[192,128]{1,0:T(8,128)S(1)} %get-tuple-element.40.after_ref.own), channel_id=1, source_target_pairs={{0,3},{1,4},{2,5},{3,6},{4,7},{5,0},{6,1},{7,2},{8,11},{9,12},{10,... | collective-permute-start | bytes 294920 | tf_op jit(solution)/shard_map/ppermute | solution.py:386
  39.6 11.4 %collective-permute-start.8 = (f32[192,128]{1,0:T(8,128)S(1)}, f32[192,128]{1,0:T(8,128)S(1)}, u32[]{:S(2)}, u32[]{:S(2)}) collective-permute-start(f32[192,128]{1,0:T(8,128)S(1)} %get-tuple-element.40.after_ref.own), channel_id=1, source_target_pairs={{0,2},{1,3},{2,4},{3,5},{4,6},{5,7},{6,0},{7,1},{8,10},{9,11},{10,... | collective-permute-start | bytes 294920 | tf_op jit(solution)/shard_map/ppermute | solution.py:386
  42.9 11.2 %collective-permute-start.7 = (f32[192,128]{1,0:T(8,128)S(1)}, f32[192,128]{1,0:T(8,128)S(1)}, u32[]{:S(2)}, u32[]{:S(2)}) collective-permute-start(f32[192,128]{1,0:T(8,128)S(1)} %get-tuple-element.40.after_ref.own), channel_id=1, source_target_pairs={{0,1},{1,2},{2,3},{3,4},{4,5},{5,6},{6,7},{7,0},{8,9},{9,10},{10,1... | collective-permute-start | bytes 294920 | tf_op jit(solution)/shard_map/ppermute | solution.py:386
  43.6 0.9 %copy-start.5 = (f32[4,128,128]{2,1,0:T(8,128)S(1)}, f32[4,128,128]{2,1,0:T(8,128)}, u32[]{:S(2)}) copy-start(f32[4,128,128]{2,1,0:T(8,128)} %init_ref.1) | copy-start | bytes 786436
  55.0 9.8 %collective-permute-start.10 = (f32[64,128]{1,0:T(8,128)S(1)}, f32[64,128]{1,0:T(8,128)S(1)}, u32[]{:S(2)}, u32[]{:S(2)}) collective-permute-start(f32[64,128]{1,0:T(8,128)S(1)} %lead.1.after_ref), channel_id=1, source_target_pairs={{0,4},{1,5},{2,6},{3,7},{4,0},{5,1},{6,2},{7,3},{8,12},{9,13},{10,... | collective-permute-start | bytes 98312 | tf_op jit(solution)/shard_map/ppermute | solution.py:400
  65.5 4.1 %collective-permute-start.11 = (f32[64,128]{1,0:T(8,128)S(1)}, f32[64,128]{1,0:T(8,128)S(1)}, u32[]{:S(2)}, u32[]{:S(2)}) collective-permute-start(f32[64,128]{1,0:T(8,128)S(1)} %get-tuple-element.50), channel_id=1, source_target_pairs={{0,16},{8,24},{16,32},{24,40},{32,48},{40,56},{48,0},{56,8},{64,80... | collective-permute-start | bytes 98312 | tf_op jit(solution)/shard_map/ppermute | solution.py:414
  65.6 4.4 %collective-permute-start.12 = (f32[64,128]{1,0:T(8,128)S(1)}, f32[64,128]{1,0:T(8,128)S(1)}, u32[]{:S(2)}, u32[]{:S(2)}) collective-permute-start(f32[64,128]{1,0:T(8,128)S(1)} %get-tuple-element.51), channel_id=1, source_target_pairs={{0,32},{8,40},{16,48},{24,56},{32,0},{40,8},{48,16},{56,24},{64,96... | collective-permute-start | bytes 98312 | tf_op jit(solution)/shard_map/ppermute | solution.py:414
  67.4 3.1 %collective-permute-start.13 = (f32[64,128]{1,0:T(8,128)S(1)}, f32[64,128]{1,0:T(8,128)S(1)}, u32[]{:S(2)}, u32[]{:S(2)}) collective-permute-start(f32[64,128]{1,0:T(8,128)S(1)} %get-tuple-element.52), channel_id=1, source_target_pairs={{0,48},{8,56},{16,0},{24,8},{32,16},{40,24},{48,32},{56,40},{64,11... | collective-permute-start | bytes 98312 | tf_op jit(solution)/shard_map/ppermute | solution.py:414
  70.5 7.6 %copy-start.6 = (f32[4,128]{1,0:T(4,128)S(1)}, f32[4,128]{1,0:T(4,128)}, u32[]{:S(2)}) copy-start(f32[4,128]{1,0:T(4,128)} %gain_ref.1) | copy-start | bytes 6148
  70.5 7.6 %collective-permute-start.14 = (f32[4,64,128]{2,1,0:T(8,128)S(1)}, f32[4,64,128]{2,1,0:T(8,128)S(1)}, u32[]{:S(2)}, u32[]{:S(2)}) collective-permute-start(f32[4,64,128]{2,1,0:T(8,128)S(1)} %pad_maximum_fusion.mine_ref), channel_id=1, source_target_pairs={{0,8},{8,0},{16,24},{24,16},{32,40},{40,32},{48,56},{56,48},{64,72... | collective-permute-start | bytes 393224 | tf_op jit(solution)/shard_map/ppermute | solution.py:416

commit v3 on v2

--- a/solution.py
+++ b/solution.py
@@ -14,6 +14,7 @@
 XS = 4
 YS = 4
 CS = 2
+ZG = 4
 HALF = D // CS
 MSG = D + HALF
 
@@ -65,9 +66,24 @@
     return lax.broadcasted_iota(jnp.int32, shape, dim)
 
 
-def factor_kernel(k_ref, v_ref, m_ref, z_ref, p_ref, r_ref, keys, values):
-    keys[...] = k_ref[...].astype(f32)
-    values[...] = v_ref[...].astype(f32)
+def factor_kernel(k_hbm, v_hbm, m_ref, z_ref, r_ref, k_ref, v_ref, keys, values, sems):
+    pieces = sems.shape[1]
+    size = k_ref.shape[0] // pieces
+    copies = [
+        [
+            pltpu.make_async_copy(
+                src.at[pl.ds(i * size, size)], dst.at[pl.ds(i * size, size)], sems.at[j, i]
+            )
+            for i in range(pieces)
+        ]
+        for j, (src, dst) in enumerate(((k_hbm, k_ref), (v_hbm, v_ref)))
+    ]
+    for group in copies:
+        for copy in group:
+            copy.start()
+    for i, copy in enumerate(copies[0]):
+        copy.wait()
+        keys[i * size : (i + 1) * size] = k_ref[i * size : (i + 1) * size].astype(f32)
     nblk = r_ref.shape[1] // BLK
     row = iota2((BLK, BLK), 0)
     col = iota2((BLK, BLK), 1)
@@ -77,7 +93,6 @@
     for h, b in chains:
         rows = pl.ds(h + HEADS * BLK * b, BLK, stride=HEADS)
         r = keys[rows, :].astype(bf16)
-        v = values[rows, :].astype(bf16)
         r_ref[h, b * BLK : (b + 1) * BLK, :] = r
         rt = r.T
         gram = dot_nn(r, rt)
@@ -89,7 +104,6 @@
         inv = jnp.where(eye, 1.0, 0.0) - jnp.where(pair, upper, 0.0)
         rs.append(r)
         rts.append(rt)
-        vts.append(v.T)
         uppers.append(upper)
         invs.append(inv)
         ccols.append(ccol)
@@ -103,6 +117,12 @@
             mm_pre(wide(jnp.where(off, upper, 0.0)), tall) for upper, tall in zip(uppers, talls)
         ]
         invs = [inv - mm(inv, mid) for inv, mid in zip(invs, mids)]
+    for i, copy in enumerate(copies[1]):
+        copy.wait()
+        values[i * size : (i + 1) * size] = v_ref[i * size : (i + 1) * size].astype(f32)
+    for h, b in chains:
+        rows = pl.ds(h + HEADS * BLK * b, BLK, stride=HEADS)
+        vts.append(values[rows, :].astype(bf16).T)
     pairs = []
     base = jnp.where(iota2((2 * D, D), 0) == iota2((2 * D, D), 1), 1.0, 0.0)
     sign = jnp.where(iota2((2 * D, D), 0) < D, -1.0, 1.0)
@@ -117,8 +137,6 @@
         pairs.append(base + sign * dot_nn(wide(z), rr))
     for h in range(HEADS):
         own = pairs[h * nblk : (h + 1) * nblk]
-        for b in range(nblk - 1):
-            p_ref[h, b] = own[b]
         while len(own) > 1:
             own = [compose(own[i], own[i + 1]) for i in range(0, len(own), 2)]
         m_ref[h] = own[0]
@@ -139,16 +157,17 @@
     nblk = steps // BLK
     return pl.pallas_call(
         factor_kernel,
-        in_specs=whole(k, v),
-        out_specs=[pl.BlockSpec(memory_space=pltpu.VMEM)] * 4,
+        in_specs=[pl.BlockSpec(memory_space=pl.ANY)] * 2,
+        out_specs=[pl.BlockSpec(memory_space=pltpu.VMEM)] * 3,
         out_shape=[
             jax.ShapeDtypeStruct((HEADS, 2 * D, D), f32),
             jax.ShapeDtypeStruct((HEADS, nblk, 2 * D, D), f32),
-            jax.ShapeDtypeStruct((HEADS, nblk - 1, 2 * D, D), f32),
             jax.ShapeDtypeStruct((HEADS, steps, D), bf16),
         ],
-        scratch_shapes=[pltpu.VMEM((HEADS * steps, D), f32)] * 2,
-        compiler_params=pltpu.CompilerParams(vmem_limit_bytes=40 << 20),
+        scratch_shapes=[pltpu.VMEM((HEADS * steps, D), bf16)] * 2
+        + [pltpu.VMEM((HEADS * steps, D), f32)] * 2
+        + [pltpu.SemaphoreType.DMA((2, 4))],
+        compiler_params=pltpu.CompilerParams(vmem_limit_bytes=16 << 20),
         name="factor",
     )(k, v)
 
@@ -196,11 +215,11 @@
     pre_ref[2] = msg_compose(second, scratch[2])
 
 
-def row_kernel(pos_ref, s0, s1, s2, s3, total_ref, pre_ref, scratch):
+def row_kernel(pos_ref, s0, s1, s2, s3, after_ref, total_ref, pre_ref, scratch):
     prefix_totals([s0, s1, s2, s3], pos_ref[0], total_ref, pre_ref, scratch)
 
 
-def column_kernel(pos_ref, s0, s1, s2, s3, total_ref, pre_ref, scratch):
+def column_kernel(pos_ref, s0, s1, s2, s3, after_ref, total_ref, pre_ref, scratch):
     prefix_totals([s0, s1, s2, s3], pos_ref[1], total_ref, pre_ref, scratch)
 
 
@@ -222,34 +241,34 @@
     start_ref[...] = hold[pl.ds(pl.multiple_of(core * HALF, HALF), HALF), :]
 
 
-def early_states(g, s2, s3, start):
-    state = jnp.where(g >= 3, advance(start, s3), start)
-    return jnp.where(g >= 2, advance(state, s2), state)
-
-
-def lead_kernel(pos_ref, own, s1, s2, s3, start_ref, lead_ref):
-    g = pos_ref[3]
-    state = early_states(g, s2[...], s3[...], start_ref[...])
-    step = jnp.where(g >= 1, msg_compose(s1[...], own[...]), own[...])
-    lead_ref[...] = advance(state, step)
-
-
-def fuse_kernel(pos_ref, s1, s2, s3, start_ref, path_ref, after_ref, fuse_ref, state_ref):
-    g = pos_ref[3]
-    state = early_states(g, s2[...], s3[...], start_ref[...])
-    state_ref[...] = jnp.where(g >= 1, advance(state, s1[...]), state)
-    window = msg_compose(msg_compose(s3[...], s2[...]), s1[...])
+def lead_kernel(pos_ref, s0, s1, s2, s3, start_ref, after_ref, lead_ref, hold):
+    ordered_load([s0, s1, s2, s3], lax.rem(pos_ref[3], ZG), hold)
+    tail = msg_compose(hold[2], hold[3])
+    state = advance(advance(start_ref[...], hold[0]), hold[1])
+    lead_ref[...] = advance(state, tail)
+
+
+def fuse_kernel(pos_ref, s0, s1, s2, s3, path_ref, after_ref, fuse_ref, hold):
+    g = lax.rem(pos_ref[3], ZG)
+    ordered_load([s0, s1, s2, s3], g, hold)
+    window = jnp.where(iota2((MSG, D), 0) == iota2((MSG, D), 1), 1.0, 0.0)
+    first = hold[0]
+    second = msg_compose(first, hold[1])
+    third = msg_compose(second, hold[2])
+    window = jnp.where(g == 1, first, window)
+    window = jnp.where(g == 2, second, window)
+    window = jnp.where(g == 3, third, window)
     left = wide(window)
     for i in range(XS):
         path = path_ref[i]
         moved = mm_pre(left, tall_wide(path[:D]))
-        moved = jnp.concatenate([moved[:D], moved[D:] + path[D:]], axis=0)
-        fuse_ref[i] = jnp.where(g >= 4, moved, path)
-
-
-def entry_kernel(pos_ref, state_ref, early_ref, fuse_ref, after_ref, o0, o1, o2, o3, scratch):
+        fuse_ref[i, :D, :] = moved[:D]
+        fuse_ref[i, D:, :] = moved[D:] + path[D:]
+
+
+def entry_kernel(pos_ref, start_ref, early_ref, fuse_ref, after_ref, o0, o1, o2, o3, scratch):
     x = pos_ref[0]
-    state = jnp.where(pos_ref[3] >= 4, early_ref[...], state_ref[...])
+    state = jnp.where(pos_ref[3] >= ZG, early_ref[...], start_ref[...])
     left = wide(state)
     for i in range(XS):
         scratch[i] = mm_pre(left, tall_wide(fuse_ref[i, :D, :])) + fuse_ref[i, D:, :]
@@ -257,36 +276,41 @@
         out[...] = scratch[lax.rem(x + k, XS)]
 
 
-def reach_kernel(pos_ref, q_ref, r_ref, z_ref, p_ref, sib_ref, after_ref, reach_ref, base_ref, rows, *, head):
-    tokens = reach_ref.shape[1]
-    nblk = z_ref.shape[1]
+def reach_kernel(
+    pos_ref, q_ref, r_ref, z_ref, sib_ref, after_ref, reach_ref, base_ref, rows, *, head
+):
+    tokens = reach_ref.shape[0]
+    nblk = z_ref.shape[0]
     span = tokens // nblk
-    group = reach_ref.shape[0]
     rows[...] = q_ref[...].astype(f32)
     visible = iota2((span, BLK), 1) <= REFL * iota2((span, BLK), 0) + (REFL - 1)
     base = jnp.where(iota2((2 * D, D), 0) == iota2((2 * D, D), 1), 1.0, 0.0)
-    prefixes = [jnp.where(pos_ref[2] == 1, sib_ref[h], base) for h in range(group)]
+    sign = jnp.where(iota2((2 * D, D), 0) < D, -1.0, 1.0)
+    prefixes = [jnp.where(pos_ref[2] == 1, sib_ref[...], base)]
+    for b in range(nblk - 1):
+        rr = jnp.concatenate([r_ref[b * BLK : (b + 1) * BLK, :]] * 2, axis=0)
+        piece = base + sign * dot_nn(wide(z_ref[b]), rr)
+        prefixes.append(compose(prefixes[b], piece))
+    projects, locals_ = [], []
     for b in range(nblk):
-        for h in range(group):
-            part = slice(b * span, (b + 1) * span)
-            q = rows[pl.ds(head + h + HEADS * span * b, span, stride=HEADS), :]
-            scores = dot_nt(q.astype(bf16), r_ref[h, b * BLK : (b + 1) * BLK, :])
-            sz = mm_nt(jnp.where(visible, scores, 0.0), z_ref[h, b])
-            project = q - sz[:, :D]
-            moved = mm_nt(project, prefixes[h])
-            reach_ref[h, part, :] = moved[:, :D]
-            base_ref[h, part, :] = moved[:, D:] + sz[:, D:]
-            if b + 1 < nblk:
-                prefixes[h] = compose(prefixes[h], p_ref[h, b])
-
-
-def reach_call(pos, q, r, z, p, sib, after, head, group):
+        q = rows[pl.ds(head + HEADS * span * b, span, stride=HEADS), :]
+        scores = dot_nt(q.astype(bf16), r_ref[b * BLK : (b + 1) * BLK, :])
+        sz = mm_nt(jnp.where(visible, scores, 0.0), z_ref[b])
+        projects.append(q - sz[:, :D])
+        locals_.append(sz[:, D:])
+    moves = [mm_nt(projects[b], prefixes[b]) for b in range(nblk)]
+    for b in range(nblk):
+        part = slice(b * span, (b + 1) * span)
+        reach_ref[part, :] = moves[b][:, :D]
+        base_ref[part, :] = moves[b][:, D:] + locals_[b]
+
+
+def reach_call(pos, q, r, z, sib, after, head):
     tokens = q.shape[0] // HEADS
-    place = head // group
 
     def spec(array):
         rest = array.shape[1:]
-        return pl.BlockSpec((group, *rest), lambda i: (place,) + (0,) * len(rest))
+        return pl.BlockSpec((None, *rest), lambda i: (head,) + (0,) * len(rest))
 
     return pl.pallas_call(
         functools.partial(reach_kernel, head=head),
@@ -296,32 +320,33 @@
             pl.BlockSpec(q.shape, lambda i: (0, 0)),
             spec(r),
             spec(z),
-            spec(p),
             spec(sib),
             pl.BlockSpec(memory_space=pl.ANY),
         ],
-        out_specs=[pl.BlockSpec((group, tokens, D), lambda i: (0, 0, 0))] * 2,
-        out_shape=[jax.ShapeDtypeStruct((group, tokens, D), f32)] * 2,
+        out_specs=[pl.BlockSpec((tokens, D), lambda i: (0, 0))] * 2,
+        out_shape=[jax.ShapeDtypeStruct((tokens, D), f32)] * 2,
         scratch_shapes=[pltpu.VMEM(q.shape, f32)],
-        compiler_params=pltpu.CompilerParams(vmem_limit_bytes=16 << 20),
-        cost_estimate=pl.CostEstimate(flops=400_000_000 * group, bytes_accessed=3_000_000 * group, transcendentals=0),
+        compiler_params=pltpu.CompilerParams(vmem_limit_bytes=6 << 20),
+        cost_estimate=pl.CostEstimate(
+            flops=400_000_000, bytes_accessed=3_000_000, transcendentals=0
+        ),
         name="reach",
-    )(pos, q, r, z, p, sib, after)
-
-
-def read_kernel(pos_ref, ra, ba, rb, bb, mine_ref, other_ref, gain_ref, out_ref, rows):
+    )(pos, q, r, z, sib, after)
+
+
+def read_kernel(pos_ref, *refs):
+    reaches, bases = refs[: 2 * HEADS : 2], refs[1 : 2 * HEADS : 2]
+    mine_ref, other_ref, gain_ref, out_ref, rows = refs[2 * HEADS :]
     x = pos_ref[0]
     lower = pos_ref[2] == 0
-    tokens = ra.shape[1]
-    group = ra.shape[0]
+    tokens = reaches[0].shape[0]
     for h in range(HEADS):
-        reach, base = (ra, ba) if h < group else (rb, bb)
         slot = lax.rem(x + HEADS - h, HEADS)
         mine, other = mine_ref[slot], other_ref[slot]
         state = jnp.concatenate(
             [jnp.where(lower, mine, other), jnp.where(lower, other, mine)], axis=0
         )
-        read = mm_nt(reach[h % group], state) + base[h % group]
+        read = mm_nt(reaches[h][...], state) + bases[h][...]
         scale = lax.rsqrt(jnp.mean(read * read, axis=-1, keepdims=True) + 1e-06)
         rows[pl.ds(h, tokens, stride=HEADS), :] = read * scale * gain_ref[h : h + 1, :]
     out_ref[...] = rows[...].astype(bf16)
@@ -366,24 +391,42 @@
     along_x = [seq_perm(lambda y, x, c, k=k: (y, (x + k) % XS, c)) for k in range(1, XS)]
     along_y = [seq_perm(lambda y, x, c, k=k: ((y + k) % YS, x, c)) for k in range(1, YS)]
     segs = 8
-    along_z = [[(i, (i + k) % segs) for i in range(segs)] for k in range(1, 4)]
-    jump = [(i, (i + 4) % segs) for i in range(segs)]
+    along_z = [
+        [(i, i // ZG * ZG + (i + k) % ZG) for i in range(segs)] for k in range(1, ZG)
+    ]
+    jump = [(i, (i + ZG) % segs) for i in range(segs)]
 
     keys = key_rows.reshape(steps * HEADS, D)
     values = value_rows.reshape(steps * HEADS, D)
     query = query_rows.reshape(tokens * HEADS, D)
-    pair, z, parts, r = factor_call(keys, values)
+    keys = pltpu.with_memory_space_constraint(keys, pltpu.HBM)
+    values = pltpu.with_memory_space_constraint(values, pltpu.HBM)
+    pair, z, r = factor_call(keys, values)
     sib = lax.ppermute(pair, "seq", swap)
     slots = small_call(chip_kernel, "chip", pos, [pair, sib], [(MSG, D)] * XS)
     slots = [slots[0]] + [lax.ppermute(s, "seq", p) for s, p in zip(slots[1:], along_x)]
+    reaches = [reach_call(pos, query, r, z, sib, slots[0], 0)]
     total, xpre = small_call(
-        row_kernel, "row", pos, slots, [(MSG, D), (XS - 1, MSG, D)], [(XS, MSG, D)]
+        row_kernel,
+        "row",
+        pos,
+        slots,
+        [(MSG, D), (XS - 1, MSG, D)],
+        [(XS, MSG, D)],
+        after=reaches[-1][0],
     )
     slots = [total] + [lax.ppermute(total, "seq", p) for p in along_y]
+    reaches.append(reach_call(pos, query, r, z, sib, total, 1))
     total, ypre = small_call(
-        column_kernel, "column", pos, slots, [(MSG, D), (YS - 1, MSG, D)], [(YS, MSG, D)]
-    )
-    slots = [lax.ppermute(total, "seg", p) for p in along_z]
+        column_kernel,
+        "column",
+        pos,
+        slots,
+        [(MSG, D), (YS - 1, MSG, D)],
+        [(YS, MSG, D)],
+        after=reaches[-1][0],
+    )
+    slots = [total] + [lax.ppermute(total, "seg", p) for p in along_z]
     path, start = small_call(
         path_kernel,
         "path",
@@ -393,23 +436,35 @@
         [(D, D)],
         after=total,
     )
-    reach_a, base_a = reach_call(pos, query, r, z, parts, sib, path, 0, 2)
+    reaches.append(reach_call(pos, query, r, z, sib, path, 2))
     (lead,) = small_call(
-        lead_kernel, "lead", pos, [total, *slots, start], [(HALF, D)]
+        lead_kernel,
+        "lead",
+        pos,
+        [*slots, start],
+        [(HALF, D)],
+        [(ZG, MSG, D)],
+        after=reaches[-1][0],
     )
     early = lax.ppermute(lead, "seg", jump)
-    fused, state = small_call(
-        fuse_kernel, "fuse", pos, [*slots, start, path], [(XS, MSG, D), (HALF, D)], after=lead
-    )
-    reach_b, base_b = reach_call(pos, query, r, z, parts, sib, lead, 2, 2)
+    (fused,) = small_call(
+        fuse_kernel,
+        "fuse",
+        pos,
+        [*slots, path],
+        [(XS, MSG, D)],
+        [(ZG, MSG, D)],
+        after=lead,
+    )
+    reaches.append(reach_call(pos, query, r, z, sib, fused, 3))
     slots = small_call(
         entry_kernel,
         "entry",
         pos,
-        [state, early, fused],
+        [start, early, fused],
         [(HALF, D)] * XS,
         [(XS, HALF, D)],
-        after=reach_b,
+        after=reaches[-1][0],
     )
     slots = [slots[0]] + [lax.ppermute(s, "seq", p) for s, p in zip(slots[1:], along_x)]
     mine = jnp.stack(slots)
@@ -418,7 +473,7 @@
         read_kernel,
         "read",
         pos,
-        [reach_a, base_a, reach_b, base_b, mine, other, out_gain],
+        [a for pair in reaches for a in pair] + [mine, other, out_gain],
         [(tokens * HEADS, D)],
         [(tokens * HEADS, D)],
         limit=8,

time: 80.2 us -> 68.1 us (0.85)
  waiting for transfers between devices: 22.2 us -> 17.9 us
  local copies, waits for them, and re-layouts: 4.24 us -> 0.02 us
  starting transfers between devices: 29 us -> 25.3 us
    unnamed x14 -> x6, local copies, waits for them, and re-layouts: 4.24 us -> 0.02 us
    ppermute x3, starting transfers between devices: 8.45 us -> 4.79 us  [per_device(): slots = [total] + [lax.ppermute(total, 'seg', p) for p in along_z]]
    ppermute x3, waiting for transfers between devices: 8.69 us -> 5.97 us  [per_device(): slots = [total] + [lax.ppermute(total, 'seg', p) for p in along_z]]
    ppermute x3, waiting for transfers between devices: 5.36 us -> 3.65 us  [per_device(): slots = [total] + [lax.ppermute(total, 'seq', p) for p in along_y]]
    ppermute x6, waiting for transfers between devices: 6.42 us -> 5.01 us  [per_device(): lax.ppermute(s, 'seq', p)]
    ppermute x1, starting transfers between devices: 3.69 us -> 5.09 us  [per_device(): other = lax.ppermute(mine, 'seq', swap)]
    pallas_call x1, Pallas kernels: 7.72 us -> 9.04 us  [factor_call(): pl.pallas_call(factor_kernel, in_specs=[pl.BlockSpec(memory_space=pl.ANY)...]
    ppermute x1, starting transfers between devices: 4.61 us -> 3.34 us  [per_device(): early = lax.ppermute(lead, 'seg', jump)]
  transfers between devices with their start and end apart: 15 -> 15, of which waited for: 12 -> 12; matrix products, arithmetic and copies ran while one was open for 0% -> 0% of each run, Pallas kernels for 12% -> 13%
where the time goes in v3:
time: 68.1 us; the launch traced here: 68 us
  starting transfers between devices  25.3 us (37%)
  Pallas kernels  24.6 us (36%)
  waiting for transfers between devices  17.9 us (26%)
    pallas_call x1, Pallas kernels, factor_call(): pl.pallas_call(factor_kernel, in_specs=[pl.BlockSpec(memory_space=pl.ANY)...  9.04 us
    pallas_call x8, Pallas kernels, small_call(): pl.pallas_call(kernel, in_specs=[pl.BlockSpec(memory_space=pltpu.SMEM)] +...  8.68 us
    pallas_call x4, Pallas kernels, reach_call(): pl.pallas_call(functools.partial(reach_kernel, head=head), grid=(1,), in_...  6.84 us
    ppermute x3, waiting for transfers between devices, per_device(): slots = [total] + [lax.ppermute(total, 'seg', p) for p in along_z]  5.97 us
    ppermute x6, starting transfers between devices, per_device(): lax.ppermute(s, 'seq', p)  5.9 us
    ppermute x1, starting transfers between devices, per_device(): other = lax.ppermute(mine, 'seq', swap)  5.09 us
    ppermute x6, waiting for transfers between devices, per_device(): lax.ppermute(s, 'seq', p)  5.01 us
    ppermute x3, starting transfers between devices, per_device(): slots = [total] + [lax.ppermute(total, 'seg', p) for p in along_z]  4.79 us
  transfers between devices with their start and end apart: 15, of which 12 were waited for; matrix products, arithmetic and copies ran while one was open for 0% of the time, Pallas kernels for 13%

profile of v3, /device:TPU:1, one launch (start us, length us, event | category | flops | bytes accessed | tf_op | source)
XLA Modules:
  0.0 68.0 jit_solution(4969915002461006669)
XLA Ops:
  0.0 9.0 %factor.1 = (f32[4,256,128]{2,1,0:T(8,128)}, f32[4,4,256,128]{3,2,1,0:T(8,128)S(1)}, bf16[4,512,128]{2,1,0:T(8,128)(2,1)S(1)}) custom-call(bf16[2048,128]{1,0:T(8,128)(2,1)} %bitcast.17, bf16[2048,128]{1,0:T(8,128)(2,1)} %bitcast.18), custom_call_target="tpu_custom_call" | custom-call | tf_op jit(solution)/shard_map/factor/pallas_call | solution.py:158
  9.1 3.3 %collective-permute-start = (f32[4,256,128]{2,1,0:T(8,128)}, f32[4,256,128]{2,1,0:T(8,128)S(1)}, u32[]{:S(2)}, u32[]{:S(2)}) collective-permute-start(f32[4,256,128]{2,1,0:T(8,128)} %get-tuple-element.32.own_ref), channel_id=1, source_target_pairs={{0,8},{8,0},{16,24},{24,16},{32,40},{40,32},{48,56},{56,48},{64,72... | collective-permute-start | bytes 1572872 | tf_op jit(solution)/shard_map/ppermute | solution.py:405
  12.4 0.1 pad_add_fusion.pos_ref
  12.5 1.7 %collective-permute-done.sib_ref = f32[4,256,128]{2,1,0:T(8,128)S(1)} collective-permute-done((f32[4,256,128]{2,1,0:T(8,128)}, f32[4,256,128]{2,1,0:T(8,128)S(1)}, u32[]{:S(2)}, u32[]{:S(2)}) %collective-permute-start) | collective-permute-done | bytes 524320 | tf_op jit(solution)/shard_map/ppermute | solution.py:405
  14.1 1.3 %chip.1 = (f32[192,128]{1,0:T(8,128)S(1)}, f32[192,128]{1,0:T(8,128)S(1)}, f32[192,128]{1,0:T(8,128)S(1)}, f32[192,128]{1,0:T(8,128)S(1)}) custom-call(s32[4]{0:T(128)S(1)} %pad_add_fusion.pos_ref, f32[4,256,128]{2,1,0:T(8,128)} %get-tuple-element.32.own_ref, f32[4,256,128]{2,1,0:T(8,128)S(1)} %collective-permute-done.sib_ref), custom_call_target="tpu_custom_call" | custom-call | tf_op jit(solution)/shard_map/chip/pallas_call | solution.py:357
  15.5 0.1 collective-permute-start.1
  15.6 1.9 %collective-permute-start.2 = (f32[192,128]{1,0:T(8,128)S(1)}, f32[192,128]{1,0:T(8,128)S(1)}, u32[]{:S(2)}, u32[]{:S(2)}) collective-permute-start(f32[192,128]{1,0:T(8,128)S(1)} %get-tuple-element.37), channel_id=1, source_target_pairs={{0,32},{8,40},{16,48},{24,56},{32,0},{40,8},{48,16},{56,24},{64,96... | collective-permute-start | bytes 294920 | tf_op jit(solution)/shard_map/ppermute | solution.py:407
  17.5 1.2 %collective-permute-start.3 = (f32[192,128]{1,0:T(8,128)S(1)}, f32[192,128]{1,0:T(8,128)S(1)}, u32[]{:S(2)}, u32[]{:S(2)}) collective-permute-start(f32[192,128]{1,0:T(8,128)S(1)} %get-tuple-element.38), channel_id=1, source_target_pairs={{0,48},{8,56},{16,0},{24,8},{32,16},{40,24},{48,32},{56,40},{64,11... | collective-permute-start | bytes 294920 | tf_op jit(solution)/shard_map/ppermute | solution.py:407
  18.6 0.0 copy-done
  18.6 1.7 %reach.4 = (f32[256,128]{1,0:T(8,128)S(1)}, f32[256,128]{1,0:T(8,128)S(1)}) custom-call(s32[4]{0:T(128)S(1)} %pad_add_fusion.pos_ref, bf16[1024,128]{1,0:T(8,128)(2,1)S(1)} %bitcast.12, bf16[4,512,128]{2,1,0:T(8,128)(2,1)S(1)} %get-tuple-element.30.r_ref, f32[4,4,256,128]{3,2,1,0:T(8,128)S(1)} %get-tuple-element.31.z_ref, ...), custom_call_target="tpu_custom_call" | custom-call | flops 400000000 | bytes 3000000 | tf_op jit(solution)/shard_map/reach/pallas_call | solution.py:315
  20.4 1.4 %collective-permute-done.1.s1 = f32[192,128]{1,0:T(8,128)S(1)} collective-permute-done((f32[192,128]{1,0:T(8,128)S(1)}, f32[192,128]{1,0:T(8,128)S(1)}, u32[]{:S(2)}, u32[]{:S(2)}) %collective-permute-start.1) | collective-permute-done | bytes 98336 | tf_op jit(solution)/shard_map/ppermute | solution.py:407
  21.7 0.4 collective-permute-done.2.s2
  22.1 1.0 %collective-permute-done.3.s3 = f32[192,128]{1,0:T(8,128)S(1)} collective-permute-done((f32[192,128]{1,0:T(8,128)S(1)}, f32[192,128]{1,0:T(8,128)S(1)}, u32[]{:S(2)}, u32[]{:S(2)}) %collective-permute-start.3) | collective-permute-done | bytes 98336 | tf_op jit(solution)/shard_map/ppermute | solution.py:407
  23.1 1.0 %row.1 = (f32[192,128]{1,0:T(8,128)S(1)}, f32[3,192,128]{2,1,0:T(8,128)S(1)}) custom-call(s32[4]{0:T(128)S(1)} %pad_add_fusion.pos_ref, f32[192,128]{1,0:T(8,128)S(1)} %get-tuple-element.33.after_ref.s0, f32[192,128]{1,0:T(8,128)S(1)} %collective-permute-done.1.s1, f32[192,128]{1,0:T(8,128)S(1)} %collective-permute-done.2.s2, ...), custom_call_target="tpu_custom_call" | custom-call | tf_op jit(solution)/shard_map/row/pallas_call | solution.py:357
  24.1 0.0 copy-start.1
  24.1 1.8 %collective-permute-start.6 = (f32[192,128]{1,0:T(8,128)S(1)}, f32[192,128]{1,0:T(8,128)S(1)}, u32[]{:S(2)}, u32[]{:S(2)}) collective-permute-start(f32[192,128]{1,0:T(8,128)S(1)} %get-tuple-element.39.after_ref.s0), channel_id=1, source_target_pairs={{0,192},{8,200},{16,208},{24,216},{32,224},{40,232},{48,240},{56,2... | collective-permute-start | bytes 294920 | tf_op jit(solution)/shard_map/ppermute | solution.py:418
  25.9 0.5 collective-permute-start.5
  26.4 0.6 collective-permute-start.4
  27.0 1.7 %reach.5 = (f32[256,128]{1,0:T(8,128)S(1)}, f32[256,128]{1,0:T(8,128)S(1)}) custom-call(s32[4]{0:T(128)S(1)} %pad_add_fusion.pos_ref, bf16[1024,128]{1,0:T(8,128)(2,1)S(1)} %bitcast.13, bf16[4,512,128]{2,1,0:T(8,128)(2,1)S(1)} %get-tuple-element.30.r_ref, f32[4,4,256,128]{3,2,1,0:T(8,128)S(1)} %get-tuple-element.31.z_ref, ...), custom_call_target="tpu_custom_call" | custom-call | flops 400000000 | bytes 3000000 | tf_op jit(solution)/shard_map/reach/pallas_call | solution.py:315
  28.7 0.0 collective-permute-done.6.s3
  28.7 2.3 %collective-permute-done.5.s2 = f32[192,128]{1,0:T(8,128)S(1)} collective-permute-done((f32[192,128]{1,0:T(8,128)S(1)}, f32[192,128]{1,0:T(8,128)S(1)}, u32[]{:S(2)}, u32[]{:S(2)}) %collective-permute-start.5) | collective-permute-done | bytes 98336 | tf_op jit(solution)/shard_map/ppermute | solution.py:418
  31.0 1.3 %collective-permute-done.4.s1 = f32[192,128]{1,0:T(8,128)S(1)} collective-permute-done((f32[192,128]{1,0:T(8,128)S(1)}, f32[192,128]{1,0:T(8,128)S(1)}, u32[]{:S(2)}, u32[]{:S(2)}) %collective-permute-start.4) | collective-permute-done | bytes 98336 | tf_op jit(solution)/shard_map/ppermute | solution.py:418
  32.3 1.0 %column.1 = (f32[192,128]{1,0:T(8,128)S(1)}, f32[3,192,128]{2,1,0:T(8,128)S(1)}) custom-call(s32[4]{0:T(128)S(1)} %pad_add_fusion.pos_ref, f32[192,128]{1,0:T(8,128)S(1)} %get-tuple-element.39.after_ref.s0, f32[192,128]{1,0:T(8,128)S(1)} %collective-permute-done.4.s1, f32[192,128]{1,0:T(8,128)S(1)} %collective-permute-done.5.s2, ...), custom_call_target="tpu_custom_call" | custom-call | tf_op jit(solution)/shard_map/column/pallas_call | solution.py:357
  33.3 4.4 %collective-permute-start.9 = (f32[192,128]{1,0:T(8,128)S(1)}, f32[192,128]{1,0:T(8,128)S(1)}, u32[]{:S(2)}, u32[]{:S(2)}) collective-permute-start(f32[192,128]{1,0:T(8,128)S(1)} %get-tuple-element.44.after_ref.s0), channel_id=1, source_target_pairs={{0,3},{1,0},{2,1},{3,2},{4,7},{5,4},{6,5},{7,6},{8,11},{9,8},{10,9... | collective-permute-start | bytes 294920 | tf_op jit(solution)/shard_map/ppermute | solution.py:429
  37.7 0.0 collective-permute-start.8
  37.7 0.4 collective-permute-start.7
  38.1 0.8 %path.1 = (f32[4,192,128]{2,1,0:T(8,128)S(1)}, f32[64,128]{1,0:T(8,128)S(1)}) custom-call(s32[4]{0:T(128)S(1)} %pad_add_fusion.pos_ref, f32[3,192,128]{2,1,0:T(8,128)S(1)} %get-tuple-element.42.ypre_ref, f32[3,192,128]{2,1,0:T(8,128)S(1)} %get-tuple-element.43.xpre_ref, f32[4,128,128]{2,1,0:T(8,128)S(1)} %copy-done.1, ...), custom_call_target="tpu_custom_call" | custom-call | tf_op jit(solution)/shard_map/path/pallas_call | solution.py:357
  38.9 1.7 %reach.6 = (f32[256,128]{1,0:T(8,128)S(1)}, f32[256,128]{1,0:T(8,128)S(1)}) custom-call(s32[4]{0:T(128)S(1)} %pad_add_fusion.pos_ref, bf16[1024,128]{1,0:T(8,128)(2,1)S(1)} %bitcast.14, bf16[4,512,128]{2,1,0:T(8,128)(2,1)S(1)} %get-tuple-element.30.r_ref, f32[4,4,256,128]{3,2,1,0:T(8,128)S(1)} %get-tuple-element.31.z_ref, ...), custom_call_target="tpu_custom_call" | custom-call | flops 400000000 | bytes 3000000 | tf_op jit(solution)/shard_map/reach/pallas_call | solution.py:315
  40.6 0.0 collective-permute-done.9.s3
  40.6 6.0 %collective-permute-done.8.s2 = f32[192,128]{1,0:T(8,128)S(1)} collective-permute-done((f32[192,128]{1,0:T(8,128)S(1)}, f32[192,128]{1,0:T(8,128)S(1)}, u32[]{:S(2)}, u32[]{:S(2)}) %collective-permute-start.8) | collective-permute-done | bytes 98336 | tf_op jit(solution)/shard_map/ppermute | solution.py:429
  46.6 0.0 collective-permute-done.7.s1
  46.6 1.0 %lead.1.after_ref = f32[64,128]{1,0:T(8,128)S(1)} custom-call(s32[4]{0:T(128)S(1)} %pad_add_fusion.pos_ref, f32[192,128]{1,0:T(8,128)S(1)} %get-tuple-element.44.after_ref.s0, f32[192,128]{1,0:T(8,128)S(1)} %collective-permute-done.7.s1, f32[192,128]{1,0:T(8,128)S(1)} %collective-permute-done.8.s2, f32[192,128]{1,0:T(8,128)S(1)} %collective-permute-done.9.s3, ...), custom_call_target="tpu_custom_call" | custom-call | tf_op jit(solution)/shard_map/lead/pallas_call | solution.py:357
  47.6 3.3 %collective-permute-start.10 = (f32[64,128]{1,0:T(8,128)S(1)}, f32[64,128]{1,0:T(8,128)S(1)}, u32[]{:S(2)}, u32[]{:S(2)}) collective-permute-start(f32[64,128]{1,0:T(8,128)S(1)} %lead.1.after_ref), channel_id=1, source_target_pairs={{0,4},{1,5},{2,6},{3,7},{4,0},{5,1},{6,2},{7,3},{8,12},{9,13},{10,... | collective-permute-start | bytes 98312 | tf_op jit(solution)/shard_map/ppermute | solution.py:449
  50.9 1.1 %fuse.1.after_ref.fuse_ref = f32[4,192,128]{2,1,0:T(8,128)S(1)} custom-call(s32[4]{0:T(128)S(1)} %pad_add_fusion.pos_ref, f32[192,128]{1,0:T(8,128)S(1)} %get-tuple-element.44.after_ref.s0, f32[192,128]{1,0:T(8,128)S(1)} %collective-permute-done.7.s1, f32[192,128]{1,0:T(8,128)S(1)} %collective-permute-done.8.s2, f32[192,128]{1,0:T(8,128)S(1)} %collective-permute-done.9.s3, ...), custom_call_target="tpu_custom_call" | custom-call | tf_op jit(solution)/shard_map/fuse/pallas_call | solution.py:357
  52.0 0.0 copy-start.2
  52.0 1.7 %reach.7 = (f32[256,128]{1,0:T(8,128)S(1)}, f32[256,128]{1,0:T(8,128)S(1)}) custom-call(s32[4]{0:T(128)S(1)} %pad_add_fusion.pos_ref, bf16[1024,128]{1,0:T(8,128)(2,1)S(1)} %bitcast.15, bf16[4,512,128]{2,1,0:T(8,128)(2,1)S(1)} %get-tuple-element.30.r_ref, f32[4,4,256,128]{3,2,1,0:T(8,128)S(1)} %get-tuple-element.31.z_ref, ...), custom_call_target="tpu_custom_call" | custom-call | flops 400000000 | bytes 3000000 | tf_op jit(solution)/shard_map/reach/pallas_call | solution.py:315
  53.7 0.6 collective-permute-done.10.early_ref
  54.3 0.8 %entry.1 = (f32[64,128]{1,0:T(8,128)S(1)}, f32[64,128]{1,0:T(8,128)S(1)}, f32[64,128]{1,0:T(8,128)S(1)}, f32[64,128]{1,0:T(8,128)S(1)}) custom-call(s32[4]{0:T(128)S(1)} %pad_add_fusion.pos_ref, f32[64,128]{1,0:T(8,128)S(1)} %get-tuple-element.48.start_ref, f32[64,128]{1,0:T(8,128)S(1)} %collective-permute-done.10.early_ref, ...), custom_call_target="tpu_custom_call" | custom-call | tf_op jit(solution)/shard_map/entry/pallas_call | solution.py:357
  55.1 0.1 collective-permute-start.11
  55.2 0.1 collective-permute-start.12
  55.3 2.5 %collective-permute-start.13 = (f32[64,128]{1,0:T(8,128)S(1)}, f32[64,128]{1,0:T(8,128)S(1)}, u32[]{:S(2)}, u32[]{:S(2)}) collective-permute-start(f32[64,128]{1,0:T(8,128)S(1)} %get-tuple-element.54), channel_id=1, source_target_pairs={{0,48},{8,56},{16,0},{24,8},{32,16},{40,24},{48,32},{56,40},{64,11... | collective-permute-start | bytes 98312 | tf_op jit(solution)/shard_map/ppermute | solution.py:469
  57.9 1.3 %collective-permute-done.11 = f32[64,128]{1,0:T(8,128)S(1)} collective-permute-done((f32[64,128]{1,0:T(8,128)S(1)}, f32[64,128]{1,0:T(8,128)S(1)}, u32[]{:S(2)}, u32[]{:S(2)}) %collective-permute-start.11) | collective-permute-done | bytes 32800 | tf_op jit(solution)/shard_map/ppermute | solution.py:469
  59.2 0.4 collective-permute-done.12
  59.6 0.5 collective-permute-done.13
  60.1 5.1 %collective-permute-start.14 = (f32[4,64,128]{2,1,0:T(8,128)S(1)}, f32[4,64,128]{2,1,0:T(8,128)S(1)}, u32[]{:S(2)}, u32[]{:S(2)}) collective-permute-start(f32[4,64,128]{2,1,0:T(8,128)S(1)} %pad_maximum_fusion.refs_8_), channel_id=1, source_target_pairs={{0,8},{8,0},{16,24},{24,16},{32,40},{40,32},{48,56},{56,48},{64,72... | collective-permute-start | bytes 393224 | tf_op jit(solution)/shard_map/ppermute | solution.py:471
  65.2 1.0 %collective-permute-done.14.refs_9_ = f32[4,64,128]{2,1,0:T(8,128)S(1)} collective-permute-done((f32[4,64,128]{2,1,0:T(8,128)S(1)}, f32[4,64,128]{2,1,0:T(8,128)S(1)}, u32[]{:S(2)}, u32[]{:S(2)}) %collective-permute-start.14) | collective-permute-done | bytes 131104 | tf_op jit(solution)/shard_map/ppermute | solution.py:471
  66.2 0.0 copy-done.2
  66.2 1.8 %read.1 = bf16[1024,128]{1,0:T(8,128)(2,1)} custom-call(s32[4]{0:T(128)S(1)} %pad_add_fusion.pos_ref, f32[256,128]{1,0:T(8,128)S(1)} %get-tuple-element.34.after_ref.refs_0_, f32[256,128]{1,0:T(8,128)S(1)} %get-tuple-element.35.refs_1_, f32[256,128]{1,0:T(8,128)S(1)} %get-tuple-element.40.after_ref.refs_2_, f32[256,128]{1,0:T(8,128)S(1)} %get-tuple-element.41.refs_3_, ...), custom_call_target="tpu_custom_call" | custom-call | tf_op jit(solution)/shard_map/read/pallas_call | solution.py:357
  (3 shorter events, 0.0 us)
Async XLA Ops:
  0.0 18.6 %copy-start = (bf16[1,256,4,128]{3,2,1,0:T(4,128)(2,1)S(1)}, bf16[1,256,4,128]{3,2,1,0:T(4,128)(2,1)}, u32[]{:S(2)}) copy-start(bf16[1,256,4,128]{3,2,1,0:T(4,128)(2,1)} %param.5) | copy-start | bytes 786436
  9.1 5.1 %collective-permute-start = (f32[4,256,128]{2,1,0:T(8,128)}, f32[4,256,128]{2,1,0:T(8,128)S(1)}, u32[]{:S(2)}, u32[]{:S(2)}) collective-permute-start(f32[4,256,128]{2,1,0:T(8,128)} %get-tuple-element.32.own_ref), channel_id=1, source_target_pairs={{0,8},{8,0},{16,24},{24,16},{32,40},{40,32},{48,56},{56,48},{64,72... | collective-permute-start | bytes 1572872 | tf_op jit(solution)/shard_map/ppermute | solution.py:405
  15.5 6.3 %collective-permute-start.1 = (f32[192,128]{1,0:T(8,128)S(1)}, f32[192,128]{1,0:T(8,128)S(1)}, u32[]{:S(2)}, u32[]{:S(2)}) collective-permute-start(f32[192,128]{1,0:T(8,128)S(1)} %get-tuple-element.36), channel_id=1, source_target_pairs={{0,16},{8,24},{16,32},{24,40},{32,48},{40,56},{48,0},{56,8},{64,80... | collective-permute-start | bytes 294920 | tf_op jit(solution)/shard_map/ppermute | solution.py:407
  15.6 6.5 %collective-permute-start.2 = (f32[192,128]{1,0:T(8,128)S(1)}, f32[192,128]{1,0:T(8,128)S(1)}, u32[]{:S(2)}, u32[]{:S(2)}) collective-permute-start(f32[192,128]{1,0:T(8,128)S(1)} %get-tuple-element.37), channel_id=1, source_target_pairs={{0,32},{8,40},{16,48},{24,56},{32,0},{40,8},{48,16},{56,24},{64,96... | collective-permute-start | bytes 294920 | tf_op jit(solution)/shard_map/ppermute | solution.py:407
  17.5 5.7 %collective-permute-start.3 = (f32[192,128]{1,0:T(8,128)S(1)}, f32[192,128]{1,0:T(8,128)S(1)}, u32[]{:S(2)}, u32[]{:S(2)}) collective-permute-start(f32[192,128]{1,0:T(8,128)S(1)} %get-tuple-element.38), channel_id=1, source_target_pairs={{0,48},{8,56},{16,0},{24,8},{32,16},{40,24},{48,32},{56,40},{64,11... | collective-permute-start | bytes 294920 | tf_op jit(solution)/shard_map/ppermute | solution.py:407
  24.1 14.0 %copy-start.1 = (f32[4,128,128]{2,1,0:T(8,128)S(1)}, f32[4,128,128]{2,1,0:T(8,128)}, u32[]{:S(2)}) copy-start(f32[4,128,128]{2,1,0:T(8,128)} %init_ref.1) | copy-start | bytes 786436
  24.1 4.6 %collective-permute-start.6 = (f32[192,128]{1,0:T(8,128)S(1)}, f32[192,128]{1,0:T(8,128)S(1)}, u32[]{:S(2)}, u32[]{:S(2)}) collective-permute-start(f32[192,128]{1,0:T(8,128)S(1)} %get-tuple-element.39.after_ref.s0), channel_id=1, source_target_pairs={{0,192},{8,200},{16,208},{24,216},{32,224},{40,232},{48,240},{56,2... | collective-permute-start | bytes 294920 | tf_op jit(solution)/shard_map/ppermute | solution.py:418
  25.9 5.1 %collective-permute-start.5 = (f32[192,128]{1,0:T(8,128)S(1)}, f32[192,128]{1,0:T(8,128)S(1)}, u32[]{:S(2)}, u32[]{:S(2)}) collective-permute-start(f32[192,128]{1,0:T(8,128)S(1)} %get-tuple-element.39.after_ref.s0), channel_id=1, source_target_pairs={{0,128},{8,136},{16,144},{24,152},{32,160},{40,168},{48,176},{56,1... | collective-permute-start | bytes 294920 | tf_op jit(solution)/shard_map/ppermute | solution.py:418
  26.4 6.0 %collective-permute-start.4 = (f32[192,128]{1,0:T(8,128)S(1)}, f32[192,128]{1,0:T(8,128)S(1)}, u32[]{:S(2)}, u32[]{:S(2)}) collective-permute-start(f32[192,128]{1,0:T(8,128)S(1)} %get-tuple-element.39.after_ref.s0), channel_id=1, source_target_pairs={{0,64},{8,72},{16,80},{24,88},{32,96},{40,104},{48,112},{56,120},{... | collective-permute-start | bytes 294920 | tf_op jit(solution)/shard_map/ppermute | solution.py:418
  33.3 7.3 %collective-permute-start.9 = (f32[192,128]{1,0:T(8,128)S(1)}, f32[192,128]{1,0:T(8,128)S(1)}, u32[]{:S(2)}, u32[]{:S(2)}) collective-permute-start(f32[192,128]{1,0:T(8,128)S(1)} %get-tuple-element.44.after_ref.s0), channel_id=1, source_target_pairs={{0,3},{1,0},{2,1},{3,2},{4,7},{5,4},{6,5},{7,6},{8,11},{9,8},{10,9... | collective-permute-start | bytes 294920 | tf_op jit(solution)/shard_map/ppermute | solution.py:429
  37.7 8.9 %collective-permute-start.8 = (f32[192,128]{1,0:T(8,128)S(1)}, f32[192,128]{1,0:T(8,128)S(1)}, u32[]{:S(2)}, u32[]{:S(2)}) collective-permute-start(f32[192,128]{1,0:T(8,128)S(1)} %get-tuple-element.44.after_ref.s0), channel_id=1, source_target_pairs={{0,2},{1,3},{2,0},{3,1},{4,6},{5,7},{6,4},{7,5},{8,10},{9,11},{10,... | collective-permute-start | bytes 294920 | tf_op jit(solution)/shard_map/ppermute | solution.py:429
  37.7 8.9 %collective-permute-start.7 = (f32[192,128]{1,0:T(8,128)S(1)}, f32[192,128]{1,0:T(8,128)S(1)}, u32[]{:S(2)}, u32[]{:S(2)}) collective-permute-start(f32[192,128]{1,0:T(8,128)S(1)} %get-tuple-element.44.after_ref.s0), channel_id=1, source_target_pairs={{0,1},{1,2},{2,3},{3,0},{4,5},{5,6},{6,7},{7,4},{8,9},{9,10},{10,1... | collective-permute-start | bytes 294920 | tf_op jit(solution)/shard_map/ppermute | solution.py:429
  47.6 6.8 %collective-permute-start.10 = (f32[64,128]{1,0:T(8,128)S(1)}, f32[64,128]{1,0:T(8,128)S(1)}, u32[]{:S(2)}, u32[]{:S(2)}) collective-permute-start(f32[64,128]{1,0:T(8,128)S(1)} %lead.1.after_ref), channel_id=1, source_target_pairs={{0,4},{1,5},{2,6},{3,7},{4,0},{5,1},{6,2},{7,3},{8,12},{9,13},{10,... | collective-permute-start | bytes 98312 | tf_op jit(solution)/shard_map/ppermute | solution.py:449
  52.0 14.2 %copy-start.2 = (f32[4,128]{1,0:T(4,128)S(1)}, f32[4,128]{1,0:T(4,128)}, u32[]{:S(2)}) copy-start(f32[4,128]{1,0:T(4,128)} %refs_10_.1) | copy-start | bytes 6148
  55.1 4.1 %collective-permute-start.11 = (f32[64,128]{1,0:T(8,128)S(1)}, f32[64,128]{1,0:T(8,128)S(1)}, u32[]{:S(2)}, u32[]{:S(2)}) collective-permute-start(f32[64,128]{1,0:T(8,128)S(1)} %get-tuple-element.52), channel_id=1, source_target_pairs={{0,16},{8,24},{16,32},{24,40},{32,48},{40,56},{48,0},{56,8},{64,80... | collective-permute-start | bytes 98312 | tf_op jit(solution)/shard_map/ppermute | solution.py:469
  55.2 4.4 %collective-permute-start.12 = (f32[64,128]{1,0:T(8,128)S(1)}, f32[64,128]{1,0:T(8,128)S(1)}, u32[]{:S(2)}, u32[]{:S(2)}) collective-permute-start(f32[64,128]{1,0:T(8,128)S(1)} %get-tuple-element.53), channel_id=1, source_target_pairs={{0,32},{8,40},{16,48},{24,56},{32,0},{40,8},{48,16},{56,24},{64,96... | collective-permute-start | bytes 98312 | tf_op jit(solution)/shard_map/ppermute | solution.py:469
  55.3 4.8 %collective-permute-start.13 = (f32[64,128]{1,0:T(8,128)S(1)}, f32[64,128]{1,0:T(8,128)S(1)}, u32[]{:S(2)}, u32[]{:S(2)}) collective-permute-start(f32[64,128]{1,0:T(8,128)S(1)} %get-tuple-element.54), channel_id=1, source_target_pairs={{0,48},{8,56},{16,0},{24,8},{32,16},{40,24},{48,32},{56,40},{64,11... | collective-permute-start | bytes 98312 | tf_op jit(solution)/shard_map/ppermute | solution.py:469
  60.1 6.1 %collective-permute-start.14 = (f32[4,64,128]{2,1,0:T(8,128)S(1)}, f32[4,64,128]{2,1,0:T(8,128)S(1)}, u32[]{:S(2)}, u32[]{:S(2)}) collective-permute-start(f32[4,64,128]{2,1,0:T(8,128)S(1)} %pad_maximum_fusion.refs_8_), channel_id=1, source_target_pairs={{0,8},{8,0},{16,24},{24,16},{32,40},{40,32},{48,56},{56,48},{64,72... | collective-permute-start | bytes 393224 | tf_op jit(solution)/shard_map/ppermute | solution.py:471

commit v4 on v3

--- a/solution.py
+++ b/solution.py
@@ -189,12 +189,17 @@
         out_refs[k][D:, :] = moved[D:] + jnp.where(lower, sib_s, own_s)
 
 
-def ordered_load(slots, place, scratch):
+def ordered_cyclic(slots, place, scratch):
     n = len(slots)
     for k in range(n):
         scratch[lax.rem(place + n - k, n)] = slots[k][...]
 
 
+def ordered_xor(slots, place, scratch):
+    for k, slot in enumerate(slots):
+        scratch[place ^ k] = slot[...]
+
+
 def msg_compose(rows, second):
     moved = mm(rows, second[:D])
     return jnp.concatenate([moved[:D], moved[D:] + second[D:]], axis=0)
@@ -204,45 +209,55 @@
     return mm(state, second[:D]) + second[D:]
 
 
-def prefix_totals(slots, place, total_ref, pre_ref, scratch):
-    ordered_load(slots, place, scratch)
-    first = scratch[0]
-    tail = msg_compose(scratch[2], scratch[3])
-    second = msg_compose(first, scratch[1])
-    total_ref[...] = msg_compose(second, tail)
-    pre_ref[0] = first
-    pre_ref[1] = second
-    pre_ref[2] = msg_compose(second, scratch[2])
-
-
-def row_kernel(pos_ref, s0, s1, s2, s3, after_ref, total_ref, pre_ref, scratch):
-    prefix_totals([s0, s1, s2, s3], pos_ref[0], total_ref, pre_ref, scratch)
-
-
-def column_kernel(pos_ref, s0, s1, s2, s3, after_ref, total_ref, pre_ref, scratch):
-    prefix_totals([s0, s1, s2, s3], pos_ref[1], total_ref, pre_ref, scratch)
-
-
-def path_kernel(pos_ref, ypre_ref, xpre_ref, init_ref, after_ref, path_ref, start_ref, hold):
+def write_total(total_ref, hold):
+    tail = msg_compose(hold[2], hold[3])
+    total_ref[...] = msg_compose(msg_compose(hold[0], hold[1]), tail)
+
+
+def row_kernel(pos_ref, s0, s1, s2, s3, after_ref, total_ref, hold):
+    ordered_cyclic([s0, s1, s2, s3], pos_ref[0], hold)
+    write_total(total_ref, hold)
+
+
+def column_kernel(pos_ref, s0, s1, s2, s3, after_ref, total_ref, hold):
+    ordered_xor([s0, s1, s2, s3], pos_ref[1], hold)
+    write_total(total_ref, hold)
+
+
+def place_prefix(place, hold):
+    first = hold[0]
+    second = msg_compose(first, hold[1])
+    third = msg_compose(second, hold[2])
+    out = jnp.where(iota2((MSG, D), 0) == iota2((MSG, D), 1), 1.0, 0.0)
+    for i, prefix in enumerate((first, second, third)):
+        out = jnp.where(place == i + 1, prefix, out)
+    return out
+
+
+def path_kernel(pos_ref, *refs):
+    xslots, yslots = refs[:4], refs[4:8]
+    init_ref, after_ref, path_ref, start_ref, xhold, yhold, turn = refs[8:]
     x = pos_ref[0]
     y = pos_ref[1]
     core = pos_ref[2]
-    here = ypre_ref[lax.max(y, 1) - 1]
-    here = jnp.where(
-        y == 0, jnp.where(iota2((MSG, D), 0) == iota2((MSG, D), 1), 1.0, 0.0), here
-    )
+    ordered_cyclic(xslots, x, xhold)
+    ordered_xor(yslots, y, yhold)
+    here = place_prefix(y, yhold)
+    first = xhold[0]
+    second = msg_compose(first, xhold[1])
+    third = msg_compose(second, xhold[2])
     path_ref[0] = here
     left = wide(here)
-    for i in range(XS - 1):
-        moved = mm_pre(left, tall_wide(xpre_ref[i, :D, :]))
+    for i, prefix in enumerate((first, second, third)):
+        moved = mm_pre(left, tall_wide(prefix[:D]))
         path_ref[i + 1, :D, :] = moved[:D]
-        path_ref[i + 1, D:, :] = moved[D:] + xpre_ref[i, D:, :]
-    hold[...] = init_ref[x].T
-    start_ref[...] = hold[pl.ds(pl.multiple_of(core * HALF, HALF), HALF), :]
+        path_ref[i + 1, D:, :] = moved[D:] + prefix[D:]
+    turn[...] = init_ref[x].T
+    start_ref[...] = turn[pl.ds(pl.multiple_of(core * HALF, HALF), HALF), :]
 
 
 def lead_kernel(pos_ref, s0, s1, s2, s3, start_ref, after_ref, lead_ref, hold):
-    ordered_load([s0, s1, s2, s3], lax.rem(pos_ref[3], ZG), hold)
+    ordered_xor([s0, s1, s2, s3], lax.rem(pos_ref[3], ZG), hold)
     tail = msg_compose(hold[2], hold[3])
     state = advance(advance(start_ref[...], hold[0]), hold[1])
     lead_ref[...] = advance(state, tail)
@@ -250,14 +265,8 @@
 
 def fuse_kernel(pos_ref, s0, s1, s2, s3, path_ref, after_ref, fuse_ref, hold):
     g = lax.rem(pos_ref[3], ZG)
-    ordered_load([s0, s1, s2, s3], g, hold)
-    window = jnp.where(iota2((MSG, D), 0) == iota2((MSG, D), 1), 1.0, 0.0)
-    first = hold[0]
-    second = msg_compose(first, hold[1])
-    third = msg_compose(second, hold[2])
-    window = jnp.where(g == 1, first, window)
-    window = jnp.where(g == 2, second, window)
-    window = jnp.where(g == 3, third, window)
+    ordered_xor([s0, s1, s2, s3], g, hold)
+    window = place_prefix(g, hold)
     left = wide(window)
     for i in range(XS):
         path = path_ref[i]
@@ -301,7 +310,7 @@
     moves = [mm_nt(projects[b], prefixes[b]) for b in range(nblk)]
     for b in range(nblk):
         part = slice(b * span, (b + 1) * span)
-        reach_ref[part, :] = moves[b][:, :D]
+        reach_ref[part, :] = wide(moves[b][:, :D])
         base_ref[part, :] = moves[b][:, D:] + locals_[b]
 
 
@@ -323,8 +332,14 @@
             spec(sib),
             pl.BlockSpec(memory_space=pl.ANY),
         ],
-        out_specs=[pl.BlockSpec((tokens, D), lambda i: (0, 0))] * 2,
-        out_shape=[jax.ShapeDtypeStruct((tokens, D), f32)] * 2,
+        out_specs=[
+            pl.BlockSpec((tokens, 2 * D), lambda i: (0, 0)),
+            pl.BlockSpec((tokens, D), lambda i: (0, 0)),
+        ],
+        out_shape=[
+            jax.ShapeDtypeStruct((tokens, 2 * D), bf16),
+            jax.ShapeDtypeStruct((tokens, D), f32),
+        ],
         scratch_shapes=[pltpu.VMEM(q.shape, f32)],
         compiler_params=pltpu.CompilerParams(vmem_limit_bytes=6 << 20),
         cost_estimate=pl.CostEstimate(
@@ -346,7 +361,10 @@
         state = jnp.concatenate(
             [jnp.where(lower, mine, other), jnp.where(lower, other, mine)], axis=0
         )
-        read = mm_nt(reaches[h][...], state) + bases[h][...]
+        high, low = split(state)
+        both = jnp.concatenate([high, low], axis=0)
+        moved = dot_nt(reaches[h][...], jnp.concatenate([both, both], axis=1))
+        read = moved[:, :D] + moved[:, D:] + bases[h][...]
         scale = lax.rsqrt(jnp.mean(read * read, axis=-1, keepdims=True) + 1e-06)
         rows[pl.ds(h, tokens, stride=HEADS), :] = read * scale * gain_ref[h : h + 1, :]
     out_ref[...] = rows[...].astype(bf16)
@@ -389,12 +407,10 @@
 
     swap = seq_perm(lambda y, x, c: (y, x, 1 - c))
     along_x = [seq_perm(lambda y, x, c, k=k: (y, (x + k) % XS, c)) for k in range(1, XS)]
-    along_y = [seq_perm(lambda y, x, c, k=k: ((y + k) % YS, x, c)) for k in range(1, YS)]
+    along_y = [seq_perm(lambda y, x, c, k=k: (y ^ k, x, c)) for k in range(1, YS)]
     segs = 8
-    along_z = [
-        [(i, i // ZG * ZG + (i + k) % ZG) for i in range(segs)] for k in range(1, ZG)
-    ]
-    jump = [(i, (i + ZG) % segs) for i in range(segs)]
+    along_z = [[(i, i ^ k) for i in range(segs)] for k in range(1, ZG)]
+    jump = [(i, segs - 1 - i) for i in range(segs)]
 
     keys = key_rows.reshape(steps * HEADS, D)
     values = value_rows.reshape(steps * HEADS, D)
@@ -406,34 +422,24 @@
     slots = small_call(chip_kernel, "chip", pos, [pair, sib], [(MSG, D)] * XS)
     slots = [slots[0]] + [lax.ppermute(s, "seq", p) for s, p in zip(slots[1:], along_x)]
     reaches = [reach_call(pos, query, r, z, sib, slots[0], 0)]
-    total, xpre = small_call(
-        row_kernel,
-        "row",
-        pos,
-        slots,
-        [(MSG, D), (XS - 1, MSG, D)],
-        [(XS, MSG, D)],
-        after=reaches[-1][0],
+    xslots = slots
+    (total,) = small_call(
+        row_kernel, "row", pos, slots, [(MSG, D)], [(XS, MSG, D)], after=reaches[-1][0]
     )
     slots = [total] + [lax.ppermute(total, "seq", p) for p in along_y]
+    yslots = slots
     reaches.append(reach_call(pos, query, r, z, sib, total, 1))
-    total, ypre = small_call(
-        column_kernel,
-        "column",
-        pos,
-        slots,
-        [(MSG, D), (YS - 1, MSG, D)],
-        [(YS, MSG, D)],
-        after=reaches[-1][0],
+    (total,) = small_call(
+        column_kernel, "column", pos, slots, [(MSG, D)], [(YS, MSG, D)], after=reaches[-1][0]
     )
     slots = [total] + [lax.ppermute(total, "seg", p) for p in along_z]
     path, start = small_call(
         path_kernel,
         "path",
         pos,
-        [ypre, xpre, initial_state],
+        [*xslots, *yslots, initial_state],
         [(XS, MSG, D), (HALF, D)],
-        [(D, D)],
+        [(XS, MSG, D), (YS, MSG, D), (D, D)],
         after=total,
     )
     reaches.append(reach_call(pos, query, r, z, sib, path, 2))

time: 68.1 us -> 65 us (0.954)
  waiting for transfers between devices: 17.9 us -> 13.3 us
  starting transfers between devices: 25.3 us -> 26.6 us
    ppermute x3, waiting for transfers between devices: 3.65 us -> 1.81 us  [per_device(): slots = [total] + [lax.ppermute(total, 'seq', p) for p in along_y]]
    ppermute x3, waiting for transfers between devices: 5.97 us -> 4.44 us  [per_device(): slots = [total] + [lax.ppermute(total, 'seg', p) for p in along_z]]
    ppermute x6, starting transfers between devices: 5.9 us -> 7.22 us  [per_device(): lax.ppermute(s, 'seq', p)]
    ppermute x1, starting transfers between devices: 5.09 us -> 3.92 us  [per_device(): other = lax.ppermute(mine, 'seq', swap)]
    ppermute x1, starting transfers between devices: 3.34 us -> 4.07 us  [per_device(): early = lax.ppermute(lead, 'seg', jump)]
  transfers between devices with their start and end apart: 15 -> 15, of which waited for: 12 -> 9; matrix products, arithmetic and copies ran while one was open for 0% -> 0% of each run, Pallas kernels for 13% -> 14%
where the time goes in v4:
time: 65 us; the launch traced here: 64.9 us
  starting transfers between devices  26.6 us (41%)
  Pallas kernels  24.8 us (38%)
  waiting for transfers between devices  13.3 us (20%)
    pallas_call x1, Pallas kernels, factor_call(): pl.pallas_call(factor_kernel, in_specs=[pl.BlockSpec(memory_space=pl.ANY)...  9.04 us
    pallas_call x8, Pallas kernels, small_call(): pl.pallas_call(kernel, in_specs=[pl.BlockSpec(memory_space=pltpu.SMEM)] +...  8.89 us
    ppermute x6, starting transfers between devices, per_device(): lax.ppermute(s, 'seq', p)  7.22 us
    pallas_call x4, Pallas kernels, reach_call(): pl.pallas_call(functools.partial(reach_kernel, head=head), grid=(1,), in_...  6.87 us
    ppermute x3, starting transfers between devices, per_device(): slots = [total] + [lax.ppermute(total, 'seg', p) for p in along_z]  4.7 us
    ppermute x3, waiting for transfers between devices, per_device(): slots = [total] + [lax.ppermute(total, 'seg', p) for p in along_z]  4.44 us
    ppermute x6, waiting for transfers between devices, per_device(): lax.ppermute(s, 'seq', p)  4.35 us
    ppermute x1, starting transfers between devices, per_device(): early = lax.ppermute(lead, 'seg', jump)  4.07 us
  transfers between devices with their start and end apart: 15, of which 9 were waited for; matrix products, arithmetic and copies ran while one was open for 0% of the time, Pallas kernels for 14%

profile of v4, /device:TPU:1, one launch (start us, length us, event | category | flops | bytes accessed | tf_op | source)
XLA Modules:
  0.0 64.9 jit_solution(18422106304778324926)
XLA Ops:
  0.0 9.0 %factor.1 = (f32[4,256,128]{2,1,0:T(8,128)}, f32[4,4,256,128]{3,2,1,0:T(8,128)S(1)}, bf16[4,512,128]{2,1,0:T(8,128)(2,1)S(1)}) custom-call(bf16[2048,128]{1,0:T(8,128)(2,1)} %bitcast.17, bf16[2048,128]{1,0:T(8,128)(2,1)} %bitcast.18), custom_call_target="tpu_custom_call" | custom-call | tf_op jit(solution)/shard_map/factor/pallas_call | solution.py:158
  9.0 3.3 %collective-permute-start = (f32[4,256,128]{2,1,0:T(8,128)}, f32[4,256,128]{2,1,0:T(8,128)S(1)}, u32[]{:S(2)}, u32[]{:S(2)}) collective-permute-start(f32[4,256,128]{2,1,0:T(8,128)} %get-tuple-element.28.own_ref), channel_id=1, source_target_pairs={{0,8},{8,0},{16,24},{24,16},{32,40},{40,32},{48,56},{56,48},{64,72... | collective-permute-start | bytes 1572872 | tf_op jit(solution)/shard_map/ppermute | solution.py:421
  12.4 0.1 pad_add_fusion.pos_ref
  12.5 1.7 %collective-permute-done.sib_ref = f32[4,256,128]{2,1,0:T(8,128)S(1)} collective-permute-done((f32[4,256,128]{2,1,0:T(8,128)}, f32[4,256,128]{2,1,0:T(8,128)S(1)}, u32[]{:S(2)}, u32[]{:S(2)}) %collective-permute-start) | collective-permute-done | bytes 524320 | tf_op jit(solution)/shard_map/ppermute | solution.py:421
  14.1 1.3 %chip.1 = (f32[192,128]{1,0:T(8,128)S(1)}, f32[192,128]{1,0:T(8,128)S(1)}, f32[192,128]{1,0:T(8,128)S(1)}, f32[192,128]{1,0:T(8,128)S(1)}) custom-call(s32[4]{0:T(128)S(1)} %pad_add_fusion.pos_ref, f32[4,256,128]{2,1,0:T(8,128)} %get-tuple-element.28.own_ref, f32[4,256,128]{2,1,0:T(8,128)S(1)} %collective-permute-done.sib_ref), custom_call_target="tpu_custom_call" | custom-call | tf_op jit(solution)/shard_map/chip/pallas_call | solution.py:375
  15.5 0.1 collective-permute-start.1
  15.6 1.9 %collective-permute-start.2 = (f32[192,128]{1,0:T(8,128)S(1)}, f32[192,128]{1,0:T(8,128)S(1)}, u32[]{:S(2)}, u32[]{:S(2)}) collective-permute-start(f32[192,128]{1,0:T(8,128)S(1)} %get-tuple-element.33), channel_id=1, source_target_pairs={{0,32},{8,40},{16,48},{24,56},{32,0},{40,8},{48,16},{56,24},{64,96... | collective-permute-start | bytes 294920 | tf_op jit(solution)/shard_map/ppermute | solution.py:423
  17.5 1.2 %collective-permute-start.3 = (f32[192,128]{1,0:T(8,128)S(1)}, f32[192,128]{1,0:T(8,128)S(1)}, u32[]{:S(2)}, u32[]{:S(2)}) collective-permute-start(f32[192,128]{1,0:T(8,128)S(1)} %get-tuple-element.34), channel_id=1, source_target_pairs={{0,48},{8,56},{16,0},{24,8},{32,16},{40,24},{48,32},{56,40},{64,11... | collective-permute-start | bytes 294920 | tf_op jit(solution)/shard_map/ppermute | solution.py:423
  18.6 0.0 copy-done
  18.6 1.7 %reach.4 = (bf16[256,256]{1,0:T(8,128)(2,1)S(1)}, f32[256,128]{1,0:T(8,128)S(1)}) custom-call(s32[4]{0:T(128)S(1)} %pad_add_fusion.pos_ref, bf16[1024,128]{1,0:T(8,128)(2,1)S(1)} %bitcast.12, bf16[4,512,128]{2,1,0:T(8,128)(2,1)S(1)} %get-tuple-element.26.r_ref, f32[4,4,256,128]{3,2,1,0:T(8,128)S(1)} %get-tuple-element.27.z_ref, ...), custom_call_target="tpu_custom_call" | custom-call | flops 400000000 | bytes 3000000 | tf_op jit(solution)/shard_map/reach/pallas_call | solution.py:324
  20.4 1.4 %collective-permute-done.1.s1.refs_1_ = f32[192,128]{1,0:T(8,128)S(1)} collective-permute-done((f32[192,128]{1,0:T(8,128)S(1)}, f32[192,128]{1,0:T(8,128)S(1)}, u32[]{:S(2)}, u32[]{:S(2)}) %collective-permute-start.1) | collective-permute-done | bytes 98336 | tf_op jit(solution)/shard_map/ppermute | solution.py:423
  21.7 0.4 collective-permute-done.2.s2.refs_2_
  22.1 1.0 %collective-permute-done.3.s3.refs_3_ = f32[192,128]{1,0:T(8,128)S(1)} collective-permute-done((f32[192,128]{1,0:T(8,128)S(1)}, f32[192,128]{1,0:T(8,128)S(1)}, u32[]{:S(2)}, u32[]{:S(2)}) %collective-permute-start.3) | collective-permute-done | bytes 98336 | tf_op jit(solution)/shard_map/ppermute | solution.py:423
  23.1 0.9 %row.1.after_ref.s0.refs_4_ = f32[192,128]{1,0:T(8,128)S(1)} custom-call(s32[4]{0:T(128)S(1)} %pad_add_fusion.pos_ref, f32[192,128]{1,0:T(8,128)S(1)} %get-tuple-element.29.after_ref.s0.refs_0_, f32[192,128]{1,0:T(8,128)S(1)} %collective-permute-done.1.s1.refs_1_, f32[192,128]{1,0:T(8,128)S(1)} %collective-permute-done.2.s2.refs_2_, ...), custom_call_target="tpu_custom_call" | custom-call | tf_op jit(solution)/shard_map/row/pallas_call | solution.py:375
  24.1 0.0 copy-start.1
  24.1 1.8 %collective-permute-start.6 = (f32[192,128]{1,0:T(8,128)S(1)}, f32[192,128]{1,0:T(8,128)S(1)}, u32[]{:S(2)}, u32[]{:S(2)}) collective-permute-start(f32[192,128]{1,0:T(8,128)S(1)} %row.1.after_ref.s0.refs_4_), channel_id=1, source_target_pairs={{0,192},{8,200},{16,208},{24,216},{32,224},{40,232},{48,240},{56,2... | collective-permute-start | bytes 294920 | tf_op jit(solution)/shard_map/ppermute | solution.py:429
  25.9 0.5 collective-permute-start.5
  26.3 1.1 %collective-permute-start.4 = (f32[192,128]{1,0:T(8,128)S(1)}, f32[192,128]{1,0:T(8,128)S(1)}, u32[]{:S(2)}, u32[]{:S(2)}) collective-permute-start(f32[192,128]{1,0:T(8,128)S(1)} %row.1.after_ref.s0.refs_4_), channel_id=1, source_target_pairs={{0,64},{8,72},{16,80},{24,88},{32,96},{40,104},{48,112},{56,120},{... | collective-permute-start | bytes 294920 | tf_op jit(solution)/shard_map/ppermute | solution.py:429
  27.4 1.7 %reach.5 = (bf16[256,256]{1,0:T(8,128)(2,1)S(1)}, f32[256,128]{1,0:T(8,128)S(1)}) custom-call(s32[4]{0:T(128)S(1)} %pad_add_fusion.pos_ref, bf16[1024,128]{1,0:T(8,128)(2,1)S(1)} %bitcast.13, bf16[4,512,128]{2,1,0:T(8,128)(2,1)S(1)} %get-tuple-element.26.r_ref, f32[4,4,256,128]{3,2,1,0:T(8,128)S(1)} %get-tuple-element.27.z_ref, ...), custom_call_target="tpu_custom_call" | custom-call | flops 400000000 | bytes 3000000 | tf_op jit(solution)/shard_map/reach/pallas_call | solution.py:324
  29.1 0.0 collective-permute-done.6.s3.refs_7_
  29.2 1.8 %collective-permute-done.5.s2.refs_6_ = f32[192,128]{1,0:T(8,128)S(1)} collective-permute-done((f32[192,128]{1,0:T(8,128)S(1)}, f32[192,128]{1,0:T(8,128)S(1)}, u32[]{:S(2)}, u32[]{:S(2)}) %collective-permute-start.5) | collective-permute-done | bytes 98336 | tf_op jit(solution)/shard_map/ppermute | solution.py:429
  31.0 0.0 collective-permute-done.4.s1.refs_5_
  31.0 0.9 %column.1.refs_9_.s0 = f32[192,128]{1,0:T(8,128)S(1)} custom-call(s32[4]{0:T(128)S(1)} %pad_add_fusion.pos_ref, f32[192,128]{1,0:T(8,128)S(1)} %row.1.after_ref.s0.refs_4_, f32[192,128]{1,0:T(8,128)S(1)} %collective-permute-done.4.s1.refs_5_, f32[192,128]{1,0:T(8,128)S(1)} %collective-permute-done.5.s2.refs_6_, ...), custom_call_target="tpu_custom_call" | custom-call | tf_op jit(solution)/shard_map/column/pallas_call | solution.py:375
  31.9 4.3 %collective-permute-start.9 = (f32[192,128]{1,0:T(8,128)S(1)}, f32[192,128]{1,0:T(8,128)S(1)}, u32[]{:S(2)}, u32[]{:S(2)}) collective-permute-start(f32[192,128]{1,0:T(8,128)S(1)} %column.1.refs_9_.s0), channel_id=1, source_target_pairs={{0,3},{1,2},{2,1},{3,0},{4,7},{5,6},{6,5},{7,4},{8,11},{9,10},{10,... | collective-permute-start | bytes 294920 | tf_op jit(solution)/shard_map/ppermute | solution.py:435
  36.2 0.0 collective-permute-start.8
  36.2 0.4 collective-permute-start.7
  36.6 1.1 %path.1 = (f32[4,192,128]{2,1,0:T(8,128)S(1)}, f32[64,128]{1,0:T(8,128)S(1)}) custom-call(s32[4]{0:T(128)S(1)} %pad_add_fusion.pos_ref, f32[192,128]{1,0:T(8,128)S(1)} %get-tuple-element.29.after_ref.s0.refs_0_, f32[192,128]{1,0:T(8,128)S(1)} %collective-permute-done.1.s1.refs_1_, f32[192,128]{1,0:T(8,128)S(1)} %collective-permute-done.2.s2.refs_2_, ...), custom_call_target="tpu_custom_call" | custom-call | tf_op jit(solution)/shard_map/path/pallas_call | solution.py:375
  37.7 1.7 %reach.6 = (bf16[256,256]{1,0:T(8,128)(2,1)S(1)}, f32[256,128]{1,0:T(8,128)S(1)}) custom-call(s32[4]{0:T(128)S(1)} %pad_add_fusion.pos_ref, bf16[1024,128]{1,0:T(8,128)(2,1)S(1)} %bitcast.14, bf16[4,512,128]{2,1,0:T(8,128)(2,1)S(1)} %get-tuple-element.26.r_ref, f32[4,4,256,128]{3,2,1,0:T(8,128)S(1)} %get-tuple-element.27.z_ref, ...), custom_call_target="tpu_custom_call" | custom-call | flops 400000000 | bytes 3000000 | tf_op jit(solution)/shard_map/reach/pallas_call | solution.py:324
  39.5 0.0 collective-permute-done.9.s3
  39.5 4.4 %collective-permute-done.8.s2 = f32[192,128]{1,0:T(8,128)S(1)} collective-permute-done((f32[192,128]{1,0:T(8,128)S(1)}, f32[192,128]{1,0:T(8,128)S(1)}, u32[]{:S(2)}, u32[]{:S(2)}) %collective-permute-start.8) | collective-permute-done | bytes 98336 | tf_op jit(solution)/shard_map/ppermute | solution.py:435
  43.9 0.0 collective-permute-done.7.s1
  43.9 1.0 %lead.1.after_ref = f32[64,128]{1,0:T(8,128)S(1)} custom-call(s32[4]{0:T(128)S(1)} %pad_add_fusion.pos_ref, f32[192,128]{1,0:T(8,128)S(1)} %column.1.refs_9_.s0, f32[192,128]{1,0:T(8,128)S(1)} %collective-permute-done.7.s1, f32[192,128]{1,0:T(8,128)S(1)} %collective-permute-done.8.s2, f32[192,128]{1,0:T(8,128)S(1)} %collective-permute-done.9.s3, ...), custom_call_target="tpu_custom_call" | custom-call | tf_op jit(solution)/shard_map/lead/pallas_call | solution.py:375
  44.9 4.1 %collective-permute-start.10 = (f32[64,128]{1,0:T(8,128)S(1)}, f32[64,128]{1,0:T(8,128)S(1)}, u32[]{:S(2)}, u32[]{:S(2)}) collective-permute-start(f32[64,128]{1,0:T(8,128)S(1)} %lead.1.after_ref), channel_id=1, source_target_pairs={{0,7},{1,6},{2,5},{3,4},{4,3},{5,2},{6,1},{7,0},{8,15},{9,14},{10,... | collective-permute-start | bytes 98312 | tf_op jit(solution)/shard_map/ppermute | solution.py:455
  49.0 1.1 %fuse.1.after_ref.fuse_ref = f32[4,192,128]{2,1,0:T(8,128)S(1)} custom-call(s32[4]{0:T(128)S(1)} %pad_add_fusion.pos_ref, f32[192,128]{1,0:T(8,128)S(1)} %column.1.refs_9_.s0, f32[192,128]{1,0:T(8,128)S(1)} %collective-permute-done.7.s1, f32[192,128]{1,0:T(8,128)S(1)} %collective-permute-done.8.s2, f32[192,128]{1,0:T(8,128)S(1)} %collective-permute-done.9.s3, ...), custom_call_target="tpu_custom_call" | custom-call | tf_op jit(solution)/shard_map/fuse/pallas_call | solution.py:375
  50.1 0.0 copy-start.2
  50.1 1.7 %reach.7 = (bf16[256,256]{1,0:T(8,128)(2,1)S(1)}, f32[256,128]{1,0:T(8,128)S(1)}) custom-call(s32[4]{0:T(128)S(1)} %pad_add_fusion.pos_ref, bf16[1024,128]{1,0:T(8,128)(2,1)S(1)} %bitcast.15, bf16[4,512,128]{2,1,0:T(8,128)(2,1)S(1)} %get-tuple-element.26.r_ref, f32[4,4,256,128]{3,2,1,0:T(8,128)S(1)} %get-tuple-element.27.z_ref, ...), custom_call_target="tpu_custom_call" | custom-call | flops 400000000 | bytes 3000000 | tf_op jit(solution)/shard_map/reach/pallas_call | solution.py:324
  51.8 0.0 collective-permute-done.10.early_ref
  51.8 0.8 %entry.1 = (f32[64,128]{1,0:T(8,128)S(1)}, f32[64,128]{1,0:T(8,128)S(1)}, f32[64,128]{1,0:T(8,128)S(1)}, f32[64,128]{1,0:T(8,128)S(1)}) custom-call(s32[4]{0:T(128)S(1)} %pad_add_fusion.pos_ref, f32[64,128]{1,0:T(8,128)S(1)} %get-tuple-element.40.start_ref, f32[64,128]{1,0:T(8,128)S(1)} %collective-permute-done.10.early_ref, ...), custom_call_target="tpu_custom_call" | custom-call | tf_op jit(solution)/shard_map/entry/pallas_call | solution.py:375
  52.6 0.6 collective-permute-start.11
  53.2 2.2 %collective-permute-start.12 = (f32[64,128]{1,0:T(8,128)S(1)}, f32[64,128]{1,0:T(8,128)S(1)}, u32[]{:S(2)}, u32[]{:S(2)}) collective-permute-start(f32[64,128]{1,0:T(8,128)S(1)} %get-tuple-element.45), channel_id=1, source_target_pairs={{0,32},{8,40},{16,48},{24,56},{32,0},{40,8},{48,16},{56,24},{64,96... | collective-permute-start | bytes 98312 | tf_op jit(solution)/shard_map/ppermute | solution.py:475
  55.5 1.2 %collective-permute-start.13 = (f32[64,128]{1,0:T(8,128)S(1)}, f32[64,128]{1,0:T(8,128)S(1)}, u32[]{:S(2)}, u32[]{:S(2)}) collective-permute-start(f32[64,128]{1,0:T(8,128)S(1)} %get-tuple-element.46), channel_id=1, source_target_pairs={{0,48},{8,56},{16,0},{24,8},{32,16},{40,24},{48,32},{56,40},{64,11... | collective-permute-start | bytes 98312 | tf_op jit(solution)/shard_map/ppermute | solution.py:475
  56.7 0.0 collective-permute-done.11
  56.7 0.8 %collective-permute-done.12 = f32[64,128]{1,0:T(8,128)S(1)} collective-permute-done((f32[64,128]{1,0:T(8,128)S(1)}, f32[64,128]{1,0:T(8,128)S(1)}, u32[]{:S(2)}, u32[]{:S(2)}) %collective-permute-start.12) | collective-permute-done | bytes 32800 | tf_op jit(solution)/shard_map/ppermute | solution.py:475
  57.5 0.7 %collective-permute-done.13 = f32[64,128]{1,0:T(8,128)S(1)} collective-permute-done((f32[64,128]{1,0:T(8,128)S(1)}, f32[64,128]{1,0:T(8,128)S(1)}, u32[]{:S(2)}, u32[]{:S(2)}) %collective-permute-start.13) | collective-permute-done | bytes 32800 | tf_op jit(solution)/shard_map/ppermute | solution.py:475
  58.3 3.9 %collective-permute-start.14 = (f32[4,64,128]{2,1,0:T(8,128)S(1)}, f32[4,64,128]{2,1,0:T(8,128)S(1)}, u32[]{:S(2)}, u32[]{:S(2)}) collective-permute-start(f32[4,64,128]{2,1,0:T(8,128)S(1)} %pad_maximum_fusion.refs_8_), channel_id=1, source_target_pairs={{0,8},{8,0},{16,24},{24,16},{32,40},{40,32},{48,56},{56,48},{64,72... | collective-permute-start | bytes 393224 | tf_op jit(solution)/shard_map/ppermute | solution.py:477
  62.2 1.0 %collective-permute-done.14.refs_9_ = f32[4,64,128]{2,1,0:T(8,128)S(1)} collective-permute-done((f32[4,64,128]{2,1,0:T(8,128)S(1)}, f32[4,64,128]{2,1,0:T(8,128)S(1)}, u32[]{:S(2)}, u32[]{:S(2)}) %collective-permute-start.14) | collective-permute-done | bytes 131104 | tf_op jit(solution)/shard_map/ppermute | solution.py:477
  63.2 0.0 copy-done.2
  63.2 1.7 %read.1 = bf16[1024,128]{1,0:T(8,128)(2,1)} custom-call(s32[4]{0:T(128)S(1)} %pad_add_fusion.pos_ref, bf16[256,256]{1,0:T(8,128)(2,1)S(1)} %get-tuple-element.30.after_ref.refs_0_, f32[256,128]{1,0:T(8,128)S(1)} %get-tuple-element.31.refs_1_, bf16[256,256]{1,0:T(8,128)(2,1)S(1)} %get-tuple-element.35.after_ref.refs_2_, ...), custom_call_target="tpu_custom_call" | custom-call | tf_op jit(solution)/shard_map/read/pallas_call | solution.py:375
  (3 shorter events, 0.0 us)
Async XLA Ops:
  0.0 18.6 %copy-start = (bf16[1,256,4,128]{3,2,1,0:T(4,128)(2,1)S(1)}, bf16[1,256,4,128]{3,2,1,0:T(4,128)(2,1)}, u32[]{:S(2)}) copy-start(bf16[1,256,4,128]{3,2,1,0:T(4,128)(2,1)} %param.5) | copy-start | bytes 786436
  9.0 5.1 %collective-permute-start = (f32[4,256,128]{2,1,0:T(8,128)}, f32[4,256,128]{2,1,0:T(8,128)S(1)}, u32[]{:S(2)}, u32[]{:S(2)}) collective-permute-start(f32[4,256,128]{2,1,0:T(8,128)} %get-tuple-element.28.own_ref), channel_id=1, source_target_pairs={{0,8},{8,0},{16,24},{24,16},{32,40},{40,32},{48,56},{56,48},{64,72... | collective-permute-start | bytes 1572872 | tf_op jit(solution)/shard_map/ppermute | solution.py:421
  15.5 6.3 %collective-permute-start.1 = (f32[192,128]{1,0:T(8,128)S(1)}, f32[192,128]{1,0:T(8,128)S(1)}, u32[]{:S(2)}, u32[]{:S(2)}) collective-permute-start(f32[192,128]{1,0:T(8,128)S(1)} %get-tuple-element.32), channel_id=1, source_target_pairs={{0,16},{8,24},{16,32},{24,40},{32,48},{40,56},{48,0},{56,8},{64,80... | collective-permute-start | bytes 294920 | tf_op jit(solution)/shard_map/ppermute | solution.py:423
  15.6 6.5 %collective-permute-start.2 = (f32[192,128]{1,0:T(8,128)S(1)}, f32[192,128]{1,0:T(8,128)S(1)}, u32[]{:S(2)}, u32[]{:S(2)}) collective-permute-start(f32[192,128]{1,0:T(8,128)S(1)} %get-tuple-element.33), channel_id=1, source_target_pairs={{0,32},{8,40},{16,48},{24,56},{32,0},{40,8},{48,16},{56,24},{64,96... | collective-permute-start | bytes 294920 | tf_op jit(solution)/shard_map/ppermute | solution.py:423
  17.5 5.7 %collective-permute-start.3 = (f32[192,128]{1,0:T(8,128)S(1)}, f32[192,128]{1,0:T(8,128)S(1)}, u32[]{:S(2)}, u32[]{:S(2)}) collective-permute-start(f32[192,128]{1,0:T(8,128)S(1)} %get-tuple-element.34), channel_id=1, source_target_pairs={{0,48},{8,56},{16,0},{24,8},{32,16},{40,24},{48,32},{56,40},{64,11... | collective-permute-start | bytes 294920 | tf_op jit(solution)/shard_map/ppermute | solution.py:423
  24.1 12.5 %copy-start.1 = (f32[4,128,128]{2,1,0:T(8,128)S(1)}, f32[4,128,128]{2,1,0:T(8,128)}, u32[]{:S(2)}) copy-start(f32[4,128,128]{2,1,0:T(8,128)} %refs_8_.1) | copy-start | bytes 786436
  24.1 5.1 %collective-permute-start.6 = (f32[192,128]{1,0:T(8,128)S(1)}, f32[192,128]{1,0:T(8,128)S(1)}, u32[]{:S(2)}, u32[]{:S(2)}) collective-permute-start(f32[192,128]{1,0:T(8,128)S(1)} %row.1.after_ref.s0.refs_4_), channel_id=1, source_target_pairs={{0,192},{8,200},{16,208},{24,216},{32,224},{40,232},{48,240},{56,2... | collective-permute-start | bytes 294920 | tf_op jit(solution)/shard_map/ppermute | solution.py:429
  25.9 5.1 %collective-permute-start.5 = (f32[192,128]{1,0:T(8,128)S(1)}, f32[192,128]{1,0:T(8,128)S(1)}, u32[]{:S(2)}, u32[]{:S(2)}) collective-permute-start(f32[192,128]{1,0:T(8,128)S(1)} %row.1.after_ref.s0.refs_4_), channel_id=1, source_target_pairs={{0,128},{8,136},{16,144},{24,152},{32,160},{40,168},{48,176},{56,1... | collective-permute-start | bytes 294920 | tf_op jit(solution)/shard_map/ppermute | solution.py:429
  26.3 4.6 %collective-permute-start.4 = (f32[192,128]{1,0:T(8,128)S(1)}, f32[192,128]{1,0:T(8,128)S(1)}, u32[]{:S(2)}, u32[]{:S(2)}) collective-permute-start(f32[192,128]{1,0:T(8,128)S(1)} %row.1.after_ref.s0.refs_4_), channel_id=1, source_target_pairs={{0,64},{8,72},{16,80},{24,88},{32,96},{40,104},{48,112},{56,120},{... | collective-permute-start | bytes 294920 | tf_op jit(solution)/shard_map/ppermute | solution.py:429
  31.9 7.6 %collective-permute-start.9 = (f32[192,128]{1,0:T(8,128)S(1)}, f32[192,128]{1,0:T(8,128)S(1)}, u32[]{:S(2)}, u32[]{:S(2)}) collective-permute-start(f32[192,128]{1,0:T(8,128)S(1)} %column.1.refs_9_.s0), channel_id=1, source_target_pairs={{0,3},{1,2},{2,1},{3,0},{4,7},{5,6},{6,5},{7,4},{8,11},{9,10},{10,... | collective-permute-start | bytes 294920 | tf_op jit(solution)/shard_map/ppermute | solution.py:435
  36.2 7.7 %collective-permute-start.8 = (f32[192,128]{1,0:T(8,128)S(1)}, f32[192,128]{1,0:T(8,128)S(1)}, u32[]{:S(2)}, u32[]{:S(2)}) collective-permute-start(f32[192,128]{1,0:T(8,128)S(1)} %column.1.refs_9_.s0), channel_id=1, source_target_pairs={{0,2},{1,3},{2,0},{3,1},{4,6},{5,7},{6,4},{7,5},{8,10},{9,11},{10,... | collective-permute-start | bytes 294920 | tf_op jit(solution)/shard_map/ppermute | solution.py:435
  36.2 7.7 %collective-permute-start.7 = (f32[192,128]{1,0:T(8,128)S(1)}, f32[192,128]{1,0:T(8,128)S(1)}, u32[]{:S(2)}, u32[]{:S(2)}) collective-permute-start(f32[192,128]{1,0:T(8,128)S(1)} %column.1.refs_9_.s0), channel_id=1, source_target_pairs={{0,1},{1,0},{2,3},{3,2},{4,5},{5,4},{6,7},{7,6},{8,9},{9,8},{10,11... | collective-permute-start | bytes 294920 | tf_op jit(solution)/shard_map/ppermute | solution.py:435
  44.9 6.9 %collective-permute-start.10 = (f32[64,128]{1,0:T(8,128)S(1)}, f32[64,128]{1,0:T(8,128)S(1)}, u32[]{:S(2)}, u32[]{:S(2)}) collective-permute-start(f32[64,128]{1,0:T(8,128)S(1)} %lead.1.after_ref), channel_id=1, source_target_pairs={{0,7},{1,6},{2,5},{3,4},{4,3},{5,2},{6,1},{7,0},{8,15},{9,14},{10,... | collective-permute-start | bytes 98312 | tf_op jit(solution)/shard_map/ppermute | solution.py:455
  50.1 13.1 %copy-start.2 = (f32[4,128]{1,0:T(4,128)S(1)}, f32[4,128]{1,0:T(4,128)}, u32[]{:S(2)}) copy-start(f32[4,128]{1,0:T(4,128)} %refs_10_.1) | copy-start | bytes 6148
  52.6 4.1 %collective-permute-start.11 = (f32[64,128]{1,0:T(8,128)S(1)}, f32[64,128]{1,0:T(8,128)S(1)}, u32[]{:S(2)}, u32[]{:S(2)}) collective-permute-start(f32[64,128]{1,0:T(8,128)S(1)} %get-tuple-element.44), channel_id=1, source_target_pairs={{0,16},{8,24},{16,32},{24,40},{32,48},{40,56},{48,0},{56,8},{64,80... | collective-permute-start | bytes 98312 | tf_op jit(solution)/shard_map/ppermute | solution.py:475
  53.2 4.3 %collective-permute-start.12 = (f32[64,128]{1,0:T(8,128)S(1)}, f32[64,128]{1,0:T(8,128)S(1)}, u32[]{:S(2)}, u32[]{:S(2)}) collective-permute-start(f32[64,128]{1,0:T(8,128)S(1)} %get-tuple-element.45), channel_id=1, source_target_pairs={{0,32},{8,40},{16,48},{24,56},{32,0},{40,8},{48,16},{56,24},{64,96... | collective-permute-start | bytes 98312 | tf_op jit(solution)/shard_map/ppermute | solution.py:475
  55.5 2.8 %collective-permute-start.13 = (f32[64,128]{1,0:T(8,128)S(1)}, f32[64,128]{1,0:T(8,128)S(1)}, u32[]{:S(2)}, u32[]{:S(2)}) collective-permute-start(f32[64,128]{1,0:T(8,128)S(1)} %get-tuple-element.46), channel_id=1, source_target_pairs={{0,48},{8,56},{16,0},{24,8},{32,16},{40,24},{48,32},{56,40},{64,11... | collective-permute-start | bytes 98312 | tf_op jit(solution)/shard_map/ppermute | solution.py:475
  58.3 4.9 %collective-permute-start.14 = (f32[4,64,128]{2,1,0:T(8,128)S(1)}, f32[4,64,128]{2,1,0:T(8,128)S(1)}, u32[]{:S(2)}, u32[]{:S(2)}) collective-permute-start(f32[4,64,128]{2,1,0:T(8,128)S(1)} %pad_maximum_fusion.refs_8_), channel_id=1, source_target_pairs={{0,8},{8,0},{16,24},{24,16},{32,40},{40,32},{48,56},{56,48},{64,72... | collective-permute-start | bytes 393224 | tf_op jit(solution)/shard_map/ppermute | solution.py:477

commit v5 on v4

--- a/solution.py
+++ b/solution.py
@@ -60,6 +60,22 @@
     ah, al = split(a)
     bh, bl = split(b)
     return dot_nt(ah, bh) + dot_nt(ah, bl) + dot_nt(al, bh)
+
+
+def place_x():
+    return lax.rem(lax.axis_index("seq") // CS, XS)
+
+
+def place_y():
+    return lax.axis_index("seq") // (CS * XS)
+
+
+def place_core():
+    return lax.rem(lax.axis_index("seq"), CS)
+
+
+def place_seg():
+    return lax.axis_index("seg")
 
 
 def iota2(shape, dim):
@@ -78,16 +94,19 @@
         ]
         for j, (src, dst) in enumerate(((k_hbm, k_ref), (v_hbm, v_ref)))
     ]
-    for group in copies:
-        for copy in group:
-            copy.start()
+    for copy in copies[0]:
+        copy.start()
     for i, copy in enumerate(copies[0]):
         copy.wait()
         keys[i * size : (i + 1) * size] = k_ref[i * size : (i + 1) * size].astype(f32)
+    for copy in copies[1]:
+        copy.start()
     nblk = r_ref.shape[1] // BLK
     row = iota2((BLK, BLK), 0)
     col = iota2((BLK, BLK), 1)
     eye = row == col
+    pair = ((row >> 1) == (col >> 1)) & (row < col)
+    quad = ((row >> 2) == (col >> 2)) & ((row >> 1) < (col >> 1))
     chains = [(h, b) for h in range(HEADS) for b in range(nblk)]
     rs, rts, vts, uppers, invs, ccols, crows = [], [], [], [], [], [], []
     for h, b in chains:
@@ -100,15 +119,20 @@
         ccol = lax.rsqrt(jnp.sum(diag, axis=1, keepdims=True) + 1e-06)
         crow = lax.rsqrt(jnp.sum(diag, axis=0, keepdims=True) + 1e-06)
         upper = jnp.where(row < col, 2.0 * ccol * crow * gram, 0.0)
-        pair = ((row >> 1) == (col >> 1)) & (row < col)
-        inv = jnp.where(eye, 1.0, 0.0) - jnp.where(pair, upper, 0.0)
+        near = jnp.where(pair, upper, 0.0)
+        across = jnp.where(quad, upper, 0.0)
+        erow = jnp.sum(near, axis=0, keepdims=True)
+        fcol = jnp.sum(near, axis=1, keepdims=True)
+        mid = across - pltpu.roll(across, 1, 1) * erow
+        down = pltpu.roll(mid.reshape(BLK // 8, 8, BLK), 7, 1).reshape(BLK, BLK)
+        inv = jnp.where(eye, 1.0, 0.0) - near - (mid - fcol * down)
         rs.append(r)
         rts.append(rt)
         uppers.append(upper)
         invs.append(inv)
         ccols.append(ccol)
         crows.append(crow)
-    for level in range(1, 7):
+    for level in range(2, 7):
         off = ((row >> (level + 1)) == (col >> (level + 1))) & (
             (row >> level) < (col >> level)
         )
@@ -172,9 +196,9 @@
     )(k, v)
 
 
-def chip_kernel(pos_ref, own_ref, sib_ref, *out_refs):
-    x = pos_ref[0]
-    core = pos_ref[2]
+def chip_kernel(own_ref, sib_ref, *out_refs):
+    x = place_x()
+    core = place_core()
     half = pl.ds(pl.multiple_of(D + core * HALF, HALF), HALF)
     lower = core == 0
     for k in range(XS):
@@ -214,13 +238,13 @@
     total_ref[...] = msg_compose(msg_compose(hold[0], hold[1]), tail)
 
 
-def row_kernel(pos_ref, s0, s1, s2, s3, after_ref, total_ref, hold):
-    ordered_cyclic([s0, s1, s2, s3], pos_ref[0], hold)
+def row_kernel(s0, s1, s2, s3, after_ref, total_ref, hold):
+    ordered_cyclic([s0, s1, s2, s3], place_x(), hold)
     write_total(total_ref, hold)
 
 
-def column_kernel(pos_ref, s0, s1, s2, s3, after_ref, total_ref, hold):
-    ordered_xor([s0, s1, s2, s3], pos_ref[1], hold)
+def column_kernel(s0, s1, s2, s3, after_ref, total_ref, hold):
+    ordered_xor([s0, s1, s2, s3], place_y(), hold)
     write_total(total_ref, hold)
 
 
@@ -234,12 +258,12 @@
     return out
 
 
-def path_kernel(pos_ref, *refs):
+def path_kernel(*refs):
     xslots, yslots = refs[:4], refs[4:8]
     init_ref, after_ref, path_ref, start_ref, xhold, yhold, turn = refs[8:]
-    x = pos_ref[0]
-    y = pos_ref[1]
-    core = pos_ref[2]
+    x = place_x()
+    y = place_y()
+    core = place_core()
     ordered_cyclic(xslots, x, xhold)
     ordered_xor(yslots, y, yhold)
     here = place_prefix(y, yhold)
@@ -256,15 +280,15 @@
     start_ref[...] = turn[pl.ds(pl.multiple_of(core * HALF, HALF), HALF), :]
 
 
-def lead_kernel(pos_ref, s0, s1, s2, s3, start_ref, after_ref, lead_ref, hold):
-    ordered_xor([s0, s1, s2, s3], lax.rem(pos_ref[3], ZG), hold)
+def lead_kernel(s0, s1, s2, s3, start_ref, after_ref, lead_ref, hold):
+    ordered_xor([s0, s1, s2, s3], lax.rem(place_seg(), ZG), hold)
     tail = msg_compose(hold[2], hold[3])
     state = advance(advance(start_ref[...], hold[0]), hold[1])
     lead_ref[...] = advance(state, tail)
 
 
-def fuse_kernel(pos_ref, s0, s1, s2, s3, path_ref, after_ref, fuse_ref, hold):
-    g = lax.rem(pos_ref[3], ZG)
+def fuse_kernel(s0, s1, s2, s3, path_ref, after_ref, fuse_ref, hold):
+    g = lax.rem(place_seg(), ZG)
     ordered_xor([s0, s1, s2, s3], g, hold)
     window = place_prefix(g, hold)
     left = wide(window)
@@ -275,9 +299,9 @@
         fuse_ref[i, D:, :] = moved[D:] + path[D:]
 
 
-def entry_kernel(pos_ref, start_ref, early_ref, fuse_ref, after_ref, o0, o1, o2, o3, scratch):
-    x = pos_ref[0]
-    state = jnp.where(pos_ref[3] >= ZG, early_ref[...], start_ref[...])
+def entry_kernel(start_ref, early_ref, fuse_ref, o0, o1, o2, o3, scratch):
+    x = place_x()
+    state = jnp.where(place_seg() >= ZG, early_ref[...], start_ref[...])
     left = wide(state)
     for i in range(XS):
         scratch[i] = mm_pre(left, tall_wide(fuse_ref[i, :D, :])) + fuse_ref[i, D:, :]
@@ -286,7 +310,7 @@
 
 
 def reach_kernel(
-    pos_ref, q_ref, r_ref, z_ref, sib_ref, after_ref, reach_ref, base_ref, rows, *, head
+    q_ref, r_ref, z_ref, sib_ref, after_ref, reach_ref, base_ref, rows, *, head
 ):
     tokens = reach_ref.shape[0]
     nblk = z_ref.shape[0]
@@ -295,7 +319,7 @@
     visible = iota2((span, BLK), 1) <= REFL * iota2((span, BLK), 0) + (REFL - 1)
     base = jnp.where(iota2((2 * D, D), 0) == iota2((2 * D, D), 1), 1.0, 0.0)
     sign = jnp.where(iota2((2 * D, D), 0) < D, -1.0, 1.0)
-    prefixes = [jnp.where(pos_ref[2] == 1, sib_ref[...], base)]
+    prefixes = [jnp.where(place_core() == 1, sib_ref[...], base)]
     for b in range(nblk - 1):
         rr = jnp.concatenate([r_ref[b * BLK : (b + 1) * BLK, :]] * 2, axis=0)
         piece = base + sign * dot_nn(wide(z_ref[b]), rr)
@@ -314,7 +338,7 @@
         base_ref[part, :] = moves[b][:, D:] + locals_[b]
 
 
-def reach_call(pos, q, r, z, sib, after, head):
+def reach_call(q, r, z, sib, after, head):
     tokens = q.shape[0] // HEADS
 
     def spec(array):
@@ -325,7 +349,6 @@
         functools.partial(reach_kernel, head=head),
         grid=(1,),
         in_specs=[
-            pl.BlockSpec(memory_space=pltpu.SMEM),
             pl.BlockSpec(q.shape, lambda i: (0, 0)),
             spec(r),
             spec(z),
@@ -346,43 +369,72 @@
             flops=400_000_000, bytes_accessed=3_000_000, transcendentals=0
         ),
         name="reach",
-    )(pos, q, r, z, sib, after)
-
-
-def read_kernel(pos_ref, *refs):
+    )(q, r, z, sib, after)
+
+
+def read_kernel(*refs):
     reaches, bases = refs[: 2 * HEADS : 2], refs[1 : 2 * HEADS : 2]
-    mine_ref, other_ref, gain_ref, out_ref, rows = refs[2 * HEADS :]
-    x = pos_ref[0]
-    lower = pos_ref[2] == 0
-    tokens = reaches[0].shape[0]
+    mine_ref, other_ref, gain_ref, out_hbm, rows, out, sems = refs[2 * HEADS :]
+    x = place_x()
+    lower = place_core() == 0
+    rights = []
     for h in range(HEADS):
         slot = lax.rem(x + HEADS - h, HEADS)
         mine, other = mine_ref[slot], other_ref[slot]
         state = jnp.concatenate(
             [jnp.where(lower, mine, other), jnp.where(lower, other, mine)], axis=0
         )
-        high, low = split(state)
-        both = jnp.concatenate([high, low], axis=0)
-        moved = dot_nt(reaches[h][...], jnp.concatenate([both, both], axis=1))
-        read = moved[:, :D] + moved[:, D:] + bases[h][...]
-        scale = lax.rsqrt(jnp.mean(read * read, axis=-1, keepdims=True) + 1e-06)
-        rows[pl.ds(h, tokens, stride=HEADS), :] = read * scale * gain_ref[h : h + 1, :]
-    out_ref[...] = rows[...].astype(bf16)
-
-
-def small_call(kernel, name, pos, arrays, outs, scratch=(), after=None, limit=4, out_dtype=f32):
+        both = jnp.concatenate(split(state), axis=0)
+        rights.append(jnp.concatenate([both, both], axis=1))
+    pieces = sems.shape[0]
+    span = reaches[0].shape[0] // pieces
+    copies = []
+    for i in range(pieces):
+        part = slice(i * span, (i + 1) * span)
+        for h in range(HEADS):
+            moved = dot_nt(reaches[h][part, :], rights[h])
+            read = moved[:, :D] + moved[:, D:] + bases[h][part, :]
+            scale = lax.rsqrt(jnp.mean(read * read, axis=-1, keepdims=True) + 1e-06)
+            rows[pl.ds(i * span * HEADS + h, span, stride=HEADS), :] = (
+                read * scale * gain_ref[h : h + 1, :]
+            )
+        block = pl.ds(i * span * HEADS, span * HEADS)
+        out[block, :] = rows[block, :].astype(bf16)
+        copies.append(pltpu.make_async_copy(out.at[block], out_hbm.at[block], sems.at[i]))
+        copies[-1].start()
+    for copy in copies:
+        copy.wait()
+
+
+def read_call(arrays, tokens):
+    shape = (tokens * HEADS, D)
+    return pl.pallas_call(
+        read_kernel,
+        in_specs=whole(*arrays),
+        out_specs=pl.BlockSpec(memory_space=pl.ANY),
+        out_shape=jax.ShapeDtypeStruct(shape, bf16),
+        scratch_shapes=[
+            pltpu.VMEM(shape, f32),
+            pltpu.VMEM(shape, bf16),
+            pltpu.SemaphoreType.DMA((2,)),
+        ],
+        compiler_params=pltpu.CompilerParams(vmem_limit_bytes=8 << 20),
+        name="read",
+    )(*arrays)
+
+
+def small_call(kernel, name, arrays, outs, scratch=(), after=None, limit=4, out_dtype=f32):
     extra = [] if after is None else [after]
     return pl.pallas_call(
         kernel,
-        in_specs=[pl.BlockSpec(memory_space=pltpu.SMEM)]
-        + whole(*arrays)
+        in_specs=whole(*arrays)
         + [pl.BlockSpec(memory_space=pl.ANY)] * len(extra),
         out_specs=whole(*outs),
         out_shape=[jax.ShapeDtypeStruct(s, out_dtype) for s in outs],
         scratch_shapes=[pltpu.VMEM(s, f32) for s in scratch],
         compiler_params=pltpu.CompilerParams(vmem_limit_bytes=limit << 20),
         name=name,
-    )(pos, *arrays, *extra)
+    )(*arrays, *extra)
 
 
 def seq_perm(move):
@@ -398,13 +450,6 @@
 def per_device(query_rows, key_rows, value_rows, out_gain, initial_state):
     tokens = query_rows.shape[1]
     steps = tokens * REFL
-    place = lax.axis_index("seq")
-    seg = lax.axis_index("seg")
-    core = place % CS
-    x = (place // CS) % XS
-    y = place // (CS * XS)
-    pos = jnp.stack([x, y, core, seg]).astype(jnp.int32)
-
     swap = seq_perm(lambda y, x, c: (y, x, 1 - c))
     along_x = [seq_perm(lambda y, x, c, k=k: (y, (x + k) % XS, c)) for k in range(1, XS)]
     along_y = [seq_perm(lambda y, x, c, k=k: (y ^ k, x, c)) for k in range(1, YS)]
@@ -419,34 +464,32 @@
     values = pltpu.with_memory_space_constraint(values, pltpu.HBM)
     pair, z, r = factor_call(keys, values)
     sib = lax.ppermute(pair, "seq", swap)
-    slots = small_call(chip_kernel, "chip", pos, [pair, sib], [(MSG, D)] * XS)
+    slots = small_call(chip_kernel, "chip", [pair, sib], [(MSG, D)] * XS)
     slots = [slots[0]] + [lax.ppermute(s, "seq", p) for s, p in zip(slots[1:], along_x)]
-    reaches = [reach_call(pos, query, r, z, sib, slots[0], 0)]
+    reaches = [reach_call(query, r, z, sib, slots[0], 0)]
     xslots = slots
     (total,) = small_call(
-        row_kernel, "row", pos, slots, [(MSG, D)], [(XS, MSG, D)], after=reaches[-1][0]
+        row_kernel, "row", slots, [(MSG, D)], [(XS, MSG, D)], after=reaches[-1][0]
     )
     slots = [total] + [lax.ppermute(total, "seq", p) for p in along_y]
     yslots = slots
-    reaches.append(reach_call(pos, query, r, z, sib, total, 1))
+    reaches.append(reach_call(query, r, z, sib, total, 1))
     (total,) = small_call(
-        column_kernel, "column", pos, slots, [(MSG, D)], [(YS, MSG, D)], after=reaches[-1][0]
+        column_kernel, "column", slots, [(MSG, D)], [(YS, MSG, D)], after=reaches[-1][0]
     )
     slots = [total] + [lax.ppermute(total, "seg", p) for p in along_z]
     path, start = small_call(
         path_kernel,
         "path",
-        pos,
         [*xslots, *yslots, initial_state],
         [(XS, MSG, D), (HALF, D)],
         [(XS, MSG, D), (YS, MSG, D), (D, D)],
         after=total,
     )
-    reaches.append(reach_call(pos, query, r, z, sib, path, 2))
+    reaches.append(reach_call(query, r, z, sib, path, 2))
     (lead,) = small_call(
         lead_kernel,
         "lead",
-        pos,
         [*slots, start],
         [(HALF, D)],
         [(ZG, MSG, D)],
@@ -456,35 +499,26 @@
     (fused,) = small_call(
         fuse_kernel,
         "fuse",
-        pos,
         [*slots, path],
         [(XS, MSG, D)],
         [(ZG, MSG, D)],
         after=lead,
     )
-    reaches.append(reach_call(pos, query, r, z, sib, fused, 3))
     slots = small_call(
         entry_kernel,
         "entry",
-        pos,
         [start, early, fused],
         [(HALF, D)] * XS,
         [(XS, HALF, D)],
-        after=reaches[-1][0],
     )
     slots = [slots[0]] + [lax.ppermute(s, "seq", p) for s, p in zip(slots[1:], along_x)]
+    reaches.append(reach_call(query, r, z, sib, slots[0], 3))
+    *slots, last = lax.optimization_barrier((*slots, reaches[-1][0]))
+    reaches[-1] = (last, reaches[-1][1])
     mine = jnp.stack(slots)
     other = lax.ppermute(mine, "seq", swap)
-    (out,) = small_call(
-        read_kernel,
-        "read",
-        pos,
-        [a for pair in reaches for a in pair] + [mine, other, out_gain],
-        [(tokens * HEADS, D)],
-        [(tokens * HEADS, D)],
-        limit=8,
-        out_dtype=bf16,
-    )
+    arrays = [a for pair in reaches for a in pair] + [mine, other, out_gain]
+    out = read_call(arrays, tokens)
     return out.reshape(1, tokens, HEADS, D)
 
 

time: 65 us -> 61.3 us (0.943)
  Pallas kernels: 24.8 us -> 18.4 us
  waiting for transfers between devices: 13.3 us -> 14.8 us
  starting transfers between devices: 26.6 us -> 27.6 us
    pallas_call x8, Pallas kernels: 8.89 us -> 4.19 us  [the longest x7 2.91 us: small_call(): pl.pallas_call(kernel, in_specs=whole(*arrays) + [pl.BlockSpec(memory_spa...]
    pallas_call x4, Pallas kernels: 6.87 us -> 4.71 us  [reach_call(): pl.pallas_call(functools.partial(reach_kernel, head=head), grid=(1,), in_...]
    ppermute x3, waiting for transfers between devices: 4.44 us -> 5.51 us  [per_device(): slots = [total] + [lax.ppermute(total, 'seg', p) for p in along_z]]
    ppermute x1, starting transfers between devices: 3.92 us -> 4.78 us  [per_device(): other = lax.ppermute(mine, 'seq', swap)]
    ppermute x1, waiting for transfers between devices: 0.01 us -> 0.73 us  [per_device(): early = lax.ppermute(lead, 'seg', jump)]
    ppermute x6, waiting for transfers between devices: 4.35 us -> 3.65 us  [per_device(): lax.ppermute(s, 'seq', p)]
  transfers between devices with their start and end apart: 15 -> 15, of which waited for: 9 -> 10; matrix products, arithmetic and copies ran while one was open for 0% -> 0% of each run, Pallas kernels for 14% -> 10%
where the time goes in v5:
time: 61.3 us; the launch traced here: 61.2 us
  starting transfers between devices  27.6 us (45%)
  Pallas kernels  18.4 us (30%)
  waiting for transfers between devices  14.8 us (24%)
    pallas_call x1, Pallas kernels, factor_call(): pl.pallas_call(factor_kernel, in_specs=[pl.BlockSpec(memory_space=pl.ANY)...  9.53 us
    ppermute x6, starting transfers between devices, per_device(): lax.ppermute(s, 'seq', p)  7.23 us
    ppermute x3, waiting for transfers between devices, per_device(): slots = [total] + [lax.ppermute(total, 'seg', p) for p in along_z]  5.51 us
    ppermute x1, starting transfers between devices, per_device(): other = lax.ppermute(mine, 'seq', swap)  4.78 us
    pallas_call x4, Pallas kernels, reach_call(): pl.pallas_call(functools.partial(reach_kernel, head=head), grid=(1,), in_...  4.71 us
    ppermute x3, starting transfers between devices, per_device(): slots = [total] + [lax.ppermute(total, 'seg', p) for p in along_z]  4.69 us
    ppermute x1, starting transfers between devices, per_device(): early = lax.ppermute(lead, 'seg', jump)  4.08 us
    ppermute x6, waiting for transfers between devices, per_device(): lax.ppermute(s, 'seq', p)  3.65 us
  transfers between devices with their start and end apart: 15, of which 10 were waited for; matrix products, arithmetic and copies ran while one was open for 0% of the time, Pallas kernels for 10%

profile of v5, /device:TPU:1, one launch (start us, length us, event | category | flops | bytes accessed | tf_op | source)
XLA Modules:
  0.0 61.2 jit_solution(7694319581256336644)
XLA Ops:
  0.0 9.5 %factor.1 = (f32[4,256,128]{2,1,0:T(8,128)S(1)}, f32[4,4,256,128]{3,2,1,0:T(8,128)S(1)}, bf16[4,512,128]{2,1,0:T(8,128)(2,1)S(1)}) custom-call(bf16[2048,128]{1,0:T(8,128)(2,1)} %bitcast.13, bf16[2048,128]{1,0:T(8,128)(2,1)} %bitcast.14), custom_call_target="tpu_custom_call" | custom-call | tf_op jit(solution)/shard_map/factor/pallas_call | solution.py:182
  9.5 3.3 %collective-permute-start = (f32[4,256,128]{2,1,0:T(8,128)S(1)}, f32[4,256,128]{2,1,0:T(8,128)S(1)}, u32[]{:S(2)}, u32[]{:S(2)}) collective-permute-start(f32[4,256,128]{2,1,0:T(8,128)S(1)} %get-tuple-element.33.own_ref), channel_id=1, source_target_pairs={{0,8},{8,0},{16,24},{24,16},{32,40},{40,32},{48,56},{56,48},{64,72... | collective-permute-start | bytes 1572872 | tf_op jit(solution)/shard_map/ppermute | solution.py:466
  12.9 1.5 %collective-permute-done.sib_ref = f32[4,256,128]{2,1,0:T(8,128)S(1)} collective-permute-done((f32[4,256,128]{2,1,0:T(8,128)S(1)}, f32[4,256,128]{2,1,0:T(8,128)S(1)}, u32[]{:S(2)}, u32[]{:S(2)}) %collective-permute-start) | collective-permute-done | bytes 524320 | tf_op jit(solution)/shard_map/ppermute | solution.py:466
  14.4 0.3 chip.1
  14.7 0.1 collective-permute-start.1
  14.8 1.9 %collective-permute-start.2 = (f32[192,128]{1,0:T(8,128)S(1)}, f32[192,128]{1,0:T(8,128)S(1)}, u32[]{:S(2)}, u32[]{:S(2)}) collective-permute-start(f32[192,128]{1,0:T(8,128)S(1)} %get-tuple-element.38), channel_id=1, source_target_pairs={{0,32},{8,40},{16,48},{24,56},{32,0},{40,8},{48,16},{56,24},{64,96... | collective-permute-start | bytes 294920 | tf_op jit(solution)/shard_map/ppermute | solution.py:468
  16.7 1.2 %collective-permute-start.3 = (f32[192,128]{1,0:T(8,128)S(1)}, f32[192,128]{1,0:T(8,128)S(1)}, u32[]{:S(2)}, u32[]{:S(2)}) collective-permute-start(f32[192,128]{1,0:T(8,128)S(1)} %get-tuple-element.39), channel_id=1, source_target_pairs={{0,48},{8,56},{16,0},{24,8},{32,16},{40,24},{48,32},{56,40},{64,11... | collective-permute-start | bytes 294920 | tf_op jit(solution)/shard_map/ppermute | solution.py:468
  17.8 0.0 copy-done
  17.8 1.2 %reach.4 = (bf16[256,256]{1,0:T(8,128)(2,1)S(1)}, f32[256,128]{1,0:T(8,128)S(1)}) custom-call(bf16[1024,128]{1,0:T(8,128)(2,1)S(1)} %bitcast.8, bf16[4,512,128]{2,1,0:T(8,128)(2,1)S(1)} %get-tuple-element.31.r_ref, f32[4,4,256,128]{3,2,1,0:T(8,128)S(1)} %get-tuple-element.32.z_ref, f32[4,256,128]{2,1,0:T(8,128)S(1)} %collective-permute-done.sib_ref, ...), custom_call_target="tpu_custom_call" | custom-call | flops 400000000 | bytes 3000000 | tf_op jit(solution)/shard_map/reach/pallas_call | solution.py:348
  19.0 1.9 %collective-permute-done.1.s1.refs_1_ = f32[192,128]{1,0:T(8,128)S(1)} collective-permute-done((f32[192,128]{1,0:T(8,128)S(1)}, f32[192,128]{1,0:T(8,128)S(1)}, u32[]{:S(2)}, u32[]{:S(2)}) %collective-permute-start.1) | collective-permute-done | bytes 98336 | tf_op jit(solution)/shard_map/ppermute | solution.py:468
  20.9 0.4 collective-permute-done.2.s2.refs_2_
  21.3 1.0 %collective-permute-done.3.s3.refs_3_ = f32[192,128]{1,0:T(8,128)S(1)} collective-permute-done((f32[192,128]{1,0:T(8,128)S(1)}, f32[192,128]{1,0:T(8,128)S(1)}, u32[]{:S(2)}, u32[]{:S(2)}) %collective-permute-start.3) | collective-permute-done | bytes 98336 | tf_op jit(solution)/shard_map/ppermute | solution.py:468
  22.3 0.4 row.1.after_ref.s0.refs_4_
  22.7 0.0 copy-start.1
  22.8 2.0 %collective-permute-start.6 = (f32[192,128]{1,0:T(8,128)S(1)}, f32[192,128]{1,0:T(8,128)S(1)}, u32[]{:S(2)}, u32[]{:S(2)}) collective-permute-start(f32[192,128]{1,0:T(8,128)S(1)} %row.1.after_ref.s0.refs_4_), channel_id=1, source_target_pairs={{0,192},{8,200},{16,208},{24,216},{32,224},{40,232},{48,240},{56,2... | collective-permute-start | bytes 294920 | tf_op jit(solution)/shard_map/ppermute | solution.py:474
  24.8 0.3 collective-permute-start.5
  25.1 1.2 %collective-permute-start.4 = (f32[192,128]{1,0:T(8,128)S(1)}, f32[192,128]{1,0:T(8,128)S(1)}, u32[]{:S(2)}, u32[]{:S(2)}) collective-permute-start(f32[192,128]{1,0:T(8,128)S(1)} %row.1.after_ref.s0.refs_4_), channel_id=1, source_target_pairs={{0,64},{8,72},{16,80},{24,88},{32,96},{40,104},{48,112},{56,120},{... | collective-permute-start | bytes 294920 | tf_op jit(solution)/shard_map/ppermute | solution.py:474
  26.3 1.2 %reach.5 = (bf16[256,256]{1,0:T(8,128)(2,1)S(1)}, f32[256,128]{1,0:T(8,128)S(1)}) custom-call(bf16[1024,128]{1,0:T(8,128)(2,1)S(1)} %bitcast.9, bf16[4,512,128]{2,1,0:T(8,128)(2,1)S(1)} %get-tuple-element.31.r_ref, f32[4,4,256,128]{3,2,1,0:T(8,128)S(1)} %get-tuple-element.32.z_ref, f32[4,256,128]{2,1,0:T(8,128)S(1)} %collective-permute-done.sib_ref, ...), custom_call_target="tpu_custom_call" | custom-call | flops 400000000 | bytes 3000000 | tf_op jit(solution)/shard_map/reach/pallas_call | solution.py:348
  27.5 0.2 collective-permute-done.6.s3.refs_7_
  27.7 2.1 %collective-permute-done.5.s2.refs_6_ = f32[192,128]{1,0:T(8,128)S(1)} collective-permute-done((f32[192,128]{1,0:T(8,128)S(1)}, f32[192,128]{1,0:T(8,128)S(1)}, u32[]{:S(2)}, u32[]{:S(2)}) %collective-permute-start.5) | collective-permute-done | bytes 98336 | tf_op jit(solution)/shard_map/ppermute | solution.py:474
  29.8 0.0 collective-permute-done.4.s1.refs_5_
  29.8 0.4 column.1.refs_9_.s0
  30.3 4.3 %collective-permute-start.9 = (f32[192,128]{1,0:T(8,128)S(1)}, f32[192,128]{1,0:T(8,128)S(1)}, u32[]{:S(2)}, u32[]{:S(2)}) collective-permute-start(f32[192,128]{1,0:T(8,128)S(1)} %column.1.refs_9_.s0), channel_id=1, source_target_pairs={{0,3},{1,2},{2,1},{3,0},{4,7},{5,6},{6,5},{7,4},{8,11},{9,10},{10,... | collective-permute-start | bytes 294920 | tf_op jit(solution)/shard_map/ppermute | solution.py:480
  34.6 0.0 collective-permute-start.8
  34.6 0.4 collective-permute-start.7
  34.9 0.0 copy-done.1
  35.0 0.6 path.1
  35.5 1.2 %reach.6 = (bf16[256,256]{1,0:T(8,128)(2,1)S(1)}, f32[256,128]{1,0:T(8,128)S(1)}) custom-call(bf16[1024,128]{1,0:T(8,128)(2,1)S(1)} %bitcast.10, bf16[4,512,128]{2,1,0:T(8,128)(2,1)S(1)} %get-tuple-element.31.r_ref, f32[4,4,256,128]{3,2,1,0:T(8,128)S(1)} %get-tuple-element.32.z_ref, f32[4,256,128]{2,1,0:T(8,128)S(1)} %collective-permute-done.sib_ref, ...), custom_call_target="tpu_custom_call" | custom-call | flops 400000000 | bytes 3000000 | tf_op jit(solution)/shard_map/reach/pallas_call | solution.py:348
  36.7 0.0 collective-permute-done.9.s3
  36.7 5.5 %collective-permute-done.8.s2 = f32[192,128]{1,0:T(8,128)S(1)} collective-permute-done((f32[192,128]{1,0:T(8,128)S(1)}, f32[192,128]{1,0:T(8,128)S(1)}, u32[]{:S(2)}, u32[]{:S(2)}) %collective-permute-start.8) | collective-permute-done | bytes 98336 | tf_op jit(solution)/shard_map/ppermute | solution.py:480
  42.2 0.0 collective-permute-done.7.s1
  42.3 0.5 lead.1.after_ref
  42.7 4.1 %collective-permute-start.10 = (f32[64,128]{1,0:T(8,128)S(1)}, f32[64,128]{1,0:T(8,128)S(1)}, u32[]{:S(2)}, u32[]{:S(2)}) collective-permute-start(f32[64,128]{1,0:T(8,128)S(1)} %lead.1.after_ref), channel_id=1, source_target_pairs={{0,7},{1,6},{2,5},{3,4},{4,3},{5,2},{6,1},{7,0},{8,15},{9,14},{10,... | collective-permute-start | bytes 98312 | tf_op jit(solution)/shard_map/ppermute | solution.py:498
  46.8 0.6 fuse.1.fuse_ref
  47.4 0.0 copy-start.2
  47.4 0.7 %collective-permute-done.10.early_ref = f32[64,128]{1,0:T(8,128)S(1)} collective-permute-done((f32[64,128]{1,0:T(8,128)S(1)}, f32[64,128]{1,0:T(8,128)S(1)}, u32[]{:S(2)}, u32[]{:S(2)}) %collective-permute-start.10) | collective-permute-done | bytes 32800 | tf_op jit(solution)/shard_map/ppermute | solution.py:498
  48.1 0.2 entry.1
  48.3 0.7 %collective-permute-start.11 = (f32[64,128]{1,0:T(8,128)S(1)}, f32[64,128]{1,0:T(8,128)S(1)}, u32[]{:S(2)}, u32[]{:S(2)}) collective-permute-start(f32[64,128]{1,0:T(8,128)S(1)} %get-tuple-element.47), channel_id=1, source_target_pairs={{0,16},{8,24},{16,32},{24,40},{32,48},{40,56},{48,0},{56,8},{64,80... | collective-permute-start | bytes 98312 | tf_op jit(solution)/shard_map/ppermute | solution.py:514
  49.0 2.2 %collective-permute-start.12 = (f32[64,128]{1,0:T(8,128)S(1)}, f32[64,128]{1,0:T(8,128)S(1)}, u32[]{:S(2)}, u32[]{:S(2)}) collective-permute-start(f32[64,128]{1,0:T(8,128)S(1)} %get-tuple-element.48), channel_id=1, source_target_pairs={{0,32},{8,40},{16,48},{24,56},{32,0},{40,8},{48,16},{56,24},{64,96... | collective-permute-start | bytes 98312 | tf_op jit(solution)/shard_map/ppermute | solution.py:514
  51.2 1.2 %collective-permute-start.13 = (f32[64,128]{1,0:T(8,128)S(1)}, f32[64,128]{1,0:T(8,128)S(1)}, u32[]{:S(2)}, u32[]{:S(2)}) collective-permute-start(f32[64,128]{1,0:T(8,128)S(1)} %get-tuple-element.49), channel_id=1, source_target_pairs={{0,48},{8,56},{16,0},{24,8},{32,16},{40,24},{48,32},{56,40},{64,11... | collective-permute-start | bytes 98312 | tf_op jit(solution)/shard_map/ppermute | solution.py:514
  52.4 1.2 %reach.7 = (bf16[256,256]{1,0:T(8,128)(2,1)S(1)}, f32[256,128]{1,0:T(8,128)S(1)}) custom-call(bf16[1024,128]{1,0:T(8,128)(2,1)S(1)} %bitcast.11, bf16[4,512,128]{2,1,0:T(8,128)(2,1)S(1)} %get-tuple-element.31.r_ref, f32[4,4,256,128]{3,2,1,0:T(8,128)S(1)} %get-tuple-element.32.z_ref, f32[4,256,128]{2,1,0:T(8,128)S(1)} %collective-permute-done.sib_ref, ...), custom_call_target="tpu_custom_call" | custom-call | flops 400000000 | bytes 3000000 | tf_op jit(solution)/shard_map/reach/pallas_call | solution.py:348
  53.6 0.0 collective-permute-done.11
  53.6 0.0 collective-permute-done.12
  53.6 0.3 collective-permute-done.13
  54.0 4.8 %collective-permute-start.14 = (f32[4,64,128]{2,1,0:T(8,128)S(1)}, f32[4,64,128]{2,1,0:T(8,128)S(1)}, u32[]{:S(2)}, u32[]{:S(2)}) collective-permute-start(f32[4,64,128]{2,1,0:T(8,128)S(1)} %pad_maximum_fusion.refs_8_), channel_id=1, source_target_pairs={{0,8},{8,0},{16,24},{24,16},{32,40},{40,32},{48,56},{56,48},{64,72... | collective-permute-start | bytes 393224 | tf_op jit(solution)/shard_map/ppermute | solution.py:519
  58.8 1.0 %collective-permute-done.14.refs_9_ = f32[4,64,128]{2,1,0:T(8,128)S(1)} collective-permute-done((f32[4,64,128]{2,1,0:T(8,128)S(1)}, f32[4,64,128]{2,1,0:T(8,128)S(1)}, u32[]{:S(2)}, u32[]{:S(2)}) %collective-permute-start.14) | collective-permute-done | bytes 131104 | tf_op jit(solution)/shard_map/ppermute | solution.py:519
  59.7 0.0 copy-done.2
  59.8 1.3 %read.1 = bf16[1024,128]{1,0:T(8,128)(2,1)} custom-call(bf16[256,256]{1,0:T(8,128)(2,1)S(1)} %get-tuple-element.35.after_ref.refs_0_, f32[256,128]{1,0:T(8,128)S(1)} %get-tuple-element.36.refs_1_, bf16[256,256]{1,0:T(8,128)(2,1)S(1)} %get-tuple-element.40.after_ref.refs_2_, f32[256,128]{1,0:T(8,128)S(1)} %get-tuple-element.41.refs_3_, ...), custom_call_target="tpu_custom_call" | custom-call | tf_op jit(solution)/shard_map/read/pallas_call | solution.py:411
  (2 shorter events, 0.0 us)
Async XLA Ops:
  0.0 17.8 %copy-start = (bf16[1,256,4,128]{3,2,1,0:T(4,128)(2,1)S(1)}, bf16[1,256,4,128]{3,2,1,0:T(4,128)(2,1)}, u32[]{:S(2)}) copy-start(bf16[1,256,4,128]{3,2,1,0:T(4,128)(2,1)} %param.5) | copy-start | bytes 786436
  9.5 4.9 %collective-permute-start = (f32[4,256,128]{2,1,0:T(8,128)S(1)}, f32[4,256,128]{2,1,0:T(8,128)S(1)}, u32[]{:S(2)}, u32[]{:S(2)}) collective-permute-start(f32[4,256,128]{2,1,0:T(8,128)S(1)} %get-tuple-element.33.own_ref), channel_id=1, source_target_pairs={{0,8},{8,0},{16,24},{24,16},{32,40},{40,32},{48,56},{56,48},{64,72... | collective-permute-start | bytes 1572872 | tf_op jit(solution)/shard_map/ppermute | solution.py:466
  14.7 6.2 %collective-permute-start.1 = (f32[192,128]{1,0:T(8,128)S(1)}, f32[192,128]{1,0:T(8,128)S(1)}, u32[]{:S(2)}, u32[]{:S(2)}) collective-permute-start(f32[192,128]{1,0:T(8,128)S(1)} %get-tuple-element.37), channel_id=1, source_target_pairs={{0,16},{8,24},{16,32},{24,40},{32,48},{40,56},{48,0},{56,8},{64,80... | collective-permute-start | bytes 294920 | tf_op jit(solution)/shard_map/ppermute | solution.py:468
  14.8 6.6 %collective-permute-start.2 = (f32[192,128]{1,0:T(8,128)S(1)}, f32[192,128]{1,0:T(8,128)S(1)}, u32[]{:S(2)}, u32[]{:S(2)}) collective-permute-start(f32[192,128]{1,0:T(8,128)S(1)} %get-tuple-element.38), channel_id=1, source_target_pairs={{0,32},{8,40},{16,48},{24,56},{32,0},{40,8},{48,16},{56,24},{64,96... | collective-permute-start | bytes 294920 | tf_op jit(solution)/shard_map/ppermute | solution.py:468
  16.7 5.7 %collective-permute-start.3 = (f32[192,128]{1,0:T(8,128)S(1)}, f32[192,128]{1,0:T(8,128)S(1)}, u32[]{:S(2)}, u32[]{:S(2)}) collective-permute-start(f32[192,128]{1,0:T(8,128)S(1)} %get-tuple-element.39), channel_id=1, source_target_pairs={{0,48},{8,56},{16,0},{24,8},{32,16},{40,24},{48,32},{56,40},{64,11... | collective-permute-start | bytes 294920 | tf_op jit(solution)/shard_map/ppermute | solution.py:468
  22.7 12.2 %copy-start.1 = (f32[4,128,128]{2,1,0:T(8,128)S(1)}, f32[4,128,128]{2,1,0:T(8,128)}, u32[]{:S(2)}) copy-start(f32[4,128,128]{2,1,0:T(8,128)} %refs_8_.1) | copy-start | bytes 786436
  22.8 4.9 %collective-permute-start.6 = (f32[192,128]{1,0:T(8,128)S(1)}, f32[192,128]{1,0:T(8,128)S(1)}, u32[]{:S(2)}, u32[]{:S(2)}) collective-permute-start(f32[192,128]{1,0:T(8,128)S(1)} %row.1.after_ref.s0.refs_4_), channel_id=1, source_target_pairs={{0,192},{8,200},{16,208},{24,216},{32,224},{40,232},{48,240},{56,2... | collective-permute-start | bytes 294920 | tf_op jit(solution)/shard_map/ppermute | solution.py:474
  24.8 5.1 %collective-permute-start.5 = (f32[192,128]{1,0:T(8,128)S(1)}, f32[192,128]{1,0:T(8,128)S(1)}, u32[]{:S(2)}, u32[]{:S(2)}) collective-permute-start(f32[192,128]{1,0:T(8,128)S(1)} %row.1.after_ref.s0.refs_4_), channel_id=1, source_target_pairs={{0,128},{8,136},{16,144},{24,152},{32,160},{40,168},{48,176},{56,1... | collective-permute-start | bytes 294920 | tf_op jit(solution)/shard_map/ppermute | solution.py:474
  25.1 4.8 %collective-permute-start.4 = (f32[192,128]{1,0:T(8,128)S(1)}, f32[192,128]{1,0:T(8,128)S(1)}, u32[]{:S(2)}, u32[]{:S(2)}) collective-permute-start(f32[192,128]{1,0:T(8,128)S(1)} %row.1.after_ref.s0.refs_4_), channel_id=1, source_target_pairs={{0,64},{8,72},{16,80},{24,88},{32,96},{40,104},{48,112},{56,120},{... | collective-permute-start | bytes 294920 | tf_op jit(solution)/shard_map/ppermute | solution.py:474
  30.3 6.5 %collective-permute-start.9 = (f32[192,128]{1,0:T(8,128)S(1)}, f32[192,128]{1,0:T(8,128)S(1)}, u32[]{:S(2)}, u32[]{:S(2)}) collective-permute-start(f32[192,128]{1,0:T(8,128)S(1)} %column.1.refs_9_.s0), channel_id=1, source_target_pairs={{0,3},{1,2},{2,1},{3,0},{4,7},{5,6},{6,5},{7,4},{8,11},{9,10},{10,... | collective-permute-start | bytes 294920 | tf_op jit(solution)/shard_map/ppermute | solution.py:480
  34.6 7.7 %collective-permute-start.8 = (f32[192,128]{1,0:T(8,128)S(1)}, f32[192,128]{1,0:T(8,128)S(1)}, u32[]{:S(2)}, u32[]{:S(2)}) collective-permute-start(f32[192,128]{1,0:T(8,128)S(1)} %column.1.refs_9_.s0), channel_id=1, source_target_pairs={{0,2},{1,3},{2,0},{3,1},{4,6},{5,7},{6,4},{7,5},{8,10},{9,11},{10,... | collective-permute-start | bytes 294920 | tf_op jit(solution)/shard_map/ppermute | solution.py:480
  34.6 7.7 %collective-permute-start.7 = (f32[192,128]{1,0:T(8,128)S(1)}, f32[192,128]{1,0:T(8,128)S(1)}, u32[]{:S(2)}, u32[]{:S(2)}) collective-permute-start(f32[192,128]{1,0:T(8,128)S(1)} %column.1.refs_9_.s0), channel_id=1, source_target_pairs={{0,1},{1,0},{2,3},{3,2},{4,5},{5,4},{6,7},{7,6},{8,9},{9,8},{10,11... | collective-permute-start | bytes 294920 | tf_op jit(solution)/shard_map/ppermute | solution.py:480
  42.7 5.4 %collective-permute-start.10 = (f32[64,128]{1,0:T(8,128)S(1)}, f32[64,128]{1,0:T(8,128)S(1)}, u32[]{:S(2)}, u32[]{:S(2)}) collective-permute-start(f32[64,128]{1,0:T(8,128)S(1)} %lead.1.after_ref), channel_id=1, source_target_pairs={{0,7},{1,6},{2,5},{3,4},{4,3},{5,2},{6,1},{7,0},{8,15},{9,14},{10,... | collective-permute-start | bytes 98312 | tf_op jit(solution)/shard_map/ppermute | solution.py:498
  47.4 12.4 %copy-start.2 = (f32[4,128]{1,0:T(4,128)S(1)}, f32[4,128]{1,0:T(4,128)}, u32[]{:S(2)}) copy-start(f32[4,128]{1,0:T(4,128)} %refs_10_.1) | copy-start | bytes 6148
  48.3 5.3 %collective-permute-start.11 = (f32[64,128]{1,0:T(8,128)S(1)}, f32[64,128]{1,0:T(8,128)S(1)}, u32[]{:S(2)}, u32[]{:S(2)}) collective-permute-start(f32[64,128]{1,0:T(8,128)S(1)} %get-tuple-element.47), channel_id=1, source_target_pairs={{0,16},{8,24},{16,32},{24,40},{32,48},{40,56},{48,0},{56,8},{64,80... | collective-permute-start | bytes 98312 | tf_op jit(solution)/shard_map/ppermute | solution.py:514
  49.0 4.6 %collective-permute-start.12 = (f32[64,128]{1,0:T(8,128)S(1)}, f32[64,128]{1,0:T(8,128)S(1)}, u32[]{:S(2)}, u32[]{:S(2)}) collective-permute-start(f32[64,128]{1,0:T(8,128)S(1)} %get-tuple-element.48), channel_id=1, source_target_pairs={{0,32},{8,40},{16,48},{24,56},{32,0},{40,8},{48,16},{56,24},{64,96... | collective-permute-start | bytes 98312 | tf_op jit(solution)/shard_map/ppermute | solution.py:514
  51.2 2.8 %collective-permute-start.13 = (f32[64,128]{1,0:T(8,128)S(1)}, f32[64,128]{1,0:T(8,128)S(1)}, u32[]{:S(2)}, u32[]{:S(2)}) collective-permute-start(f32[64,128]{1,0:T(8,128)S(1)} %get-tuple-element.49), channel_id=1, source_target_pairs={{0,48},{8,56},{16,0},{24,8},{32,16},{40,24},{48,32},{56,40},{64,11... | collective-permute-start | bytes 98312 | tf_op jit(solution)/shard_map/ppermute | solution.py:514
  54.0 5.8 %collective-permute-start.14 = (f32[4,64,128]{2,1,0:T(8,128)S(1)}, f32[4,64,128]{2,1,0:T(8,128)S(1)}, u32[]{:S(2)}, u32[]{:S(2)}) collective-permute-start(f32[4,64,128]{2,1,0:T(8,128)S(1)} %pad_maximum_fusion.refs_8_), channel_id=1, source_target_pairs={{0,8},{8,0},{16,24},{24,16},{32,40},{40,32},{48,56},{56,48},{64,72... | collective-permute-start | bytes 393224 | tf_op jit(solution)/shard_map/ppermute | solution.py:519

commit v6 on v5

--- a/solution.py
+++ b/solution.py
@@ -15,8 +15,7 @@
 YS = 4
 CS = 2
 ZG = 4
-HALF = D // CS
-MSG = D + HALF
+MSG = 2 * D
 
 f32 = jnp.float32
 bf16 = jnp.bfloat16
@@ -198,19 +197,9 @@
 
 def chip_kernel(own_ref, sib_ref, *out_refs):
     x = place_x()
-    core = place_core()
-    half = pl.ds(pl.multiple_of(D + core * HALF, HALF), HALF)
-    lower = core == 0
     for k in range(XS):
         head = lax.rem(x + k, HEADS)
-        own_t, sib_t = own_ref[head, :D, :], sib_ref[head, :D, :]
-        own_s, sib_s = own_ref[head, half, :], sib_ref[head, half, :]
-        rows = jnp.concatenate(
-            [jnp.where(lower, own_t, sib_t), jnp.where(lower, own_s, sib_s)], axis=0
-        )
-        moved = mm(rows, jnp.where(lower, sib_t, own_t))
-        out_refs[k][:D, :] = moved[:D]
-        out_refs[k][D:, :] = moved[D:] + jnp.where(lower, sib_s, own_s)
+        out_refs[k][...] = compose(sib_ref[head], own_ref[head])
 
 
 def ordered_cyclic(slots, place, scratch):
@@ -260,10 +249,9 @@
 
 def path_kernel(*refs):
     xslots, yslots = refs[:4], refs[4:8]
-    init_ref, after_ref, path_ref, start_ref, xhold, yhold, turn = refs[8:]
+    init_ref, after_ref, path_ref, start_ref, xhold, yhold = refs[8:]
     x = place_x()
     y = place_y()
-    core = place_core()
     ordered_cyclic(xslots, x, xhold)
     ordered_xor(yslots, y, yhold)
     here = place_prefix(y, yhold)
@@ -276,8 +264,7 @@
         moved = mm_pre(left, tall_wide(prefix[:D]))
         path_ref[i + 1, :D, :] = moved[:D]
         path_ref[i + 1, D:, :] = moved[D:] + prefix[D:]
-    turn[...] = init_ref[x].T
-    start_ref[...] = turn[pl.ds(pl.multiple_of(core * HALF, HALF), HALF), :]
+    start_ref[...] = init_ref[x].T
 
 
 def lead_kernel(s0, s1, s2, s3, start_ref, after_ref, lead_ref, hold):
@@ -374,17 +361,22 @@
 
 def read_kernel(*refs):
     reaches, bases = refs[: 2 * HEADS : 2], refs[1 : 2 * HEADS : 2]
-    mine_ref, other_ref, gain_ref, out_hbm, rows, out, sems = refs[2 * HEADS :]
+    refs = refs[2 * HEADS :]
+    mine, other = refs[:HEADS], refs[HEADS : 2 * HEADS]
+    gain_ref, out_hbm, states, rows, out, sems = refs[2 * HEADS :]
     x = place_x()
-    lower = place_core() == 0
+
+    @pl.when(place_core() == 0)
+    def _():
+        ordered_cyclic(other, x, states)
+
+    @pl.when(place_core() != 0)
+    def _():
+        ordered_cyclic(mine, x, states)
+
     rights = []
     for h in range(HEADS):
-        slot = lax.rem(x + HEADS - h, HEADS)
-        mine, other = mine_ref[slot], other_ref[slot]
-        state = jnp.concatenate(
-            [jnp.where(lower, mine, other), jnp.where(lower, other, mine)], axis=0
-        )
-        both = jnp.concatenate(split(state), axis=0)
+        both = jnp.concatenate(split(states[h]), axis=0)
         rights.append(jnp.concatenate([both, both], axis=1))
     pieces = sems.shape[0]
     span = reaches[0].shape[0] // pieces
@@ -414,6 +406,7 @@
         out_specs=pl.BlockSpec(memory_space=pl.ANY),
         out_shape=jax.ShapeDtypeStruct(shape, bf16),
         scratch_shapes=[
+            pltpu.VMEM((HEADS, D, D), f32),
             pltpu.VMEM(shape, f32),
             pltpu.VMEM(shape, bf16),
             pltpu.SemaphoreType.DMA((2,)),
@@ -437,25 +430,42 @@
     )(*arrays, *extra)
 
 
-def seq_perm(move):
-    pairs = []
-    for y in range(YS):
-        for x in range(XS):
-            for c in range(CS):
-                ny, nx, nc = move(y, x, c)
-                pairs.append(((y * XS + x) * CS + c, (ny * XS + nx) * CS + nc))
-    return pairs
+def seat(y, x, c):
+    return (y * XS + x) * CS + c
+
+
+def plane_perm(move):
+    last = CS - 1
+    return [
+        (seat(y, x, last), seat(*move(y, x), last)) for y in range(YS) for x in range(XS)
+    ]
+
+
+def depth_perm(segs, move):
+    last = CS - 1
+    return [
+        (seat(y, x, last) * segs + g, seat(y, x, last) * segs + move(g))
+        for y in range(YS)
+        for x in range(XS)
+        for g in range(segs)
+    ]
+
+
+def chip_perm(source):
+    return [
+        (seat(y, x, source), seat(y, x, 1 - source)) for y in range(YS) for x in range(XS)
+    ]
 
 
 def per_device(query_rows, key_rows, value_rows, out_gain, initial_state):
     tokens = query_rows.shape[1]
     steps = tokens * REFL
-    swap = seq_perm(lambda y, x, c: (y, x, 1 - c))
-    along_x = [seq_perm(lambda y, x, c, k=k: (y, (x + k) % XS, c)) for k in range(1, XS)]
-    along_y = [seq_perm(lambda y, x, c, k=k: (y ^ k, x, c)) for k in range(1, YS)]
-    segs = 8
-    along_z = [[(i, i ^ k) for i in range(segs)] for k in range(1, ZG)]
-    jump = [(i, segs - 1 - i) for i in range(segs)]
+    up, down = chip_perm(0), chip_perm(1)
+    along_x = [plane_perm(lambda y, x, k=k: (y, (x + k) % XS)) for k in range(1, XS)]
+    along_y = [plane_perm(lambda y, x, k=k: (y ^ k, x)) for k in range(1, YS)]
+    segs = lax.axis_size("seg")
+    along_z = [depth_perm(segs, lambda g, k=k: g ^ k) for k in range(1, ZG)]
+    jump = depth_perm(segs, lambda g: segs - 1 - g)
 
     keys = key_rows.reshape(steps * HEADS, D)
     values = value_rows.reshape(steps * HEADS, D)
@@ -463,7 +473,7 @@
     keys = pltpu.with_memory_space_constraint(keys, pltpu.HBM)
     values = pltpu.with_memory_space_constraint(values, pltpu.HBM)
     pair, z, r = factor_call(keys, values)
-    sib = lax.ppermute(pair, "seq", swap)
+    sib = lax.ppermute(pair, "seq", up)
     slots = small_call(chip_kernel, "chip", [pair, sib], [(MSG, D)] * XS)
     slots = [slots[0]] + [lax.ppermute(s, "seq", p) for s, p in zip(slots[1:], along_x)]
     reaches = [reach_call(query, r, z, sib, slots[0], 0)]
@@ -477,13 +487,13 @@
     (total,) = small_call(
         column_kernel, "column", slots, [(MSG, D)], [(YS, MSG, D)], after=reaches[-1][0]
     )
-    slots = [total] + [lax.ppermute(total, "seg", p) for p in along_z]
+    slots = [total] + [lax.ppermute(total, ("seq", "seg"), p) for p in along_z]
     path, start = small_call(
         path_kernel,
         "path",
         [*xslots, *yslots, initial_state],
-        [(XS, MSG, D), (HALF, D)],
-        [(XS, MSG, D), (YS, MSG, D), (D, D)],
+        [(XS, MSG, D), (D, D)],
+        [(XS, MSG, D), (YS, MSG, D)],
         after=total,
     )
     reaches.append(reach_call(query, r, z, sib, path, 2))
@@ -491,11 +501,11 @@
         lead_kernel,
         "lead",
         [*slots, start],
-        [(HALF, D)],
+        [(D, D)],
         [(ZG, MSG, D)],
         after=reaches[-1][0],
     )
-    early = lax.ppermute(lead, "seg", jump)
+    early = lax.ppermute(lead, ("seq", "seg"), jump)
     (fused,) = small_call(
         fuse_kernel,
         "fuse",
@@ -508,16 +518,17 @@
         entry_kernel,
         "entry",
         [start, early, fused],
-        [(HALF, D)] * XS,
-        [(XS, HALF, D)],
+        [(D, D)] * XS,
+        [(XS, D, D)],
     )
     slots = [slots[0]] + [lax.ppermute(s, "seq", p) for s, p in zip(slots[1:], along_x)]
     reaches.append(reach_call(query, r, z, sib, slots[0], 3))
-    *slots, last = lax.optimization_barrier((*slots, reaches[-1][0]))
+    last = reaches[-1][0]
+    for k in range(1, XS):
+        slots[k], last = lax.optimization_barrier((slots[k], last))
     reaches[-1] = (last, reaches[-1][1])
-    mine = jnp.stack(slots)
-    other = lax.ppermute(mine, "seq", swap)
-    arrays = [a for pair in reaches for a in pair] + [mine, other, out_gain]
+    others = [lax.ppermute(s, "seq", down) for s in slots]
+    arrays = [a for pair in reaches for a in pair] + [*slots, *others, out_gain]
     out = read_call(arrays, tokens)
     return out.reshape(1, tokens, HEADS, D)
 

time: 61.3 us -> 83.7 us (1.37)
  starting transfers between devices: 27.6 us -> 50.4 us
  waiting for transfers between devices: 14.8 us -> 13.4 us
    ppermute x6, starting transfers between devices: 7.23 us -> 18.5 us  [per_device(): lax.ppermute(s, 'seq', p)]
    ppermute x6 -> x9, starting transfers between devices: 16.9 us -> 22.7 us  [the longest x3 10.5 us: per_device(): slots = [total] + [lax.ppermute(total, ('seq', 'seg'), p) for p in along_z]]
    ppermute x3, starting transfers between devices: 3.52 us -> 9.18 us  [per_device(): slots = [total] + [lax.ppermute(total, 'seq', p) for p in along_y]]
    ppermute x6, waiting for transfers between devices: 3.65 us -> 2 us  [per_device(): lax.ppermute(s, 'seq', p)]
    ppermute x6 -> x9, waiting for transfers between devices: 8.77 us -> 9.08 us  [the longest x1 4.61 us: per_device(): sib = lax.ppermute(pair, 'seq', up)]
  transfers between devices with their start and end apart: 15 -> 18, of which waited for: 10 -> 9; matrix products, arithmetic and copies ran while one was open for 0% -> 0% of each run, Pallas kernels for 10% -> 7%
where the time goes in v6:
time: 83.7 us; the launch traced here: 83.1 us
  starting transfers between devices  50.4 us (60%)
  Pallas kernels  18.8 us (22%)
  waiting for transfers between devices  13.4 us (16%)
    ppermute x6, starting transfers between devices, per_device(): lax.ppermute(s, 'seq', p)  18.5 us
    ppermute x3, starting transfers between devices, per_device(): slots = [total] + [lax.ppermute(total, ('seq', 'seg'), p) for p in along_z]  10.5 us
    pallas_call x1, Pallas kernels, factor_call(): pl.pallas_call(factor_kernel, in_specs=[pl.BlockSpec(memory_space=pl.ANY)...  9.53 us
    ppermute x3, starting transfers between devices, per_device(): slots = [total] + [lax.ppermute(total, 'seq', p) for p in along_y]  9.18 us
    ppermute x1, starting transfers between devices, per_device(): early = lax.ppermute(lead, ('seq', 'seg'), jump)  5.66 us
    ppermute x4, starting transfers between devices, per_device(): others = [lax.ppermute(s, 'seq', down) for s in slots]  5.16 us
    pallas_call x4, Pallas kernels, reach_call(): pl.pallas_call(functools.partial(reach_kernel, head=head), grid=(1,), in_...  4.72 us
    ppermute x1, waiting for transfers between devices, per_device(): sib = lax.ppermute(pair, 'seq', up)  4.61 us
  transfers between devices with their start and end apart: 18, of which 9 were waited for; matrix products, arithmetic and copies ran while one was open for 0% of the time, Pallas kernels for 7%

profile of v6, /device:TPU:1, one launch (start us, length us, event | category | flops | bytes accessed | tf_op | source)
XLA Modules:
  0.0 83.1 jit_solution(4786605123229394811)
XLA Ops:
  0.0 9.5 %factor.1 = (f32[4,256,128]{2,1,0:T(8,128)S(1)}, f32[4,4,256,128]{3,2,1,0:T(8,128)S(1)}, bf16[4,512,128]{2,1,0:T(8,128)(2,1)S(1)}) custom-call(bf16[2048,128]{1,0:T(8,128)(2,1)} %bitcast.8, bf16[2048,128]{1,0:T(8,128)(2,1)} %bitcast.9), custom_call_target="tpu_custom_call" | custom-call | tf_op jit(solution)/shard_map/factor/pallas_call | solution.py:181
  9.5 1.3 %collective-permute-start = (f32[4,256,128]{2,1,0:T(8,128)S(1)}, f32[4,256,128]{2,1,0:T(8,128)S(1)}, u32[]{:S(2)}, u32[]{:S(2)}) collective-permute-start(f32[4,256,128]{2,1,0:T(8,128)S(1)} %get-tuple-element.34.own_ref), channel_id=1, source_target_pairs={{0,8},{16,24},{32,40},{48,56},{64,72},{80,88},{96,104},{112,120},{... | collective-permute-start | bytes 1572872 | tf_op jit(solution)/shard_map/ppermute | solution.py:476
  10.8 4.6 %collective-permute-done.sib_ref = f32[4,256,128]{2,1,0:T(8,128)S(1)} collective-permute-done((f32[4,256,128]{2,1,0:T(8,128)S(1)}, f32[4,256,128]{2,1,0:T(8,128)S(1)}, u32[]{:S(2)}, u32[]{:S(2)}) %collective-permute-start) | collective-permute-done | bytes 524320 | tf_op jit(solution)/shard_map/ppermute | solution.py:476
  15.5 0.3 chip.1
  15.8 1.9 %collective-permute-start.1 = (f32[256,128]{1,0:T(8,128)S(1)}, f32[256,128]{1,0:T(8,128)S(1)}, u32[]{:S(2)}, u32[]{:S(2)}) collective-permute-start(f32[256,128]{1,0:T(8,128)S(1)} %get-tuple-element.38), channel_id=1, source_target_pairs={{8,24},{24,40},{40,56},{56,8},{72,88},{88,104},{104,120},{120,72},... | collective-permute-start | bytes 393224 | tf_op jit(solution)/shard_map/ppermute | solution.py:478
  17.7 4.3 %collective-permute-start.2 = (f32[256,128]{1,0:T(8,128)S(1)}, f32[256,128]{1,0:T(8,128)S(1)}, u32[]{:S(2)}, u32[]{:S(2)}) collective-permute-start(f32[256,128]{1,0:T(8,128)S(1)} %get-tuple-element.39), channel_id=1, source_target_pairs={{8,40},{24,56},{40,8},{56,24},{72,104},{88,120},{104,72},{120,88},... | collective-permute-start | bytes 393224 | tf_op jit(solution)/shard_map/ppermute | solution.py:478
  22.0 3.1 %collective-permute-start.3 = (f32[256,128]{1,0:T(8,128)S(1)}, f32[256,128]{1,0:T(8,128)S(1)}, u32[]{:S(2)}, u32[]{:S(2)}) collective-permute-start(f32[256,128]{1,0:T(8,128)S(1)} %get-tuple-element.40), channel_id=1, source_target_pairs={{8,56},{24,8},{40,24},{56,40},{72,120},{88,72},{104,88},{120,104},... | collective-permute-start | bytes 393224 | tf_op jit(solution)/shard_map/ppermute | solution.py:478
  25.1 1.2 %reach.4 = (bf16[256,256]{1,0:T(8,128)(2,1)S(1)}, f32[256,128]{1,0:T(8,128)S(1)}) custom-call(bf16[1024,128]{1,0:T(8,128)(2,1)S(1)} %bitcast.4, bf16[4,512,128]{2,1,0:T(8,128)(2,1)S(1)} %get-tuple-element.32.r_ref, f32[4,4,256,128]{3,2,1,0:T(8,128)S(1)} %get-tuple-element.33.z_ref, f32[4,256,128]{2,1,0:T(8,128)S(1)} %collective-permute-done.sib_ref, ...), custom_call_target="tpu_custom_call" | custom-call | flops 400000000 | bytes 3000000 | tf_op jit(solution)/shard_map/reach/pallas_call | solution.py:335
  26.3 0.0 collective-permute-done.2.s2.refs_2_
  26.3 1.4 %collective-permute-done.3.s3.refs_3_ = f32[256,128]{1,0:T(8,128)S(1)} collective-permute-done((f32[256,128]{1,0:T(8,128)S(1)}, f32[256,128]{1,0:T(8,128)S(1)}, u32[]{:S(2)}, u32[]{:S(2)}) %collective-permute-start.3) | collective-permute-done | bytes 131104 | tf_op jit(solution)/shard_map/ppermute | solution.py:478
  27.7 0.5 row.1.after_ref.s0.refs_4_
  28.2 0.0 copy-start.1
  28.2 4.8 %collective-permute-start.6 = (f32[256,128]{1,0:T(8,128)S(1)}, f32[256,128]{1,0:T(8,128)S(1)}, u32[]{:S(2)}, u32[]{:S(2)}) collective-permute-start(f32[256,128]{1,0:T(8,128)S(1)} %row.1.after_ref.s0.refs_4_), channel_id=1, source_target_pairs={{8,200},{24,216},{40,232},{56,248},{72,136},{88,152},{104,168},{12... | collective-permute-start | bytes 393224 | tf_op jit(solution)/shard_map/ppermute | solution.py:484
  33.0 2.3 %collective-permute-start.5 = (f32[256,128]{1,0:T(8,128)S(1)}, f32[256,128]{1,0:T(8,128)S(1)}, u32[]{:S(2)}, u32[]{:S(2)}) collective-permute-start(f32[256,128]{1,0:T(8,128)S(1)} %row.1.after_ref.s0.refs_4_), channel_id=1, source_target_pairs={{8,136},{24,152},{40,168},{56,184},{72,200},{88,216},{104,232},{12... | collective-permute-start | bytes 393224 | tf_op jit(solution)/shard_map/ppermute | solution.py:484
  35.2 2.1 %collective-permute-start.4 = (f32[256,128]{1,0:T(8,128)S(1)}, f32[256,128]{1,0:T(8,128)S(1)}, u32[]{:S(2)}, u32[]{:S(2)}) collective-permute-start(f32[256,128]{1,0:T(8,128)S(1)} %row.1.after_ref.s0.refs_4_), channel_id=1, source_target_pairs={{8,72},{24,88},{40,104},{56,120},{72,8},{88,24},{104,40},{120,56},... | collective-permute-start | bytes 393224 | tf_op jit(solution)/shard_map/ppermute | solution.py:484
  37.4 1.2 %reach.5 = (bf16[256,256]{1,0:T(8,128)(2,1)S(1)}, f32[256,128]{1,0:T(8,128)S(1)}) custom-call(bf16[1024,128]{1,0:T(8,128)(2,1)S(1)} %bitcast.5, bf16[4,512,128]{2,1,0:T(8,128)(2,1)S(1)} %get-tuple-element.32.r_ref, f32[4,4,256,128]{3,2,1,0:T(8,128)S(1)} %get-tuple-element.33.z_ref, f32[4,256,128]{2,1,0:T(8,128)S(1)} %collective-permute-done.sib_ref, ...), custom_call_target="tpu_custom_call" | custom-call | flops 400000000 | bytes 3000000 | tf_op jit(solution)/shard_map/reach/pallas_call | solution.py:335
  38.6 0.0 collective-permute-done.6.s3.refs_7_
  38.6 1.6 %collective-permute-done.5.s2.refs_6_ = f32[256,128]{1,0:T(8,128)S(1)} collective-permute-done((f32[256,128]{1,0:T(8,128)S(1)}, f32[256,128]{1,0:T(8,128)S(1)}, u32[]{:S(2)}, u32[]{:S(2)}) %collective-permute-start.5) | collective-permute-done | bytes 131104 | tf_op jit(solution)/shard_map/ppermute | solution.py:484
  40.2 0.8 collective-permute-done.4.s1.refs_5_
  40.9 0.5 column.1.refs_9_.s0
  41.4 6.3 %collective-permute-start.9 = (f32[256,128]{1,0:T(8,128)S(1)}, f32[256,128]{1,0:T(8,128)S(1)}, u32[]{:S(2)}, u32[]{:S(2)}) collective-permute-start(f32[256,128]{1,0:T(8,128)S(1)} %column.1.refs_9_.s0), channel_id=1, source_target_pairs={{8,11},{9,10},{10,9},{11,8},{12,15},{13,14},{14,13},{15,12},{24,27... | collective-permute-start | bytes 393224 | tf_op jit(solution)/shard_map/ppermute | solution.py:490
  47.7 1.9 %collective-permute-start.8 = (f32[256,128]{1,0:T(8,128)S(1)}, f32[256,128]{1,0:T(8,128)S(1)}, u32[]{:S(2)}, u32[]{:S(2)}) collective-permute-start(f32[256,128]{1,0:T(8,128)S(1)} %column.1.refs_9_.s0), channel_id=1, source_target_pairs={{8,10},{9,11},{10,8},{11,9},{12,14},{13,15},{14,12},{15,13},{24,26... | collective-permute-start | bytes 393224 | tf_op jit(solution)/shard_map/ppermute | solution.py:490
  49.6 2.4 %collective-permute-start.7 = (f32[256,128]{1,0:T(8,128)S(1)}, f32[256,128]{1,0:T(8,128)S(1)}, u32[]{:S(2)}, u32[]{:S(2)}) collective-permute-start(f32[256,128]{1,0:T(8,128)S(1)} %column.1.refs_9_.s0), channel_id=1, source_target_pairs={{8,9},{9,8},{10,11},{11,10},{12,13},{13,12},{14,15},{15,14},{24,25... | collective-permute-start | bytes 393224 | tf_op jit(solution)/shard_map/ppermute | solution.py:490
  52.0 0.7 path.1
  52.6 1.2 %reach.6 = (bf16[256,256]{1,0:T(8,128)(2,1)S(1)}, f32[256,128]{1,0:T(8,128)S(1)}) custom-call(bf16[1024,128]{1,0:T(8,128)(2,1)S(1)} %bitcast.6, bf16[4,512,128]{2,1,0:T(8,128)(2,1)S(1)} %get-tuple-element.32.r_ref, f32[4,4,256,128]{3,2,1,0:T(8,128)S(1)} %get-tuple-element.33.z_ref, f32[4,256,128]{2,1,0:T(8,128)S(1)} %collective-permute-done.sib_ref, ...), custom_call_target="tpu_custom_call" | custom-call | flops 400000000 | bytes 3000000 | tf_op jit(solution)/shard_map/reach/pallas_call | solution.py:335
  53.8 0.0 collective-permute-done.9.s3
  53.8 0.5 collective-permute-done.8.s2
  54.4 1.4 %collective-permute-done.7.s1 = f32[256,128]{1,0:T(8,128)S(1)} collective-permute-done((f32[256,128]{1,0:T(8,128)S(1)}, f32[256,128]{1,0:T(8,128)S(1)}, u32[]{:S(2)}, u32[]{:S(2)}) %collective-permute-start.7) | collective-permute-done | bytes 131104 | tf_op jit(solution)/shard_map/ppermute | solution.py:490
  55.7 0.5 lead.1.after_ref
  56.2 5.7 %collective-permute-start.10 = (f32[128,128]{1,0:T(8,128)S(1)}, f32[128,128]{1,0:T(8,128)S(1)}, u32[]{:S(2)}, u32[]{:S(2)}) collective-permute-start(f32[128,128]{1,0:T(8,128)S(1)} %lead.1.after_ref), channel_id=1, source_target_pairs={{8,15},{9,14},{10,13},{11,12},{12,11},{13,10},{14,9},{15,8},{24,31... | collective-permute-start | bytes 196616 | tf_op jit(solution)/shard_map/ppermute | solution.py:508
  61.9 0.6 fuse.1.fuse_ref
  62.5 0.0 copy-start.2
  62.5 1.7 %collective-permute-done.10.early_ref = f32[128,128]{1,0:T(8,128)S(1)} collective-permute-done((f32[128,128]{1,0:T(8,128)S(1)}, f32[128,128]{1,0:T(8,128)S(1)}, u32[]{:S(2)}, u32[]{:S(2)}) %collective-permute-start.10) | collective-permute-done | bytes 65568 | tf_op jit(solution)/shard_map/ppermute | solution.py:508
  64.2 0.3 entry.1
  64.5 1.9 %collective-permute-start.13 = (f32[128,128]{1,0:T(8,128)S(1)}, f32[128,128]{1,0:T(8,128)S(1)}, u32[]{:S(2)}, u32[]{:S(2)}) collective-permute-start(f32[128,128]{1,0:T(8,128)S(1)} %get-tuple-element.49), channel_id=1, source_target_pairs={{8,24},{24,40},{40,56},{56,8},{72,88},{88,104},{104,120},{120,72},... | collective-permute-start | bytes 196616 | tf_op jit(solution)/shard_map/ppermute | solution.py:524
  66.5 5.4 %collective-permute-start.12 = (f32[128,128]{1,0:T(8,128)S(1)}, f32[128,128]{1,0:T(8,128)S(1)}, u32[]{:S(2)}, u32[]{:S(2)}) collective-permute-start(f32[128,128]{1,0:T(8,128)S(1)} %get-tuple-element.48), channel_id=1, source_target_pairs={{8,40},{24,56},{40,8},{56,24},{72,104},{88,120},{104,72},{120,88},... | collective-permute-start | bytes 196616 | tf_op jit(solution)/shard_map/ppermute | solution.py:524
  71.9 1.9 %collective-permute-start.11 = (f32[128,128]{1,0:T(8,128)S(1)}, f32[128,128]{1,0:T(8,128)S(1)}, u32[]{:S(2)}, u32[]{:S(2)}) collective-permute-start(f32[128,128]{1,0:T(8,128)S(1)} %get-tuple-element.47), channel_id=1, source_target_pairs={{8,56},{24,8},{40,24},{56,40},{72,120},{88,72},{104,88},{120,104},... | collective-permute-start | bytes 196616 | tf_op jit(solution)/shard_map/ppermute | solution.py:524
  73.8 1.3 %collective-permute-start.14 = (f32[128,128]{1,0:T(8,128)S(1)}, f32[128,128]{1,0:T(8,128)S(1)}, u32[]{:S(2)}, u32[]{:S(2)}) collective-permute-start(f32[128,128]{1,0:T(8,128)S(1)} %get-tuple-element.50.after_ref.refs_8_), channel_id=1, source_target_pairs={{8,0},{24,16},{40,32},{56,48},{72,64},{88,80},{104,96},{120,112},{... | collective-permute-start | bytes 196616 | tf_op jit(solution)/shard_map/ppermute | solution.py:530
  75.1 1.2 %reach.7 = (bf16[256,256]{1,0:T(8,128)(2,1)S(1)}, f32[256,128]{1,0:T(8,128)S(1)}) custom-call(bf16[1024,128]{1,0:T(8,128)(2,1)S(1)} %bitcast.7, bf16[4,512,128]{2,1,0:T(8,128)(2,1)S(1)} %get-tuple-element.32.r_ref, f32[4,4,256,128]{3,2,1,0:T(8,128)S(1)} %get-tuple-element.33.z_ref, f32[4,256,128]{2,1,0:T(8,128)S(1)} %collective-permute-done.sib_ref, ...), custom_call_target="tpu_custom_call" | custom-call | flops 400000000 | bytes 3000000 | tf_op jit(solution)/shard_map/reach/pallas_call | solution.py:335
  76.3 0.0 collective-permute-done.12.refs_10_
  76.3 0.6 collective-permute-done.11.refs_11_
  76.9 1.3 %collective-permute-start.17 = (f32[128,128]{1,0:T(8,128)S(1)}, f32[128,128]{1,0:T(8,128)S(1)}, u32[]{:S(2)}, u32[]{:S(2)}) collective-permute-start(f32[128,128]{1,0:T(8,128)S(1)} %collective-permute-done.11.refs_11_), channel_id=1, source_target_pairs={{8,0},{24,16},{40,32},{56,48},{72,64},{88,80},{104,96},{120,112},{... | collective-permute-start | bytes 196616 | tf_op jit(solution)/shard_map/ppermute | solution.py:530
  78.2 1.3 %collective-permute-start.16 = (f32[128,128]{1,0:T(8,128)S(1)}, f32[128,128]{1,0:T(8,128)S(1)}, u32[]{:S(2)}, u32[]{:S(2)}) collective-permute-start(f32[128,128]{1,0:T(8,128)S(1)} %collective-permute-done.12.refs_10_), channel_id=1, source_target_pairs={{8,0},{24,16},{40,32},{56,48},{72,64},{88,80},{104,96},{120,112},{... | collective-permute-start | bytes 196616 | tf_op jit(solution)/shard_map/ppermute | solution.py:530
  79.5 1.3 %collective-permute-start.15 = (f32[128,128]{1,0:T(8,128)S(1)}, f32[128,128]{1,0:T(8,128)S(1)}, u32[]{:S(2)}, u32[]{:S(2)}) collective-permute-start(f32[128,128]{1,0:T(8,128)S(1)} %collective-permute-done.13.refs_9_), channel_id=1, source_target_pairs={{8,0},{24,16},{40,32},{56,48},{72,64},{88,80},{104,96},{120,112},{... | collective-permute-start | bytes 196616 | tf_op jit(solution)/shard_map/ppermute | solution.py:530
  80.8 0.0 collective-permute-done.17.refs_15_
  80.8 0.0 collective-permute-done.16.refs_14_
  80.8 0.8 %collective-permute-done.15.refs_13_ = f32[128,128]{1,0:T(8,128)S(1)} collective-permute-done((f32[128,128]{1,0:T(8,128)S(1)}, f32[128,128]{1,0:T(8,128)S(1)}, u32[]{:S(2)}, u32[]{:S(2)}) %collective-permute-start.15) | collective-permute-done | bytes 65568 | tf_op jit(solution)/shard_map/ppermute | solution.py:530
  81.7 1.3 %read.1 = bf16[1024,128]{1,0:T(8,128)(2,1)} custom-call(bf16[256,256]{1,0:T(8,128)(2,1)S(1)} %get-tuple-element.36.after_ref.refs_0_, f32[256,128]{1,0:T(8,128)S(1)} %get-tuple-element.37.refs_1_, bf16[256,256]{1,0:T(8,128)(2,1)S(1)} %get-tuple-element.41.after_ref.refs_2_, f32[256,128]{1,0:T(8,128)S(1)} %get-tuple-element.42.refs_3_, ...), custom_call_target="tpu_custom_call" | custom-call | tf_op jit(solution)/shard_map/read/pallas_call | solution.py:403
  (7 shorter events, 0.0 us)
Async XLA Ops:
  0.0 25.1 %copy-start = (bf16[1,256,4,128]{3,2,1,0:T(4,128)(2,1)S(1)}, bf16[1,256,4,128]{3,2,1,0:T(4,128)(2,1)}, u32[]{:S(2)}) copy-start(bf16[1,256,4,128]{3,2,1,0:T(4,128)(2,1)} %param.5) | copy-start | bytes 786436
  9.5 5.9 %collective-permute-start = (f32[4,256,128]{2,1,0:T(8,128)S(1)}, f32[4,256,128]{2,1,0:T(8,128)S(1)}, u32[]{:S(2)}, u32[]{:S(2)}) collective-permute-start(f32[4,256,128]{2,1,0:T(8,128)S(1)} %get-tuple-element.34.own_ref), channel_id=1, source_target_pairs={{0,8},{16,24},{32,40},{48,56},{64,72},{80,88},{96,104},{112,120},{... | collective-permute-start | bytes 1572872 | tf_op jit(solution)/shard_map/ppermute | solution.py:476
  15.8 10.5 %collective-permute-start.1 = (f32[256,128]{1,0:T(8,128)S(1)}, f32[256,128]{1,0:T(8,128)S(1)}, u32[]{:S(2)}, u32[]{:S(2)}) collective-permute-start(f32[256,128]{1,0:T(8,128)S(1)} %get-tuple-element.38), channel_id=1, source_target_pairs={{8,24},{24,40},{40,56},{56,8},{72,88},{88,104},{104,120},{120,72},... | collective-permute-start | bytes 393224 | tf_op jit(solution)/shard_map/ppermute | solution.py:478
  17.7 8.6 %collective-permute-start.2 = (f32[256,128]{1,0:T(8,128)S(1)}, f32[256,128]{1,0:T(8,128)S(1)}, u32[]{:S(2)}, u32[]{:S(2)}) collective-permute-start(f32[256,128]{1,0:T(8,128)S(1)} %get-tuple-element.39), channel_id=1, source_target_pairs={{8,40},{24,56},{40,8},{56,24},{72,104},{88,120},{104,72},{120,88},... | collective-permute-start | bytes 393224 | tf_op jit(solution)/shard_map/ppermute | solution.py:478
  22.0 5.7 %collective-permute-start.3 = (f32[256,128]{1,0:T(8,128)S(1)}, f32[256,128]{1,0:T(8,128)S(1)}, u32[]{:S(2)}, u32[]{:S(2)}) collective-permute-start(f32[256,128]{1,0:T(8,128)S(1)} %get-tuple-element.40), channel_id=1, source_target_pairs={{8,56},{24,8},{40,24},{56,40},{72,120},{88,72},{104,88},{120,104},... | collective-permute-start | bytes 393224 | tf_op jit(solution)/shard_map/ppermute | solution.py:478
  28.2 23.8 %copy-start.1 = (f32[4,128,128]{2,1,0:T(8,128)S(1)}, f32[4,128,128]{2,1,0:T(8,128)}, u32[]{:S(2)}) copy-start(f32[4,128,128]{2,1,0:T(8,128)} %refs_8_.1) | copy-start | bytes 786436
  28.2 10.4 %collective-permute-start.6 = (f32[256,128]{1,0:T(8,128)S(1)}, f32[256,128]{1,0:T(8,128)S(1)}, u32[]{:S(2)}, u32[]{:S(2)}) collective-permute-start(f32[256,128]{1,0:T(8,128)S(1)} %row.1.after_ref.s0.refs_4_), channel_id=1, source_target_pairs={{8,200},{24,216},{40,232},{56,248},{72,136},{88,152},{104,168},{12... | collective-permute-start | bytes 393224 | tf_op jit(solution)/shard_map/ppermute | solution.py:484
  33.0 7.2 %collective-permute-start.5 = (f32[256,128]{1,0:T(8,128)S(1)}, f32[256,128]{1,0:T(8,128)S(1)}, u32[]{:S(2)}, u32[]{:S(2)}) collective-permute-start(f32[256,128]{1,0:T(8,128)S(1)} %row.1.after_ref.s0.refs_4_), channel_id=1, source_target_pairs={{8,136},{24,152},{40,168},{56,184},{72,200},{88,216},{104,232},{12... | collective-permute-start | bytes 393224 | tf_op jit(solution)/shard_map/ppermute | solution.py:484
  35.2 5.7 %collective-permute-start.4 = (f32[256,128]{1,0:T(8,128)S(1)}, f32[256,128]{1,0:T(8,128)S(1)}, u32[]{:S(2)}, u32[]{:S(2)}) collective-permute-start(f32[256,128]{1,0:T(8,128)S(1)} %row.1.after_ref.s0.refs_4_), channel_id=1, source_target_pairs={{8,72},{24,88},{40,104},{56,120},{72,8},{88,24},{104,40},{120,56},... | collective-permute-start | bytes 393224 | tf_op jit(solution)/shard_map/ppermute | solution.py:484
  41.4 12.4 %collective-permute-start.9 = (f32[256,128]{1,0:T(8,128)S(1)}, f32[256,128]{1,0:T(8,128)S(1)}, u32[]{:S(2)}, u32[]{:S(2)}) collective-permute-start(f32[256,128]{1,0:T(8,128)S(1)} %column.1.refs_9_.s0), channel_id=1, source_target_pairs={{8,11},{9,10},{10,9},{11,8},{12,15},{13,14},{14,13},{15,12},{24,27... | collective-permute-start | bytes 393224 | tf_op jit(solution)/shard_map/ppermute | solution.py:490
  47.7 6.7 %collective-permute-start.8 = (f32[256,128]{1,0:T(8,128)S(1)}, f32[256,128]{1,0:T(8,128)S(1)}, u32[]{:S(2)}, u32[]{:S(2)}) collective-permute-start(f32[256,128]{1,0:T(8,128)S(1)} %column.1.refs_9_.s0), channel_id=1, source_target_pairs={{8,10},{9,11},{10,8},{11,9},{12,14},{13,15},{14,12},{15,13},{24,26... | collective-permute-start | bytes 393224 | tf_op jit(solution)/shard_map/ppermute | solution.py:490
  49.6 6.1 %collective-permute-start.7 = (f32[256,128]{1,0:T(8,128)S(1)}, f32[256,128]{1,0:T(8,128)S(1)}, u32[]{:S(2)}, u32[]{:S(2)}) collective-permute-start(f32[256,128]{1,0:T(8,128)S(1)} %column.1.refs_9_.s0), channel_id=1, source_target_pairs={{8,9},{9,8},{10,11},{11,10},{12,13},{13,12},{14,15},{15,14},{24,25... | collective-permute-start | bytes 393224 | tf_op jit(solution)/shard_map/ppermute | solution.py:490
  56.2 8.0 %collective-permute-start.10 = (f32[128,128]{1,0:T(8,128)S(1)}, f32[128,128]{1,0:T(8,128)S(1)}, u32[]{:S(2)}, u32[]{:S(2)}) collective-permute-start(f32[128,128]{1,0:T(8,128)S(1)} %lead.1.after_ref), channel_id=1, source_target_pairs={{8,15},{9,14},{10,13},{11,12},{12,11},{13,10},{14,9},{15,8},{24,31... | collective-permute-start | bytes 196616 | tf_op jit(solution)/shard_map/ppermute | solution.py:508
  62.5 19.2 %copy-start.2 = (f32[4,128]{1,0:T(4,128)S(1)}, f32[4,128]{1,0:T(4,128)}, u32[]{:S(2)}) copy-start(f32[4,128]{1,0:T(4,128)} %refs_16_.1) | copy-start | bytes 6148
  64.5 11.8 %collective-permute-start.13 = (f32[128,128]{1,0:T(8,128)S(1)}, f32[128,128]{1,0:T(8,128)S(1)}, u32[]{:S(2)}, u32[]{:S(2)}) collective-permute-start(f32[128,128]{1,0:T(8,128)S(1)} %get-tuple-element.49), channel_id=1, source_target_pairs={{8,24},{24,40},{40,56},{56,8},{72,88},{88,104},{104,120},{120,72},... | collective-permute-start | bytes 196616 | tf_op jit(solution)/shard_map/ppermute | solution.py:524
  66.5 9.9 %collective-permute-start.12 = (f32[128,128]{1,0:T(8,128)S(1)}, f32[128,128]{1,0:T(8,128)S(1)}, u32[]{:S(2)}, u32[]{:S(2)}) collective-permute-start(f32[128,128]{1,0:T(8,128)S(1)} %get-tuple-element.48), channel_id=1, source_target_pairs={{8,40},{24,56},{40,8},{56,24},{72,104},{88,120},{104,72},{120,88},... | collective-permute-start | bytes 196616 | tf_op jit(solution)/shard_map/ppermute | solution.py:524
  71.9 5.0 %collective-permute-start.11 = (f32[128,128]{1,0:T(8,128)S(1)}, f32[128,128]{1,0:T(8,128)S(1)}, u32[]{:S(2)}, u32[]{:S(2)}) collective-permute-start(f32[128,128]{1,0:T(8,128)S(1)} %get-tuple-element.47), channel_id=1, source_target_pairs={{8,56},{24,8},{40,24},{56,40},{72,120},{88,72},{104,88},{120,104},... | collective-permute-start | bytes 196616 | tf_op jit(solution)/shard_map/ppermute | solution.py:524
  73.8 7.0 %collective-permute-start.14 = (f32[128,128]{1,0:T(8,128)S(1)}, f32[128,128]{1,0:T(8,128)S(1)}, u32[]{:S(2)}, u32[]{:S(2)}) collective-permute-start(f32[128,128]{1,0:T(8,128)S(1)} %get-tuple-element.50.after_ref.refs_8_), channel_id=1, source_target_pairs={{8,0},{24,16},{40,32},{56,48},{72,64},{88,80},{104,96},{120,112},{... | collective-permute-start | bytes 196616 | tf_op jit(solution)/shard_map/ppermute | solution.py:530
  76.9 3.9 %collective-permute-start.17 = (f32[128,128]{1,0:T(8,128)S(1)}, f32[128,128]{1,0:T(8,128)S(1)}, u32[]{:S(2)}, u32[]{:S(2)}) collective-permute-start(f32[128,128]{1,0:T(8,128)S(1)} %collective-permute-done.11.refs_11_), channel_id=1, source_target_pairs={{8,0},{24,16},{40,32},{56,48},{72,64},{88,80},{104,96},{120,112},{... | collective-permute-start | bytes 196616 | tf_op jit(solution)/shard_map/ppermute | solution.py:530
  78.2 2.6 %collective-permute-start.16 = (f32[128,128]{1,0:T(8,128)S(1)}, f32[128,128]{1,0:T(8,128)S(1)}, u32[]{:S(2)}, u32[]{:S(2)}) collective-permute-start(f32[128,128]{1,0:T(8,128)S(1)} %collective-permute-done.12.refs_10_), channel_id=1, source_target_pairs={{8,0},{24,16},{40,32},{56,48},{72,64},{88,80},{104,96},{120,112},{... | collective-permute-start | bytes 196616 | tf_op jit(solution)/shard_map/ppermute | solution.py:530
  79.5 2.2 %collective-permute-start.15 = (f32[128,128]{1,0:T(8,128)S(1)}, f32[128,128]{1,0:T(8,128)S(1)}, u32[]{:S(2)}, u32[]{:S(2)}) collective-permute-start(f32[128,128]{1,0:T(8,128)S(1)} %collective-permute-done.13.refs_9_), channel_id=1, source_target_pairs={{8,0},{24,16},{40,32},{56,48},{72,64},{88,80},{104,96},{120,112},{... | collective-permute-start | bytes 196616 | tf_op jit(solution)/shard_map/ppermute | solution.py:530

commit v7 on v6

--- a/solution.py
+++ b/solution.py
@@ -435,32 +435,33 @@
 
 
 def plane_perm(move):
-    last = CS - 1
-    return [
-        (seat(y, x, last), seat(*move(y, x), last)) for y in range(YS) for x in range(XS)
-    ]
+    pairs = []
+    for y in range(YS):
+        for x in range(XS):
+            pairs.append((seat(y, x, 0), seat(y, x, 0)))
+            pairs.append((seat(y, x, 1), seat(*move(y, x), 1)))
+    return pairs
 
 
 def depth_perm(segs, move):
-    last = CS - 1
-    return [
-        (seat(y, x, last) * segs + g, seat(y, x, last) * segs + move(g))
-        for y in range(YS)
-        for x in range(XS)
-        for g in range(segs)
-    ]
-
-
-def chip_perm(source):
-    return [
-        (seat(y, x, source), seat(y, x, 1 - source)) for y in range(YS) for x in range(XS)
-    ]
+    pairs = []
+    for y in range(YS):
+        for x in range(XS):
+            for g in range(segs):
+                for c in range(CS):
+                    at = seat(y, x, c) * segs
+                    pairs.append((at + g, at + (move(g) if c else g)))
+    return pairs
+
+
+def chip_perm():
+    return [(seat(y, x, c), seat(y, x, 1 - c)) for y in range(YS) for x in range(XS) for c in range(CS)]
 
 
 def per_device(query_rows, key_rows, value_rows, out_gain, initial_state):
     tokens = query_rows.shape[1]
     steps = tokens * REFL
-    up, down = chip_perm(0), chip_perm(1)
+    swap = chip_perm()
     along_x = [plane_perm(lambda y, x, k=k: (y, (x + k) % XS)) for k in range(1, XS)]
     along_y = [plane_perm(lambda y, x, k=k: (y ^ k, x)) for k in range(1, YS)]
     segs = lax.axis_size("seg")
@@ -473,7 +474,7 @@
     keys = pltpu.with_memory_space_constraint(keys, pltpu.HBM)
     values = pltpu.with_memory_space_constraint(values, pltpu.HBM)
     pair, z, r = factor_call(keys, values)
-    sib = lax.ppermute(pair, "seq", up)
+    sib = lax.ppermute(pair, "seq", swap)
     slots = small_call(chip_kernel, "chip", [pair, sib], [(MSG, D)] * XS)
     slots = [slots[0]] + [lax.ppermute(s, "seq", p) for s, p in zip(slots[1:], along_x)]
     reaches = [reach_call(query, r, z, sib, slots[0], 0)]
@@ -527,7 +528,7 @@
     for k in range(1, XS):
         slots[k], last = lax.optimization_barrier((slots[k], last))
     reaches[-1] = (last, reaches[-1][1])
-    others = [lax.ppermute(s, "seq", down) for s in slots]
+    others = [lax.ppermute(s, "seq", swap) for s in slots]
     arrays = [a for pair in reaches for a in pair] + [*slots, *others, out_gain]
     out = read_call(arrays, tokens)
     return out.reshape(1, tokens, HEADS, D)

time: 83.7 us -> 79.1 us (0.945)
  starting transfers between devices: 50.4 us -> 47.4 us
  waiting for transfers between devices: 13.4 us -> 12 us
    ppermute x5, waiting for transfers between devices: 5.47 us -> 2.79 us  [the longest x1 1.54 us: per_device(): sib = lax.ppermute(pair, 'seq', swap)]
    ppermute x5, starting transfers between devices: 6.45 us -> 3.93 us  [the longest x1 3.32 us: per_device(): sib = lax.ppermute(pair, 'seq', swap)]
    ppermute x6, waiting for transfers between devices: 2 us -> 3.2 us  [per_device(): lax.ppermute(s, 'seq', p)]
  transfers between devices with their start and end apart: 18 -> 18, of which waited for: 9 -> 11; matrix products, arithmetic and copies ran while one was open for 0% -> 0% of each run, Pallas kernels for 7% -> 8%
where the time goes in v7:
time: 79.1 us; the launch traced here: 78.6 us
  starting transfers between devices  47.4 us (60%)
  Pallas kernels  18.8 us (24%)
  waiting for transfers between devices  12 us (15%)
    ppermute x6, starting transfers between devices, per_device(): lax.ppermute(s, 'seq', p)  18.1 us
    ppermute x3, starting transfers between devices, per_device(): slots = [total] + [lax.ppermute(total, ('seq', 'seg'), p) for p in along_z]  10.6 us
    pallas_call x1, Pallas kernels, factor_call(): pl.pallas_call(factor_kernel, in_specs=[pl.BlockSpec(memory_space=pl.ANY)...  9.53 us
    ppermute x3, starting transfers between devices, per_device(): slots = [total] + [lax.ppermute(total, 'seq', p) for p in along_y]  9.18 us
    ppermute x1, starting transfers between devices, per_device(): early = lax.ppermute(lead, ('seq', 'seg'), jump)  5.67 us
    pallas_call x4, Pallas kernels, reach_call(): pl.pallas_call(functools.partial(reach_kernel, head=head), grid=(1,), in_...  4.72 us
    ppermute x1, starting transfers between devices, per_device(): sib = lax.ppermute(pair, 'seq', swap)  3.32 us
    pallas_call x7, Pallas kernels, small_call(): pl.pallas_call(kernel, in_specs=whole(*arrays) + [pl.BlockSpec(memory_spa...  3.26 us
  transfers between devices with their start and end apart: 18, of which 11 were waited for; matrix products, arithmetic and copies ran while one was open for 0% of the time, Pallas kernels for 8%

profile of v7, /device:TPU:1, one launch (start us, length us, event | category | flops | bytes accessed | tf_op | source)
XLA Modules:
  0.0 78.6 jit_solution(3203965688715838198)
XLA Ops:
  0.0 9.5 %factor.1 = (f32[4,256,128]{2,1,0:T(8,128)S(1)}, f32[4,4,256,128]{3,2,1,0:T(8,128)S(1)}, bf16[4,512,128]{2,1,0:T(8,128)(2,1)S(1)}) custom-call(bf16[2048,128]{1,0:T(8,128)(2,1)} %bitcast.8, bf16[2048,128]{1,0:T(8,128)(2,1)} %bitcast.9), custom_call_target="tpu_custom_call" | custom-call | tf_op jit(solution)/shard_map/factor/pallas_call | solution.py:181
  9.5 3.3 %collective-permute-start = (f32[4,256,128]{2,1,0:T(8,128)S(1)}, f32[4,256,128]{2,1,0:T(8,128)S(1)}, u32[]{:S(2)}, u32[]{:S(2)}) collective-permute-start(f32[4,256,128]{2,1,0:T(8,128)S(1)} %get-tuple-element.34.own_ref), channel_id=1, source_target_pairs={{0,8},{8,0},{16,24},{24,16},{32,40},{40,32},{48,56},{56,48},{64,72... | collective-permute-start | bytes 1572872 | tf_op jit(solution)/shard_map/ppermute | solution.py:477
  12.9 1.5 %collective-permute-done.sib_ref = f32[4,256,128]{2,1,0:T(8,128)S(1)} collective-permute-done((f32[4,256,128]{2,1,0:T(8,128)S(1)}, f32[4,256,128]{2,1,0:T(8,128)S(1)}, u32[]{:S(2)}, u32[]{:S(2)}) %collective-permute-start) | collective-permute-done | bytes 524320 | tf_op jit(solution)/shard_map/ppermute | solution.py:477
  14.4 0.3 chip.1
  14.7 1.9 %collective-permute-start.1 = (f32[256,128]{1,0:T(8,128)S(1)}, f32[256,128]{1,0:T(8,128)S(1)}, u32[]{:S(2)}, u32[]{:S(2)}) collective-permute-start(f32[256,128]{1,0:T(8,128)S(1)} %get-tuple-element.38), channel_id=1, source_target_pairs={{0,0},{8,24},{16,16},{24,40},{32,32},{40,56},{48,48},{56,8},{64,64... | collective-permute-start | bytes 393224 | tf_op jit(solution)/shard_map/ppermute | solution.py:479
  16.6 3.8 %collective-permute-start.2 = (f32[256,128]{1,0:T(8,128)S(1)}, f32[256,128]{1,0:T(8,128)S(1)}, u32[]{:S(2)}, u32[]{:S(2)}) collective-permute-start(f32[256,128]{1,0:T(8,128)S(1)} %get-tuple-element.39), channel_id=1, source_target_pairs={{0,0},{8,40},{16,16},{24,56},{32,32},{40,8},{48,48},{56,24},{64,64... | collective-permute-start | bytes 393224 | tf_op jit(solution)/shard_map/ppermute | solution.py:479
  20.5 3.1 %collective-permute-start.3 = (f32[256,128]{1,0:T(8,128)S(1)}, f32[256,128]{1,0:T(8,128)S(1)}, u32[]{:S(2)}, u32[]{:S(2)}) collective-permute-start(f32[256,128]{1,0:T(8,128)S(1)} %get-tuple-element.40), channel_id=1, source_target_pairs={{0,0},{8,56},{16,16},{24,8},{32,32},{40,24},{48,48},{56,40},{64,64... | collective-permute-start | bytes 393224 | tf_op jit(solution)/shard_map/ppermute | solution.py:479
  23.6 1.2 %reach.4 = (bf16[256,256]{1,0:T(8,128)(2,1)S(1)}, f32[256,128]{1,0:T(8,128)S(1)}) custom-call(bf16[1024,128]{1,0:T(8,128)(2,1)S(1)} %bitcast.4, bf16[4,512,128]{2,1,0:T(8,128)(2,1)S(1)} %get-tuple-element.32.r_ref, f32[4,4,256,128]{3,2,1,0:T(8,128)S(1)} %get-tuple-element.33.z_ref, f32[4,256,128]{2,1,0:T(8,128)S(1)} %collective-permute-done.sib_ref, ...), custom_call_target="tpu_custom_call" | custom-call | flops 400000000 | bytes 3000000 | tf_op jit(solution)/shard_map/reach/pallas_call | solution.py:335
  24.8 0.0 collective-permute-done.2.s2.refs_2_
  24.8 1.4 %collective-permute-done.3.s3.refs_3_ = f32[256,128]{1,0:T(8,128)S(1)} collective-permute-done((f32[256,128]{1,0:T(8,128)S(1)}, f32[256,128]{1,0:T(8,128)S(1)}, u32[]{:S(2)}, u32[]{:S(2)}) %collective-permute-start.3) | collective-permute-done | bytes 131104 | tf_op jit(solution)/shard_map/ppermute | solution.py:479
  26.2 0.5 row.1.after_ref.s0.refs_4_
  26.6 0.0 copy-start.1
  26.7 4.8 %collective-permute-start.6 = (f32[256,128]{1,0:T(8,128)S(1)}, f32[256,128]{1,0:T(8,128)S(1)}, u32[]{:S(2)}, u32[]{:S(2)}) collective-permute-start(f32[256,128]{1,0:T(8,128)S(1)} %row.1.after_ref.s0.refs_4_), channel_id=1, source_target_pairs={{0,0},{8,200},{16,16},{24,216},{32,32},{40,232},{48,48},{56,248},{... | collective-permute-start | bytes 393224 | tf_op jit(solution)/shard_map/ppermute | solution.py:485
  31.4 2.3 %collective-permute-start.5 = (f32[256,128]{1,0:T(8,128)S(1)}, f32[256,128]{1,0:T(8,128)S(1)}, u32[]{:S(2)}, u32[]{:S(2)}) collective-permute-start(f32[256,128]{1,0:T(8,128)S(1)} %row.1.after_ref.s0.refs_4_), channel_id=1, source_target_pairs={{0,0},{8,136},{16,16},{24,152},{32,32},{40,168},{48,48},{56,184},{... | collective-permute-start | bytes 393224 | tf_op jit(solution)/shard_map/ppermute | solution.py:485
  33.7 2.1 %collective-permute-start.4 = (f32[256,128]{1,0:T(8,128)S(1)}, f32[256,128]{1,0:T(8,128)S(1)}, u32[]{:S(2)}, u32[]{:S(2)}) collective-permute-start(f32[256,128]{1,0:T(8,128)S(1)} %row.1.after_ref.s0.refs_4_), channel_id=1, source_target_pairs={{0,0},{8,72},{16,16},{24,88},{32,32},{40,104},{48,48},{56,120},{64... | collective-permute-start | bytes 393224 | tf_op jit(solution)/shard_map/ppermute | solution.py:485
  35.9 1.2 %reach.5 = (bf16[256,256]{1,0:T(8,128)(2,1)S(1)}, f32[256,128]{1,0:T(8,128)S(1)}) custom-call(bf16[1024,128]{1,0:T(8,128)(2,1)S(1)} %bitcast.5, bf16[4,512,128]{2,1,0:T(8,128)(2,1)S(1)} %get-tuple-element.32.r_ref, f32[4,4,256,128]{3,2,1,0:T(8,128)S(1)} %get-tuple-element.33.z_ref, f32[4,256,128]{2,1,0:T(8,128)S(1)} %collective-permute-done.sib_ref, ...), custom_call_target="tpu_custom_call" | custom-call | flops 400000000 | bytes 3000000 | tf_op jit(solution)/shard_map/reach/pallas_call | solution.py:335
  37.0 0.0 collective-permute-done.6.s3.refs_7_
  37.1 1.6 %collective-permute-done.5.s2.refs_6_ = f32[256,128]{1,0:T(8,128)S(1)} collective-permute-done((f32[256,128]{1,0:T(8,128)S(1)}, f32[256,128]{1,0:T(8,128)S(1)}, u32[]{:S(2)}, u32[]{:S(2)}) %collective-permute-start.5) | collective-permute-done | bytes 131104 | tf_op jit(solution)/shard_map/ppermute | solution.py:485
  38.7 0.8 collective-permute-done.4.s1.refs_5_
  39.4 0.5 column.1.refs_9_.s0
  39.9 6.3 %collective-permute-start.9 = (f32[256,128]{1,0:T(8,128)S(1)}, f32[256,128]{1,0:T(8,128)S(1)}, u32[]{:S(2)}, u32[]{:S(2)}) collective-permute-start(f32[256,128]{1,0:T(8,128)S(1)} %column.1.refs_9_.s0), channel_id=1, source_target_pairs={{0,0},{8,11},{1,1},{9,10},{2,2},{10,9},{3,3},{11,8},{4,4},{12,15},... | collective-permute-start | bytes 393224 | tf_op jit(solution)/shard_map/ppermute | solution.py:491
  46.2 1.9 %collective-permute-start.8 = (f32[256,128]{1,0:T(8,128)S(1)}, f32[256,128]{1,0:T(8,128)S(1)}, u32[]{:S(2)}, u32[]{:S(2)}) collective-permute-start(f32[256,128]{1,0:T(8,128)S(1)} %column.1.refs_9_.s0), channel_id=1, source_target_pairs={{0,0},{8,10},{1,1},{9,11},{2,2},{10,8},{3,3},{11,9},{4,4},{12,14},... | collective-permute-start | bytes 393224 | tf_op jit(solution)/shard_map/ppermute | solution.py:491
  48.1 2.4 %collective-permute-start.7 = (f32[256,128]{1,0:T(8,128)S(1)}, f32[256,128]{1,0:T(8,128)S(1)}, u32[]{:S(2)}, u32[]{:S(2)}) collective-permute-start(f32[256,128]{1,0:T(8,128)S(1)} %column.1.refs_9_.s0), channel_id=1, source_target_pairs={{0,0},{8,9},{1,1},{9,8},{2,2},{10,11},{3,3},{11,10},{4,4},{12,13},... | collective-permute-start | bytes 393224 | tf_op jit(solution)/shard_map/ppermute | solution.py:491
  50.5 0.7 path.1
  51.1 1.2 %reach.6 = (bf16[256,256]{1,0:T(8,128)(2,1)S(1)}, f32[256,128]{1,0:T(8,128)S(1)}) custom-call(bf16[1024,128]{1,0:T(8,128)(2,1)S(1)} %bitcast.6, bf16[4,512,128]{2,1,0:T(8,128)(2,1)S(1)} %get-tuple-element.32.r_ref, f32[4,4,256,128]{3,2,1,0:T(8,128)S(1)} %get-tuple-element.33.z_ref, f32[4,256,128]{2,1,0:T(8,128)S(1)} %collective-permute-done.sib_ref, ...), custom_call_target="tpu_custom_call" | custom-call | flops 400000000 | bytes 3000000 | tf_op jit(solution)/shard_map/reach/pallas_call | solution.py:335
  52.3 0.0 collective-permute-done.9.s3
  52.3 0.5 collective-permute-done.8.s2
  52.9 1.4 %collective-permute-done.7.s1 = f32[256,128]{1,0:T(8,128)S(1)} collective-permute-done((f32[256,128]{1,0:T(8,128)S(1)}, f32[256,128]{1,0:T(8,128)S(1)}, u32[]{:S(2)}, u32[]{:S(2)}) %collective-permute-start.7) | collective-permute-done | bytes 131104 | tf_op jit(solution)/shard_map/ppermute | solution.py:491
  54.2 0.5 lead.1.after_ref
  54.7 5.7 %collective-permute-start.10 = (f32[128,128]{1,0:T(8,128)S(1)}, f32[128,128]{1,0:T(8,128)S(1)}, u32[]{:S(2)}, u32[]{:S(2)}) collective-permute-start(f32[128,128]{1,0:T(8,128)S(1)} %lead.1.after_ref), channel_id=1, source_target_pairs={{0,0},{8,15},{1,1},{9,14},{2,2},{10,13},{3,3},{11,12},{4,4},{12,11... | collective-permute-start | bytes 196616 | tf_op jit(solution)/shard_map/ppermute | solution.py:509
  60.4 0.6 fuse.1.fuse_ref
  61.0 0.0 copy-start.2
  61.0 1.7 %collective-permute-done.10.early_ref = f32[128,128]{1,0:T(8,128)S(1)} collective-permute-done((f32[128,128]{1,0:T(8,128)S(1)}, f32[128,128]{1,0:T(8,128)S(1)}, u32[]{:S(2)}, u32[]{:S(2)}) %collective-permute-start.10) | collective-permute-done | bytes 65568 | tf_op jit(solution)/shard_map/ppermute | solution.py:509
  62.7 0.3 entry.1
  63.0 1.9 %collective-permute-start.13 = (f32[128,128]{1,0:T(8,128)S(1)}, f32[128,128]{1,0:T(8,128)S(1)}, u32[]{:S(2)}, u32[]{:S(2)}) collective-permute-start(f32[128,128]{1,0:T(8,128)S(1)} %get-tuple-element.49), channel_id=1, source_target_pairs={{0,0},{8,24},{16,16},{24,40},{32,32},{40,56},{48,48},{56,8},{64,64... | collective-permute-start | bytes 196616 | tf_op jit(solution)/shard_map/ppermute | solution.py:525
  64.9 5.4 %collective-permute-start.12 = (f32[128,128]{1,0:T(8,128)S(1)}, f32[128,128]{1,0:T(8,128)S(1)}, u32[]{:S(2)}, u32[]{:S(2)}) collective-permute-start(f32[128,128]{1,0:T(8,128)S(1)} %get-tuple-element.48), channel_id=1, source_target_pairs={{0,0},{8,40},{16,16},{24,56},{32,32},{40,8},{48,48},{56,24},{64,64... | collective-permute-start | bytes 196616 | tf_op jit(solution)/shard_map/ppermute | solution.py:525
  70.4 1.9 %collective-permute-start.11 = (f32[128,128]{1,0:T(8,128)S(1)}, f32[128,128]{1,0:T(8,128)S(1)}, u32[]{:S(2)}, u32[]{:S(2)}) collective-permute-start(f32[128,128]{1,0:T(8,128)S(1)} %get-tuple-element.47), channel_id=1, source_target_pairs={{0,0},{8,56},{16,16},{24,8},{32,32},{40,24},{48,48},{56,40},{64,64... | collective-permute-start | bytes 196616 | tf_op jit(solution)/shard_map/ppermute | solution.py:525
  72.3 0.1 collective-permute-start.14
  72.4 1.2 %reach.7 = (bf16[256,256]{1,0:T(8,128)(2,1)S(1)}, f32[256,128]{1,0:T(8,128)S(1)}) custom-call(bf16[1024,128]{1,0:T(8,128)(2,1)S(1)} %bitcast.7, bf16[4,512,128]{2,1,0:T(8,128)(2,1)S(1)} %get-tuple-element.32.r_ref, f32[4,4,256,128]{3,2,1,0:T(8,128)S(1)} %get-tuple-element.33.z_ref, f32[4,256,128]{2,1,0:T(8,128)S(1)} %collective-permute-done.sib_ref, ...), custom_call_target="tpu_custom_call" | custom-call | flops 400000000 | bytes 3000000 | tf_op jit(solution)/shard_map/reach/pallas_call | solution.py:335
  73.6 0.0 collective-permute-done.13.refs_9_
  73.6 0.0 collective-permute-done.12.refs_10_
  73.6 1.8 %collective-permute-done.11.refs_11_ = f32[128,128]{1,0:T(8,128)S(1)} collective-permute-done((f32[128,128]{1,0:T(8,128)S(1)}, f32[128,128]{1,0:T(8,128)S(1)}, u32[]{:S(2)}, u32[]{:S(2)}) %collective-permute-start.11) | collective-permute-done | bytes 65568 | tf_op jit(solution)/shard_map/ppermute | solution.py:525
  75.4 0.5 collective-permute-start.16
  75.9 0.0 collective-permute-start.15
  75.9 0.7 collective-permute-done.17.refs_15_
  76.7 0.2 collective-permute-done.16.refs_14_
  76.8 0.4 collective-permute-done.15.refs_13_
  77.2 1.3 %read.1 = bf16[1024,128]{1,0:T(8,128)(2,1)} custom-call(bf16[256,256]{1,0:T(8,128)(2,1)S(1)} %get-tuple-element.36.after_ref.refs_0_, f32[256,128]{1,0:T(8,128)S(1)} %get-tuple-element.37.refs_1_, bf16[256,256]{1,0:T(8,128)(2,1)S(1)} %get-tuple-element.41.after_ref.refs_2_, f32[256,128]{1,0:T(8,128)S(1)} %get-tuple-element.42.refs_3_, ...), custom_call_target="tpu_custom_call" | custom-call | tf_op jit(solution)/shard_map/read/pallas_call | solution.py:403
  (7 shorter events, 0.0 us)
Async XLA Ops:
  0.0 23.5 %copy-start = (bf16[1,256,4,128]{3,2,1,0:T(4,128)(2,1)S(1)}, bf16[1,256,4,128]{3,2,1,0:T(4,128)(2,1)}, u32[]{:S(2)}) copy-start(bf16[1,256,4,128]{3,2,1,0:T(4,128)(2,1)} %param.5) | copy-start | bytes 786436
  9.5 4.9 %collective-permute-start = (f32[4,256,128]{2,1,0:T(8,128)S(1)}, f32[4,256,128]{2,1,0:T(8,128)S(1)}, u32[]{:S(2)}, u32[]{:S(2)}) collective-permute-start(f32[4,256,128]{2,1,0:T(8,128)S(1)} %get-tuple-element.34.own_ref), channel_id=1, source_target_pairs={{0,8},{8,0},{16,24},{24,16},{32,40},{40,32},{48,56},{56,48},{64,72... | collective-permute-start | bytes 1572872 | tf_op jit(solution)/shard_map/ppermute | solution.py:477
  14.7 10.0 %collective-permute-start.1 = (f32[256,128]{1,0:T(8,128)S(1)}, f32[256,128]{1,0:T(8,128)S(1)}, u32[]{:S(2)}, u32[]{:S(2)}) collective-permute-start(f32[256,128]{1,0:T(8,128)S(1)} %get-tuple-element.38), channel_id=1, source_target_pairs={{0,0},{8,24},{16,16},{24,40},{32,32},{40,56},{48,48},{56,8},{64,64... | collective-permute-start | bytes 393224 | tf_op jit(solution)/shard_map/ppermute | solution.py:479
  16.6 8.1 %collective-permute-start.2 = (f32[256,128]{1,0:T(8,128)S(1)}, f32[256,128]{1,0:T(8,128)S(1)}, u32[]{:S(2)}, u32[]{:S(2)}) collective-permute-start(f32[256,128]{1,0:T(8,128)S(1)} %get-tuple-element.39), channel_id=1, source_target_pairs={{0,0},{8,40},{16,16},{24,56},{32,32},{40,8},{48,48},{56,24},{64,64... | collective-permute-start | bytes 393224 | tf_op jit(solution)/shard_map/ppermute | solution.py:479
  20.5 5.7 %collective-permute-start.3 = (f32[256,128]{1,0:T(8,128)S(1)}, f32[256,128]{1,0:T(8,128)S(1)}, u32[]{:S(2)}, u32[]{:S(2)}) collective-permute-start(f32[256,128]{1,0:T(8,128)S(1)} %get-tuple-element.40), channel_id=1, source_target_pairs={{0,0},{8,56},{16,16},{24,8},{32,32},{40,24},{48,48},{56,40},{64,64... | collective-permute-start | bytes 393224 | tf_op jit(solution)/shard_map/ppermute | solution.py:479
  26.6 23.8 %copy-start.1 = (f32[4,128,128]{2,1,0:T(8,128)S(1)}, f32[4,128,128]{2,1,0:T(8,128)}, u32[]{:S(2)}) copy-start(f32[4,128,128]{2,1,0:T(8,128)} %refs_8_.1) | copy-start | bytes 786436
  26.7 10.4 %collective-permute-start.6 = (f32[256,128]{1,0:T(8,128)S(1)}, f32[256,128]{1,0:T(8,128)S(1)}, u32[]{:S(2)}, u32[]{:S(2)}) collective-permute-start(f32[256,128]{1,0:T(8,128)S(1)} %row.1.after_ref.s0.refs_4_), channel_id=1, source_target_pairs={{0,0},{8,200},{16,16},{24,216},{32,32},{40,232},{48,48},{56,248},{... | collective-permute-start | bytes 393224 | tf_op jit(solution)/shard_map/ppermute | solution.py:485
  31.4 7.2 %collective-permute-start.5 = (f32[256,128]{1,0:T(8,128)S(1)}, f32[256,128]{1,0:T(8,128)S(1)}, u32[]{:S(2)}, u32[]{:S(2)}) collective-permute-start(f32[256,128]{1,0:T(8,128)S(1)} %row.1.after_ref.s0.refs_4_), channel_id=1, source_target_pairs={{0,0},{8,136},{16,16},{24,152},{32,32},{40,168},{48,48},{56,184},{... | collective-permute-start | bytes 393224 | tf_op jit(solution)/shard_map/ppermute | solution.py:485
  33.7 5.7 %collective-permute-start.4 = (f32[256,128]{1,0:T(8,128)S(1)}, f32[256,128]{1,0:T(8,128)S(1)}, u32[]{:S(2)}, u32[]{:S(2)}) collective-permute-start(f32[256,128]{1,0:T(8,128)S(1)} %row.1.after_ref.s0.refs_4_), channel_id=1, source_target_pairs={{0,0},{8,72},{16,16},{24,88},{32,32},{40,104},{48,48},{56,120},{64... | collective-permute-start | bytes 393224 | tf_op jit(solution)/shard_map/ppermute | solution.py:485
  39.9 12.4 %collective-permute-start.9 = (f32[256,128]{1,0:T(8,128)S(1)}, f32[256,128]{1,0:T(8,128)S(1)}, u32[]{:S(2)}, u32[]{:S(2)}) collective-permute-start(f32[256,128]{1,0:T(8,128)S(1)} %column.1.refs_9_.s0), channel_id=1, source_target_pairs={{0,0},{8,11},{1,1},{9,10},{2,2},{10,9},{3,3},{11,8},{4,4},{12,15},... | collective-permute-start | bytes 393224 | tf_op jit(solution)/shard_map/ppermute | solution.py:491
  46.2 6.7 %collective-permute-start.8 = (f32[256,128]{1,0:T(8,128)S(1)}, f32[256,128]{1,0:T(8,128)S(1)}, u32[]{:S(2)}, u32[]{:S(2)}) collective-permute-start(f32[256,128]{1,0:T(8,128)S(1)} %column.1.refs_9_.s0), channel_id=1, source_target_pairs={{0,0},{8,10},{1,1},{9,11},{2,2},{10,8},{3,3},{11,9},{4,4},{12,14},... | collective-permute-start | bytes 393224 | tf_op jit(solution)/shard_map/ppermute | solution.py:491
  48.1 6.1 %collective-permute-start.7 = (f32[256,128]{1,0:T(8,128)S(1)}, f32[256,128]{1,0:T(8,128)S(1)}, u32[]{:S(2)}, u32[]{:S(2)}) collective-permute-start(f32[256,128]{1,0:T(8,128)S(1)} %column.1.refs_9_.s0), channel_id=1, source_target_pairs={{0,0},{8,9},{1,1},{9,8},{2,2},{10,11},{3,3},{11,10},{4,4},{12,13},... | collective-permute-start | bytes 393224 | tf_op jit(solution)/shard_map/ppermute | solution.py:491
  54.7 8.0 %collective-permute-start.10 = (f32[128,128]{1,0:T(8,128)S(1)}, f32[128,128]{1,0:T(8,128)S(1)}, u32[]{:S(2)}, u32[]{:S(2)}) collective-permute-start(f32[128,128]{1,0:T(8,128)S(1)} %lead.1.after_ref), channel_id=1, source_target_pairs={{0,0},{8,15},{1,1},{9,14},{2,2},{10,13},{3,3},{11,12},{4,4},{12,11... | collective-permute-start | bytes 196616 | tf_op jit(solution)/shard_map/ppermute | solution.py:509
  61.0 16.2 %copy-start.2 = (f32[4,128]{1,0:T(4,128)S(1)}, f32[4,128]{1,0:T(4,128)}, u32[]{:S(2)}) copy-start(f32[4,128]{1,0:T(4,128)} %refs_16_.1) | copy-start | bytes 6148
  63.0 10.6 %collective-permute-start.13 = (f32[128,128]{1,0:T(8,128)S(1)}, f32[128,128]{1,0:T(8,128)S(1)}, u32[]{:S(2)}, u32[]{:S(2)}) collective-permute-start(f32[128,128]{1,0:T(8,128)S(1)} %get-tuple-element.49), channel_id=1, source_target_pairs={{0,0},{8,24},{16,16},{24,40},{32,32},{40,56},{48,48},{56,8},{64,64... | collective-permute-start | bytes 196616 | tf_op jit(solution)/shard_map/ppermute | solution.py:525
  64.9 8.7 %collective-permute-start.12 = (f32[128,128]{1,0:T(8,128)S(1)}, f32[128,128]{1,0:T(8,128)S(1)}, u32[]{:S(2)}, u32[]{:S(2)}) collective-permute-start(f32[128,128]{1,0:T(8,128)S(1)} %get-tuple-element.48), channel_id=1, source_target_pairs={{0,0},{8,40},{16,16},{24,56},{32,32},{40,8},{48,48},{56,24},{64,64... | collective-permute-start | bytes 196616 | tf_op jit(solution)/shard_map/ppermute | solution.py:525
  70.4 5.0 %collective-permute-start.11 = (f32[128,128]{1,0:T(8,128)S(1)}, f32[128,128]{1,0:T(8,128)S(1)}, u32[]{:S(2)}, u32[]{:S(2)}) collective-permute-start(f32[128,128]{1,0:T(8,128)S(1)} %get-tuple-element.47), channel_id=1, source_target_pairs={{0,0},{8,56},{16,16},{24,8},{32,32},{40,24},{48,48},{56,40},{64,64... | collective-permute-start | bytes 196616 | tf_op jit(solution)/shard_map/ppermute | solution.py:525
  72.3 3.6 %collective-permute-start.14 = (f32[128,128]{1,0:T(8,128)S(1)}, f32[128,128]{1,0:T(8,128)S(1)}, u32[]{:S(2)}, u32[]{:S(2)}) collective-permute-start(f32[128,128]{1,0:T(8,128)S(1)} %get-tuple-element.50.after_ref.refs_8_), channel_id=1, source_target_pairs={{0,8},{8,0},{16,24},{24,16},{32,40},{40,32},{48,56},{56,48},{64,72... | collective-permute-start | bytes 196616 | tf_op jit(solution)/shard_map/ppermute | solution.py:531
  75.4 1.3 %collective-permute-start.17 = (f32[128,128]{1,0:T(8,128)S(1)}, f32[128,128]{1,0:T(8,128)S(1)}, u32[]{:S(2)}, u32[]{:S(2)}) collective-permute-start(f32[128,128]{1,0:T(8,128)S(1)} %collective-permute-done.11.refs_11_), channel_id=1, source_target_pairs={{0,8},{8,0},{16,24},{24,16},{32,40},{40,32},{48,56},{56,48},{64,72... | collective-permute-start | bytes 196616 | tf_op jit(solution)/shard_map/ppermute | solution.py:531
  75.4 1.4 %collective-permute-start.16 = (f32[128,128]{1,0:T(8,128)S(1)}, f32[128,128]{1,0:T(8,128)S(1)}, u32[]{:S(2)}, u32[]{:S(2)}) collective-permute-start(f32[128,128]{1,0:T(8,128)S(1)} %collective-permute-done.12.refs_10_), channel_id=1, source_target_pairs={{0,8},{8,0},{16,24},{24,16},{32,40},{40,32},{48,56},{56,48},{64,72... | collective-permute-start | bytes 196616 | tf_op jit(solution)/shard_map/ppermute | solution.py:531
  75.9 1.3 %collective-permute-start.15 = (f32[128,128]{1,0:T(8,128)S(1)}, f32[128,128]{1,0:T(8,128)S(1)}, u32[]{:S(2)}, u32[]{:S(2)}) collective-permute-start(f32[128,128]{1,0:T(8,128)S(1)} %collective-permute-done.13.refs_9_), channel_id=1, source_target_pairs={{0,8},{8,0},{16,24},{24,16},{32,40},{40,32},{48,56},{56,48},{64,72... | collective-permute-start | bytes 196616 | tf_op jit(solution)/shard_map/ppermute | solution.py:531

commit v8 on v7

--- a/solution.py
+++ b/solution.py
@@ -434,11 +434,11 @@
     return (y * XS + x) * CS + c
 
 
-def plane_perm(move):
+def plane_perm(move, spare):
     pairs = []
     for y in range(YS):
         for x in range(XS):
-            pairs.append((seat(y, x, 0), seat(y, x, 0)))
+            pairs.append((seat(y, x, 0), seat(*spare(y, x), 0)))
             pairs.append((seat(y, x, 1), seat(*move(y, x), 1)))
     return pairs
 
@@ -448,9 +448,9 @@
     for y in range(YS):
         for x in range(XS):
             for g in range(segs):
-                for c in range(CS):
-                    at = seat(y, x, c) * segs
-                    pairs.append((at + g, at + (move(g) if c else g)))
+                pairs.append((seat(y, x, 0) * segs + g, seat(y, x ^ 1, 0) * segs + g))
+                at = seat(y, x, 1) * segs
+                pairs.append((at + g, at + move(g)))
     return pairs
 
 
@@ -462,8 +462,12 @@
     tokens = query_rows.shape[1]
     steps = tokens * REFL
     swap = chip_perm()
-    along_x = [plane_perm(lambda y, x, k=k: (y, (x + k) % XS)) for k in range(1, XS)]
-    along_y = [plane_perm(lambda y, x, k=k: (y ^ k, x)) for k in range(1, YS)]
+    near_x = lambda y, x: (y, x ^ 1)
+    near_y = lambda y, x: (y ^ 1, x)
+    along_x = [
+        plane_perm(lambda y, x, k=k: (y, (x + k) % XS), near_y) for k in range(1, XS)
+    ]
+    along_y = [plane_perm(lambda y, x, k=k: (y ^ k, x), near_x) for k in range(1, YS)]
     segs = lax.axis_size("seg")
     along_z = [depth_perm(segs, lambda g, k=k: g ^ k) for k in range(1, ZG)]
     jump = depth_perm(segs, lambda g: segs - 1 - g)

time: 79.1 us -> 57.2 us (0.72)
  starting transfers between devices: 47.4 us -> 23.8 us
  waiting for transfers between devices: 12 us -> 14.2 us
    ppermute x6, starting transfers between devices: 18.1 us -> 7.63 us  [per_device(): lax.ppermute(s, 'seq', p)]
    ppermute x3, starting transfers between devices: 10.6 us -> 4.29 us  [per_device(): slots = [total] + [lax.ppermute(total, ('seq', 'seg'), p) for p in along_z]]
    ppermute x3, starting transfers between devices: 9.18 us -> 3.52 us  [per_device(): slots = [total] + [lax.ppermute(total, 'seq', p) for p in along_y]]
    ppermute x3, waiting for transfers between devices: 1.88 us -> 2.99 us  [per_device(): slots = [total] + [lax.ppermute(total, ('seq', 'seg'), p) for p in along_z]]
    ppermute x1, starting transfers between devices: 5.67 us -> 4.57 us  [per_device(): early = lax.ppermute(lead, ('seq', 'seg'), jump)]
  transfers between devices with their start and end apart: 18 -> 18, of which waited for: 11 -> 13; matrix products, arithmetic and copies ran while one was open for 0% -> 0% of each run, Pallas kernels for 8% -> 10%
where the time goes in v8:
time: 57.2 us; the launch traced here: 57.1 us
  starting transfers between devices  23.8 us (42%)
  Pallas kernels  18.8 us (33%)
  waiting for transfers between devices  14.2 us (25%)
    pallas_call x1, Pallas kernels, factor_call(): pl.pallas_call(factor_kernel, in_specs=[pl.BlockSpec(memory_space=pl.ANY)...  9.53 us
    ppermute x6, starting transfers between devices, per_device(): lax.ppermute(s, 'seq', p)  7.63 us
    pallas_call x4, Pallas kernels, reach_call(): pl.pallas_call(functools.partial(reach_kernel, head=head), grid=(1,), in_...  4.72 us
    ppermute x1, starting transfers between devices, per_device(): early = lax.ppermute(lead, ('seq', 'seg'), jump)  4.57 us
    ppermute x3, starting transfers between devices, per_device(): slots = [total] + [lax.ppermute(total, ('seq', 'seg'), p) for p in along_z]  4.29 us
    ppermute x6, waiting for transfers between devices, per_device(): lax.ppermute(s, 'seq', p)  3.81 us
    ppermute x3, starting transfers between devices, per_device(): slots = [total] + [lax.ppermute(total, 'seq', p) for p in along_y]  3.52 us
    ppermute x1, starting transfers between devices, per_device(): sib = lax.ppermute(pair, 'seq', swap)  3.32 us
  transfers between devices with their start and end apart: 18, of which 13 were waited for; matrix products, arithmetic and copies ran while one was open for 0% of the time, Pallas kernels for 10%

profile of v8, /device:TPU:1, one launch (start us, length us, event | category | flops | bytes accessed | tf_op | source)
XLA Modules:
  0.0 57.1 jit_solution(5374372525783466638)
XLA Ops:
  0.0 9.5 %factor.1 = (f32[4,256,128]{2,1,0:T(8,128)S(1)}, f32[4,4,256,128]{3,2,1,0:T(8,128)S(1)}, bf16[4,512,128]{2,1,0:T(8,128)(2,1)S(1)}) custom-call(bf16[2048,128]{1,0:T(8,128)(2,1)} %bitcast.8, bf16[2048,128]{1,0:T(8,128)(2,1)} %bitcast.9), custom_call_target="tpu_custom_call" | custom-call | tf_op jit(solution)/shard_map/factor/pallas_call | solution.py:181
  9.5 3.3 %collective-permute-start = (f32[4,256,128]{2,1,0:T(8,128)S(1)}, f32[4,256,128]{2,1,0:T(8,128)S(1)}, u32[]{:S(2)}, u32[]{:S(2)}) collective-permute-start(f32[4,256,128]{2,1,0:T(8,128)S(1)} %get-tuple-element.34.own_ref), channel_id=1, source_target_pairs={{0,8},{8,0},{16,24},{24,16},{32,40},{40,32},{48,56},{56,48},{64,72... | collective-permute-start | bytes 1572872 | tf_op jit(solution)/shard_map/ppermute | solution.py:481
  12.9 1.5 %collective-permute-done.sib_ref = f32[4,256,128]{2,1,0:T(8,128)S(1)} collective-permute-done((f32[4,256,128]{2,1,0:T(8,128)S(1)}, f32[4,256,128]{2,1,0:T(8,128)S(1)}, u32[]{:S(2)}, u32[]{:S(2)}) %collective-permute-start) | collective-permute-done | bytes 524320 | tf_op jit(solution)/shard_map/ppermute | solution.py:481
  14.4 0.3 chip.1
  14.7 0.1 collective-permute-start.1
  14.8 1.9 %collective-permute-start.2 = (f32[256,128]{1,0:T(8,128)S(1)}, f32[256,128]{1,0:T(8,128)S(1)}, u32[]{:S(2)}, u32[]{:S(2)}) collective-permute-start(f32[256,128]{1,0:T(8,128)S(1)} %get-tuple-element.39), channel_id=1, source_target_pairs={{0,64},{8,40},{16,80},{24,56},{32,96},{40,8},{48,112},{56,24},{64,... | collective-permute-start | bytes 393224 | tf_op jit(solution)/shard_map/ppermute | solution.py:483
  16.7 1.2 %collective-permute-start.3 = (f32[256,128]{1,0:T(8,128)S(1)}, f32[256,128]{1,0:T(8,128)S(1)}, u32[]{:S(2)}, u32[]{:S(2)}) collective-permute-start(f32[256,128]{1,0:T(8,128)S(1)} %get-tuple-element.40), channel_id=1, source_target_pairs={{0,64},{8,56},{16,80},{24,8},{32,96},{40,24},{48,112},{56,40},{64,... | collective-permute-start | bytes 393224 | tf_op jit(solution)/shard_map/ppermute | solution.py:483
  17.9 1.2 %reach.4 = (bf16[256,256]{1,0:T(8,128)(2,1)S(1)}, f32[256,128]{1,0:T(8,128)S(1)}) custom-call(bf16[1024,128]{1,0:T(8,128)(2,1)S(1)} %bitcast.4, bf16[4,512,128]{2,1,0:T(8,128)(2,1)S(1)} %get-tuple-element.32.r_ref, f32[4,4,256,128]{3,2,1,0:T(8,128)S(1)} %get-tuple-element.33.z_ref, f32[4,256,128]{2,1,0:T(8,128)S(1)} %collective-permute-done.sib_ref, ...), custom_call_target="tpu_custom_call" | custom-call | flops 400000000 | bytes 3000000 | tf_op jit(solution)/shard_map/reach/pallas_call | solution.py:335
  19.1 2.2 %collective-permute-done.1.s1.refs_1_ = f32[256,128]{1,0:T(8,128)S(1)} collective-permute-done((f32[256,128]{1,0:T(8,128)S(1)}, f32[256,128]{1,0:T(8,128)S(1)}, u32[]{:S(2)}, u32[]{:S(2)}) %collective-permute-start.1) | collective-permute-done | bytes 131104 | tf_op jit(solution)/shard_map/ppermute | solution.py:483
  21.2 0.9 %collective-permute-done.3.s3.refs_3_ = f32[256,128]{1,0:T(8,128)S(1)} collective-permute-done((f32[256,128]{1,0:T(8,128)S(1)}, f32[256,128]{1,0:T(8,128)S(1)}, u32[]{:S(2)}, u32[]{:S(2)}) %collective-permute-start.3) | collective-permute-done | bytes 131104 | tf_op jit(solution)/shard_map/ppermute | solution.py:483
  22.1 0.5 row.1.after_ref.s0.refs_4_
  22.6 0.0 copy-start.1
  22.6 1.7 %collective-permute-start.6 = (f32[256,128]{1,0:T(8,128)S(1)}, f32[256,128]{1,0:T(8,128)S(1)}, u32[]{:S(2)}, u32[]{:S(2)}) collective-permute-start(f32[256,128]{1,0:T(8,128)S(1)} %row.1.after_ref.s0.refs_4_), channel_id=1, source_target_pairs={{0,16},{8,200},{16,0},{24,216},{32,48},{40,232},{48,32},{56,248},{... | collective-permute-start | bytes 393224 | tf_op jit(solution)/shard_map/ppermute | solution.py:489
  24.3 0.4 collective-permute-start.5
  24.7 1.4 %collective-permute-start.4 = (f32[256,128]{1,0:T(8,128)S(1)}, f32[256,128]{1,0:T(8,128)S(1)}, u32[]{:S(2)}, u32[]{:S(2)}) collective-permute-start(f32[256,128]{1,0:T(8,128)S(1)} %row.1.after_ref.s0.refs_4_), channel_id=1, source_target_pairs={{0,16},{8,72},{16,0},{24,88},{32,48},{40,104},{48,32},{56,120},{64... | collective-permute-start | bytes 393224 | tf_op jit(solution)/shard_map/ppermute | solution.py:489
  26.1 1.2 %reach.5 = (bf16[256,256]{1,0:T(8,128)(2,1)S(1)}, f32[256,128]{1,0:T(8,128)S(1)}) custom-call(bf16[1024,128]{1,0:T(8,128)(2,1)S(1)} %bitcast.5, bf16[4,512,128]{2,1,0:T(8,128)(2,1)S(1)} %get-tuple-element.32.r_ref, f32[4,4,256,128]{3,2,1,0:T(8,128)S(1)} %get-tuple-element.33.z_ref, f32[4,256,128]{2,1,0:T(8,128)S(1)} %collective-permute-done.sib_ref, ...), custom_call_target="tpu_custom_call" | custom-call | flops 400000000 | bytes 3000000 | tf_op jit(solution)/shard_map/reach/pallas_call | solution.py:335
  27.3 0.6 %collective-permute-done.6.s3.refs_7_ = f32[256,128]{1,0:T(8,128)S(1)} collective-permute-done((f32[256,128]{1,0:T(8,128)S(1)}, f32[256,128]{1,0:T(8,128)S(1)}, u32[]{:S(2)}, u32[]{:S(2)}) %collective-permute-start.6) | collective-permute-done | bytes 131104 | tf_op jit(solution)/shard_map/ppermute | solution.py:489
  27.9 1.7 %collective-permute-done.5.s2.refs_6_ = f32[256,128]{1,0:T(8,128)S(1)} collective-permute-done((f32[256,128]{1,0:T(8,128)S(1)}, f32[256,128]{1,0:T(8,128)S(1)}, u32[]{:S(2)}, u32[]{:S(2)}) %collective-permute-start.5) | collective-permute-done | bytes 131104 | tf_op jit(solution)/shard_map/ppermute | solution.py:489
  29.6 0.5 collective-permute-done.4.s1.refs_5_
  30.1 0.5 column.1.refs_9_.s0
  30.6 3.9 %collective-permute-start.9 = (f32[256,128]{1,0:T(8,128)S(1)}, f32[256,128]{1,0:T(8,128)S(1)}, u32[]{:S(2)}, u32[]{:S(2)}) collective-permute-start(f32[256,128]{1,0:T(8,128)S(1)} %column.1.refs_9_.s0), channel_id=1, source_target_pairs={{0,16},{8,11},{1,17},{9,10},{2,18},{10,9},{3,19},{11,8},{4,20},{12... | collective-permute-start | bytes 393224 | tf_op jit(solution)/shard_map/ppermute | solution.py:495
  34.5 0.0 collective-permute-start.8
  34.5 0.4 collective-permute-start.7
  34.9 0.7 %path.1 = (f32[4,256,128]{2,1,0:T(8,128)S(1)}, f32[128,128]{1,0:T(8,128)S(1)}) custom-call(f32[256,128]{1,0:T(8,128)S(1)} %get-tuple-element.35.after_ref.s0.refs_0_, f32[256,128]{1,0:T(8,128)S(1)} %collective-permute-done.1.s1.refs_1_, f32[256,128]{1,0:T(8,128)S(1)} %collective-permute-done.2.s2.refs_2_, f32[256,128]{1,0:T(8,128)S(1)} %collective-permute-done.3.s3.refs_3_, ...), custom_call_target="tpu_custom_call" | custom-call | tf_op jit(solution)/shard_map/path/pallas_call | solution.py:421
  35.6 1.2 %reach.6 = (bf16[256,256]{1,0:T(8,128)(2,1)S(1)}, f32[256,128]{1,0:T(8,128)S(1)}) custom-call(bf16[1024,128]{1,0:T(8,128)(2,1)S(1)} %bitcast.6, bf16[4,512,128]{2,1,0:T(8,128)(2,1)S(1)} %get-tuple-element.32.r_ref, f32[4,4,256,128]{3,2,1,0:T(8,128)S(1)} %get-tuple-element.33.z_ref, f32[4,256,128]{2,1,0:T(8,128)S(1)} %collective-permute-done.sib_ref, ...), custom_call_target="tpu_custom_call" | custom-call | flops 400000000 | bytes 3000000 | tf_op jit(solution)/shard_map/reach/pallas_call | solution.py:335
  36.8 0.2 collective-permute-done.9.s3
  36.9 2.8 %collective-permute-done.8.s2 = f32[256,128]{1,0:T(8,128)S(1)} collective-permute-done((f32[256,128]{1,0:T(8,128)S(1)}, f32[256,128]{1,0:T(8,128)S(1)}, u32[]{:S(2)}, u32[]{:S(2)}) %collective-permute-start.8) | collective-permute-done | bytes 131104 | tf_op jit(solution)/shard_map/ppermute | solution.py:495
  39.7 0.0 collective-permute-done.7.s1
  39.7 0.5 lead.1.after_ref
  40.2 4.6 %collective-permute-start.10 = (f32[128,128]{1,0:T(8,128)S(1)}, f32[128,128]{1,0:T(8,128)S(1)}, u32[]{:S(2)}, u32[]{:S(2)}) collective-permute-start(f32[128,128]{1,0:T(8,128)S(1)} %lead.1.after_ref), channel_id=1, source_target_pairs={{0,16},{8,15},{1,17},{9,14},{2,18},{10,13},{3,19},{11,12},{4,20},{... | collective-permute-start | bytes 196616 | tf_op jit(solution)/shard_map/ppermute | solution.py:513
  44.8 0.6 %fuse.1.fuse_ref = f32[4,256,128]{2,1,0:T(8,128)S(1)} custom-call(f32[256,128]{1,0:T(8,128)S(1)} %column.1.refs_9_.s0, f32[256,128]{1,0:T(8,128)S(1)} %collective-permute-done.7.s1, f32[256,128]{1,0:T(8,128)S(1)} %collective-permute-done.8.s2, f32[256,128]{1,0:T(8,128)S(1)} %collective-permute-done.9.s3, ...), custom_call_target="tpu_custom_call" | custom-call | tf_op jit(solution)/shard_map/fuse/pallas_call | solution.py:421
  45.4 0.0 copy-start.2
  45.4 1.7 %collective-permute-done.10.early_ref = f32[128,128]{1,0:T(8,128)S(1)} collective-permute-done((f32[128,128]{1,0:T(8,128)S(1)}, f32[128,128]{1,0:T(8,128)S(1)}, u32[]{:S(2)}, u32[]{:S(2)}) %collective-permute-start.10) | collective-permute-done | bytes 65568 | tf_op jit(solution)/shard_map/ppermute | solution.py:513
  47.2 0.3 entry.1
  47.5 1.1 %collective-permute-start.13 = (f32[128,128]{1,0:T(8,128)S(1)}, f32[128,128]{1,0:T(8,128)S(1)}, u32[]{:S(2)}, u32[]{:S(2)}) collective-permute-start(f32[128,128]{1,0:T(8,128)S(1)} %get-tuple-element.49), channel_id=1, source_target_pairs={{0,64},{8,24},{16,80},{24,40},{32,96},{40,56},{48,112},{56,8},{64,... | collective-permute-start | bytes 196616 | tf_op jit(solution)/shard_map/ppermute | solution.py:529
  48.5 2.3 %collective-permute-start.12 = (f32[128,128]{1,0:T(8,128)S(1)}, f32[128,128]{1,0:T(8,128)S(1)}, u32[]{:S(2)}, u32[]{:S(2)}) collective-permute-start(f32[128,128]{1,0:T(8,128)S(1)} %get-tuple-element.48), channel_id=1, source_target_pairs={{0,64},{8,40},{16,80},{24,56},{32,96},{40,8},{48,112},{56,24},{64,... | collective-permute-start | bytes 196616 | tf_op jit(solution)/shard_map/ppermute | solution.py:529
  50.8 1.1 %collective-permute-start.11 = (f32[128,128]{1,0:T(8,128)S(1)}, f32[128,128]{1,0:T(8,128)S(1)}, u32[]{:S(2)}, u32[]{:S(2)}) collective-permute-start(f32[128,128]{1,0:T(8,128)S(1)} %get-tuple-element.47), channel_id=1, source_target_pairs={{0,64},{8,56},{16,80},{24,8},{32,96},{40,24},{48,112},{56,40},{64,... | collective-permute-start | bytes 196616 | tf_op jit(solution)/shard_map/ppermute | solution.py:529
  51.9 0.0 collective-permute-start.14
  51.9 1.2 %reach.7 = (bf16[256,256]{1,0:T(8,128)(2,1)S(1)}, f32[256,128]{1,0:T(8,128)S(1)}) custom-call(bf16[1024,128]{1,0:T(8,128)(2,1)S(1)} %bitcast.7, bf16[4,512,128]{2,1,0:T(8,128)(2,1)S(1)} %get-tuple-element.32.r_ref, f32[4,4,256,128]{3,2,1,0:T(8,128)S(1)} %get-tuple-element.33.z_ref, f32[4,256,128]{2,1,0:T(8,128)S(1)} %collective-permute-done.sib_ref, ...), custom_call_target="tpu_custom_call" | custom-call | flops 400000000 | bytes 3000000 | tf_op jit(solution)/shard_map/reach/pallas_call | solution.py:335
  53.1 0.0 collective-permute-done.12.refs_10_
  53.2 0.7 %collective-permute-done.11.refs_11_ = f32[128,128]{1,0:T(8,128)S(1)} collective-permute-done((f32[128,128]{1,0:T(8,128)S(1)}, f32[128,128]{1,0:T(8,128)S(1)}, u32[]{:S(2)}, u32[]{:S(2)}) %collective-permute-start.11) | collective-permute-done | bytes 65568 | tf_op jit(solution)/shard_map/ppermute | solution.py:529
  53.9 0.0 collective-permute-start.17
  53.9 0.5 collective-permute-start.16
  54.4 0.0 collective-permute-start.15
  54.4 0.7 %collective-permute-done.17.refs_15_ = f32[128,128]{1,0:T(8,128)S(1)} collective-permute-done((f32[128,128]{1,0:T(8,128)S(1)}, f32[128,128]{1,0:T(8,128)S(1)}, u32[]{:S(2)}, u32[]{:S(2)}) %collective-permute-start.17) | collective-permute-done | bytes 65568 | tf_op jit(solution)/shard_map/ppermute | solution.py:535
  55.2 0.2 collective-permute-done.16.refs_14_
  55.3 0.4 collective-permute-done.15.refs_13_
  55.7 1.3 %read.1 = bf16[1024,128]{1,0:T(8,128)(2,1)} custom-call(bf16[256,256]{1,0:T(8,128)(2,1)S(1)} %get-tuple-element.36.after_ref.refs_0_, f32[256,128]{1,0:T(8,128)S(1)} %get-tuple-element.37.refs_1_, bf16[256,256]{1,0:T(8,128)(2,1)S(1)} %get-tuple-element.41.after_ref.refs_2_, f32[256,128]{1,0:T(8,128)S(1)} %get-tuple-element.42.refs_3_, ...), custom_call_target="tpu_custom_call" | custom-call | tf_op jit(solution)/shard_map/read/pallas_call | solution.py:403
  (7 shorter events, 0.0 us)
Async XLA Ops:
  0.0 17.9 %copy-start = (bf16[1,256,4,128]{3,2,1,0:T(4,128)(2,1)S(1)}, bf16[1,256,4,128]{3,2,1,0:T(4,128)(2,1)}, u32[]{:S(2)}) copy-start(bf16[1,256,4,128]{3,2,1,0:T(4,128)(2,1)} %param.5) | copy-start | bytes 786436
  9.5 4.9 %collective-permute-start = (f32[4,256,128]{2,1,0:T(8,128)S(1)}, f32[4,256,128]{2,1,0:T(8,128)S(1)}, u32[]{:S(2)}, u32[]{:S(2)}) collective-permute-start(f32[4,256,128]{2,1,0:T(8,128)S(1)} %get-tuple-element.34.own_ref), channel_id=1, source_target_pairs={{0,8},{8,0},{16,24},{24,16},{32,40},{40,32},{48,56},{56,48},{64,72... | collective-permute-start | bytes 1572872 | tf_op jit(solution)/shard_map/ppermute | solution.py:481
  14.7 6.5 %collective-permute-start.1 = (f32[256,128]{1,0:T(8,128)S(1)}, f32[256,128]{1,0:T(8,128)S(1)}, u32[]{:S(2)}, u32[]{:S(2)}) collective-permute-start(f32[256,128]{1,0:T(8,128)S(1)} %get-tuple-element.38), channel_id=1, source_target_pairs={{0,64},{8,24},{16,80},{24,40},{32,96},{40,56},{48,112},{56,8},{64,... | collective-permute-start | bytes 393224 | tf_op jit(solution)/shard_map/ppermute | solution.py:483
  14.8 6.4 %collective-permute-start.2 = (f32[256,128]{1,0:T(8,128)S(1)}, f32[256,128]{1,0:T(8,128)S(1)}, u32[]{:S(2)}, u32[]{:S(2)}) collective-permute-start(f32[256,128]{1,0:T(8,128)S(1)} %get-tuple-element.39), channel_id=1, source_target_pairs={{0,64},{8,40},{16,80},{24,56},{32,96},{40,8},{48,112},{56,24},{64,... | collective-permute-start | bytes 393224 | tf_op jit(solution)/shard_map/ppermute | solution.py:483
  16.7 5.4 %collective-permute-start.3 = (f32[256,128]{1,0:T(8,128)S(1)}, f32[256,128]{1,0:T(8,128)S(1)}, u32[]{:S(2)}, u32[]{:S(2)}) collective-permute-start(f32[256,128]{1,0:T(8,128)S(1)} %get-tuple-element.40), channel_id=1, source_target_pairs={{0,64},{8,56},{16,80},{24,8},{32,96},{40,24},{48,112},{56,40},{64,... | collective-permute-start | bytes 393224 | tf_op jit(solution)/shard_map/ppermute | solution.py:483
  22.6 12.3 %copy-start.1 = (f32[4,128,128]{2,1,0:T(8,128)S(1)}, f32[4,128,128]{2,1,0:T(8,128)}, u32[]{:S(2)}) copy-start(f32[4,128,128]{2,1,0:T(8,128)} %refs_8_.1) | copy-start | bytes 786436
  22.6 5.3 %collective-permute-start.6 = (f32[256,128]{1,0:T(8,128)S(1)}, f32[256,128]{1,0:T(8,128)S(1)}, u32[]{:S(2)}, u32[]{:S(2)}) collective-permute-start(f32[256,128]{1,0:T(8,128)S(1)} %row.1.after_ref.s0.refs_4_), channel_id=1, source_target_pairs={{0,16},{8,200},{16,0},{24,216},{32,48},{40,232},{48,32},{56,248},{... | collective-permute-start | bytes 393224 | tf_op jit(solution)/shard_map/ppermute | solution.py:489
  24.3 5.3 %collective-permute-start.5 = (f32[256,128]{1,0:T(8,128)S(1)}, f32[256,128]{1,0:T(8,128)S(1)}, u32[]{:S(2)}, u32[]{:S(2)}) collective-permute-start(f32[256,128]{1,0:T(8,128)S(1)} %row.1.after_ref.s0.refs_4_), channel_id=1, source_target_pairs={{0,16},{8,136},{16,0},{24,152},{32,48},{40,168},{48,32},{56,184},{... | collective-permute-start | bytes 393224 | tf_op jit(solution)/shard_map/ppermute | solution.py:489
  24.7 5.5 %collective-permute-start.4 = (f32[256,128]{1,0:T(8,128)S(1)}, f32[256,128]{1,0:T(8,128)S(1)}, u32[]{:S(2)}, u32[]{:S(2)}) collective-permute-start(f32[256,128]{1,0:T(8,128)S(1)} %row.1.after_ref.s0.refs_4_), channel_id=1, source_target_pairs={{0,16},{8,72},{16,0},{24,88},{32,48},{40,104},{48,32},{56,120},{64... | collective-permute-start | bytes 393224 | tf_op jit(solution)/shard_map/ppermute | solution.py:489
  30.6 6.3 %collective-permute-start.9 = (f32[256,128]{1,0:T(8,128)S(1)}, f32[256,128]{1,0:T(8,128)S(1)}, u32[]{:S(2)}, u32[]{:S(2)}) collective-permute-start(f32[256,128]{1,0:T(8,128)S(1)} %column.1.refs_9_.s0), channel_id=1, source_target_pairs={{0,16},{8,11},{1,17},{9,10},{2,18},{10,9},{3,19},{11,8},{4,20},{12... | collective-permute-start | bytes 393224 | tf_op jit(solution)/shard_map/ppermute | solution.py:495
  34.5 5.2 %collective-permute-start.8 = (f32[256,128]{1,0:T(8,128)S(1)}, f32[256,128]{1,0:T(8,128)S(1)}, u32[]{:S(2)}, u32[]{:S(2)}) collective-permute-start(f32[256,128]{1,0:T(8,128)S(1)} %column.1.refs_9_.s0), channel_id=1, source_target_pairs={{0,16},{8,10},{1,17},{9,11},{2,18},{10,8},{3,19},{11,9},{4,20},{12... | collective-permute-start | bytes 393224 | tf_op jit(solution)/shard_map/ppermute | solution.py:495
  34.5 5.2 %collective-permute-start.7 = (f32[256,128]{1,0:T(8,128)S(1)}, f32[256,128]{1,0:T(8,128)S(1)}, u32[]{:S(2)}, u32[]{:S(2)}) collective-permute-start(f32[256,128]{1,0:T(8,128)S(1)} %column.1.refs_9_.s0), channel_id=1, source_target_pairs={{0,16},{8,9},{1,17},{9,8},{2,18},{10,11},{3,19},{11,10},{4,20},{12... | collective-permute-start | bytes 393224 | tf_op jit(solution)/shard_map/ppermute | solution.py:495
  40.2 6.9 %collective-permute-start.10 = (f32[128,128]{1,0:T(8,128)S(1)}, f32[128,128]{1,0:T(8,128)S(1)}, u32[]{:S(2)}, u32[]{:S(2)}) collective-permute-start(f32[128,128]{1,0:T(8,128)S(1)} %lead.1.after_ref), channel_id=1, source_target_pairs={{0,16},{8,15},{1,17},{9,14},{2,18},{10,13},{3,19},{11,12},{4,20},{... | collective-permute-start | bytes 196616 | tf_op jit(solution)/shard_map/ppermute | solution.py:513
  45.4 10.3 %copy-start.2 = (f32[4,128]{1,0:T(4,128)S(1)}, f32[4,128]{1,0:T(4,128)}, u32[]{:S(2)}) copy-start(f32[4,128]{1,0:T(4,128)} %refs_16_.1) | copy-start | bytes 6148
  47.5 5.7 %collective-permute-start.13 = (f32[128,128]{1,0:T(8,128)S(1)}, f32[128,128]{1,0:T(8,128)S(1)}, u32[]{:S(2)}, u32[]{:S(2)}) collective-permute-start(f32[128,128]{1,0:T(8,128)S(1)} %get-tuple-element.49), channel_id=1, source_target_pairs={{0,64},{8,24},{16,80},{24,40},{32,96},{40,56},{48,112},{56,8},{64,... | collective-permute-start | bytes 196616 | tf_op jit(solution)/shard_map/ppermute | solution.py:529
  48.5 4.6 %collective-permute-start.12 = (f32[128,128]{1,0:T(8,128)S(1)}, f32[128,128]{1,0:T(8,128)S(1)}, u32[]{:S(2)}, u32[]{:S(2)}) collective-permute-start(f32[128,128]{1,0:T(8,128)S(1)} %get-tuple-element.48), channel_id=1, source_target_pairs={{0,64},{8,40},{16,80},{24,56},{32,96},{40,8},{48,112},{56,24},{64,... | collective-permute-start | bytes 196616 | tf_op jit(solution)/shard_map/ppermute | solution.py:529
  50.8 3.1 %collective-permute-start.11 = (f32[128,128]{1,0:T(8,128)S(1)}, f32[128,128]{1,0:T(8,128)S(1)}, u32[]{:S(2)}, u32[]{:S(2)}) collective-permute-start(f32[128,128]{1,0:T(8,128)S(1)} %get-tuple-element.47), channel_id=1, source_target_pairs={{0,64},{8,56},{16,80},{24,8},{32,96},{40,24},{48,112},{56,40},{64,... | collective-permute-start | bytes 196616 | tf_op jit(solution)/shard_map/ppermute | solution.py:529
  51.9 2.5 %collective-permute-start.14 = (f32[128,128]{1,0:T(8,128)S(1)}, f32[128,128]{1,0:T(8,128)S(1)}, u32[]{:S(2)}, u32[]{:S(2)}) collective-permute-start(f32[128,128]{1,0:T(8,128)S(1)} %get-tuple-element.50.after_ref.refs_8_), channel_id=1, source_target_pairs={{0,8},{8,0},{16,24},{24,16},{32,40},{40,32},{48,56},{56,48},{64,72... | collective-permute-start | bytes 196616 | tf_op jit(solution)/shard_map/ppermute | solution.py:535
  53.9 1.3 %collective-permute-start.17 = (f32[128,128]{1,0:T(8,128)S(1)}, f32[128,128]{1,0:T(8,128)S(1)}, u32[]{:S(2)}, u32[]{:S(2)}) collective-permute-start(f32[128,128]{1,0:T(8,128)S(1)} %collective-permute-done.11.refs_11_), channel_id=1, source_target_pairs={{0,8},{8,0},{16,24},{24,16},{32,40},{40,32},{48,56},{56,48},{64,72... | collective-permute-start | bytes 196616 | tf_op jit(solution)/shard_map/ppermute | solution.py:535
  53.9 1.4 %collective-permute-start.16 = (f32[128,128]{1,0:T(8,128)S(1)}, f32[128,128]{1,0:T(8,128)S(1)}, u32[]{:S(2)}, u32[]{:S(2)}) collective-permute-start(f32[128,128]{1,0:T(8,128)S(1)} %collective-permute-done.12.refs_10_), channel_id=1, source_target_pairs={{0,8},{8,0},{16,24},{24,16},{32,40},{40,32},{48,56},{56,48},{64,72... | collective-permute-start | bytes 196616 | tf_op jit(solution)/shard_map/ppermute | solution.py:535
  54.4 1.3 %collective-permute-start.15 = (f32[128,128]{1,0:T(8,128)S(1)}, f32[128,128]{1,0:T(8,128)S(1)}, u32[]{:S(2)}, u32[]{:S(2)}) collective-permute-start(f32[128,128]{1,0:T(8,128)S(1)} %collective-permute-done.13.refs_9_), channel_id=1, source_target_pairs={{0,8},{8,0},{16,24},{24,16},{32,40},{40,32},{48,56},{56,48},{64,72... | collective-permute-start | bytes 196616 | tf_op jit(solution)/shard_map/ppermute | solution.py:535

commit v9 on v8

--- a/solution.py
+++ b/solution.py
@@ -14,7 +14,6 @@
 XS = 4
 YS = 4
 CS = 2
-ZG = 4
 MSG = 2 * D
 
 f32 = jnp.float32
@@ -105,7 +104,6 @@
     col = iota2((BLK, BLK), 1)
     eye = row == col
     pair = ((row >> 1) == (col >> 1)) & (row < col)
-    quad = ((row >> 2) == (col >> 2)) & ((row >> 1) < (col >> 1))
     chains = [(h, b) for h in range(HEADS) for b in range(nblk)]
     rs, rts, vts, uppers, invs, ccols, crows = [], [], [], [], [], [], []
     for h, b in chains:
@@ -118,20 +116,14 @@
         ccol = lax.rsqrt(jnp.sum(diag, axis=1, keepdims=True) + 1e-06)
         crow = lax.rsqrt(jnp.sum(diag, axis=0, keepdims=True) + 1e-06)
         upper = jnp.where(row < col, 2.0 * ccol * crow * gram, 0.0)
-        near = jnp.where(pair, upper, 0.0)
-        across = jnp.where(quad, upper, 0.0)
-        erow = jnp.sum(near, axis=0, keepdims=True)
-        fcol = jnp.sum(near, axis=1, keepdims=True)
-        mid = across - pltpu.roll(across, 1, 1) * erow
-        down = pltpu.roll(mid.reshape(BLK // 8, 8, BLK), 7, 1).reshape(BLK, BLK)
-        inv = jnp.where(eye, 1.0, 0.0) - near - (mid - fcol * down)
+        inv = jnp.where(eye, 1.0, 0.0) - jnp.where(pair, upper, 0.0)
         rs.append(r)
         rts.append(rt)
         uppers.append(upper)
         invs.append(inv)
         ccols.append(ccol)
         crows.append(crow)
-    for level in range(2, 7):
+    for level in range(1, 7):
         off = ((row >> (level + 1)) == (col >> (level + 1))) & (
             (row >> level) < (col >> level)
         )
@@ -267,28 +259,29 @@
     start_ref[...] = init_ref[x].T
 
 
-def lead_kernel(s0, s1, s2, s3, start_ref, after_ref, lead_ref, hold):
-    ordered_xor([s0, s1, s2, s3], lax.rem(place_seg(), ZG), hold)
-    tail = msg_compose(hold[2], hold[3])
-    state = advance(advance(start_ref[...], hold[0]), hold[1])
-    lead_ref[...] = advance(state, tail)
-
-
-def fuse_kernel(s0, s1, s2, s3, path_ref, after_ref, fuse_ref, hold):
-    g = lax.rem(place_seg(), ZG)
-    ordered_xor([s0, s1, s2, s3], g, hold)
-    window = place_prefix(g, hold)
-    left = wide(window)
+def pair_kernel(own_ref, near_ref, after_ref, total_ref):
+    later = lax.rem(place_seg(), 2) == 1
+    own, near = own_ref[...], near_ref[...]
+    total_ref[...] = msg_compose(jnp.where(later, near, own), jnp.where(later, own, near))
+
+
+def fuse_kernel(near_ref, path_ref, after_ref, fuse_ref):
+    later = lax.rem(place_seg(), 2) == 1
+    left = wide(near_ref[...])
     for i in range(XS):
         path = path_ref[i]
         moved = mm_pre(left, tall_wide(path[:D]))
-        fuse_ref[i, :D, :] = moved[:D]
-        fuse_ref[i, D:, :] = moved[D:] + path[D:]
-
-
-def entry_kernel(start_ref, early_ref, fuse_ref, o0, o1, o2, o3, scratch):
+        moved = jnp.concatenate([moved[:D], moved[D:] + path[D:]], axis=0)
+        fuse_ref[i] = jnp.where(later, moved, path)
+
+
+def entry_kernel(s0, s1, s2, s3, start_ref, fuse_ref, after_ref, o0, o1, o2, o3, hold, scratch):
     x = place_x()
-    state = jnp.where(place_seg() >= ZG, early_ref[...], start_ref[...])
+    place = place_seg() // 2
+    ordered_xor([s0, s1, s2, s3], place, hold)
+    state = start_ref[...]
+    for i in range(3):
+        state = jnp.where(place > i, advance(state, hold[i]), state)
     left = wide(state)
     for i in range(XS):
         scratch[i] = mm_pre(left, tall_wide(fuse_ref[i, :D, :])) + fuse_ref[i, D:, :]
@@ -469,8 +462,7 @@
     ]
     along_y = [plane_perm(lambda y, x, k=k: (y ^ k, x), near_x) for k in range(1, YS)]
     segs = lax.axis_size("seg")
-    along_z = [depth_perm(segs, lambda g, k=k: g ^ k) for k in range(1, ZG)]
-    jump = depth_perm(segs, lambda g: segs - 1 - g)
+    near_z, *along_z = [depth_perm(segs, lambda g, k=k: g ^ k) for k in (1, 2, 5, 6)]
 
     keys = key_rows.reshape(steps * HEADS, D)
     values = value_rows.reshape(steps * HEADS, D)
@@ -492,7 +484,7 @@
     (total,) = small_call(
         column_kernel, "column", slots, [(MSG, D)], [(YS, MSG, D)], after=reaches[-1][0]
     )
-    slots = [total] + [lax.ppermute(total, ("seq", "seg"), p) for p in along_z]
+    near = lax.ppermute(total, ("seq", "seg"), near_z)
     path, start = small_call(
         path_kernel,
         "path",
@@ -501,30 +493,17 @@
         [(XS, MSG, D), (YS, MSG, D)],
         after=total,
     )
-    reaches.append(reach_call(query, r, z, sib, path, 2))
-    (lead,) = small_call(
-        lead_kernel,
-        "lead",
-        [*slots, start],
-        [(D, D)],
-        [(ZG, MSG, D)],
-        after=reaches[-1][0],
-    )
-    early = lax.ppermute(lead, ("seq", "seg"), jump)
-    (fused,) = small_call(
-        fuse_kernel,
-        "fuse",
-        [*slots, path],
-        [(XS, MSG, D)],
-        [(ZG, MSG, D)],
-        after=lead,
-    )
+    (total,) = small_call(pair_kernel, "pair", [total, near], [(MSG, D)], after=path)
+    slots = [total] + [lax.ppermute(total, ("seq", "seg"), p) for p in along_z]
+    (fused,) = small_call(fuse_kernel, "fuse", [near, path], [(XS, MSG, D)], after=total)
+    reaches.append(reach_call(query, r, z, sib, fused, 2))
     slots = small_call(
         entry_kernel,
         "entry",
-        [start, early, fused],
+        [*slots, start, fused],
         [(D, D)] * XS,
-        [(XS, D, D)],
+        [(XS, MSG, D), (XS, D, D)],
+        after=reaches[-1][0],
     )
     slots = [slots[0]] + [lax.ppermute(s, "seq", p) for s, p in zip(slots[1:], along_x)]
     reaches.append(reach_call(query, r, z, sib, slots[0], 3))

time: 57.2 us -> 57.6 us (level)
  waiting for transfers between devices: 14.2 us -> 16.2 us
  Pallas kernels: 18.8 us -> 17.3 us
    ppermute x1, starting transfers between devices: 4.57 us -> 1.19 us  [per_device(): near = lax.ppermute(total, ('seq', 'seg'), near_z)]
    ppermute x3, starting transfers between devices: 4.29 us -> 7.6 us  [per_device(): slots = [total] + [lax.ppermute(total, ('seq', 'seg'), p) for p in along_z]]
    ppermute x3, waiting for transfers between devices: 2.99 us -> 4.71 us  [per_device(): slots = [total] + [lax.ppermute(total, ('seq', 'seg'), p) for p in along_z]]
    pallas_call x1, Pallas kernels: 9.53 us -> 8.23 us  [factor_call(): pl.pallas_call(factor_kernel, in_specs=[pl.BlockSpec(memory_space=pl.ANY)...]
  transfers between devices with their start and end apart: 18 -> 18, of which waited for: 13 -> 14; matrix products, arithmetic and copies ran while one was open for 0% -> 0% of each run, Pallas kernels for 10% -> 10%
where the time goes in v9:
time: 57.6 us; the launch traced here: 57.5 us
  starting transfers between devices  23.6 us (41%)
  Pallas kernels  17.3 us (30%)
  waiting for transfers between devices  16.2 us (28%)
    pallas_call x1, Pallas kernels, factor_call(): pl.pallas_call(factor_kernel, in_specs=[pl.BlockSpec(memory_space=pl.ANY)...  8.23 us
    ppermute x6, starting transfers between devices, per_device(): lax.ppermute(s, 'seq', p)  7.64 us
    ppermute x3, starting transfers between devices, per_device(): slots = [total] + [lax.ppermute(total, ('seq', 'seg'), p) for p in along_z]  7.6 us
    ppermute x3, waiting for transfers between devices, per_device(): slots = [total] + [lax.ppermute(total, ('seq', 'seg'), p) for p in along_z]  4.71 us
    pallas_call x4, Pallas kernels, reach_call(): pl.pallas_call(functools.partial(reach_kernel, head=head), grid=(1,), in_...  4.71 us
    ppermute x6, waiting for transfers between devices, per_device(): lax.ppermute(s, 'seq', p)  3.82 us
    ppermute x3, starting transfers between devices, per_device(): slots = [total] + [lax.ppermute(total, 'seq', p) for p in along_y]  3.34 us
    ppermute x1, starting transfers between devices, per_device(): sib = lax.ppermute(pair, 'seq', swap)  3.33 us
  transfers between devices with their start and end apart: 18, of which 14 were waited for; matrix products, arithmetic and copies ran while one was open for 0% of the time, Pallas kernels for 10%

profile of v9, /device:TPU:1, one launch (start us, length us, event | category | flops | bytes accessed | tf_op | source)
XLA Modules:
  0.0 57.5 jit_solution(5920090812338449669)
XLA Ops:
  0.0 8.2 %factor.1 = (f32[4,256,128]{2,1,0:T(8,128)S(1)}, f32[4,4,256,128]{3,2,1,0:T(8,128)S(1)}, bf16[4,512,128]{2,1,0:T(8,128)(2,1)S(1)}) custom-call(bf16[2048,128]{1,0:T(8,128)(2,1)} %bitcast.8, bf16[2048,128]{1,0:T(8,128)(2,1)} %bitcast.9), custom_call_target="tpu_custom_call" | custom-call | tf_op jit(solution)/shard_map/factor/pallas_call | solution.py:173
  8.2 3.3 %collective-permute-start = (f32[4,256,128]{2,1,0:T(8,128)S(1)}, f32[4,256,128]{2,1,0:T(8,128)S(1)}, u32[]{:S(2)}, u32[]{:S(2)}) collective-permute-start(f32[4,256,128]{2,1,0:T(8,128)S(1)} %get-tuple-element.34.own_ref), channel_id=1, source_target_pairs={{0,8},{8,0},{16,24},{24,16},{32,40},{40,32},{48,56},{56,48},{64,72... | collective-permute-start | bytes 1572872 | tf_op jit(solution)/shard_map/ppermute | solution.py:473
  11.6 1.5 %collective-permute-done.sib_ref = f32[4,256,128]{2,1,0:T(8,128)S(1)} collective-permute-done((f32[4,256,128]{2,1,0:T(8,128)S(1)}, f32[4,256,128]{2,1,0:T(8,128)S(1)}, u32[]{:S(2)}, u32[]{:S(2)}) %collective-permute-start) | collective-permute-done | bytes 524320 | tf_op jit(solution)/shard_map/ppermute | solution.py:473
  13.1 0.3 chip.1
  13.4 0.1 collective-permute-start.1
  13.5 1.9 %collective-permute-start.2 = (f32[256,128]{1,0:T(8,128)S(1)}, f32[256,128]{1,0:T(8,128)S(1)}, u32[]{:S(2)}, u32[]{:S(2)}) collective-permute-start(f32[256,128]{1,0:T(8,128)S(1)} %get-tuple-element.39), channel_id=1, source_target_pairs={{0,64},{8,40},{16,80},{24,56},{32,96},{40,8},{48,112},{56,24},{64,... | collective-permute-start | bytes 393224 | tf_op jit(solution)/shard_map/ppermute | solution.py:475
  15.4 1.2 %collective-permute-start.3 = (f32[256,128]{1,0:T(8,128)S(1)}, f32[256,128]{1,0:T(8,128)S(1)}, u32[]{:S(2)}, u32[]{:S(2)}) collective-permute-start(f32[256,128]{1,0:T(8,128)S(1)} %get-tuple-element.40), channel_id=1, source_target_pairs={{0,64},{8,56},{16,80},{24,8},{32,96},{40,24},{48,112},{56,40},{64,... | collective-permute-start | bytes 393224 | tf_op jit(solution)/shard_map/ppermute | solution.py:475
  16.6 1.2 %reach.4 = (bf16[256,256]{1,0:T(8,128)(2,1)S(1)}, f32[256,128]{1,0:T(8,128)S(1)}) custom-call(bf16[1024,128]{1,0:T(8,128)(2,1)S(1)} %bitcast.4, bf16[4,512,128]{2,1,0:T(8,128)(2,1)S(1)} %get-tuple-element.32.r_ref, f32[4,4,256,128]{3,2,1,0:T(8,128)S(1)} %get-tuple-element.33.z_ref, f32[4,256,128]{2,1,0:T(8,128)S(1)} %collective-permute-done.sib_ref, ...), custom_call_target="tpu_custom_call" | custom-call | flops 400000000 | bytes 3000000 | tf_op jit(solution)/shard_map/reach/pallas_call | solution.py:328
  17.8 2.2 %collective-permute-done.1.s1.refs_1_ = f32[256,128]{1,0:T(8,128)S(1)} collective-permute-done((f32[256,128]{1,0:T(8,128)S(1)}, f32[256,128]{1,0:T(8,128)S(1)}, u32[]{:S(2)}, u32[]{:S(2)}) %collective-permute-start.1) | collective-permute-done | bytes 131104 | tf_op jit(solution)/shard_map/ppermute | solution.py:475
  19.9 0.9 %collective-permute-done.3.s3.refs_3_ = f32[256,128]{1,0:T(8,128)S(1)} collective-permute-done((f32[256,128]{1,0:T(8,128)S(1)}, f32[256,128]{1,0:T(8,128)S(1)}, u32[]{:S(2)}, u32[]{:S(2)}) %collective-permute-start.3) | collective-permute-done | bytes 131104 | tf_op jit(solution)/shard_map/ppermute | solution.py:475
  20.8 0.5 row.1.after_ref.s0.refs_4_
  21.3 0.0 copy-start.1
  21.3 1.5 %collective-permute-start.6 = (f32[256,128]{1,0:T(8,128)S(1)}, f32[256,128]{1,0:T(8,128)S(1)}, u32[]{:S(2)}, u32[]{:S(2)}) collective-permute-start(f32[256,128]{1,0:T(8,128)S(1)} %row.1.after_ref.s0.refs_4_), channel_id=1, source_target_pairs={{0,16},{8,200},{16,0},{24,216},{32,48},{40,232},{48,32},{56,248},{... | collective-permute-start | bytes 393224 | tf_op jit(solution)/shard_map/ppermute | solution.py:481
  22.8 0.5 collective-permute-start.5
  23.3 1.3 %collective-permute-start.4 = (f32[256,128]{1,0:T(8,128)S(1)}, f32[256,128]{1,0:T(8,128)S(1)}, u32[]{:S(2)}, u32[]{:S(2)}) collective-permute-start(f32[256,128]{1,0:T(8,128)S(1)} %row.1.after_ref.s0.refs_4_), channel_id=1, source_target_pairs={{0,16},{8,72},{16,0},{24,88},{32,48},{40,104},{48,32},{56,120},{64... | collective-permute-start | bytes 393224 | tf_op jit(solution)/shard_map/ppermute | solution.py:481
  24.6 1.2 %reach.5 = (bf16[256,256]{1,0:T(8,128)(2,1)S(1)}, f32[256,128]{1,0:T(8,128)S(1)}) custom-call(bf16[1024,128]{1,0:T(8,128)(2,1)S(1)} %bitcast.5, bf16[4,512,128]{2,1,0:T(8,128)(2,1)S(1)} %get-tuple-element.32.r_ref, f32[4,4,256,128]{3,2,1,0:T(8,128)S(1)} %get-tuple-element.33.z_ref, f32[4,256,128]{2,1,0:T(8,128)S(1)} %collective-permute-done.sib_ref, ...), custom_call_target="tpu_custom_call" | custom-call | flops 400000000 | bytes 3000000 | tf_op jit(solution)/shard_map/reach/pallas_call | solution.py:328
  25.8 0.6 %collective-permute-done.6.s3.refs_7_ = f32[256,128]{1,0:T(8,128)S(1)} collective-permute-done((f32[256,128]{1,0:T(8,128)S(1)}, f32[256,128]{1,0:T(8,128)S(1)}, u32[]{:S(2)}, u32[]{:S(2)}) %collective-permute-start.6) | collective-permute-done | bytes 131104 | tf_op jit(solution)/shard_map/ppermute | solution.py:481
  26.4 1.7 %collective-permute-done.5.s2.refs_6_ = f32[256,128]{1,0:T(8,128)S(1)} collective-permute-done((f32[256,128]{1,0:T(8,128)S(1)}, f32[256,128]{1,0:T(8,128)S(1)}, u32[]{:S(2)}, u32[]{:S(2)}) %collective-permute-start.5) | collective-permute-done | bytes 131104 | tf_op jit(solution)/shard_map/ppermute | solution.py:481
  28.1 0.5 collective-permute-done.4.s1.refs_5_
  28.7 0.5 column.1.refs_9_.own_ref
  29.1 1.2 %collective-permute-start.7 = (f32[256,128]{1,0:T(8,128)S(1)}, f32[256,128]{1,0:T(8,128)S(1)}, u32[]{:S(2)}, u32[]{:S(2)}) collective-permute-start(f32[256,128]{1,0:T(8,128)S(1)} %column.1.refs_9_.own_ref), channel_id=1, source_target_pairs={{0,16},{8,9},{1,17},{9,8},{2,18},{10,11},{3,19},{11,10},{4,20},{12... | collective-permute-start | bytes 393224 | tf_op jit(solution)/shard_map/ppermute | solution.py:487
  30.3 0.7 %path.1 = (f32[4,256,128]{2,1,0:T(8,128)S(1)}, f32[128,128]{1,0:T(8,128)S(1)}) custom-call(f32[256,128]{1,0:T(8,128)S(1)} %get-tuple-element.35.after_ref.s0.refs_0_, f32[256,128]{1,0:T(8,128)S(1)} %collective-permute-done.1.s1.refs_1_, f32[256,128]{1,0:T(8,128)S(1)} %collective-permute-done.2.s2.refs_2_, f32[256,128]{1,0:T(8,128)S(1)} %collective-permute-done.3.s3.refs_3_, ...), custom_call_target="tpu_custom_call" | custom-call | tf_op jit(solution)/shard_map/path/pallas_call | solution.py:414
  31.0 2.0 %collective-permute-done.7.near_ref = f32[256,128]{1,0:T(8,128)S(1)} collective-permute-done((f32[256,128]{1,0:T(8,128)S(1)}, f32[256,128]{1,0:T(8,128)S(1)}, u32[]{:S(2)}, u32[]{:S(2)}) %collective-permute-start.7) | collective-permute-done | bytes 131104 | tf_op jit(solution)/shard_map/ppermute | solution.py:487
  33.1 0.2 pair.1.after_ref.s0
  33.3 5.9 %collective-permute-start.10 = (f32[256,128]{1,0:T(8,128)S(1)}, f32[256,128]{1,0:T(8,128)S(1)}, u32[]{:S(2)}, u32[]{:S(2)}) collective-permute-start(f32[256,128]{1,0:T(8,128)S(1)} %pair.1.after_ref.s0), channel_id=1, source_target_pairs={{0,16},{8,14},{1,17},{9,15},{2,18},{10,12},{3,19},{11,13},{4,20},{... | collective-permute-start | bytes 393224 | tf_op jit(solution)/shard_map/ppermute | solution.py:497
  39.1 0.7 %collective-permute-start.9 = (f32[256,128]{1,0:T(8,128)S(1)}, f32[256,128]{1,0:T(8,128)S(1)}, u32[]{:S(2)}, u32[]{:S(2)}) collective-permute-start(f32[256,128]{1,0:T(8,128)S(1)} %pair.1.after_ref.s0), channel_id=1, source_target_pairs={{0,16},{8,13},{1,17},{9,12},{2,18},{10,15},{3,19},{11,14},{4,20},{... | collective-permute-start | bytes 393224 | tf_op jit(solution)/shard_map/ppermute | solution.py:497
  39.8 1.0 %collective-permute-start.8 = (f32[256,128]{1,0:T(8,128)S(1)}, f32[256,128]{1,0:T(8,128)S(1)}, u32[]{:S(2)}, u32[]{:S(2)}) collective-permute-start(f32[256,128]{1,0:T(8,128)S(1)} %pair.1.after_ref.s0), channel_id=1, source_target_pairs={{0,16},{8,10},{1,17},{9,11},{2,18},{10,8},{3,19},{11,9},{4,20},{12... | collective-permute-start | bytes 393224 | tf_op jit(solution)/shard_map/ppermute | solution.py:497
  40.9 0.3 fuse.1.after_ref.fuse_ref
  41.2 1.2 %reach.6 = (bf16[256,256]{1,0:T(8,128)(2,1)S(1)}, f32[256,128]{1,0:T(8,128)S(1)}) custom-call(bf16[1024,128]{1,0:T(8,128)(2,1)S(1)} %bitcast.6, bf16[4,512,128]{2,1,0:T(8,128)(2,1)S(1)} %get-tuple-element.32.r_ref, f32[4,4,256,128]{3,2,1,0:T(8,128)S(1)} %get-tuple-element.33.z_ref, f32[4,256,128]{2,1,0:T(8,128)S(1)} %collective-permute-done.sib_ref, ...), custom_call_target="tpu_custom_call" | custom-call | flops 400000000 | bytes 3000000 | tf_op jit(solution)/shard_map/reach/pallas_call | solution.py:328
  42.4 1.5 %collective-permute-done.10.s3 = f32[256,128]{1,0:T(8,128)S(1)} collective-permute-done((f32[256,128]{1,0:T(8,128)S(1)}, f32[256,128]{1,0:T(8,128)S(1)}, u32[]{:S(2)}, u32[]{:S(2)}) %collective-permute-start.10) | collective-permute-done | bytes 131104 | tf_op jit(solution)/shard_map/ppermute | solution.py:497
  43.9 2.2 %collective-permute-done.9.s2 = f32[256,128]{1,0:T(8,128)S(1)} collective-permute-done((f32[256,128]{1,0:T(8,128)S(1)}, f32[256,128]{1,0:T(8,128)S(1)}, u32[]{:S(2)}, u32[]{:S(2)}) %collective-permute-start.9) | collective-permute-done | bytes 131104 | tf_op jit(solution)/shard_map/ppermute | solution.py:497
  46.1 1.0 %collective-permute-done.8.s1 = f32[256,128]{1,0:T(8,128)S(1)} collective-permute-done((f32[256,128]{1,0:T(8,128)S(1)}, f32[256,128]{1,0:T(8,128)S(1)}, u32[]{:S(2)}, u32[]{:S(2)}) %collective-permute-start.8) | collective-permute-done | bytes 131104 | tf_op jit(solution)/shard_map/ppermute | solution.py:497
  47.1 0.7 %entry.1 = (f32[128,128]{1,0:T(8,128)S(1)}, f32[128,128]{1,0:T(8,128)S(1)}, f32[128,128]{1,0:T(8,128)S(1)}, f32[128,128]{1,0:T(8,128)S(1)}) custom-call(f32[256,128]{1,0:T(8,128)S(1)} %pair.1.after_ref.s0, f32[256,128]{1,0:T(8,128)S(1)} %collective-permute-done.8.s1, f32[256,128]{1,0:T(8,128)S(1)} %collective-permute-done.9.s2, ...), custom_call_target="tpu_custom_call" | custom-call | tf_op jit(solution)/shard_map/entry/pallas_call | solution.py:414
  47.8 1.1 %collective-permute-start.13 = (f32[128,128]{1,0:T(8,128)S(1)}, f32[128,128]{1,0:T(8,128)S(1)}, u32[]{:S(2)}, u32[]{:S(2)}) collective-permute-start(f32[128,128]{1,0:T(8,128)S(1)} %get-tuple-element.49), channel_id=1, source_target_pairs={{0,64},{8,24},{16,80},{24,40},{32,96},{40,56},{48,112},{56,8},{64,... | collective-permute-start | bytes 196616 | tf_op jit(solution)/shard_map/ppermute | solution.py:508
  48.9 2.3 %collective-permute-start.12 = (f32[128,128]{1,0:T(8,128)S(1)}, f32[128,128]{1,0:T(8,128)S(1)}, u32[]{:S(2)}, u32[]{:S(2)}) collective-permute-start(f32[128,128]{1,0:T(8,128)S(1)} %get-tuple-element.48), channel_id=1, source_target_pairs={{0,64},{8,40},{16,80},{24,56},{32,96},{40,8},{48,112},{56,24},{64,... | collective-permute-start | bytes 196616 | tf_op jit(solution)/shard_map/ppermute | solution.py:508
  51.1 1.1 %collective-permute-start.11 = (f32[128,128]{1,0:T(8,128)S(1)}, f32[128,128]{1,0:T(8,128)S(1)}, u32[]{:S(2)}, u32[]{:S(2)}) collective-permute-start(f32[128,128]{1,0:T(8,128)S(1)} %get-tuple-element.47), channel_id=1, source_target_pairs={{0,64},{8,56},{16,80},{24,8},{32,96},{40,24},{48,112},{56,40},{64,... | collective-permute-start | bytes 196616 | tf_op jit(solution)/shard_map/ppermute | solution.py:508
  52.3 0.0 collective-permute-start.14
  52.3 1.2 %reach.7 = (bf16[256,256]{1,0:T(8,128)(2,1)S(1)}, f32[256,128]{1,0:T(8,128)S(1)}) custom-call(bf16[1024,128]{1,0:T(8,128)(2,1)S(1)} %bitcast.7, bf16[4,512,128]{2,1,0:T(8,128)(2,1)S(1)} %get-tuple-element.32.r_ref, f32[4,4,256,128]{3,2,1,0:T(8,128)S(1)} %get-tuple-element.33.z_ref, f32[4,256,128]{2,1,0:T(8,128)S(1)} %collective-permute-done.sib_ref, ...), custom_call_target="tpu_custom_call" | custom-call | flops 400000000 | bytes 3000000 | tf_op jit(solution)/shard_map/reach/pallas_call | solution.py:328
  53.5 0.0 collective-permute-done.13.refs_9_
  53.5 0.0 collective-permute-done.12.refs_10_
  53.5 0.8 %collective-permute-done.11.refs_11_ = f32[128,128]{1,0:T(8,128)S(1)} collective-permute-done((f32[128,128]{1,0:T(8,128)S(1)}, f32[128,128]{1,0:T(8,128)S(1)}, u32[]{:S(2)}, u32[]{:S(2)}) %collective-permute-start.11) | collective-permute-done | bytes 65568 | tf_op jit(solution)/shard_map/ppermute | solution.py:508
  54.3 0.0 collective-permute-start.17
  54.3 0.5 collective-permute-start.16
  54.8 0.0 collective-permute-start.15
  54.8 0.7 %collective-permute-done.17.refs_15_ = f32[128,128]{1,0:T(8,128)S(1)} collective-permute-done((f32[128,128]{1,0:T(8,128)S(1)}, f32[128,128]{1,0:T(8,128)S(1)}, u32[]{:S(2)}, u32[]{:S(2)}) %collective-permute-start.17) | collective-permute-done | bytes 65568 | tf_op jit(solution)/shard_map/ppermute | solution.py:514
  55.5 0.2 collective-permute-done.16.refs_14_
  55.7 0.4 collective-permute-done.15.refs_13_
  56.0 1.3 %read.1 = bf16[1024,128]{1,0:T(8,128)(2,1)} custom-call(bf16[256,256]{1,0:T(8,128)(2,1)S(1)} %get-tuple-element.36.after_ref.refs_0_, f32[256,128]{1,0:T(8,128)S(1)} %get-tuple-element.37.refs_1_, bf16[256,256]{1,0:T(8,128)(2,1)S(1)} %get-tuple-element.41.after_ref.refs_2_, f32[256,128]{1,0:T(8,128)S(1)} %get-tuple-element.42.refs_3_, ...), custom_call_target="tpu_custom_call" | custom-call | tf_op jit(solution)/shard_map/read/pallas_call | solution.py:396
  (7 shorter events, 0.0 us)
Async XLA Ops:
  0.0 16.6 %copy-start = (bf16[1,256,4,128]{3,2,1,0:T(4,128)(2,1)S(1)}, bf16[1,256,4,128]{3,2,1,0:T(4,128)(2,1)}, u32[]{:S(2)}) copy-start(bf16[1,256,4,128]{3,2,1,0:T(4,128)(2,1)} %param.5) | copy-start | bytes 786436
  8.2 4.9 %collective-permute-start = (f32[4,256,128]{2,1,0:T(8,128)S(1)}, f32[4,256,128]{2,1,0:T(8,128)S(1)}, u32[]{:S(2)}, u32[]{:S(2)}) collective-permute-start(f32[4,256,128]{2,1,0:T(8,128)S(1)} %get-tuple-element.34.own_ref), channel_id=1, source_target_pairs={{0,8},{8,0},{16,24},{24,16},{32,40},{40,32},{48,56},{56,48},{64,72... | collective-permute-start | bytes 1572872 | tf_op jit(solution)/shard_map/ppermute | solution.py:473
  13.4 6.5 %collective-permute-start.1 = (f32[256,128]{1,0:T(8,128)S(1)}, f32[256,128]{1,0:T(8,128)S(1)}, u32[]{:S(2)}, u32[]{:S(2)}) collective-permute-start(f32[256,128]{1,0:T(8,128)S(1)} %get-tuple-element.38), channel_id=1, source_target_pairs={{0,64},{8,24},{16,80},{24,40},{32,96},{40,56},{48,112},{56,8},{64,... | collective-permute-start | bytes 393224 | tf_op jit(solution)/shard_map/ppermute | solution.py:475
  13.5 6.4 %collective-permute-start.2 = (f32[256,128]{1,0:T(8,128)S(1)}, f32[256,128]{1,0:T(8,128)S(1)}, u32[]{:S(2)}, u32[]{:S(2)}) collective-permute-start(f32[256,128]{1,0:T(8,128)S(1)} %get-tuple-element.39), channel_id=1, source_target_pairs={{0,64},{8,40},{16,80},{24,56},{32,96},{40,8},{48,112},{56,24},{64,... | collective-permute-start | bytes 393224 | tf_op jit(solution)/shard_map/ppermute | solution.py:475
  15.4 5.4 %collective-permute-start.3 = (f32[256,128]{1,0:T(8,128)S(1)}, f32[256,128]{1,0:T(8,128)S(1)}, u32[]{:S(2)}, u32[]{:S(2)}) collective-permute-start(f32[256,128]{1,0:T(8,128)S(1)} %get-tuple-element.40), channel_id=1, source_target_pairs={{0,64},{8,56},{16,80},{24,8},{32,96},{40,24},{48,112},{56,40},{64,... | collective-permute-start | bytes 393224 | tf_op jit(solution)/shard_map/ppermute | solution.py:475
  21.3 9.1 %copy-start.1 = (f32[4,128,128]{2,1,0:T(8,128)S(1)}, f32[4,128,128]{2,1,0:T(8,128)}, u32[]{:S(2)}) copy-start(f32[4,128,128]{2,1,0:T(8,128)} %refs_8_.1) | copy-start | bytes 786436
  21.3 5.1 %collective-permute-start.6 = (f32[256,128]{1,0:T(8,128)S(1)}, f32[256,128]{1,0:T(8,128)S(1)}, u32[]{:S(2)}, u32[]{:S(2)}) collective-permute-start(f32[256,128]{1,0:T(8,128)S(1)} %row.1.after_ref.s0.refs_4_), channel_id=1, source_target_pairs={{0,16},{8,200},{16,0},{24,216},{32,48},{40,232},{48,32},{56,248},{... | collective-permute-start | bytes 393224 | tf_op jit(solution)/shard_map/ppermute | solution.py:481
  22.8 5.3 %collective-permute-start.5 = (f32[256,128]{1,0:T(8,128)S(1)}, f32[256,128]{1,0:T(8,128)S(1)}, u32[]{:S(2)}, u32[]{:S(2)}) collective-permute-start(f32[256,128]{1,0:T(8,128)S(1)} %row.1.after_ref.s0.refs_4_), channel_id=1, source_target_pairs={{0,16},{8,136},{16,0},{24,152},{32,48},{40,168},{48,32},{56,184},{... | collective-permute-start | bytes 393224 | tf_op jit(solution)/shard_map/ppermute | solution.py:481
  23.3 5.4 %collective-permute-start.4 = (f32[256,128]{1,0:T(8,128)S(1)}, f32[256,128]{1,0:T(8,128)S(1)}, u32[]{:S(2)}, u32[]{:S(2)}) collective-permute-start(f32[256,128]{1,0:T(8,128)S(1)} %row.1.after_ref.s0.refs_4_), channel_id=1, source_target_pairs={{0,16},{8,72},{16,0},{24,88},{32,48},{40,104},{48,32},{56,120},{64... | collective-permute-start | bytes 393224 | tf_op jit(solution)/shard_map/ppermute | solution.py:481
  29.1 3.9 %collective-permute-start.7 = (f32[256,128]{1,0:T(8,128)S(1)}, f32[256,128]{1,0:T(8,128)S(1)}, u32[]{:S(2)}, u32[]{:S(2)}) collective-permute-start(f32[256,128]{1,0:T(8,128)S(1)} %column.1.refs_9_.own_ref), channel_id=1, source_target_pairs={{0,16},{8,9},{1,17},{9,8},{2,18},{10,11},{3,19},{11,10},{4,20},{12... | collective-permute-start | bytes 393224 | tf_op jit(solution)/shard_map/ppermute | solution.py:487
  33.3 10.6 %collective-permute-start.10 = (f32[256,128]{1,0:T(8,128)S(1)}, f32[256,128]{1,0:T(8,128)S(1)}, u32[]{:S(2)}, u32[]{:S(2)}) collective-permute-start(f32[256,128]{1,0:T(8,128)S(1)} %pair.1.after_ref.s0), channel_id=1, source_target_pairs={{0,16},{8,14},{1,17},{9,15},{2,18},{10,12},{3,19},{11,13},{4,20},{... | collective-permute-start | bytes 393224 | tf_op jit(solution)/shard_map/ppermute | solution.py:497
  39.1 6.9 %collective-permute-start.9 = (f32[256,128]{1,0:T(8,128)S(1)}, f32[256,128]{1,0:T(8,128)S(1)}, u32[]{:S(2)}, u32[]{:S(2)}) collective-permute-start(f32[256,128]{1,0:T(8,128)S(1)} %pair.1.after_ref.s0), channel_id=1, source_target_pairs={{0,16},{8,13},{1,17},{9,12},{2,18},{10,15},{3,19},{11,14},{4,20},{... | collective-permute-start | bytes 393224 | tf_op jit(solution)/shard_map/ppermute | solution.py:497
  39.8 7.2 %collective-permute-start.8 = (f32[256,128]{1,0:T(8,128)S(1)}, f32[256,128]{1,0:T(8,128)S(1)}, u32[]{:S(2)}, u32[]{:S(2)}) collective-permute-start(f32[256,128]{1,0:T(8,128)S(1)} %pair.1.after_ref.s0), channel_id=1, source_target_pairs={{0,16},{8,10},{1,17},{9,11},{2,18},{10,8},{3,19},{11,9},{4,20},{12... | collective-permute-start | bytes 393224 | tf_op jit(solution)/shard_map/ppermute | solution.py:497
  47.1 8.9 %copy-start.2 = (f32[4,128]{1,0:T(4,128)S(1)}, f32[4,128]{1,0:T(4,128)}, u32[]{:S(2)}) copy-start(f32[4,128]{1,0:T(4,128)} %refs_16_.1) | copy-start | bytes 6148
  47.8 5.7 %collective-permute-start.13 = (f32[128,128]{1,0:T(8,128)S(1)}, f32[128,128]{1,0:T(8,128)S(1)}, u32[]{:S(2)}, u32[]{:S(2)}) collective-permute-start(f32[128,128]{1,0:T(8,128)S(1)} %get-tuple-element.49), channel_id=1, source_target_pairs={{0,64},{8,24},{16,80},{24,40},{32,96},{40,56},{48,112},{56,8},{64,... | collective-permute-start | bytes 196616 | tf_op jit(solution)/shard_map/ppermute | solution.py:508
  48.9 4.6 %collective-permute-start.12 = (f32[128,128]{1,0:T(8,128)S(1)}, f32[128,128]{1,0:T(8,128)S(1)}, u32[]{:S(2)}, u32[]{:S(2)}) collective-permute-start(f32[128,128]{1,0:T(8,128)S(1)} %get-tuple-element.48), channel_id=1, source_target_pairs={{0,64},{8,40},{16,80},{24,56},{32,96},{40,8},{48,112},{56,24},{64,... | collective-permute-start | bytes 196616 | tf_op jit(solution)/shard_map/ppermute | solution.py:508
  51.1 3.1 %collective-permute-start.11 = (f32[128,128]{1,0:T(8,128)S(1)}, f32[128,128]{1,0:T(8,128)S(1)}, u32[]{:S(2)}, u32[]{:S(2)}) collective-permute-start(f32[128,128]{1,0:T(8,128)S(1)} %get-tuple-element.47), channel_id=1, source_target_pairs={{0,64},{8,56},{16,80},{24,8},{32,96},{40,24},{48,112},{56,40},{64,... | collective-permute-start | bytes 196616 | tf_op jit(solution)/shard_map/ppermute | solution.py:508
  52.3 2.5 %collective-permute-start.14 = (f32[128,128]{1,0:T(8,128)S(1)}, f32[128,128]{1,0:T(8,128)S(1)}, u32[]{:S(2)}, u32[]{:S(2)}) collective-permute-start(f32[128,128]{1,0:T(8,128)S(1)} %get-tuple-element.50.after_ref.refs_8_), channel_id=1, source_target_pairs={{0,8},{8,0},{16,24},{24,16},{32,40},{40,32},{48,56},{56,48},{64,72... | collective-permute-start | bytes 196616 | tf_op jit(solution)/shard_map/ppermute | solution.py:514
  54.3 1.3 %collective-permute-start.17 = (f32[128,128]{1,0:T(8,128)S(1)}, f32[128,128]{1,0:T(8,128)S(1)}, u32[]{:S(2)}, u32[]{:S(2)}) collective-permute-start(f32[128,128]{1,0:T(8,128)S(1)} %collective-permute-done.11.refs_11_), channel_id=1, source_target_pairs={{0,8},{8,0},{16,24},{24,16},{32,40},{40,32},{48,56},{56,48},{64,72... | collective-permute-start | bytes 196616 | tf_op jit(solution)/shard_map/ppermute | solution.py:514
  54.3 1.4 %collective-permute-start.16 = (f32[128,128]{1,0:T(8,128)S(1)}, f32[128,128]{1,0:T(8,128)S(1)}, u32[]{:S(2)}, u32[]{:S(2)}) collective-permute-start(f32[128,128]{1,0:T(8,128)S(1)} %collective-permute-done.12.refs_10_), channel_id=1, source_target_pairs={{0,8},{8,0},{16,24},{24,16},{32,40},{40,32},{48,56},{56,48},{64,72... | collective-permute-start | bytes 196616 | tf_op jit(solution)/shard_map/ppermute | solution.py:514
  54.8 1.3 %collective-permute-start.15 = (f32[128,128]{1,0:T(8,128)S(1)}, f32[128,128]{1,0:T(8,128)S(1)}, u32[]{:S(2)}, u32[]{:S(2)}) collective-permute-start(f32[128,128]{1,0:T(8,128)S(1)} %collective-permute-done.13.refs_9_), channel_id=1, source_target_pairs={{0,8},{8,0},{16,24},{24,16},{32,40},{40,32},{48,56},{56,48},{64,72... | collective-permute-start | bytes 196616 | tf_op jit(solution)/shard_map/ppermute | solution.py:514

commit v10 on v8

--- a/solution.py
+++ b/solution.py
@@ -105,7 +105,6 @@
     col = iota2((BLK, BLK), 1)
     eye = row == col
     pair = ((row >> 1) == (col >> 1)) & (row < col)
-    quad = ((row >> 2) == (col >> 2)) & ((row >> 1) < (col >> 1))
     chains = [(h, b) for h in range(HEADS) for b in range(nblk)]
     rs, rts, vts, uppers, invs, ccols, crows = [], [], [], [], [], [], []
     for h, b in chains:
@@ -118,20 +117,14 @@
         ccol = lax.rsqrt(jnp.sum(diag, axis=1, keepdims=True) + 1e-06)
         crow = lax.rsqrt(jnp.sum(diag, axis=0, keepdims=True) + 1e-06)
         upper = jnp.where(row < col, 2.0 * ccol * crow * gram, 0.0)
-        near = jnp.where(pair, upper, 0.0)
-        across = jnp.where(quad, upper, 0.0)
-        erow = jnp.sum(near, axis=0, keepdims=True)
-        fcol = jnp.sum(near, axis=1, keepdims=True)
-        mid = across - pltpu.roll(across, 1, 1) * erow
-        down = pltpu.roll(mid.reshape(BLK // 8, 8, BLK), 7, 1).reshape(BLK, BLK)
-        inv = jnp.where(eye, 1.0, 0.0) - near - (mid - fcol * down)
+        inv = jnp.where(eye, 1.0, 0.0) - jnp.where(pair, upper, 0.0)
         rs.append(r)
         rts.append(rt)
         uppers.append(upper)
         invs.append(inv)
         ccols.append(ccol)
         crows.append(crow)
-    for level in range(2, 7):
+    for level in range(1, 7):
         off = ((row >> (level + 1)) == (col >> (level + 1))) & (
             (row >> level) < (col >> level)
         )
@@ -227,12 +220,12 @@
     total_ref[...] = msg_compose(msg_compose(hold[0], hold[1]), tail)
 
 
-def row_kernel(s0, s1, s2, s3, after_ref, total_ref, hold):
+def row_kernel(s0, s2, s1, s3, after_ref, total_ref, hold):
     ordered_cyclic([s0, s1, s2, s3], place_x(), hold)
     write_total(total_ref, hold)
 
 
-def column_kernel(s0, s1, s2, s3, after_ref, total_ref, hold):
+def column_kernel(s0, s1, s3, s2, after_ref, total_ref, hold):
     ordered_xor([s0, s1, s2, s3], place_y(), hold)
     write_total(total_ref, hold)
 
@@ -458,6 +451,13 @@
     return [(seat(y, x, c), seat(y, x, 1 - c)) for y in range(YS) for x in range(XS) for c in range(CS)]
 
 
+def exchange(slots, axis, perms, order):
+    out = list(slots)
+    for k in order:
+        out[k] = lax.ppermute(slots[k], axis, perms[k - 1])
+    return out
+
+
 def per_device(query_rows, key_rows, value_rows, out_gain, initial_state):
     tokens = query_rows.shape[1]
     steps = tokens * REFL
@@ -480,19 +480,19 @@
     pair, z, r = factor_call(keys, values)
     sib = lax.ppermute(pair, "seq", swap)
     slots = small_call(chip_kernel, "chip", [pair, sib], [(MSG, D)] * XS)
-    slots = [slots[0]] + [lax.ppermute(s, "seq", p) for s, p in zip(slots[1:], along_x)]
+    slots = exchange(slots, "seq", along_x, (2, 1, 3))
     reaches = [reach_call(query, r, z, sib, slots[0], 0)]
     xslots = slots
     (total,) = small_call(
-        row_kernel, "row", slots, [(MSG, D)], [(XS, MSG, D)], after=reaches[-1][0]
-    )
-    slots = [total] + [lax.ppermute(total, "seq", p) for p in along_y]
+        row_kernel, "row", [slots[i] for i in (0, 2, 1, 3)], [(MSG, D)], [(XS, MSG, D)], after=reaches[-1][0]
+    )
+    slots = exchange([total] * YS, "seq", along_y, (1, 3, 2))
     yslots = slots
     reaches.append(reach_call(query, r, z, sib, total, 1))
     (total,) = small_call(
-        column_kernel, "column", slots, [(MSG, D)], [(YS, MSG, D)], after=reaches[-1][0]
-    )
-    slots = [total] + [lax.ppermute(total, ("seq", "seg"), p) for p in along_z]
+        column_kernel, "column", [slots[i] for i in (0, 1, 3, 2)], [(MSG, D)], [(YS, MSG, D)], after=reaches[-1][0]
+    )
+    slots = exchange([total] * ZG, ("seq", "seg"), along_z, (1, 2, 3))
     path, start = small_call(
         path_kernel,
         "path",
@@ -526,7 +526,7 @@
         [(D, D)] * XS,
         [(XS, D, D)],
     )
-    slots = [slots[0]] + [lax.ppermute(s, "seq", p) for s, p in zip(slots[1:], along_x)]
+    slots = exchange(slots, "seq", along_x, (2, 1, 3))
     reaches.append(reach_call(query, r, z, sib, slots[0], 3))
     last = reaches[-1][0]
     for k in range(1, XS):

time: 57.2 us -> 56.4 us (0.986)
  Pallas kernels: 18.8 us -> 17.5 us
    pallas_call x1, Pallas kernels: 9.53 us -> 8.23 us  [factor_call(): pl.pallas_call(factor_kernel, in_specs=[pl.BlockSpec(memory_space=pl.ANY)...]
  transfers between devices with their start and end apart: 18 -> 18, of which waited for: 13 -> 13; matrix products, arithmetic and copies ran while one was open for 0% -> 0% of each run, Pallas kernels for 10% -> 11%
where the time goes in v10:
time: 56.4 us; the launch traced here: 56.3 us
  starting transfers between devices  24.3 us (43%)
  Pallas kernels  17.5 us (31%)
  waiting for transfers between devices  14.2 us (25%)
    ppermute x12, starting transfers between devices, exchange(): out[k] = lax.ppermute(slots[k], axis, perms[k - 1])  15.9 us
    ppermute x12, waiting for transfers between devices, exchange(): out[k] = lax.ppermute(slots[k], axis, perms[k - 1])  9.7 us
    pallas_call x1, Pallas kernels, factor_call(): pl.pallas_call(factor_kernel, in_specs=[pl.BlockSpec(memory_space=pl.ANY)...  8.23 us
    pallas_call x4, Pallas kernels, reach_call(): pl.pallas_call(functools.partial(reach_kernel, head=head), grid=(1,), in_...  4.71 us
    ppermute x1, starting transfers between devices, per_device(): early = lax.ppermute(lead, ('seq', 'seg'), jump)  4.56 us
    ppermute x1, starting transfers between devices, per_device(): sib = lax.ppermute(pair, 'seq', swap)  3.33 us
    pallas_call x7, Pallas kernels, small_call(): pl.pallas_call(kernel, in_specs=whole(*arrays) + [pl.BlockSpec(memory_spa...  3.26 us
    ppermute x1, waiting for transfers between devices, per_device(): early = lax.ppermute(lead, ('seq', 'seg'), jump)  1.74 us
  transfers between devices with their start and end apart: 18, of which 13 were waited for; matrix products, arithmetic and copies ran while one was open for 0% of the time, Pallas kernels for 11%

profile of v10, /device:TPU:1, one launch (start us, length us, event | category | flops | bytes accessed | tf_op | source)
XLA Modules:
  0.0 56.3 jit_solution(6876718664025538523)
XLA Ops:
  0.0 8.2 %factor.1 = (f32[4,256,128]{2,1,0:T(8,128)S(1)}, f32[4,4,256,128]{3,2,1,0:T(8,128)S(1)}, bf16[4,512,128]{2,1,0:T(8,128)(2,1)S(1)}) custom-call(bf16[2048,128]{1,0:T(8,128)(2,1)} %bitcast.8, bf16[2048,128]{1,0:T(8,128)(2,1)} %bitcast.9), custom_call_target="tpu_custom_call" | custom-call | tf_op jit(solution)/shard_map/factor/pallas_call | solution.py:174
  8.2 3.3 %collective-permute-start = (f32[4,256,128]{2,1,0:T(8,128)S(1)}, f32[4,256,128]{2,1,0:T(8,128)S(1)}, u32[]{:S(2)}, u32[]{:S(2)}) collective-permute-start(f32[4,256,128]{2,1,0:T(8,128)S(1)} %get-tuple-element.34.own_ref), channel_id=1, source_target_pairs={{0,8},{8,0},{16,24},{24,16},{32,40},{40,32},{48,56},{56,48},{64,72... | collective-permute-start | bytes 1572872 | tf_op jit(solution)/shard_map/ppermute | solution.py:481
  11.6 1.5 %collective-permute-done.sib_ref = f32[4,256,128]{2,1,0:T(8,128)S(1)} collective-permute-done((f32[4,256,128]{2,1,0:T(8,128)S(1)}, f32[4,256,128]{2,1,0:T(8,128)S(1)}, u32[]{:S(2)}, u32[]{:S(2)}) %collective-permute-start) | collective-permute-done | bytes 524320 | tf_op jit(solution)/shard_map/ppermute | solution.py:481
  13.1 0.3 chip.1
  13.4 1.1 %collective-permute-start.1 = (f32[256,128]{1,0:T(8,128)S(1)}, f32[256,128]{1,0:T(8,128)S(1)}, u32[]{:S(2)}, u32[]{:S(2)}) collective-permute-start(f32[256,128]{1,0:T(8,128)S(1)} %get-tuple-element.38), channel_id=1, source_target_pairs={{0,64},{8,40},{16,80},{24,56},{32,96},{40,8},{48,112},{56,24},{64,... | collective-permute-start | bytes 393224 | tf_op jit(solution)/shard_map/ppermute | solution.py:457
  14.5 0.3 collective-permute-start.2
  14.8 2.4 %collective-permute-start.3 = (f32[256,128]{1,0:T(8,128)S(1)}, f32[256,128]{1,0:T(8,128)S(1)}, u32[]{:S(2)}, u32[]{:S(2)}) collective-permute-start(f32[256,128]{1,0:T(8,128)S(1)} %get-tuple-element.40), channel_id=1, source_target_pairs={{0,64},{8,56},{16,80},{24,8},{32,96},{40,24},{48,112},{56,40},{64,... | collective-permute-start | bytes 393224 | tf_op jit(solution)/shard_map/ppermute | solution.py:457
  17.2 1.2 %reach.4 = (bf16[256,256]{1,0:T(8,128)(2,1)S(1)}, f32[256,128]{1,0:T(8,128)S(1)}) custom-call(bf16[1024,128]{1,0:T(8,128)(2,1)S(1)} %bitcast.4, bf16[4,512,128]{2,1,0:T(8,128)(2,1)S(1)} %get-tuple-element.32.r_ref, f32[4,4,256,128]{3,2,1,0:T(8,128)S(1)} %get-tuple-element.33.z_ref, f32[4,256,128]{2,1,0:T(8,128)S(1)} %collective-permute-done.sib_ref, ...), custom_call_target="tpu_custom_call" | custom-call | flops 400000000 | bytes 3000000 | tf_op jit(solution)/shard_map/reach/pallas_call | solution.py:328
  18.4 0.5 collective-permute-done.1.s2.refs_2_
  18.9 1.3 %collective-permute-done.2.s1.refs_1_ = f32[256,128]{1,0:T(8,128)S(1)} collective-permute-done((f32[256,128]{1,0:T(8,128)S(1)}, f32[256,128]{1,0:T(8,128)S(1)}, u32[]{:S(2)}, u32[]{:S(2)}) %collective-permute-start.2) | collective-permute-done | bytes 131104 | tf_op jit(solution)/shard_map/ppermute | solution.py:457
  20.2 0.0 collective-permute-done.3.s3.refs_3_
  20.3 0.5 row.1.after_ref.s0.refs_4_
  20.7 0.0 copy-start.1
  20.7 2.1 %collective-permute-start.6 = (f32[256,128]{1,0:T(8,128)S(1)}, f32[256,128]{1,0:T(8,128)S(1)}, u32[]{:S(2)}, u32[]{:S(2)}) collective-permute-start(f32[256,128]{1,0:T(8,128)S(1)} %row.1.after_ref.s0.refs_4_), channel_id=1, source_target_pairs={{0,16},{8,200},{16,0},{24,216},{32,48},{40,232},{48,32},{56,248},{... | collective-permute-start | bytes 393224 | tf_op jit(solution)/shard_map/ppermute | solution.py:457
  22.9 0.5 collective-permute-start.5
  23.3 0.8 %collective-permute-start.4 = (f32[256,128]{1,0:T(8,128)S(1)}, f32[256,128]{1,0:T(8,128)S(1)}, u32[]{:S(2)}, u32[]{:S(2)}) collective-permute-start(f32[256,128]{1,0:T(8,128)S(1)} %row.1.after_ref.s0.refs_4_), channel_id=1, source_target_pairs={{0,16},{8,72},{16,0},{24,88},{32,48},{40,104},{48,32},{56,120},{64... | collective-permute-start | bytes 393224 | tf_op jit(solution)/shard_map/ppermute | solution.py:457
  24.1 1.2 %reach.5 = (bf16[256,256]{1,0:T(8,128)(2,1)S(1)}, f32[256,128]{1,0:T(8,128)S(1)}) custom-call(bf16[1024,128]{1,0:T(8,128)(2,1)S(1)} %bitcast.5, bf16[4,512,128]{2,1,0:T(8,128)(2,1)S(1)} %get-tuple-element.32.r_ref, f32[4,4,256,128]{3,2,1,0:T(8,128)S(1)} %get-tuple-element.33.z_ref, f32[4,256,128]{2,1,0:T(8,128)S(1)} %collective-permute-done.sib_ref, ...), custom_call_target="tpu_custom_call" | custom-call | flops 400000000 | bytes 3000000 | tf_op jit(solution)/shard_map/reach/pallas_call | solution.py:328
  25.3 0.9 %collective-permute-done.6.s3.refs_7_ = f32[256,128]{1,0:T(8,128)S(1)} collective-permute-done((f32[256,128]{1,0:T(8,128)S(1)}, f32[256,128]{1,0:T(8,128)S(1)}, u32[]{:S(2)}, u32[]{:S(2)}) %collective-permute-start.6) | collective-permute-done | bytes 131104 | tf_op jit(solution)/shard_map/ppermute | solution.py:457
  26.2 2.0 %collective-permute-done.5.s2.refs_6_ = f32[256,128]{1,0:T(8,128)S(1)} collective-permute-done((f32[256,128]{1,0:T(8,128)S(1)}, f32[256,128]{1,0:T(8,128)S(1)}, u32[]{:S(2)}, u32[]{:S(2)}) %collective-permute-start.5) | collective-permute-done | bytes 131104 | tf_op jit(solution)/shard_map/ppermute | solution.py:457
  28.2 0.5 column.1.refs_9_.s0
  28.6 4.4 %collective-permute-start.9 = (f32[256,128]{1,0:T(8,128)S(1)}, f32[256,128]{1,0:T(8,128)S(1)}, u32[]{:S(2)}, u32[]{:S(2)}) collective-permute-start(f32[256,128]{1,0:T(8,128)S(1)} %column.1.refs_9_.s0), channel_id=1, source_target_pairs={{0,16},{8,11},{1,17},{9,10},{2,18},{10,9},{3,19},{11,8},{4,20},{12... | collective-permute-start | bytes 393224 | tf_op jit(solution)/shard_map/ppermute | solution.py:457
  33.1 0.0 collective-permute-start.8
  33.1 0.4 collective-permute-start.7
  33.5 0.7 %path.1 = (f32[4,256,128]{2,1,0:T(8,128)S(1)}, f32[128,128]{1,0:T(8,128)S(1)}) custom-call(f32[256,128]{1,0:T(8,128)S(1)} %get-tuple-element.35.after_ref.s0.refs_0_, f32[256,128]{1,0:T(8,128)S(1)} %collective-permute-done.2.s1.refs_1_, f32[256,128]{1,0:T(8,128)S(1)} %collective-permute-done.1.s2.refs_2_, f32[256,128]{1,0:T(8,128)S(1)} %collective-permute-done.3.s3.refs_3_, ...), custom_call_target="tpu_custom_call" | custom-call | tf_op jit(solution)/shard_map/path/pallas_call | solution.py:414
  34.1 1.2 %reach.6 = (bf16[256,256]{1,0:T(8,128)(2,1)S(1)}, f32[256,128]{1,0:T(8,128)S(1)}) custom-call(bf16[1024,128]{1,0:T(8,128)(2,1)S(1)} %bitcast.6, bf16[4,512,128]{2,1,0:T(8,128)(2,1)S(1)} %get-tuple-element.32.r_ref, f32[4,4,256,128]{3,2,1,0:T(8,128)S(1)} %get-tuple-element.33.z_ref, f32[4,256,128]{2,1,0:T(8,128)S(1)} %collective-permute-done.sib_ref, ...), custom_call_target="tpu_custom_call" | custom-call | flops 400000000 | bytes 3000000 | tf_op jit(solution)/shard_map/reach/pallas_call | solution.py:328
  35.3 0.2 collective-permute-done.9.s3
  35.5 2.8 %collective-permute-done.8.s2 = f32[256,128]{1,0:T(8,128)S(1)} collective-permute-done((f32[256,128]{1,0:T(8,128)S(1)}, f32[256,128]{1,0:T(8,128)S(1)}, u32[]{:S(2)}, u32[]{:S(2)}) %collective-permute-start.8) | collective-permute-done | bytes 131104 | tf_op jit(solution)/shard_map/ppermute | solution.py:457
  38.3 0.0 collective-permute-done.7.s1
  38.3 0.5 lead.1.after_ref
  38.8 4.6 %collective-permute-start.10 = (f32[128,128]{1,0:T(8,128)S(1)}, f32[128,128]{1,0:T(8,128)S(1)}, u32[]{:S(2)}, u32[]{:S(2)}) collective-permute-start(f32[128,128]{1,0:T(8,128)S(1)} %lead.1.after_ref), channel_id=1, source_target_pairs={{0,16},{8,15},{1,17},{9,14},{2,18},{10,13},{3,19},{11,12},{4,20},{... | collective-permute-start | bytes 196616 | tf_op jit(solution)/shard_map/ppermute | solution.py:513
  43.4 0.6 %fuse.1.fuse_ref = f32[4,256,128]{2,1,0:T(8,128)S(1)} custom-call(f32[256,128]{1,0:T(8,128)S(1)} %column.1.refs_9_.s0, f32[256,128]{1,0:T(8,128)S(1)} %collective-permute-done.7.s1, f32[256,128]{1,0:T(8,128)S(1)} %collective-permute-done.8.s2, f32[256,128]{1,0:T(8,128)S(1)} %collective-permute-done.9.s3, ...), custom_call_target="tpu_custom_call" | custom-call | tf_op jit(solution)/shard_map/fuse/pallas_call | solution.py:414
  44.0 0.0 copy-start.2
  44.0 1.7 %collective-permute-done.10.early_ref = f32[128,128]{1,0:T(8,128)S(1)} collective-permute-done((f32[128,128]{1,0:T(8,128)S(1)}, f32[128,128]{1,0:T(8,128)S(1)}, u32[]{:S(2)}, u32[]{:S(2)}) %collective-permute-start.10) | collective-permute-done | bytes 65568 | tf_op jit(solution)/shard_map/ppermute | solution.py:513
  45.7 0.3 entry.1
  46.0 0.6 %collective-permute-start.13 = (f32[128,128]{1,0:T(8,128)S(1)}, f32[128,128]{1,0:T(8,128)S(1)}, u32[]{:S(2)}, u32[]{:S(2)}) collective-permute-start(f32[128,128]{1,0:T(8,128)S(1)} %get-tuple-element.49), channel_id=1, source_target_pairs={{0,64},{8,24},{16,80},{24,40},{32,96},{40,56},{48,112},{56,8},{64,... | collective-permute-start | bytes 196616 | tf_op jit(solution)/shard_map/ppermute | solution.py:457
  46.6 3.3 %collective-permute-start.12 = (f32[128,128]{1,0:T(8,128)S(1)}, f32[128,128]{1,0:T(8,128)S(1)}, u32[]{:S(2)}, u32[]{:S(2)}) collective-permute-start(f32[128,128]{1,0:T(8,128)S(1)} %get-tuple-element.48), channel_id=1, source_target_pairs={{0,64},{8,40},{16,80},{24,56},{32,96},{40,8},{48,112},{56,24},{64,... | collective-permute-start | bytes 196616 | tf_op jit(solution)/shard_map/ppermute | solution.py:457
  49.9 0.0 collective-permute-start.11
  50.0 0.0 collective-permute-start.14
  50.0 1.2 %reach.7 = (bf16[256,256]{1,0:T(8,128)(2,1)S(1)}, f32[256,128]{1,0:T(8,128)S(1)}) custom-call(bf16[1024,128]{1,0:T(8,128)(2,1)S(1)} %bitcast.7, bf16[4,512,128]{2,1,0:T(8,128)(2,1)S(1)} %get-tuple-element.32.r_ref, f32[4,4,256,128]{3,2,1,0:T(8,128)S(1)} %get-tuple-element.33.z_ref, f32[4,256,128]{2,1,0:T(8,128)S(1)} %collective-permute-done.sib_ref, ...), custom_call_target="tpu_custom_call" | custom-call | flops 400000000 | bytes 3000000 | tf_op jit(solution)/shard_map/reach/pallas_call | solution.py:328
  51.1 0.0 collective-permute-done.13.refs_9_
  51.1 1.2 %collective-permute-done.12.refs_10_ = f32[128,128]{1,0:T(8,128)S(1)} collective-permute-done((f32[128,128]{1,0:T(8,128)S(1)}, f32[128,128]{1,0:T(8,128)S(1)}, u32[]{:S(2)}, u32[]{:S(2)}) %collective-permute-start.12) | collective-permute-done | bytes 65568 | tf_op jit(solution)/shard_map/ppermute | solution.py:457
  52.3 0.8 %collective-permute-done.11.refs_11_ = f32[128,128]{1,0:T(8,128)S(1)} collective-permute-done((f32[128,128]{1,0:T(8,128)S(1)}, f32[128,128]{1,0:T(8,128)S(1)}, u32[]{:S(2)}, u32[]{:S(2)}) %collective-permute-start.11) | collective-permute-done | bytes 65568 | tf_op jit(solution)/shard_map/ppermute | solution.py:457
  53.1 0.5 collective-permute-start.16
  53.6 0.0 collective-permute-start.15
  53.6 0.7 %collective-permute-done.17.refs_15_ = f32[128,128]{1,0:T(8,128)S(1)} collective-permute-done((f32[128,128]{1,0:T(8,128)S(1)}, f32[128,128]{1,0:T(8,128)S(1)}, u32[]{:S(2)}, u32[]{:S(2)}) %collective-permute-start.17) | collective-permute-done | bytes 65568 | tf_op jit(solution)/shard_map/ppermute | solution.py:535
  54.3 0.2 collective-permute-done.16.refs_14_
  54.5 0.4 collective-permute-done.15.refs_13_
  54.8 1.3 %read.1 = bf16[1024,128]{1,0:T(8,128)(2,1)} custom-call(bf16[256,256]{1,0:T(8,128)(2,1)S(1)} %get-tuple-element.36.after_ref.refs_0_, f32[256,128]{1,0:T(8,128)S(1)} %get-tuple-element.37.refs_1_, bf16[256,256]{1,0:T(8,128)(2,1)S(1)} %get-tuple-element.41.after_ref.refs_2_, f32[256,128]{1,0:T(8,128)S(1)} %get-tuple-element.42.refs_3_, ...), custom_call_target="tpu_custom_call" | custom-call | tf_op jit(solution)/shard_map/read/pallas_call | solution.py:396
  (7 shorter events, 0.0 us)
Async XLA Ops:
  0.0 17.2 %copy-start = (bf16[1,256,4,128]{3,2,1,0:T(4,128)(2,1)S(1)}, bf16[1,256,4,128]{3,2,1,0:T(4,128)(2,1)}, u32[]{:S(2)}) copy-start(bf16[1,256,4,128]{3,2,1,0:T(4,128)(2,1)} %param.5) | copy-start | bytes 786436
  8.2 4.9 %collective-permute-start = (f32[4,256,128]{2,1,0:T(8,128)S(1)}, f32[4,256,128]{2,1,0:T(8,128)S(1)}, u32[]{:S(2)}, u32[]{:S(2)}) collective-permute-start(f32[4,256,128]{2,1,0:T(8,128)S(1)} %get-tuple-element.34.own_ref), channel_id=1, source_target_pairs={{0,8},{8,0},{16,24},{24,16},{32,40},{40,32},{48,56},{56,48},{64,72... | collective-permute-start | bytes 1572872 | tf_op jit(solution)/shard_map/ppermute | solution.py:481
  13.4 5.5 %collective-permute-start.1 = (f32[256,128]{1,0:T(8,128)S(1)}, f32[256,128]{1,0:T(8,128)S(1)}, u32[]{:S(2)}, u32[]{:S(2)}) collective-permute-start(f32[256,128]{1,0:T(8,128)S(1)} %get-tuple-element.38), channel_id=1, source_target_pairs={{0,64},{8,40},{16,80},{24,56},{32,96},{40,8},{48,112},{56,24},{64,... | collective-permute-start | bytes 393224 | tf_op jit(solution)/shard_map/ppermute | solution.py:457
  14.5 5.7 %collective-permute-start.2 = (f32[256,128]{1,0:T(8,128)S(1)}, f32[256,128]{1,0:T(8,128)S(1)}, u32[]{:S(2)}, u32[]{:S(2)}) collective-permute-start(f32[256,128]{1,0:T(8,128)S(1)} %get-tuple-element.39), channel_id=1, source_target_pairs={{0,64},{8,24},{16,80},{24,40},{32,96},{40,56},{48,112},{56,8},{64,... | collective-permute-start | bytes 393224 | tf_op jit(solution)/shard_map/ppermute | solution.py:457
  14.8 5.4 %collective-permute-start.3 = (f32[256,128]{1,0:T(8,128)S(1)}, f32[256,128]{1,0:T(8,128)S(1)}, u32[]{:S(2)}, u32[]{:S(2)}) collective-permute-start(f32[256,128]{1,0:T(8,128)S(1)} %get-tuple-element.40), channel_id=1, source_target_pairs={{0,64},{8,56},{16,80},{24,8},{32,96},{40,24},{48,112},{56,40},{64,... | collective-permute-start | bytes 393224 | tf_op jit(solution)/shard_map/ppermute | solution.py:457
  20.7 12.8 %copy-start.1 = (f32[4,128,128]{2,1,0:T(8,128)S(1)}, f32[4,128,128]{2,1,0:T(8,128)}, u32[]{:S(2)}) copy-start(f32[4,128,128]{2,1,0:T(8,128)} %refs_8_.1) | copy-start | bytes 786436
  20.7 5.4 %collective-permute-start.6 = (f32[256,128]{1,0:T(8,128)S(1)}, f32[256,128]{1,0:T(8,128)S(1)}, u32[]{:S(2)}, u32[]{:S(2)}) collective-permute-start(f32[256,128]{1,0:T(8,128)S(1)} %row.1.after_ref.s0.refs_4_), channel_id=1, source_target_pairs={{0,16},{8,200},{16,0},{24,216},{32,48},{40,232},{48,32},{56,248},{... | collective-permute-start | bytes 393224 | tf_op jit(solution)/shard_map/ppermute | solution.py:457
  22.9 5.3 %collective-permute-start.5 = (f32[256,128]{1,0:T(8,128)S(1)}, f32[256,128]{1,0:T(8,128)S(1)}, u32[]{:S(2)}, u32[]{:S(2)}) collective-permute-start(f32[256,128]{1,0:T(8,128)S(1)} %row.1.after_ref.s0.refs_4_), channel_id=1, source_target_pairs={{0,16},{8,136},{16,0},{24,152},{32,48},{40,168},{48,32},{56,184},{... | collective-permute-start | bytes 393224 | tf_op jit(solution)/shard_map/ppermute | solution.py:457
  23.3 4.9 %collective-permute-start.4 = (f32[256,128]{1,0:T(8,128)S(1)}, f32[256,128]{1,0:T(8,128)S(1)}, u32[]{:S(2)}, u32[]{:S(2)}) collective-permute-start(f32[256,128]{1,0:T(8,128)S(1)} %row.1.after_ref.s0.refs_4_), channel_id=1, source_target_pairs={{0,16},{8,72},{16,0},{24,88},{32,48},{40,104},{48,32},{56,120},{64... | collective-permute-start | bytes 393224 | tf_op jit(solution)/shard_map/ppermute | solution.py:457
  28.6 6.8 %collective-permute-start.9 = (f32[256,128]{1,0:T(8,128)S(1)}, f32[256,128]{1,0:T(8,128)S(1)}, u32[]{:S(2)}, u32[]{:S(2)}) collective-permute-start(f32[256,128]{1,0:T(8,128)S(1)} %column.1.refs_9_.s0), channel_id=1, source_target_pairs={{0,16},{8,11},{1,17},{9,10},{2,18},{10,9},{3,19},{11,8},{4,20},{12... | collective-permute-start | bytes 393224 | tf_op jit(solution)/shard_map/ppermute | solution.py:457
  33.1 5.2 %collective-permute-start.8 = (f32[256,128]{1,0:T(8,128)S(1)}, f32[256,128]{1,0:T(8,128)S(1)}, u32[]{:S(2)}, u32[]{:S(2)}) collective-permute-start(f32[256,128]{1,0:T(8,128)S(1)} %column.1.refs_9_.s0), channel_id=1, source_target_pairs={{0,16},{8,10},{1,17},{9,11},{2,18},{10,8},{3,19},{11,9},{4,20},{12... | collective-permute-start | bytes 393224 | tf_op jit(solution)/shard_map/ppermute | solution.py:457
  33.1 5.2 %collective-permute-start.7 = (f32[256,128]{1,0:T(8,128)S(1)}, f32[256,128]{1,0:T(8,128)S(1)}, u32[]{:S(2)}, u32[]{:S(2)}) collective-permute-start(f32[256,128]{1,0:T(8,128)S(1)} %column.1.refs_9_.s0), channel_id=1, source_target_pairs={{0,16},{8,9},{1,17},{9,8},{2,18},{10,11},{3,19},{11,10},{4,20},{12... | collective-permute-start | bytes 393224 | tf_op jit(solution)/shard_map/ppermute | solution.py:457
  38.8 6.9 %collective-permute-start.10 = (f32[128,128]{1,0:T(8,128)S(1)}, f32[128,128]{1,0:T(8,128)S(1)}, u32[]{:S(2)}, u32[]{:S(2)}) collective-permute-start(f32[128,128]{1,0:T(8,128)S(1)} %lead.1.after_ref), channel_id=1, source_target_pairs={{0,16},{8,15},{1,17},{9,14},{2,18},{10,13},{3,19},{11,12},{4,20},{... | collective-permute-start | bytes 196616 | tf_op jit(solution)/shard_map/ppermute | solution.py:513
  44.0 10.9 %copy-start.2 = (f32[4,128]{1,0:T(4,128)S(1)}, f32[4,128]{1,0:T(4,128)}, u32[]{:S(2)}) copy-start(f32[4,128]{1,0:T(4,128)} %refs_16_.1) | copy-start | bytes 6148
  46.0 5.1 %collective-permute-start.13 = (f32[128,128]{1,0:T(8,128)S(1)}, f32[128,128]{1,0:T(8,128)S(1)}, u32[]{:S(2)}, u32[]{:S(2)}) collective-permute-start(f32[128,128]{1,0:T(8,128)S(1)} %get-tuple-element.49), channel_id=1, source_target_pairs={{0,64},{8,24},{16,80},{24,40},{32,96},{40,56},{48,112},{56,8},{64,... | collective-permute-start | bytes 196616 | tf_op jit(solution)/shard_map/ppermute | solution.py:457
  46.6 5.7 %collective-permute-start.12 = (f32[128,128]{1,0:T(8,128)S(1)}, f32[128,128]{1,0:T(8,128)S(1)}, u32[]{:S(2)}, u32[]{:S(2)}) collective-permute-start(f32[128,128]{1,0:T(8,128)S(1)} %get-tuple-element.48), channel_id=1, source_target_pairs={{0,64},{8,40},{16,80},{24,56},{32,96},{40,8},{48,112},{56,24},{64,... | collective-permute-start | bytes 196616 | tf_op jit(solution)/shard_map/ppermute | solution.py:457
  49.9 3.1 %collective-permute-start.11 = (f32[128,128]{1,0:T(8,128)S(1)}, f32[128,128]{1,0:T(8,128)S(1)}, u32[]{:S(2)}, u32[]{:S(2)}) collective-permute-start(f32[128,128]{1,0:T(8,128)S(1)} %get-tuple-element.47), channel_id=1, source_target_pairs={{0,64},{8,56},{16,80},{24,8},{32,96},{40,24},{48,112},{56,40},{64,... | collective-permute-start | bytes 196616 | tf_op jit(solution)/shard_map/ppermute | solution.py:457
  50.0 3.6 %collective-permute-start.14 = (f32[128,128]{1,0:T(8,128)S(1)}, f32[128,128]{1,0:T(8,128)S(1)}, u32[]{:S(2)}, u32[]{:S(2)}) collective-permute-start(f32[128,128]{1,0:T(8,128)S(1)} %get-tuple-element.50.after_ref.refs_8_), channel_id=1, source_target_pairs={{0,8},{8,0},{16,24},{24,16},{32,40},{40,32},{48,56},{56,48},{64,72... | collective-permute-start | bytes 196616 | tf_op jit(solution)/shard_map/ppermute | solution.py:535
  53.1 1.3 %collective-permute-start.17 = (f32[128,128]{1,0:T(8,128)S(1)}, f32[128,128]{1,0:T(8,128)S(1)}, u32[]{:S(2)}, u32[]{:S(2)}) collective-permute-start(f32[128,128]{1,0:T(8,128)S(1)} %collective-permute-done.11.refs_11_), channel_id=1, source_target_pairs={{0,8},{8,0},{16,24},{24,16},{32,40},{40,32},{48,56},{56,48},{64,72... | collective-permute-start | bytes 196616 | tf_op jit(solution)/shard_map/ppermute | solution.py:535
  53.1 1.4 %collective-permute-start.16 = (f32[128,128]{1,0:T(8,128)S(1)}, f32[128,128]{1,0:T(8,128)S(1)}, u32[]{:S(2)}, u32[]{:S(2)}) collective-permute-start(f32[128,128]{1,0:T(8,128)S(1)} %collective-permute-done.12.refs_10_), channel_id=1, source_target_pairs={{0,8},{8,0},{16,24},{24,16},{32,40},{40,32},{48,56},{56,48},{64,72... | collective-permute-start | bytes 196616 | tf_op jit(solution)/shard_map/ppermute | solution.py:535
  53.6 1.3 %collective-permute-start.15 = (f32[128,128]{1,0:T(8,128)S(1)}, f32[128,128]{1,0:T(8,128)S(1)}, u32[]{:S(2)}, u32[]{:S(2)}) collective-permute-start(f32[128,128]{1,0:T(8,128)S(1)} %collective-permute-done.13.refs_9_), channel_id=1, source_target_pairs={{0,8},{8,0},{16,24},{24,16},{32,40},{40,32},{48,56},{56,48},{64,72... | collective-permute-start | bytes 196616 | tf_op jit(solution)/shard_map/ppermute | solution.py:535

commit v11 on v10

--- a/solution.py
+++ b/solution.py
@@ -241,7 +241,7 @@
 
 
 def path_kernel(*refs):
-    xslots, yslots = refs[:4], refs[4:8]
+    xslots, yslots = refs[:4], [refs[i] for i in (4, 5, 7, 6)]
     init_ref, after_ref, path_ref, start_ref, xhold, yhold = refs[8:]
     x = place_x()
     y = place_y()
@@ -356,6 +356,7 @@
     reaches, bases = refs[: 2 * HEADS : 2], refs[1 : 2 * HEADS : 2]
     refs = refs[2 * HEADS :]
     mine, other = refs[:HEADS], refs[HEADS : 2 * HEADS]
+    mine, other = ([part[i] for i in (0, 2, 1, 3)] for part in (mine, other))
     gain_ref, out_hbm, states, rows, out, sems = refs[2 * HEADS :]
     x = place_x()
 
@@ -496,7 +497,7 @@
     path, start = small_call(
         path_kernel,
         "path",
-        [*xslots, *yslots, initial_state],
+        [*xslots, *(yslots[i] for i in (0, 1, 3, 2)), initial_state],
         [(XS, MSG, D), (D, D)],
         [(XS, MSG, D), (YS, MSG, D)],
         after=total,
@@ -529,11 +530,12 @@
     slots = exchange(slots, "seq", along_x, (2, 1, 3))
     reaches.append(reach_call(query, r, z, sib, slots[0], 3))
     last = reaches[-1][0]
-    for k in range(1, XS):
+    for k in (2, 1, 3):
         slots[k], last = lax.optimization_barrier((slots[k], last))
     reaches[-1] = (last, reaches[-1][1])
-    others = [lax.ppermute(s, "seq", swap) for s in slots]
-    arrays = [a for pair in reaches for a in pair] + [*slots, *others, out_gain]
+    others = exchange(slots, "seq", [swap] * XS, (2, 1, 3))
+    others[0] = lax.ppermute(slots[0], "seq", swap)
+    arrays = [a for pair in reaches for a in pair] + [part[i] for part in (slots, others) for i in (0, 2, 1, 3)] + [out_gain]
     out = read_call(arrays, tokens)
     return out.reshape(1, tokens, HEADS, D)
 

time: 56.4 us -> 55.7 us (0.988)
  waiting for transfers between devices: 14.2 us -> 13.5 us
    ppermute x4 -> x1, waiting for transfers between devices: 1.25 us -> 0.01 us  [per_device(): others[0] = lax.ppermute(slots[0], 'seq', swap)]
    ppermute x12 -> x15, starting transfers between devices: 15.9 us -> 16.4 us  [exchange(): out[k] = lax.ppermute(slots[k], axis, perms[k - 1])]
    ppermute x12 -> x15, waiting for transfers between devices: 9.7 us -> 10.2 us  [exchange(): out[k] = lax.ppermute(slots[k], axis, perms[k - 1])]
where the time goes in v11:
time: 55.7 us; the launch traced here: 55.6 us
  starting transfers between devices  24.3 us (44%)
  Pallas kernels  17.5 us (31%)
  waiting for transfers between devices  13.5 us (24%)
    ppermute x15, starting transfers between devices, exchange(): out[k] = lax.ppermute(slots[k], axis, perms[k - 1])  16.4 us
    ppermute x15, waiting for transfers between devices, exchange(): out[k] = lax.ppermute(slots[k], axis, perms[k - 1])  10.2 us
    pallas_call x1, Pallas kernels, factor_call(): pl.pallas_call(factor_kernel, in_specs=[pl.BlockSpec(memory_space=pl.ANY)...  8.23 us
    pallas_call x4, Pallas kernels, reach_call(): pl.pallas_call(functools.partial(reach_kernel, head=head), grid=(1,), in_...  4.71 us
    ppermute x1, starting transfers between devices, per_device(): early = lax.ppermute(lead, ('seq', 'seg'), jump)  4.56 us
    ppermute x1, starting transfers between devices, per_device(): sib = lax.ppermute(pair, 'seq', swap)  3.33 us
    pallas_call x7, Pallas kernels, small_call(): pl.pallas_call(kernel, in_specs=whole(*arrays) + [pl.BlockSpec(memory_spa...  3.26 us
    ppermute x1, waiting for transfers between devices, per_device(): early = lax.ppermute(lead, ('seq', 'seg'), jump)  1.74 us
  transfers between devices with their start and end apart: 18, of which 13 were waited for; matrix products, arithmetic and copies ran while one was open for 0% of the time, Pallas kernels for 11%

profile of v11, /device:TPU:1, one launch (start us, length us, event | category | flops | bytes accessed | tf_op | source)
XLA Modules:
  0.0 55.6 jit_solution(13114439180680619601)
XLA Ops:
  0.0 8.2 %factor.1 = (f32[4,256,128]{2,1,0:T(8,128)S(1)}, f32[4,4,256,128]{3,2,1,0:T(8,128)S(1)}, bf16[4,512,128]{2,1,0:T(8,128)(2,1)S(1)}) custom-call(bf16[2048,128]{1,0:T(8,128)(2,1)} %bitcast.8, bf16[2048,128]{1,0:T(8,128)(2,1)} %bitcast.9), custom_call_target="tpu_custom_call" | custom-call | tf_op jit(solution)/shard_map/factor/pallas_call | solution.py:174
  8.2 3.3 %collective-permute-start = (f32[4,256,128]{2,1,0:T(8,128)S(1)}, f32[4,256,128]{2,1,0:T(8,128)S(1)}, u32[]{:S(2)}, u32[]{:S(2)}) collective-permute-start(f32[4,256,128]{2,1,0:T(8,128)S(1)} %get-tuple-element.34.own_ref), channel_id=1, source_target_pairs={{0,8},{8,0},{16,24},{24,16},{32,40},{40,32},{48,56},{56,48},{64,72... | collective-permute-start | bytes 1572872 | tf_op jit(solution)/shard_map/ppermute | solution.py:482
  11.6 1.5 %collective-permute-done.sib_ref = f32[4,256,128]{2,1,0:T(8,128)S(1)} collective-permute-done((f32[4,256,128]{2,1,0:T(8,128)S(1)}, f32[4,256,128]{2,1,0:T(8,128)S(1)}, u32[]{:S(2)}, u32[]{:S(2)}) %collective-permute-start) | collective-permute-done | bytes 524320 | tf_op jit(solution)/shard_map/ppermute | solution.py:482
  13.1 0.3 chip.1
  13.4 1.1 %collective-permute-start.1 = (f32[256,128]{1,0:T(8,128)S(1)}, f32[256,128]{1,0:T(8,128)S(1)}, u32[]{:S(2)}, u32[]{:S(2)}) collective-permute-start(f32[256,128]{1,0:T(8,128)S(1)} %get-tuple-element.38), channel_id=1, source_target_pairs={{0,64},{8,40},{16,80},{24,56},{32,96},{40,8},{48,112},{56,24},{64,... | collective-permute-start | bytes 393224 | tf_op jit(solution)/shard_map/ppermute | solution.py:458
  14.5 0.3 collective-permute-start.2
  14.8 2.4 %collective-permute-start.3 = (f32[256,128]{1,0:T(8,128)S(1)}, f32[256,128]{1,0:T(8,128)S(1)}, u32[]{:S(2)}, u32[]{:S(2)}) collective-permute-start(f32[256,128]{1,0:T(8,128)S(1)} %get-tuple-element.40), channel_id=1, source_target_pairs={{0,64},{8,56},{16,80},{24,8},{32,96},{40,24},{48,112},{56,40},{64,... | collective-permute-start | bytes 393224 | tf_op jit(solution)/shard_map/ppermute | solution.py:458
  17.2 1.2 %reach.4 = (bf16[256,256]{1,0:T(8,128)(2,1)S(1)}, f32[256,128]{1,0:T(8,128)S(1)}) custom-call(bf16[1024,128]{1,0:T(8,128)(2,1)S(1)} %bitcast.4, bf16[4,512,128]{2,1,0:T(8,128)(2,1)S(1)} %get-tuple-element.32.r_ref, f32[4,4,256,128]{3,2,1,0:T(8,128)S(1)} %get-tuple-element.33.z_ref, f32[4,256,128]{2,1,0:T(8,128)S(1)} %collective-permute-done.sib_ref, ...), custom_call_target="tpu_custom_call" | custom-call | flops 400000000 | bytes 3000000 | tf_op jit(solution)/shard_map/reach/pallas_call | solution.py:328
  18.4 0.5 collective-permute-done.1.s2.refs_2_
  18.9 1.3 %collective-permute-done.2.s1.refs_1_ = f32[256,128]{1,0:T(8,128)S(1)} collective-permute-done((f32[256,128]{1,0:T(8,128)S(1)}, f32[256,128]{1,0:T(8,128)S(1)}, u32[]{:S(2)}, u32[]{:S(2)}) %collective-permute-start.2) | collective-permute-done | bytes 131104 | tf_op jit(solution)/shard_map/ppermute | solution.py:458
  20.2 0.0 collective-permute-done.3.s3.refs_3_
  20.3 0.5 row.1.after_ref.s0.refs_4_
  20.7 0.0 copy-start.1
  20.7 2.3 %collective-permute-start.6 = (f32[256,128]{1,0:T(8,128)S(1)}, f32[256,128]{1,0:T(8,128)S(1)}, u32[]{:S(2)}, u32[]{:S(2)}) collective-permute-start(f32[256,128]{1,0:T(8,128)S(1)} %row.1.after_ref.s0.refs_4_), channel_id=1, source_target_pairs={{0,16},{8,136},{16,0},{24,152},{32,48},{40,168},{48,32},{56,184},{... | collective-permute-start | bytes 393224 | tf_op jit(solution)/shard_map/ppermute | solution.py:458
  23.0 0.8 %collective-permute-start.5 = (f32[256,128]{1,0:T(8,128)S(1)}, f32[256,128]{1,0:T(8,128)S(1)}, u32[]{:S(2)}, u32[]{:S(2)}) collective-permute-start(f32[256,128]{1,0:T(8,128)S(1)} %row.1.after_ref.s0.refs_4_), channel_id=1, source_target_pairs={{0,16},{8,200},{16,0},{24,216},{32,48},{40,232},{48,32},{56,248},{... | collective-permute-start | bytes 393224 | tf_op jit(solution)/shard_map/ppermute | solution.py:458
  23.8 0.0 collective-permute-start.4
  23.8 1.2 %reach.5 = (bf16[256,256]{1,0:T(8,128)(2,1)S(1)}, f32[256,128]{1,0:T(8,128)S(1)}) custom-call(bf16[1024,128]{1,0:T(8,128)(2,1)S(1)} %bitcast.5, bf16[4,512,128]{2,1,0:T(8,128)(2,1)S(1)} %get-tuple-element.32.r_ref, f32[4,4,256,128]{3,2,1,0:T(8,128)S(1)} %get-tuple-element.33.z_ref, f32[4,256,128]{2,1,0:T(8,128)S(1)} %collective-permute-done.sib_ref, ...), custom_call_target="tpu_custom_call" | custom-call | flops 400000000 | bytes 3000000 | tf_op jit(solution)/shard_map/reach/pallas_call | solution.py:328
  25.0 1.1 %collective-permute-done.6.s2.refs_7_ = f32[256,128]{1,0:T(8,128)S(1)} collective-permute-done((f32[256,128]{1,0:T(8,128)S(1)}, f32[256,128]{1,0:T(8,128)S(1)}, u32[]{:S(2)}, u32[]{:S(2)}) %collective-permute-start.6) | collective-permute-done | bytes 131104 | tf_op jit(solution)/shard_map/ppermute | solution.py:458
  26.1 1.9 %collective-permute-done.5.s3.refs_6_ = f32[256,128]{1,0:T(8,128)S(1)} collective-permute-done((f32[256,128]{1,0:T(8,128)S(1)}, f32[256,128]{1,0:T(8,128)S(1)}, u32[]{:S(2)}, u32[]{:S(2)}) %collective-permute-start.5) | collective-permute-done | bytes 131104 | tf_op jit(solution)/shard_map/ppermute | solution.py:458
  28.1 0.0 collective-permute-done.4.s1.refs_5_
  28.1 0.5 column.1.refs_9_.s0
  28.5 4.4 %collective-permute-start.9 = (f32[256,128]{1,0:T(8,128)S(1)}, f32[256,128]{1,0:T(8,128)S(1)}, u32[]{:S(2)}, u32[]{:S(2)}) collective-permute-start(f32[256,128]{1,0:T(8,128)S(1)} %column.1.refs_9_.s0), channel_id=1, source_target_pairs={{0,16},{8,11},{1,17},{9,10},{2,18},{10,9},{3,19},{11,8},{4,20},{12... | collective-permute-start | bytes 393224 | tf_op jit(solution)/shard_map/ppermute | solution.py:458
  33.0 0.0 collective-permute-start.8
  33.0 0.4 collective-permute-start.7
  33.4 0.7 %path.1 = (f32[4,256,128]{2,1,0:T(8,128)S(1)}, f32[128,128]{1,0:T(8,128)S(1)}) custom-call(f32[256,128]{1,0:T(8,128)S(1)} %get-tuple-element.35.after_ref.s0.refs_0_, f32[256,128]{1,0:T(8,128)S(1)} %collective-permute-done.2.s1.refs_1_, f32[256,128]{1,0:T(8,128)S(1)} %collective-permute-done.1.s2.refs_2_, f32[256,128]{1,0:T(8,128)S(1)} %collective-permute-done.3.s3.refs_3_, ...), custom_call_target="tpu_custom_call" | custom-call | tf_op jit(solution)/shard_map/path/pallas_call | solution.py:415
  34.0 1.2 %reach.6 = (bf16[256,256]{1,0:T(8,128)(2,1)S(1)}, f32[256,128]{1,0:T(8,128)S(1)}) custom-call(bf16[1024,128]{1,0:T(8,128)(2,1)S(1)} %bitcast.6, bf16[4,512,128]{2,1,0:T(8,128)(2,1)S(1)} %get-tuple-element.32.r_ref, f32[4,4,256,128]{3,2,1,0:T(8,128)S(1)} %get-tuple-element.33.z_ref, f32[4,256,128]{2,1,0:T(8,128)S(1)} %collective-permute-done.sib_ref, ...), custom_call_target="tpu_custom_call" | custom-call | flops 400000000 | bytes 3000000 | tf_op jit(solution)/shard_map/reach/pallas_call | solution.py:328
  35.2 0.2 collective-permute-done.9.s3
  35.4 2.8 %collective-permute-done.8.s2 = f32[256,128]{1,0:T(8,128)S(1)} collective-permute-done((f32[256,128]{1,0:T(8,128)S(1)}, f32[256,128]{1,0:T(8,128)S(1)}, u32[]{:S(2)}, u32[]{:S(2)}) %collective-permute-start.8) | collective-permute-done | bytes 131104 | tf_op jit(solution)/shard_map/ppermute | solution.py:458
  38.2 0.5 lead.1.after_ref
  38.7 4.6 %collective-permute-start.10 = (f32[128,128]{1,0:T(8,128)S(1)}, f32[128,128]{1,0:T(8,128)S(1)}, u32[]{:S(2)}, u32[]{:S(2)}) collective-permute-start(f32[128,128]{1,0:T(8,128)S(1)} %lead.1.after_ref), channel_id=1, source_target_pairs={{0,16},{8,15},{1,17},{9,14},{2,18},{10,13},{3,19},{11,12},{4,20},{... | collective-permute-start | bytes 196616 | tf_op jit(solution)/shard_map/ppermute | solution.py:514
  43.2 0.6 %fuse.1.fuse_ref = f32[4,256,128]{2,1,0:T(8,128)S(1)} custom-call(f32[256,128]{1,0:T(8,128)S(1)} %column.1.refs_9_.s0, f32[256,128]{1,0:T(8,128)S(1)} %collective-permute-done.7.s1, f32[256,128]{1,0:T(8,128)S(1)} %collective-permute-done.8.s2, f32[256,128]{1,0:T(8,128)S(1)} %collective-permute-done.9.s3, ...), custom_call_target="tpu_custom_call" | custom-call | tf_op jit(solution)/shard_map/fuse/pallas_call | solution.py:415
  43.9 0.0 copy-start.2
  43.9 1.7 %collective-permute-done.10.early_ref = f32[128,128]{1,0:T(8,128)S(1)} collective-permute-done((f32[128,128]{1,0:T(8,128)S(1)}, f32[128,128]{1,0:T(8,128)S(1)}, u32[]{:S(2)}, u32[]{:S(2)}) %collective-permute-start.10) | collective-permute-done | bytes 65568 | tf_op jit(solution)/shard_map/ppermute | solution.py:514
  45.6 0.3 entry.1
  45.9 1.6 %collective-permute-start.13 = (f32[128,128]{1,0:T(8,128)S(1)}, f32[128,128]{1,0:T(8,128)S(1)}, u32[]{:S(2)}, u32[]{:S(2)}) collective-permute-start(f32[128,128]{1,0:T(8,128)S(1)} %get-tuple-element.49), channel_id=1, source_target_pairs={{0,64},{8,40},{16,80},{24,56},{32,96},{40,8},{48,112},{56,24},{64,... | collective-permute-start | bytes 196616 | tf_op jit(solution)/shard_map/ppermute | solution.py:458
  47.5 1.8 %collective-permute-start.12 = (f32[128,128]{1,0:T(8,128)S(1)}, f32[128,128]{1,0:T(8,128)S(1)}, u32[]{:S(2)}, u32[]{:S(2)}) collective-permute-start(f32[128,128]{1,0:T(8,128)S(1)} %get-tuple-element.48), channel_id=1, source_target_pairs={{0,64},{8,24},{16,80},{24,40},{32,96},{40,56},{48,112},{56,8},{64,... | collective-permute-start | bytes 196616 | tf_op jit(solution)/shard_map/ppermute | solution.py:458
  49.2 0.9 %collective-permute-start.11 = (f32[128,128]{1,0:T(8,128)S(1)}, f32[128,128]{1,0:T(8,128)S(1)}, u32[]{:S(2)}, u32[]{:S(2)}) collective-permute-start(f32[128,128]{1,0:T(8,128)S(1)} %get-tuple-element.47), channel_id=1, source_target_pairs={{0,64},{8,56},{16,80},{24,8},{32,96},{40,24},{48,112},{56,40},{64,... | collective-permute-start | bytes 196616 | tf_op jit(solution)/shard_map/ppermute | solution.py:458
  50.1 0.0 collective-permute-start.14
  50.1 1.2 %reach.7 = (bf16[256,256]{1,0:T(8,128)(2,1)S(1)}, f32[256,128]{1,0:T(8,128)S(1)}) custom-call(bf16[1024,128]{1,0:T(8,128)(2,1)S(1)} %bitcast.7, bf16[4,512,128]{2,1,0:T(8,128)(2,1)S(1)} %get-tuple-element.32.r_ref, f32[4,4,256,128]{3,2,1,0:T(8,128)S(1)} %get-tuple-element.33.z_ref, f32[4,256,128]{2,1,0:T(8,128)S(1)} %collective-permute-done.sib_ref, ...), custom_call_target="tpu_custom_call" | custom-call | flops 400000000 | bytes 3000000 | tf_op jit(solution)/shard_map/reach/pallas_call | solution.py:328
  51.3 0.0 collective-permute-done.13.refs_9_
  51.3 0.5 collective-permute-done.12.refs_10_
  51.8 0.6 %collective-permute-done.11.refs_11_ = f32[128,128]{1,0:T(8,128)S(1)} collective-permute-done((f32[128,128]{1,0:T(8,128)S(1)}, f32[128,128]{1,0:T(8,128)S(1)}, u32[]{:S(2)}, u32[]{:S(2)}) %collective-permute-start.11) | collective-permute-done | bytes 65568 | tf_op jit(solution)/shard_map/ppermute | solution.py:458
  52.4 0.5 collective-permute-start.16
  52.9 0.0 collective-permute-start.15
  52.9 0.7 %collective-permute-done.17.refs_15_ = f32[128,128]{1,0:T(8,128)S(1)} collective-permute-done((f32[128,128]{1,0:T(8,128)S(1)}, f32[128,128]{1,0:T(8,128)S(1)}, u32[]{:S(2)}, u32[]{:S(2)}) %collective-permute-start.17) | collective-permute-done | bytes 65568 | tf_op jit(solution)/shard_map/ppermute | solution.py:458
  53.6 0.2 collective-permute-done.16.refs_14_
  53.8 0.4 collective-permute-done.15.refs_13_
  54.1 1.3 %read.1 = bf16[1024,128]{1,0:T(8,128)(2,1)} custom-call(bf16[256,256]{1,0:T(8,128)(2,1)S(1)} %get-tuple-element.36.after_ref.refs_0_, f32[256,128]{1,0:T(8,128)S(1)} %get-tuple-element.37.refs_1_, bf16[256,256]{1,0:T(8,128)(2,1)S(1)} %get-tuple-element.41.after_ref.refs_2_, f32[256,128]{1,0:T(8,128)S(1)} %get-tuple-element.42.refs_3_, ...), custom_call_target="tpu_custom_call" | custom-call | tf_op jit(solution)/shard_map/read/pallas_call | solution.py:397
  (7 shorter events, 0.0 us)
Async XLA Ops:
  0.0 17.2 %copy-start = (bf16[1,256,4,128]{3,2,1,0:T(4,128)(2,1)S(1)}, bf16[1,256,4,128]{3,2,1,0:T(4,128)(2,1)}, u32[]{:S(2)}) copy-start(bf16[1,256,4,128]{3,2,1,0:T(4,128)(2,1)} %param.5) | copy-start | bytes 786436
  8.2 4.9 %collective-permute-start = (f32[4,256,128]{2,1,0:T(8,128)S(1)}, f32[4,256,128]{2,1,0:T(8,128)S(1)}, u32[]{:S(2)}, u32[]{:S(2)}) collective-permute-start(f32[4,256,128]{2,1,0:T(8,128)S(1)} %get-tuple-element.34.own_ref), channel_id=1, source_target_pairs={{0,8},{8,0},{16,24},{24,16},{32,40},{40,32},{48,56},{56,48},{64,72... | collective-permute-start | bytes 1572872 | tf_op jit(solution)/shard_map/ppermute | solution.py:482
  13.4 5.5 %collective-permute-start.1 = (f32[256,128]{1,0:T(8,128)S(1)}, f32[256,128]{1,0:T(8,128)S(1)}, u32[]{:S(2)}, u32[]{:S(2)}) collective-permute-start(f32[256,128]{1,0:T(8,128)S(1)} %get-tuple-element.38), channel_id=1, source_target_pairs={{0,64},{8,40},{16,80},{24,56},{32,96},{40,8},{48,112},{56,24},{64,... | collective-permute-start | bytes 393224 | tf_op jit(solution)/shard_map/ppermute | solution.py:458
  14.5 5.7 %collective-permute-start.2 = (f32[256,128]{1,0:T(8,128)S(1)}, f32[256,128]{1,0:T(8,128)S(1)}, u32[]{:S(2)}, u32[]{:S(2)}) collective-permute-start(f32[256,128]{1,0:T(8,128)S(1)} %get-tuple-element.39), channel_id=1, source_target_pairs={{0,64},{8,24},{16,80},{24,40},{32,96},{40,56},{48,112},{56,8},{64,... | collective-permute-start | bytes 393224 | tf_op jit(solution)/shard_map/ppermute | solution.py:458
  14.8 5.4 %collective-permute-start.3 = (f32[256,128]{1,0:T(8,128)S(1)}, f32[256,128]{1,0:T(8,128)S(1)}, u32[]{:S(2)}, u32[]{:S(2)}) collective-permute-start(f32[256,128]{1,0:T(8,128)S(1)} %get-tuple-element.40), channel_id=1, source_target_pairs={{0,64},{8,56},{16,80},{24,8},{32,96},{40,24},{48,112},{56,40},{64,... | collective-permute-start | bytes 393224 | tf_op jit(solution)/shard_map/ppermute | solution.py:458
  20.7 12.6 %copy-start.1 = (f32[4,128,128]{2,1,0:T(8,128)S(1)}, f32[4,128,128]{2,1,0:T(8,128)}, u32[]{:S(2)}) copy-start(f32[4,128,128]{2,1,0:T(8,128)} %refs_8_.1) | copy-start | bytes 786436
  20.7 5.4 %collective-permute-start.6 = (f32[256,128]{1,0:T(8,128)S(1)}, f32[256,128]{1,0:T(8,128)S(1)}, u32[]{:S(2)}, u32[]{:S(2)}) collective-permute-start(f32[256,128]{1,0:T(8,128)S(1)} %row.1.after_ref.s0.refs_4_), channel_id=1, source_target_pairs={{0,16},{8,136},{16,0},{24,152},{32,48},{40,168},{48,32},{56,184},{... | collective-permute-start | bytes 393224 | tf_op jit(solution)/shard_map/ppermute | solution.py:458
  23.0 5.0 %collective-permute-start.5 = (f32[256,128]{1,0:T(8,128)S(1)}, f32[256,128]{1,0:T(8,128)S(1)}, u32[]{:S(2)}, u32[]{:S(2)}) collective-permute-start(f32[256,128]{1,0:T(8,128)S(1)} %row.1.after_ref.s0.refs_4_), channel_id=1, source_target_pairs={{0,16},{8,200},{16,0},{24,216},{32,48},{40,232},{48,32},{56,248},{... | collective-permute-start | bytes 393224 | tf_op jit(solution)/shard_map/ppermute | solution.py:458
  23.8 4.3 %collective-permute-start.4 = (f32[256,128]{1,0:T(8,128)S(1)}, f32[256,128]{1,0:T(8,128)S(1)}, u32[]{:S(2)}, u32[]{:S(2)}) collective-permute-start(f32[256,128]{1,0:T(8,128)S(1)} %row.1.after_ref.s0.refs_4_), channel_id=1, source_target_pairs={{0,16},{8,72},{16,0},{24,88},{32,48},{40,104},{48,32},{56,120},{64... | collective-permute-start | bytes 393224 | tf_op jit(solution)/shard_map/ppermute | solution.py:458
  28.5 6.8 %collective-permute-start.9 = (f32[256,128]{1,0:T(8,128)S(1)}, f32[256,128]{1,0:T(8,128)S(1)}, u32[]{:S(2)}, u32[]{:S(2)}) collective-permute-start(f32[256,128]{1,0:T(8,128)S(1)} %column.1.refs_9_.s0), channel_id=1, source_target_pairs={{0,16},{8,11},{1,17},{9,10},{2,18},{10,9},{3,19},{11,8},{4,20},{12... | collective-permute-start | bytes 393224 | tf_op jit(solution)/shard_map/ppermute | solution.py:458
  33.0 5.2 %collective-permute-start.8 = (f32[256,128]{1,0:T(8,128)S(1)}, f32[256,128]{1,0:T(8,128)S(1)}, u32[]{:S(2)}, u32[]{:S(2)}) collective-permute-start(f32[256,128]{1,0:T(8,128)S(1)} %column.1.refs_9_.s0), channel_id=1, source_target_pairs={{0,16},{8,10},{1,17},{9,11},{2,18},{10,8},{3,19},{11,9},{4,20},{12... | collective-permute-start | bytes 393224 | tf_op jit(solution)/shard_map/ppermute | solution.py:458
  33.0 5.2 %collective-permute-start.7 = (f32[256,128]{1,0:T(8,128)S(1)}, f32[256,128]{1,0:T(8,128)S(1)}, u32[]{:S(2)}, u32[]{:S(2)}) collective-permute-start(f32[256,128]{1,0:T(8,128)S(1)} %column.1.refs_9_.s0), channel_id=1, source_target_pairs={{0,16},{8,9},{1,17},{9,8},{2,18},{10,11},{3,19},{11,10},{4,20},{12... | collective-permute-start | bytes 393224 | tf_op jit(solution)/shard_map/ppermute | solution.py:458
  38.7 6.9 %collective-permute-start.10 = (f32[128,128]{1,0:T(8,128)S(1)}, f32[128,128]{1,0:T(8,128)S(1)}, u32[]{:S(2)}, u32[]{:S(2)}) collective-permute-start(f32[128,128]{1,0:T(8,128)S(1)} %lead.1.after_ref), channel_id=1, source_target_pairs={{0,16},{8,15},{1,17},{9,14},{2,18},{10,13},{3,19},{11,12},{4,20},{... | collective-permute-start | bytes 196616 | tf_op jit(solution)/shard_map/ppermute | solution.py:514
  43.9 10.3 %copy-start.2 = (f32[4,128]{1,0:T(4,128)S(1)}, f32[4,128]{1,0:T(4,128)}, u32[]{:S(2)}) copy-start(f32[4,128]{1,0:T(4,128)} %refs_16_.1) | copy-start | bytes 6148
  45.9 5.4 %collective-permute-start.13 = (f32[128,128]{1,0:T(8,128)S(1)}, f32[128,128]{1,0:T(8,128)S(1)}, u32[]{:S(2)}, u32[]{:S(2)}) collective-permute-start(f32[128,128]{1,0:T(8,128)S(1)} %get-tuple-element.49), channel_id=1, source_target_pairs={{0,64},{8,40},{16,80},{24,56},{32,96},{40,8},{48,112},{56,24},{64,... | collective-permute-start | bytes 196616 | tf_op jit(solution)/shard_map/ppermute | solution.py:458
  47.5 4.3 %collective-permute-start.12 = (f32[128,128]{1,0:T(8,128)S(1)}, f32[128,128]{1,0:T(8,128)S(1)}, u32[]{:S(2)}, u32[]{:S(2)}) collective-permute-start(f32[128,128]{1,0:T(8,128)S(1)} %get-tuple-element.48), channel_id=1, source_target_pairs={{0,64},{8,24},{16,80},{24,40},{32,96},{40,56},{48,112},{56,8},{64,... | collective-permute-start | bytes 196616 | tf_op jit(solution)/shard_map/ppermute | solution.py:458
  49.2 3.1 %collective-permute-start.11 = (f32[128,128]{1,0:T(8,128)S(1)}, f32[128,128]{1,0:T(8,128)S(1)}, u32[]{:S(2)}, u32[]{:S(2)}) collective-permute-start(f32[128,128]{1,0:T(8,128)S(1)} %get-tuple-element.47), channel_id=1, source_target_pairs={{0,64},{8,56},{16,80},{24,8},{32,96},{40,24},{48,112},{56,40},{64,... | collective-permute-start | bytes 196616 | tf_op jit(solution)/shard_map/ppermute | solution.py:458
  50.1 2.7 %collective-permute-start.14 = (f32[128,128]{1,0:T(8,128)S(1)}, f32[128,128]{1,0:T(8,128)S(1)}, u32[]{:S(2)}, u32[]{:S(2)}) collective-permute-start(f32[128,128]{1,0:T(8,128)S(1)} %get-tuple-element.50.after_ref.refs_8_), channel_id=1, source_target_pairs={{0,8},{8,0},{16,24},{24,16},{32,40},{40,32},{48,56},{56,48},{64,72... | collective-permute-start | bytes 196616 | tf_op jit(solution)/shard_map/ppermute | solution.py:537
  52.4 1.3 %collective-permute-start.17 = (f32[128,128]{1,0:T(8,128)S(1)}, f32[128,128]{1,0:T(8,128)S(1)}, u32[]{:S(2)}, u32[]{:S(2)}) collective-permute-start(f32[128,128]{1,0:T(8,128)S(1)} %collective-permute-done.11.refs_11_), channel_id=1, source_target_pairs={{0,8},{8,0},{16,24},{24,16},{32,40},{40,32},{48,56},{56,48},{64,72... | collective-permute-start | bytes 196616 | tf_op jit(solution)/shard_map/ppermute | solution.py:458
  52.4 1.4 %collective-permute-start.16 = (f32[128,128]{1,0:T(8,128)S(1)}, f32[128,128]{1,0:T(8,128)S(1)}, u32[]{:S(2)}, u32[]{:S(2)}) collective-permute-start(f32[128,128]{1,0:T(8,128)S(1)} %collective-permute-done.12.refs_10_), channel_id=1, source_target_pairs={{0,8},{8,0},{16,24},{24,16},{32,40},{40,32},{48,56},{56,48},{64,72... | collective-permute-start | bytes 196616 | tf_op jit(solution)/shard_map/ppermute | solution.py:458
  52.9 1.3 %collective-permute-start.15 = (f32[128,128]{1,0:T(8,128)S(1)}, f32[128,128]{1,0:T(8,128)S(1)}, u32[]{:S(2)}, u32[]{:S(2)}) collective-permute-start(f32[128,128]{1,0:T(8,128)S(1)} %collective-permute-done.13.refs_9_), channel_id=1, source_target_pairs={{0,8},{8,0},{16,24},{24,16},{32,40},{40,32},{48,56},{56,48},{64,72... | collective-permute-start | bytes 196616 | tf_op jit(solution)/shard_map/ppermute | solution.py:458

commit v12 on v11

--- a/solution.py
+++ b/solution.py
@@ -191,14 +191,8 @@
 def chip_kernel(own_ref, sib_ref, *out_refs):
     x = place_x()
     for k in range(XS):
-        head = lax.rem(x + k, HEADS)
+        head = x ^ k
         out_refs[k][...] = compose(sib_ref[head], own_ref[head])
-
-
-def ordered_cyclic(slots, place, scratch):
-    n = len(slots)
-    for k in range(n):
-        scratch[lax.rem(place + n - k, n)] = slots[k][...]
 
 
 def ordered_xor(slots, place, scratch):
@@ -221,7 +215,7 @@
 
 
 def row_kernel(s0, s2, s1, s3, after_ref, total_ref, hold):
-    ordered_cyclic([s0, s1, s2, s3], place_x(), hold)
+    ordered_xor([s0, s1, s2, s3], place_x(), hold)
     write_total(total_ref, hold)
 
 
@@ -245,7 +239,7 @@
     init_ref, after_ref, path_ref, start_ref, xhold, yhold = refs[8:]
     x = place_x()
     y = place_y()
-    ordered_cyclic(xslots, x, xhold)
+    ordered_xor(xslots, x, xhold)
     ordered_xor(yslots, y, yhold)
     here = place_prefix(y, yhold)
     first = xhold[0]
@@ -286,7 +280,7 @@
     for i in range(XS):
         scratch[i] = mm_pre(left, tall_wide(fuse_ref[i, :D, :])) + fuse_ref[i, D:, :]
     for k, out in enumerate((o0, o1, o2, o3)):
-        out[...] = scratch[lax.rem(x + k, XS)]
+        out[...] = scratch[x ^ k]
 
 
 def reach_kernel(
@@ -362,11 +356,11 @@
 
     @pl.when(place_core() == 0)
     def _():
-        ordered_cyclic(other, x, states)
+        ordered_xor(other, x, states)
 
     @pl.when(place_core() != 0)
     def _():
-        ordered_cyclic(mine, x, states)
+        ordered_xor(mine, x, states)
 
     rights = []
     for h in range(HEADS):
@@ -466,7 +460,7 @@
     near_x = lambda y, x: (y, x ^ 1)
     near_y = lambda y, x: (y ^ 1, x)
     along_x = [
-        plane_perm(lambda y, x, k=k: (y, (x + k) % XS), near_y) for k in range(1, XS)
+        plane_perm(lambda y, x, k=k: (y, x ^ k), near_y) for k in range(1, XS)
     ]
     along_y = [plane_perm(lambda y, x, k=k: (y ^ k, x), near_x) for k in range(1, YS)]
     segs = lax.axis_size("seg")

time: 55.7 us -> 55.6 us (level)
  starting transfers between devices: 24.3 us -> 23.3 us
  waiting for transfers between devices: 13.5 us -> 14.5 us
    ppermute x15, starting transfers between devices: 16.4 us -> 15.4 us  [exchange(): out[k] = lax.ppermute(slots[k], axis, perms[k - 1])]
    ppermute x15, waiting for transfers between devices: 10.2 us -> 11.2 us  [exchange(): out[k] = lax.ppermute(slots[k], axis, perms[k - 1])]
  transfers between devices with their start and end apart: 18 -> 18, of which waited for: 13 -> 14; matrix products, arithmetic and copies ran while one was open for 0% -> 0% of each run, Pallas kernels for 11% -> 11%
where the time goes in v12:
time: 55.6 us; the launch traced here: 55.5 us
  starting transfers between devices  23.3 us (42%)
  Pallas kernels  17.5 us (31%)
  waiting for transfers between devices  14.5 us (26%)
    ppermute x15, starting transfers between devices, exchange(): out[k] = lax.ppermute(slots[k], axis, perms[k - 1])  15.4 us
    ppermute x15, waiting for transfers between devices, exchange(): out[k] = lax.ppermute(slots[k], axis, perms[k - 1])  11.2 us
    pallas_call x1, Pallas kernels, factor_call(): pl.pallas_call(factor_kernel, in_specs=[pl.BlockSpec(memory_space=pl.ANY)...  8.23 us
    pallas_call x4, Pallas kernels, reach_call(): pl.pallas_call(functools.partial(reach_kernel, head=head), grid=(1,), in_...  4.71 us
    ppermute x1, starting transfers between devices, per_device(): early = lax.ppermute(lead, ('seq', 'seg'), jump)  4.57 us
    ppermute x1, starting transfers between devices, per_device(): sib = lax.ppermute(pair, 'seq', swap)  3.33 us
    pallas_call x7, Pallas kernels, small_call(): pl.pallas_call(kernel, in_specs=whole(*arrays) + [pl.BlockSpec(memory_spa...  3.24 us
    ppermute x1, waiting for transfers between devices, per_device(): early = lax.ppermute(lead, ('seq', 'seg'), jump)  1.74 us
  transfers between devices with their start and end apart: 18, of which 14 were waited for; matrix products, arithmetic and copies ran while one was open for 0% of the time, Pallas kernels for 11%

profile of v12, /device:TPU:1, one launch (start us, length us, event | category | flops | bytes accessed | tf_op | source)
XLA Modules:
  0.0 55.5 jit_solution(1176525912626642281)
XLA Ops:
  0.0 8.2 %factor.1 = (f32[4,256,128]{2,1,0:T(8,128)S(1)}, f32[4,4,256,128]{3,2,1,0:T(8,128)S(1)}, bf16[4,512,128]{2,1,0:T(8,128)(2,1)S(1)}) custom-call(bf16[2048,128]{1,0:T(8,128)(2,1)} %bitcast.8, bf16[2048,128]{1,0:T(8,128)(2,1)} %bitcast.9), custom_call_target="tpu_custom_call" | custom-call | tf_op jit(solution)/shard_map/factor/pallas_call | solution.py:174
  8.2 3.3 %collective-permute-start = (f32[4,256,128]{2,1,0:T(8,128)S(1)}, f32[4,256,128]{2,1,0:T(8,128)S(1)}, u32[]{:S(2)}, u32[]{:S(2)}) collective-permute-start(f32[4,256,128]{2,1,0:T(8,128)S(1)} %get-tuple-element.34.own_ref), channel_id=1, source_target_pairs={{0,8},{8,0},{16,24},{24,16},{32,40},{40,32},{48,56},{56,48},{64,72... | collective-permute-start | bytes 1572872 | tf_op jit(solution)/shard_map/ppermute | solution.py:476
  11.6 1.5 %collective-permute-done.sib_ref = f32[4,256,128]{2,1,0:T(8,128)S(1)} collective-permute-done((f32[4,256,128]{2,1,0:T(8,128)S(1)}, f32[4,256,128]{2,1,0:T(8,128)S(1)}, u32[]{:S(2)}, u32[]{:S(2)}) %collective-permute-start) | collective-permute-done | bytes 524320 | tf_op jit(solution)/shard_map/ppermute | solution.py:476
  13.1 0.3 chip.1
  13.4 1.1 %collective-permute-start.1 = (f32[256,128]{1,0:T(8,128)S(1)}, f32[256,128]{1,0:T(8,128)S(1)}, u32[]{:S(2)}, u32[]{:S(2)}) collective-permute-start(f32[256,128]{1,0:T(8,128)S(1)} %get-tuple-element.38), channel_id=1, source_target_pairs={{0,64},{8,40},{16,80},{24,56},{32,96},{40,8},{48,112},{56,24},{64,... | collective-permute-start | bytes 393224 | tf_op jit(solution)/shard_map/ppermute | solution.py:452
  14.5 0.3 collective-permute-start.2
  14.8 1.9 %collective-permute-start.3 = (f32[256,128]{1,0:T(8,128)S(1)}, f32[256,128]{1,0:T(8,128)S(1)}, u32[]{:S(2)}, u32[]{:S(2)}) collective-permute-start(f32[256,128]{1,0:T(8,128)S(1)} %get-tuple-element.40), channel_id=1, source_target_pairs={{0,64},{8,56},{16,80},{24,40},{32,96},{40,24},{48,112},{56,8},{64,... | collective-permute-start | bytes 393224 | tf_op jit(solution)/shard_map/ppermute | solution.py:452
  16.8 1.2 %reach.4 = (bf16[256,256]{1,0:T(8,128)(2,1)S(1)}, f32[256,128]{1,0:T(8,128)S(1)}) custom-call(bf16[1024,128]{1,0:T(8,128)(2,1)S(1)} %bitcast.4, bf16[4,512,128]{2,1,0:T(8,128)(2,1)S(1)} %get-tuple-element.32.r_ref, f32[4,4,256,128]{3,2,1,0:T(8,128)S(1)} %get-tuple-element.33.z_ref, f32[4,256,128]{2,1,0:T(8,128)S(1)} %collective-permute-done.sib_ref, ...), custom_call_target="tpu_custom_call" | custom-call | flops 400000000 | bytes 3000000 | tf_op jit(solution)/shard_map/reach/pallas_call | solution.py:322
  18.0 0.9 %collective-permute-done.1.s2.refs_2_ = f32[256,128]{1,0:T(8,128)S(1)} collective-permute-done((f32[256,128]{1,0:T(8,128)S(1)}, f32[256,128]{1,0:T(8,128)S(1)}, u32[]{:S(2)}, u32[]{:S(2)}) %collective-permute-start.1) | collective-permute-done | bytes 131104 | tf_op jit(solution)/shard_map/ppermute | solution.py:452
  18.9 0.0 collective-permute-done.2.s1.refs_1_
  18.9 1.4 %collective-permute-done.3.s3.refs_3_ = f32[256,128]{1,0:T(8,128)S(1)} collective-permute-done((f32[256,128]{1,0:T(8,128)S(1)}, f32[256,128]{1,0:T(8,128)S(1)}, u32[]{:S(2)}, u32[]{:S(2)}) %collective-permute-start.3) | collective-permute-done | bytes 131104 | tf_op jit(solution)/shard_map/ppermute | solution.py:452
  20.2 0.5 row.1.after_ref.s0.refs_4_
  20.7 0.0 copy-start.1
  20.7 2.6 %collective-permute-start.6 = (f32[256,128]{1,0:T(8,128)S(1)}, f32[256,128]{1,0:T(8,128)S(1)}, u32[]{:S(2)}, u32[]{:S(2)}) collective-permute-start(f32[256,128]{1,0:T(8,128)S(1)} %row.1.after_ref.s0.refs_4_), channel_id=1, source_target_pairs={{0,16},{8,136},{16,0},{24,152},{32,48},{40,168},{48,32},{56,184},{... | collective-permute-start | bytes 393224 | tf_op jit(solution)/shard_map/ppermute | solution.py:452
  23.4 0.8 %collective-permute-start.5 = (f32[256,128]{1,0:T(8,128)S(1)}, f32[256,128]{1,0:T(8,128)S(1)}, u32[]{:S(2)}, u32[]{:S(2)}) collective-permute-start(f32[256,128]{1,0:T(8,128)S(1)} %row.1.after_ref.s0.refs_4_), channel_id=1, source_target_pairs={{0,16},{8,200},{16,0},{24,216},{32,48},{40,232},{48,32},{56,248},{... | collective-permute-start | bytes 393224 | tf_op jit(solution)/shard_map/ppermute | solution.py:452
  24.1 0.0 collective-permute-start.4
  24.1 1.2 %reach.5 = (bf16[256,256]{1,0:T(8,128)(2,1)S(1)}, f32[256,128]{1,0:T(8,128)S(1)}) custom-call(bf16[1024,128]{1,0:T(8,128)(2,1)S(1)} %bitcast.5, bf16[4,512,128]{2,1,0:T(8,128)(2,1)S(1)} %get-tuple-element.32.r_ref, f32[4,4,256,128]{3,2,1,0:T(8,128)S(1)} %get-tuple-element.33.z_ref, f32[4,256,128]{2,1,0:T(8,128)S(1)} %collective-permute-done.sib_ref, ...), custom_call_target="tpu_custom_call" | custom-call | flops 400000000 | bytes 3000000 | tf_op jit(solution)/shard_map/reach/pallas_call | solution.py:322
  25.3 0.8 %collective-permute-done.6.s2.refs_7_ = f32[256,128]{1,0:T(8,128)S(1)} collective-permute-done((f32[256,128]{1,0:T(8,128)S(1)}, f32[256,128]{1,0:T(8,128)S(1)}, u32[]{:S(2)}, u32[]{:S(2)}) %collective-permute-start.6) | collective-permute-done | bytes 131104 | tf_op jit(solution)/shard_map/ppermute | solution.py:452
  26.1 2.2 %collective-permute-done.5.s3.refs_6_ = f32[256,128]{1,0:T(8,128)S(1)} collective-permute-done((f32[256,128]{1,0:T(8,128)S(1)}, f32[256,128]{1,0:T(8,128)S(1)}, u32[]{:S(2)}, u32[]{:S(2)}) %collective-permute-start.5) | collective-permute-done | bytes 131104 | tf_op jit(solution)/shard_map/ppermute | solution.py:452
  28.4 0.0 collective-permute-done.4.s1.refs_5_
  28.4 0.5 column.1.refs_9_.s0
  28.9 4.4 %collective-permute-start.9 = (f32[256,128]{1,0:T(8,128)S(1)}, f32[256,128]{1,0:T(8,128)S(1)}, u32[]{:S(2)}, u32[]{:S(2)}) collective-permute-start(f32[256,128]{1,0:T(8,128)S(1)} %column.1.refs_9_.s0), channel_id=1, source_target_pairs={{0,16},{8,11},{1,17},{9,10},{2,18},{10,9},{3,19},{11,8},{4,20},{12... | collective-permute-start | bytes 393224 | tf_op jit(solution)/shard_map/ppermute | solution.py:452
  33.3 0.4 collective-permute-start.7
  33.7 0.7 %path.1 = (f32[4,256,128]{2,1,0:T(8,128)S(1)}, f32[128,128]{1,0:T(8,128)S(1)}) custom-call(f32[256,128]{1,0:T(8,128)S(1)} %get-tuple-element.35.after_ref.s0.refs_0_, f32[256,128]{1,0:T(8,128)S(1)} %collective-permute-done.2.s1.refs_1_, f32[256,128]{1,0:T(8,128)S(1)} %collective-permute-done.1.s2.refs_2_, f32[256,128]{1,0:T(8,128)S(1)} %collective-permute-done.3.s3.refs_3_, ...), custom_call_target="tpu_custom_call" | custom-call | tf_op jit(solution)/shard_map/path/pallas_call | solution.py:409
  34.3 1.2 %reach.6 = (bf16[256,256]{1,0:T(8,128)(2,1)S(1)}, f32[256,128]{1,0:T(8,128)S(1)}) custom-call(bf16[1024,128]{1,0:T(8,128)(2,1)S(1)} %bitcast.6, bf16[4,512,128]{2,1,0:T(8,128)(2,1)S(1)} %get-tuple-element.32.r_ref, f32[4,4,256,128]{3,2,1,0:T(8,128)S(1)} %get-tuple-element.33.z_ref, f32[4,256,128]{2,1,0:T(8,128)S(1)} %collective-permute-done.sib_ref, ...), custom_call_target="tpu_custom_call" | custom-call | flops 400000000 | bytes 3000000 | tf_op jit(solution)/shard_map/reach/pallas_call | solution.py:322
  35.5 0.2 collective-permute-done.9.s3
  35.7 2.8 %collective-permute-done.8.s2 = f32[256,128]{1,0:T(8,128)S(1)} collective-permute-done((f32[256,128]{1,0:T(8,128)S(1)}, f32[256,128]{1,0:T(8,128)S(1)}, u32[]{:S(2)}, u32[]{:S(2)}) %collective-permute-start.8) | collective-permute-done | bytes 131104 | tf_op jit(solution)/shard_map/ppermute | solution.py:452
  38.5 0.0 collective-permute-done.7.s1
  38.5 0.5 lead.1.after_ref
  39.0 4.6 %collective-permute-start.10 = (f32[128,128]{1,0:T(8,128)S(1)}, f32[128,128]{1,0:T(8,128)S(1)}, u32[]{:S(2)}, u32[]{:S(2)}) collective-permute-start(f32[128,128]{1,0:T(8,128)S(1)} %lead.1.after_ref), channel_id=1, source_target_pairs={{0,16},{8,15},{1,17},{9,14},{2,18},{10,13},{3,19},{11,12},{4,20},{... | collective-permute-start | bytes 196616 | tf_op jit(solution)/shard_map/ppermute | solution.py:508
  43.6 0.6 %fuse.1.fuse_ref = f32[4,256,128]{2,1,0:T(8,128)S(1)} custom-call(f32[256,128]{1,0:T(8,128)S(1)} %column.1.refs_9_.s0, f32[256,128]{1,0:T(8,128)S(1)} %collective-permute-done.7.s1, f32[256,128]{1,0:T(8,128)S(1)} %collective-permute-done.8.s2, f32[256,128]{1,0:T(8,128)S(1)} %collective-permute-done.9.s3, ...), custom_call_target="tpu_custom_call" | custom-call | tf_op jit(solution)/shard_map/fuse/pallas_call | solution.py:409
  44.2 0.0 copy-start.2
  44.2 1.7 %collective-permute-done.10.early_ref = f32[128,128]{1,0:T(8,128)S(1)} collective-permute-done((f32[128,128]{1,0:T(8,128)S(1)}, f32[128,128]{1,0:T(8,128)S(1)}, u32[]{:S(2)}, u32[]{:S(2)}) %collective-permute-start.10) | collective-permute-done | bytes 65568 | tf_op jit(solution)/shard_map/ppermute | solution.py:508
  45.9 0.3 entry.1
  46.2 1.8 %collective-permute-start.13 = (f32[128,128]{1,0:T(8,128)S(1)}, f32[128,128]{1,0:T(8,128)S(1)}, u32[]{:S(2)}, u32[]{:S(2)}) collective-permute-start(f32[128,128]{1,0:T(8,128)S(1)} %get-tuple-element.49), channel_id=1, source_target_pairs={{0,64},{8,40},{16,80},{24,56},{32,96},{40,8},{48,112},{56,24},{64,... | collective-permute-start | bytes 196616 | tf_op jit(solution)/shard_map/ppermute | solution.py:452
  48.0 0.0 collective-permute-start.12
  48.0 1.5 %collective-permute-start.11 = (f32[128,128]{1,0:T(8,128)S(1)}, f32[128,128]{1,0:T(8,128)S(1)}, u32[]{:S(2)}, u32[]{:S(2)}) collective-permute-start(f32[128,128]{1,0:T(8,128)S(1)} %get-tuple-element.47), channel_id=1, source_target_pairs={{0,64},{8,56},{16,80},{24,40},{32,96},{40,24},{48,112},{56,8},{64,... | collective-permute-start | bytes 196616 | tf_op jit(solution)/shard_map/ppermute | solution.py:452
  49.5 0.0 collective-permute-start.14
  49.5 1.2 %reach.7 = (bf16[256,256]{1,0:T(8,128)(2,1)S(1)}, f32[256,128]{1,0:T(8,128)S(1)}) custom-call(bf16[1024,128]{1,0:T(8,128)(2,1)S(1)} %bitcast.7, bf16[4,512,128]{2,1,0:T(8,128)(2,1)S(1)} %get-tuple-element.32.r_ref, f32[4,4,256,128]{3,2,1,0:T(8,128)S(1)} %get-tuple-element.33.z_ref, f32[4,256,128]{2,1,0:T(8,128)S(1)} %collective-permute-done.sib_ref, ...), custom_call_target="tpu_custom_call" | custom-call | flops 400000000 | bytes 3000000 | tf_op jit(solution)/shard_map/reach/pallas_call | solution.py:322
  50.7 0.2 collective-permute-done.13.refs_9_
  50.9 0.2 collective-permute-done.12.refs_10_
  51.1 1.2 %collective-permute-done.11.refs_11_ = f32[128,128]{1,0:T(8,128)S(1)} collective-permute-done((f32[128,128]{1,0:T(8,128)S(1)}, f32[128,128]{1,0:T(8,128)S(1)}, u32[]{:S(2)}, u32[]{:S(2)}) %collective-permute-start.11) | collective-permute-done | bytes 65568 | tf_op jit(solution)/shard_map/ppermute | solution.py:452
  52.3 0.5 collective-permute-start.16
  52.8 0.0 collective-permute-start.15
  52.8 0.7 %collective-permute-done.17.refs_15_ = f32[128,128]{1,0:T(8,128)S(1)} collective-permute-done((f32[128,128]{1,0:T(8,128)S(1)}, f32[128,128]{1,0:T(8,128)S(1)}, u32[]{:S(2)}, u32[]{:S(2)}) %collective-permute-start.17) | collective-permute-done | bytes 65568 | tf_op jit(solution)/shard_map/ppermute | solution.py:452
  53.6 0.2 collective-permute-done.16.refs_14_
  53.7 0.4 collective-permute-done.15.refs_13_
  54.1 1.3 %read.1 = bf16[1024,128]{1,0:T(8,128)(2,1)} custom-call(bf16[256,256]{1,0:T(8,128)(2,1)S(1)} %get-tuple-element.36.after_ref.refs_0_, f32[256,128]{1,0:T(8,128)S(1)} %get-tuple-element.37.refs_1_, bf16[256,256]{1,0:T(8,128)(2,1)S(1)} %get-tuple-element.41.after_ref.refs_2_, f32[256,128]{1,0:T(8,128)S(1)} %get-tuple-element.42.refs_3_, ...), custom_call_target="tpu_custom_call" | custom-call | tf_op jit(solution)/shard_map/read/pallas_call | solution.py:391
  (7 shorter events, 0.0 us)
Async XLA Ops:
  0.0 16.8 %copy-start = (bf16[1,256,4,128]{3,2,1,0:T(4,128)(2,1)S(1)}, bf16[1,256,4,128]{3,2,1,0:T(4,128)(2,1)}, u32[]{:S(2)}) copy-start(bf16[1,256,4,128]{3,2,1,0:T(4,128)(2,1)} %param.5) | copy-start | bytes 786436
  8.2 4.9 %collective-permute-start = (f32[4,256,128]{2,1,0:T(8,128)S(1)}, f32[4,256,128]{2,1,0:T(8,128)S(1)}, u32[]{:S(2)}, u32[]{:S(2)}) collective-permute-start(f32[4,256,128]{2,1,0:T(8,128)S(1)} %get-tuple-element.34.own_ref), channel_id=1, source_target_pairs={{0,8},{8,0},{16,24},{24,16},{32,40},{40,32},{48,56},{56,48},{64,72... | collective-permute-start | bytes 1572872 | tf_op jit(solution)/shard_map/ppermute | solution.py:476
  13.4 5.4 %collective-permute-start.1 = (f32[256,128]{1,0:T(8,128)S(1)}, f32[256,128]{1,0:T(8,128)S(1)}, u32[]{:S(2)}, u32[]{:S(2)}) collective-permute-start(f32[256,128]{1,0:T(8,128)S(1)} %get-tuple-element.38), channel_id=1, source_target_pairs={{0,64},{8,40},{16,80},{24,56},{32,96},{40,8},{48,112},{56,24},{64,... | collective-permute-start | bytes 393224 | tf_op jit(solution)/shard_map/ppermute | solution.py:452
  14.5 4.4 %collective-permute-start.2 = (f32[256,128]{1,0:T(8,128)S(1)}, f32[256,128]{1,0:T(8,128)S(1)}, u32[]{:S(2)}, u32[]{:S(2)}) collective-permute-start(f32[256,128]{1,0:T(8,128)S(1)} %get-tuple-element.39), channel_id=1, source_target_pairs={{0,64},{8,24},{16,80},{24,8},{32,96},{40,56},{48,112},{56,40},{64,... | collective-permute-start | bytes 393224 | tf_op jit(solution)/shard_map/ppermute | solution.py:452
  14.8 5.4 %collective-permute-start.3 = (f32[256,128]{1,0:T(8,128)S(1)}, f32[256,128]{1,0:T(8,128)S(1)}, u32[]{:S(2)}, u32[]{:S(2)}) collective-permute-start(f32[256,128]{1,0:T(8,128)S(1)} %get-tuple-element.40), channel_id=1, source_target_pairs={{0,64},{8,56},{16,80},{24,40},{32,96},{40,24},{48,112},{56,8},{64,... | collective-permute-start | bytes 393224 | tf_op jit(solution)/shard_map/ppermute | solution.py:452
  20.7 13.0 %copy-start.1 = (f32[4,128,128]{2,1,0:T(8,128)S(1)}, f32[4,128,128]{2,1,0:T(8,128)}, u32[]{:S(2)}) copy-start(f32[4,128,128]{2,1,0:T(8,128)} %refs_8_.1) | copy-start | bytes 786436
  20.7 5.4 %collective-permute-start.6 = (f32[256,128]{1,0:T(8,128)S(1)}, f32[256,128]{1,0:T(8,128)S(1)}, u32[]{:S(2)}, u32[]{:S(2)}) collective-permute-start(f32[256,128]{1,0:T(8,128)S(1)} %row.1.after_ref.s0.refs_4_), channel_id=1, source_target_pairs={{0,16},{8,136},{16,0},{24,152},{32,48},{40,168},{48,32},{56,184},{... | collective-permute-start | bytes 393224 | tf_op jit(solution)/shard_map/ppermute | solution.py:452
  23.4 5.0 %collective-permute-start.5 = (f32[256,128]{1,0:T(8,128)S(1)}, f32[256,128]{1,0:T(8,128)S(1)}, u32[]{:S(2)}, u32[]{:S(2)}) collective-permute-start(f32[256,128]{1,0:T(8,128)S(1)} %row.1.after_ref.s0.refs_4_), channel_id=1, source_target_pairs={{0,16},{8,200},{16,0},{24,216},{32,48},{40,232},{48,32},{56,248},{... | collective-permute-start | bytes 393224 | tf_op jit(solution)/shard_map/ppermute | solution.py:452
  24.1 4.3 %collective-permute-start.4 = (f32[256,128]{1,0:T(8,128)S(1)}, f32[256,128]{1,0:T(8,128)S(1)}, u32[]{:S(2)}, u32[]{:S(2)}) collective-permute-start(f32[256,128]{1,0:T(8,128)S(1)} %row.1.after_ref.s0.refs_4_), channel_id=1, source_target_pairs={{0,16},{8,72},{16,0},{24,88},{32,48},{40,104},{48,32},{56,120},{64... | collective-permute-start | bytes 393224 | tf_op jit(solution)/shard_map/ppermute | solution.py:452
  28.9 6.8 %collective-permute-start.9 = (f32[256,128]{1,0:T(8,128)S(1)}, f32[256,128]{1,0:T(8,128)S(1)}, u32[]{:S(2)}, u32[]{:S(2)}) collective-permute-start(f32[256,128]{1,0:T(8,128)S(1)} %column.1.refs_9_.s0), channel_id=1, source_target_pairs={{0,16},{8,11},{1,17},{9,10},{2,18},{10,9},{3,19},{11,8},{4,20},{12... | collective-permute-start | bytes 393224 | tf_op jit(solution)/shard_map/ppermute | solution.py:452
  33.3 5.2 %collective-permute-start.8 = (f32[256,128]{1,0:T(8,128)S(1)}, f32[256,128]{1,0:T(8,128)S(1)}, u32[]{:S(2)}, u32[]{:S(2)}) collective-permute-start(f32[256,128]{1,0:T(8,128)S(1)} %column.1.refs_9_.s0), channel_id=1, source_target_pairs={{0,16},{8,10},{1,17},{9,11},{2,18},{10,8},{3,19},{11,9},{4,20},{12... | collective-permute-start | bytes 393224 | tf_op jit(solution)/shard_map/ppermute | solution.py:452
  33.3 5.2 %collective-permute-start.7 = (f32[256,128]{1,0:T(8,128)S(1)}, f32[256,128]{1,0:T(8,128)S(1)}, u32[]{:S(2)}, u32[]{:S(2)}) collective-permute-start(f32[256,128]{1,0:T(8,128)S(1)} %column.1.refs_9_.s0), channel_id=1, source_target_pairs={{0,16},{8,9},{1,17},{9,8},{2,18},{10,11},{3,19},{11,10},{4,20},{12... | collective-permute-start | bytes 393224 | tf_op jit(solution)/shard_map/ppermute | solution.py:452
  39.0 6.9 %collective-permute-start.10 = (f32[128,128]{1,0:T(8,128)S(1)}, f32[128,128]{1,0:T(8,128)S(1)}, u32[]{:S(2)}, u32[]{:S(2)}) collective-permute-start(f32[128,128]{1,0:T(8,128)S(1)} %lead.1.after_ref), channel_id=1, source_target_pairs={{0,16},{8,15},{1,17},{9,14},{2,18},{10,13},{3,19},{11,12},{4,20},{... | collective-permute-start | bytes 196616 | tf_op jit(solution)/shard_map/ppermute | solution.py:508
  44.2 9.9 %copy-start.2 = (f32[4,128]{1,0:T(4,128)S(1)}, f32[4,128]{1,0:T(4,128)}, u32[]{:S(2)}) copy-start(f32[4,128]{1,0:T(4,128)} %refs_16_.1) | copy-start | bytes 6148
  46.2 4.7 %collective-permute-start.13 = (f32[128,128]{1,0:T(8,128)S(1)}, f32[128,128]{1,0:T(8,128)S(1)}, u32[]{:S(2)}, u32[]{:S(2)}) collective-permute-start(f32[128,128]{1,0:T(8,128)S(1)} %get-tuple-element.49), channel_id=1, source_target_pairs={{0,64},{8,40},{16,80},{24,56},{32,96},{40,8},{48,112},{56,24},{64,... | collective-permute-start | bytes 196616 | tf_op jit(solution)/shard_map/ppermute | solution.py:452
  48.0 3.1 %collective-permute-start.12 = (f32[128,128]{1,0:T(8,128)S(1)}, f32[128,128]{1,0:T(8,128)S(1)}, u32[]{:S(2)}, u32[]{:S(2)}) collective-permute-start(f32[128,128]{1,0:T(8,128)S(1)} %get-tuple-element.48), channel_id=1, source_target_pairs={{0,64},{8,24},{16,80},{24,8},{32,96},{40,56},{48,112},{56,40},{64,... | collective-permute-start | bytes 196616 | tf_op jit(solution)/shard_map/ppermute | solution.py:452
  48.0 4.3 %collective-permute-start.11 = (f32[128,128]{1,0:T(8,128)S(1)}, f32[128,128]{1,0:T(8,128)S(1)}, u32[]{:S(2)}, u32[]{:S(2)}) collective-permute-start(f32[128,128]{1,0:T(8,128)S(1)} %get-tuple-element.47), channel_id=1, source_target_pairs={{0,64},{8,56},{16,80},{24,40},{32,96},{40,24},{48,112},{56,8},{64,... | collective-permute-start | bytes 196616 | tf_op jit(solution)/shard_map/ppermute | solution.py:452
  49.5 3.3 %collective-permute-start.14 = (f32[128,128]{1,0:T(8,128)S(1)}, f32[128,128]{1,0:T(8,128)S(1)}, u32[]{:S(2)}, u32[]{:S(2)}) collective-permute-start(f32[128,128]{1,0:T(8,128)S(1)} %get-tuple-element.50.after_ref.refs_8_), channel_id=1, source_target_pairs={{0,8},{8,0},{16,24},{24,16},{32,40},{40,32},{48,56},{56,48},{64,72... | collective-permute-start | bytes 196616 | tf_op jit(solution)/shard_map/ppermute | solution.py:531
  52.3 1.3 %collective-permute-start.17 = (f32[128,128]{1,0:T(8,128)S(1)}, f32[128,128]{1,0:T(8,128)S(1)}, u32[]{:S(2)}, u32[]{:S(2)}) collective-permute-start(f32[128,128]{1,0:T(8,128)S(1)} %collective-permute-done.11.refs_11_), channel_id=1, source_target_pairs={{0,8},{8,0},{16,24},{24,16},{32,40},{40,32},{48,56},{56,48},{64,72... | collective-permute-start | bytes 196616 | tf_op jit(solution)/shard_map/ppermute | solution.py:452
  52.3 1.4 %collective-permute-start.16 = (f32[128,128]{1,0:T(8,128)S(1)}, f32[128,128]{1,0:T(8,128)S(1)}, u32[]{:S(2)}, u32[]{:S(2)}) collective-permute-start(f32[128,128]{1,0:T(8,128)S(1)} %collective-permute-done.12.refs_10_), channel_id=1, source_target_pairs={{0,8},{8,0},{16,24},{24,16},{32,40},{40,32},{48,56},{56,48},{64,72... | collective-permute-start | bytes 196616 | tf_op jit(solution)/shard_map/ppermute | solution.py:452
  52.8 1.3 %collective-permute-start.15 = (f32[128,128]{1,0:T(8,128)S(1)}, f32[128,128]{1,0:T(8,128)S(1)}, u32[]{:S(2)}, u32[]{:S(2)}) collective-permute-start(f32[128,128]{1,0:T(8,128)S(1)} %collective-permute-done.13.refs_9_), channel_id=1, source_target_pairs={{0,8},{8,0},{16,24},{24,16},{32,40},{40,32},{48,56},{56,48},{64,72... | collective-permute-start | bytes 196616 | tf_op jit(solution)/shard_map/ppermute | solution.py:452

commit v13 on v12

--- a/solution.py
+++ b/solution.py
@@ -254,7 +254,7 @@
     start_ref[...] = init_ref[x].T
 
 
-def lead_kernel(s0, s1, s2, s3, start_ref, after_ref, lead_ref, hold):
+def lead_kernel(s0, s1, s3, s2, start_ref, after_ref, lead_ref, hold):
     ordered_xor([s0, s1, s2, s3], lax.rem(place_seg(), ZG), hold)
     tail = msg_compose(hold[2], hold[3])
     state = advance(advance(start_ref[...], hold[0]), hold[1])
@@ -500,7 +500,7 @@
     (lead,) = small_call(
         lead_kernel,
         "lead",
-        [*slots, start],
+        [*(slots[i] for i in (0, 1, 3, 2)), start],
         [(D, D)],
         [(ZG, MSG, D)],
         after=reaches[-1][0],

time: 55.6 us -> 56 us (level)
  no operation moved by 1% of the time
where the time goes in v13:
time: 56 us; the launch traced here: 55.9 us
  starting transfers between devices  23.5 us (42%)
  Pallas kernels  17.5 us (31%)
  waiting for transfers between devices  14.6 us (26%)
    ppermute x15, starting transfers between devices, exchange(): out[k] = lax.ppermute(slots[k], axis, perms[k - 1])  15.3 us
    ppermute x15, waiting for transfers between devices, exchange(): out[k] = lax.ppermute(slots[k], axis, perms[k - 1])  11.4 us
    pallas_call x1, Pallas kernels, factor_call(): pl.pallas_call(factor_kernel, in_specs=[pl.BlockSpec(memory_space=pl.ANY)...  8.23 us
    ppermute x1, starting transfers between devices, per_device(): early = lax.ppermute(lead, ('seq', 'seg'), jump)  4.88 us
    pallas_call x4, Pallas kernels, reach_call(): pl.pallas_call(functools.partial(reach_kernel, head=head), grid=(1,), in_...  4.71 us
    ppermute x1, starting transfers between devices, per_device(): sib = lax.ppermute(pair, 'seq', swap)  3.33 us
    pallas_call x7, Pallas kernels, small_call(): pl.pallas_call(kernel, in_specs=whole(*arrays) + [pl.BlockSpec(memory_spa...  3.24 us
    ppermute x1, waiting for transfers between devices, per_device(): early = lax.ppermute(lead, ('seq', 'seg'), jump)  1.74 us
  transfers between devices with their start and end apart: 18, of which 14 were waited for; matrix products, arithmetic and copies ran while one was open for 0% of the time, Pallas kernels for 11%

profile of v13, /device:TPU:1, one launch (start us, length us, event | category | flops | bytes accessed | tf_op | source)
XLA Modules:
  0.0 55.9 jit_solution(215129710218110581)
XLA Ops:
  0.0 8.2 %factor.1 = (f32[4,256,128]{2,1,0:T(8,128)S(1)}, f32[4,4,256,128]{3,2,1,0:T(8,128)S(1)}, bf16[4,512,128]{2,1,0:T(8,128)(2,1)S(1)}) custom-call(bf16[2048,128]{1,0:T(8,128)(2,1)} %bitcast.8, bf16[2048,128]{1,0:T(8,128)(2,1)} %bitcast.9), custom_call_target="tpu_custom_call" | custom-call | tf_op jit(solution)/shard_map/factor/pallas_call | solution.py:174
  8.2 3.3 %collective-permute-start = (f32[4,256,128]{2,1,0:T(8,128)S(1)}, f32[4,256,128]{2,1,0:T(8,128)S(1)}, u32[]{:S(2)}, u32[]{:S(2)}) collective-permute-start(f32[4,256,128]{2,1,0:T(8,128)S(1)} %get-tuple-element.34.own_ref), channel_id=1, source_target_pairs={{0,8},{8,0},{16,24},{24,16},{32,40},{40,32},{48,56},{56,48},{64,72... | collective-permute-start | bytes 1572872 | tf_op jit(solution)/shard_map/ppermute | solution.py:476
  11.6 1.5 %collective-permute-done.sib_ref = f32[4,256,128]{2,1,0:T(8,128)S(1)} collective-permute-done((f32[4,256,128]{2,1,0:T(8,128)S(1)}, f32[4,256,128]{2,1,0:T(8,128)S(1)}, u32[]{:S(2)}, u32[]{:S(2)}) %collective-permute-start) | collective-permute-done | bytes 524320 | tf_op jit(solution)/shard_map/ppermute | solution.py:476
  13.1 0.3 chip.1
  13.4 1.1 %collective-permute-start.1 = (f32[256,128]{1,0:T(8,128)S(1)}, f32[256,128]{1,0:T(8,128)S(1)}, u32[]{:S(2)}, u32[]{:S(2)}) collective-permute-start(f32[256,128]{1,0:T(8,128)S(1)} %get-tuple-element.38), channel_id=1, source_target_pairs={{0,64},{8,40},{16,80},{24,56},{32,96},{40,8},{48,112},{56,24},{64,... | collective-permute-start | bytes 393224 | tf_op jit(solution)/shard_map/ppermute | solution.py:452
  14.5 0.3 collective-permute-start.2
  14.8 1.9 %collective-permute-start.3 = (f32[256,128]{1,0:T(8,128)S(1)}, f32[256,128]{1,0:T(8,128)S(1)}, u32[]{:S(2)}, u32[]{:S(2)}) collective-permute-start(f32[256,128]{1,0:T(8,128)S(1)} %get-tuple-element.40), channel_id=1, source_target_pairs={{0,64},{8,56},{16,80},{24,40},{32,96},{40,24},{48,112},{56,8},{64,... | collective-permute-start | bytes 393224 | tf_op jit(solution)/shard_map/ppermute | solution.py:452
  16.8 1.2 %reach.4 = (bf16[256,256]{1,0:T(8,128)(2,1)S(1)}, f32[256,128]{1,0:T(8,128)S(1)}) custom-call(bf16[1024,128]{1,0:T(8,128)(2,1)S(1)} %bitcast.4, bf16[4,512,128]{2,1,0:T(8,128)(2,1)S(1)} %get-tuple-element.32.r_ref, f32[4,4,256,128]{3,2,1,0:T(8,128)S(1)} %get-tuple-element.33.z_ref, f32[4,256,128]{2,1,0:T(8,128)S(1)} %collective-permute-done.sib_ref, ...), custom_call_target="tpu_custom_call" | custom-call | flops 400000000 | bytes 3000000 | tf_op jit(solution)/shard_map/reach/pallas_call | solution.py:322
  18.0 0.9 %collective-permute-done.1.s2.refs_2_ = f32[256,128]{1,0:T(8,128)S(1)} collective-permute-done((f32[256,128]{1,0:T(8,128)S(1)}, f32[256,128]{1,0:T(8,128)S(1)}, u32[]{:S(2)}, u32[]{:S(2)}) %collective-permute-start.1) | collective-permute-done | bytes 131104 | tf_op jit(solution)/shard_map/ppermute | solution.py:452
  18.9 0.0 collective-permute-done.2.s1.refs_1_
  18.9 1.4 %collective-permute-done.3.s3.refs_3_ = f32[256,128]{1,0:T(8,128)S(1)} collective-permute-done((f32[256,128]{1,0:T(8,128)S(1)}, f32[256,128]{1,0:T(8,128)S(1)}, u32[]{:S(2)}, u32[]{:S(2)}) %collective-permute-start.3) | collective-permute-done | bytes 131104 | tf_op jit(solution)/shard_map/ppermute | solution.py:452
  20.2 0.5 row.1.after_ref.s0.refs_4_
  20.7 0.0 copy-start.1
  20.7 2.6 %collective-permute-start.6 = (f32[256,128]{1,0:T(8,128)S(1)}, f32[256,128]{1,0:T(8,128)S(1)}, u32[]{:S(2)}, u32[]{:S(2)}) collective-permute-start(f32[256,128]{1,0:T(8,128)S(1)} %row.1.after_ref.s0.refs_4_), channel_id=1, source_target_pairs={{0,16},{8,136},{16,0},{24,152},{32,48},{40,168},{48,32},{56,184},{... | collective-permute-start | bytes 393224 | tf_op jit(solution)/shard_map/ppermute | solution.py:452
  23.4 0.8 %collective-permute-start.5 = (f32[256,128]{1,0:T(8,128)S(1)}, f32[256,128]{1,0:T(8,128)S(1)}, u32[]{:S(2)}, u32[]{:S(2)}) collective-permute-start(f32[256,128]{1,0:T(8,128)S(1)} %row.1.after_ref.s0.refs_4_), channel_id=1, source_target_pairs={{0,16},{8,200},{16,0},{24,216},{32,48},{40,232},{48,32},{56,248},{... | collective-permute-start | bytes 393224 | tf_op jit(solution)/shard_map/ppermute | solution.py:452
  24.1 0.0 collective-permute-start.4
  24.1 1.2 %reach.5 = (bf16[256,256]{1,0:T(8,128)(2,1)S(1)}, f32[256,128]{1,0:T(8,128)S(1)}) custom-call(bf16[1024,128]{1,0:T(8,128)(2,1)S(1)} %bitcast.5, bf16[4,512,128]{2,1,0:T(8,128)(2,1)S(1)} %get-tuple-element.32.r_ref, f32[4,4,256,128]{3,2,1,0:T(8,128)S(1)} %get-tuple-element.33.z_ref, f32[4,256,128]{2,1,0:T(8,128)S(1)} %collective-permute-done.sib_ref, ...), custom_call_target="tpu_custom_call" | custom-call | flops 400000000 | bytes 3000000 | tf_op jit(solution)/shard_map/reach/pallas_call | solution.py:322
  25.3 0.8 %collective-permute-done.6.s2.refs_7_ = f32[256,128]{1,0:T(8,128)S(1)} collective-permute-done((f32[256,128]{1,0:T(8,128)S(1)}, f32[256,128]{1,0:T(8,128)S(1)}, u32[]{:S(2)}, u32[]{:S(2)}) %collective-permute-start.6) | collective-permute-done | bytes 131104 | tf_op jit(solution)/shard_map/ppermute | solution.py:452
  26.1 2.2 %collective-permute-done.5.s3.refs_6_ = f32[256,128]{1,0:T(8,128)S(1)} collective-permute-done((f32[256,128]{1,0:T(8,128)S(1)}, f32[256,128]{1,0:T(8,128)S(1)}, u32[]{:S(2)}, u32[]{:S(2)}) %collective-permute-start.5) | collective-permute-done | bytes 131104 | tf_op jit(solution)/shard_map/ppermute | solution.py:452
  28.4 0.0 collective-permute-done.4.s1.refs_5_
  28.4 0.5 column.1.refs_9_.s0
  28.9 3.1 %collective-permute-start.9 = (f32[256,128]{1,0:T(8,128)S(1)}, f32[256,128]{1,0:T(8,128)S(1)}, u32[]{:S(2)}, u32[]{:S(2)}) collective-permute-start(f32[256,128]{1,0:T(8,128)S(1)} %column.1.refs_9_.s0), channel_id=1, source_target_pairs={{0,16},{8,10},{1,17},{9,11},{2,18},{10,8},{3,19},{11,9},{4,20},{12... | collective-permute-start | bytes 393224 | tf_op jit(solution)/shard_map/ppermute | solution.py:452
  31.9 1.4 %collective-permute-start.8 = (f32[256,128]{1,0:T(8,128)S(1)}, f32[256,128]{1,0:T(8,128)S(1)}, u32[]{:S(2)}, u32[]{:S(2)}) collective-permute-start(f32[256,128]{1,0:T(8,128)S(1)} %column.1.refs_9_.s0), channel_id=1, source_target_pairs={{0,16},{8,11},{1,17},{9,10},{2,18},{10,9},{3,19},{11,8},{4,20},{12... | collective-permute-start | bytes 393224 | tf_op jit(solution)/shard_map/ppermute | solution.py:452
  33.4 0.2 collective-permute-start.7
  33.6 0.7 %path.1 = (f32[4,256,128]{2,1,0:T(8,128)S(1)}, f32[128,128]{1,0:T(8,128)S(1)}) custom-call(f32[256,128]{1,0:T(8,128)S(1)} %get-tuple-element.35.after_ref.s0.refs_0_, f32[256,128]{1,0:T(8,128)S(1)} %collective-permute-done.2.s1.refs_1_, f32[256,128]{1,0:T(8,128)S(1)} %collective-permute-done.1.s2.refs_2_, f32[256,128]{1,0:T(8,128)S(1)} %collective-permute-done.3.s3.refs_3_, ...), custom_call_target="tpu_custom_call" | custom-call | tf_op jit(solution)/shard_map/path/pallas_call | solution.py:409
  34.2 1.2 %reach.6 = (bf16[256,256]{1,0:T(8,128)(2,1)S(1)}, f32[256,128]{1,0:T(8,128)S(1)}) custom-call(bf16[1024,128]{1,0:T(8,128)(2,1)S(1)} %bitcast.6, bf16[4,512,128]{2,1,0:T(8,128)(2,1)S(1)} %get-tuple-element.32.r_ref, f32[4,4,256,128]{3,2,1,0:T(8,128)S(1)} %get-tuple-element.33.z_ref, f32[4,256,128]{2,1,0:T(8,128)S(1)} %collective-permute-done.sib_ref, ...), custom_call_target="tpu_custom_call" | custom-call | flops 400000000 | bytes 3000000 | tf_op jit(solution)/shard_map/reach/pallas_call | solution.py:322
  35.4 2.3 %collective-permute-done.8.s3 = f32[256,128]{1,0:T(8,128)S(1)} collective-permute-done((f32[256,128]{1,0:T(8,128)S(1)}, f32[256,128]{1,0:T(8,128)S(1)}, u32[]{:S(2)}, u32[]{:S(2)}) %collective-permute-start.8) | collective-permute-done | bytes 131104 | tf_op jit(solution)/shard_map/ppermute | solution.py:452
  37.7 0.9 %collective-permute-done.7.s1 = f32[256,128]{1,0:T(8,128)S(1)} collective-permute-done((f32[256,128]{1,0:T(8,128)S(1)}, f32[256,128]{1,0:T(8,128)S(1)}, u32[]{:S(2)}, u32[]{:S(2)}) %collective-permute-start.7) | collective-permute-done | bytes 131104 | tf_op jit(solution)/shard_map/ppermute | solution.py:452
  38.6 0.5 lead.1.after_ref
  39.1 4.9 %collective-permute-start.10 = (f32[128,128]{1,0:T(8,128)S(1)}, f32[128,128]{1,0:T(8,128)S(1)}, u32[]{:S(2)}, u32[]{:S(2)}) collective-permute-start(f32[128,128]{1,0:T(8,128)S(1)} %lead.1.after_ref), channel_id=1, source_target_pairs={{0,16},{8,15},{1,17},{9,14},{2,18},{10,13},{3,19},{11,12},{4,20},{... | collective-permute-start | bytes 196616 | tf_op jit(solution)/shard_map/ppermute | solution.py:508
  44.0 0.6 %fuse.1.fuse_ref = f32[4,256,128]{2,1,0:T(8,128)S(1)} custom-call(f32[256,128]{1,0:T(8,128)S(1)} %column.1.refs_9_.s0, f32[256,128]{1,0:T(8,128)S(1)} %collective-permute-done.7.s1, f32[256,128]{1,0:T(8,128)S(1)} %collective-permute-done.9.s2, f32[256,128]{1,0:T(8,128)S(1)} %collective-permute-done.8.s3, ...), custom_call_target="tpu_custom_call" | custom-call | tf_op jit(solution)/shard_map/fuse/pallas_call | solution.py:409
  44.6 0.0 copy-start.2
  44.6 1.7 %collective-permute-done.10.early_ref = f32[128,128]{1,0:T(8,128)S(1)} collective-permute-done((f32[128,128]{1,0:T(8,128)S(1)}, f32[128,128]{1,0:T(8,128)S(1)}, u32[]{:S(2)}, u32[]{:S(2)}) %collective-permute-start.10) | collective-permute-done | bytes 65568 | tf_op jit(solution)/shard_map/ppermute | solution.py:508
  46.3 0.3 entry.1
  46.6 1.8 %collective-permute-start.13 = (f32[128,128]{1,0:T(8,128)S(1)}, f32[128,128]{1,0:T(8,128)S(1)}, u32[]{:S(2)}, u32[]{:S(2)}) collective-permute-start(f32[128,128]{1,0:T(8,128)S(1)} %get-tuple-element.49), channel_id=1, source_target_pairs={{0,64},{8,40},{16,80},{24,56},{32,96},{40,8},{48,112},{56,24},{64,... | collective-permute-start | bytes 196616 | tf_op jit(solution)/shard_map/ppermute | solution.py:452
  48.4 0.0 collective-permute-start.12
  48.4 1.5 %collective-permute-start.11 = (f32[128,128]{1,0:T(8,128)S(1)}, f32[128,128]{1,0:T(8,128)S(1)}, u32[]{:S(2)}, u32[]{:S(2)}) collective-permute-start(f32[128,128]{1,0:T(8,128)S(1)} %get-tuple-element.47), channel_id=1, source_target_pairs={{0,64},{8,56},{16,80},{24,40},{32,96},{40,24},{48,112},{56,8},{64,... | collective-permute-start | bytes 196616 | tf_op jit(solution)/shard_map/ppermute | solution.py:452
  49.9 1.2 %reach.7 = (bf16[256,256]{1,0:T(8,128)(2,1)S(1)}, f32[256,128]{1,0:T(8,128)S(1)}) custom-call(bf16[1024,128]{1,0:T(8,128)(2,1)S(1)} %bitcast.7, bf16[4,512,128]{2,1,0:T(8,128)(2,1)S(1)} %get-tuple-element.32.r_ref, f32[4,4,256,128]{3,2,1,0:T(8,128)S(1)} %get-tuple-element.33.z_ref, f32[4,256,128]{2,1,0:T(8,128)S(1)} %collective-permute-done.sib_ref, ...), custom_call_target="tpu_custom_call" | custom-call | flops 400000000 | bytes 3000000 | tf_op jit(solution)/shard_map/reach/pallas_call | solution.py:322
  51.1 0.2 collective-permute-done.13.refs_9_
  51.3 0.2 collective-permute-done.12.refs_10_
  51.5 1.2 %collective-permute-done.11.refs_11_ = f32[128,128]{1,0:T(8,128)S(1)} collective-permute-done((f32[128,128]{1,0:T(8,128)S(1)}, f32[128,128]{1,0:T(8,128)S(1)}, u32[]{:S(2)}, u32[]{:S(2)}) %collective-permute-start.11) | collective-permute-done | bytes 65568 | tf_op jit(solution)/shard_map/ppermute | solution.py:452
  52.7 0.0 collective-permute-start.17
  52.7 0.5 collective-permute-start.16
  53.2 0.0 collective-permute-start.15
  53.2 0.7 %collective-permute-done.17.refs_15_ = f32[128,128]{1,0:T(8,128)S(1)} collective-permute-done((f32[128,128]{1,0:T(8,128)S(1)}, f32[128,128]{1,0:T(8,128)S(1)}, u32[]{:S(2)}, u32[]{:S(2)}) %collective-permute-start.17) | collective-permute-done | bytes 65568 | tf_op jit(solution)/shard_map/ppermute | solution.py:452
  54.0 0.2 collective-permute-done.16.refs_14_
  54.1 0.4 collective-permute-done.15.refs_13_
  54.5 1.3 %read.1 = bf16[1024,128]{1,0:T(8,128)(2,1)} custom-call(bf16[256,256]{1,0:T(8,128)(2,1)S(1)} %get-tuple-element.36.after_ref.refs_0_, f32[256,128]{1,0:T(8,128)S(1)} %get-tuple-element.37.refs_1_, bf16[256,256]{1,0:T(8,128)(2,1)S(1)} %get-tuple-element.41.after_ref.refs_2_, f32[256,128]{1,0:T(8,128)S(1)} %get-tuple-element.42.refs_3_, ...), custom_call_target="tpu_custom_call" | custom-call | tf_op jit(solution)/shard_map/read/pallas_call | solution.py:391
  (7 shorter events, 0.0 us)
Async XLA Ops:
  0.0 16.8 %copy-start = (bf16[1,256,4,128]{3,2,1,0:T(4,128)(2,1)S(1)}, bf16[1,256,4,128]{3,2,1,0:T(4,128)(2,1)}, u32[]{:S(2)}) copy-start(bf16[1,256,4,128]{3,2,1,0:T(4,128)(2,1)} %param.5) | copy-start | bytes 786436
  8.2 4.9 %collective-permute-start = (f32[4,256,128]{2,1,0:T(8,128)S(1)}, f32[4,256,128]{2,1,0:T(8,128)S(1)}, u32[]{:S(2)}, u32[]{:S(2)}) collective-permute-start(f32[4,256,128]{2,1,0:T(8,128)S(1)} %get-tuple-element.34.own_ref), channel_id=1, source_target_pairs={{0,8},{8,0},{16,24},{24,16},{32,40},{40,32},{48,56},{56,48},{64,72... | collective-permute-start | bytes 1572872 | tf_op jit(solution)/shard_map/ppermute | solution.py:476
  13.4 5.4 %collective-permute-start.1 = (f32[256,128]{1,0:T(8,128)S(1)}, f32[256,128]{1,0:T(8,128)S(1)}, u32[]{:S(2)}, u32[]{:S(2)}) collective-permute-start(f32[256,128]{1,0:T(8,128)S(1)} %get-tuple-element.38), channel_id=1, source_target_pairs={{0,64},{8,40},{16,80},{24,56},{32,96},{40,8},{48,112},{56,24},{64,... | collective-permute-start | bytes 393224 | tf_op jit(solution)/shard_map/ppermute | solution.py:452
  14.5 4.4 %collective-permute-start.2 = (f32[256,128]{1,0:T(8,128)S(1)}, f32[256,128]{1,0:T(8,128)S(1)}, u32[]{:S(2)}, u32[]{:S(2)}) collective-permute-start(f32[256,128]{1,0:T(8,128)S(1)} %get-tuple-element.39), channel_id=1, source_target_pairs={{0,64},{8,24},{16,80},{24,8},{32,96},{40,56},{48,112},{56,40},{64,... | collective-permute-start | bytes 393224 | tf_op jit(solution)/shard_map/ppermute | solution.py:452
  14.8 5.4 %collective-permute-start.3 = (f32[256,128]{1,0:T(8,128)S(1)}, f32[256,128]{1,0:T(8,128)S(1)}, u32[]{:S(2)}, u32[]{:S(2)}) collective-permute-start(f32[256,128]{1,0:T(8,128)S(1)} %get-tuple-element.40), channel_id=1, source_target_pairs={{0,64},{8,56},{16,80},{24,40},{32,96},{40,24},{48,112},{56,8},{64,... | collective-permute-start | bytes 393224 | tf_op jit(solution)/shard_map/ppermute | solution.py:452
  20.7 12.9 %copy-start.1 = (f32[4,128,128]{2,1,0:T(8,128)S(1)}, f32[4,128,128]{2,1,0:T(8,128)}, u32[]{:S(2)}) copy-start(f32[4,128,128]{2,1,0:T(8,128)} %refs_8_.1) | copy-start | bytes 786436
  20.7 5.4 %collective-permute-start.6 = (f32[256,128]{1,0:T(8,128)S(1)}, f32[256,128]{1,0:T(8,128)S(1)}, u32[]{:S(2)}, u32[]{:S(2)}) collective-permute-start(f32[256,128]{1,0:T(8,128)S(1)} %row.1.after_ref.s0.refs_4_), channel_id=1, source_target_pairs={{0,16},{8,136},{16,0},{24,152},{32,48},{40,168},{48,32},{56,184},{... | collective-permute-start | bytes 393224 | tf_op jit(solution)/shard_map/ppermute | solution.py:452
  23.4 5.0 %collective-permute-start.5 = (f32[256,128]{1,0:T(8,128)S(1)}, f32[256,128]{1,0:T(8,128)S(1)}, u32[]{:S(2)}, u32[]{:S(2)}) collective-permute-start(f32[256,128]{1,0:T(8,128)S(1)} %row.1.after_ref.s0.refs_4_), channel_id=1, source_target_pairs={{0,16},{8,200},{16,0},{24,216},{32,48},{40,232},{48,32},{56,248},{... | collective-permute-start | bytes 393224 | tf_op jit(solution)/shard_map/ppermute | solution.py:452
  24.1 4.3 %collective-permute-start.4 = (f32[256,128]{1,0:T(8,128)S(1)}, f32[256,128]{1,0:T(8,128)S(1)}, u32[]{:S(2)}, u32[]{:S(2)}) collective-permute-start(f32[256,128]{1,0:T(8,128)S(1)} %row.1.after_ref.s0.refs_4_), channel_id=1, source_target_pairs={{0,16},{8,72},{16,0},{24,88},{32,48},{40,104},{48,32},{56,120},{64... | collective-permute-start | bytes 393224 | tf_op jit(solution)/shard_map/ppermute | solution.py:452
  28.9 6.6 %collective-permute-start.9 = (f32[256,128]{1,0:T(8,128)S(1)}, f32[256,128]{1,0:T(8,128)S(1)}, u32[]{:S(2)}, u32[]{:S(2)}) collective-permute-start(f32[256,128]{1,0:T(8,128)S(1)} %column.1.refs_9_.s0), channel_id=1, source_target_pairs={{0,16},{8,10},{1,17},{9,11},{2,18},{10,8},{3,19},{11,9},{4,20},{12... | collective-permute-start | bytes 393224 | tf_op jit(solution)/shard_map/ppermute | solution.py:452
  31.9 5.8 %collective-permute-start.8 = (f32[256,128]{1,0:T(8,128)S(1)}, f32[256,128]{1,0:T(8,128)S(1)}, u32[]{:S(2)}, u32[]{:S(2)}) collective-permute-start(f32[256,128]{1,0:T(8,128)S(1)} %column.1.refs_9_.s0), channel_id=1, source_target_pairs={{0,16},{8,11},{1,17},{9,10},{2,18},{10,9},{3,19},{11,8},{4,20},{12... | collective-permute-start | bytes 393224 | tf_op jit(solution)/shard_map/ppermute | solution.py:452
  33.4 5.2 %collective-permute-start.7 = (f32[256,128]{1,0:T(8,128)S(1)}, f32[256,128]{1,0:T(8,128)S(1)}, u32[]{:S(2)}, u32[]{:S(2)}) collective-permute-start(f32[256,128]{1,0:T(8,128)S(1)} %column.1.refs_9_.s0), channel_id=1, source_target_pairs={{0,16},{8,9},{1,17},{9,8},{2,18},{10,11},{3,19},{11,10},{4,20},{12... | collective-permute-start | bytes 393224 | tf_op jit(solution)/shard_map/ppermute | solution.py:452
  39.1 7.2 %collective-permute-start.10 = (f32[128,128]{1,0:T(8,128)S(1)}, f32[128,128]{1,0:T(8,128)S(1)}, u32[]{:S(2)}, u32[]{:S(2)}) collective-permute-start(f32[128,128]{1,0:T(8,128)S(1)} %lead.1.after_ref), channel_id=1, source_target_pairs={{0,16},{8,15},{1,17},{9,14},{2,18},{10,13},{3,19},{11,12},{4,20},{... | collective-permute-start | bytes 196616 | tf_op jit(solution)/shard_map/ppermute | solution.py:508
  44.6 9.9 %copy-start.2 = (f32[4,128]{1,0:T(4,128)S(1)}, f32[4,128]{1,0:T(4,128)}, u32[]{:S(2)}) copy-start(f32[4,128]{1,0:T(4,128)} %refs_16_.1) | copy-start | bytes 6148
  46.6 4.7 %collective-permute-start.13 = (f32[128,128]{1,0:T(8,128)S(1)}, f32[128,128]{1,0:T(8,128)S(1)}, u32[]{:S(2)}, u32[]{:S(2)}) collective-permute-start(f32[128,128]{1,0:T(8,128)S(1)} %get-tuple-element.49), channel_id=1, source_target_pairs={{0,64},{8,40},{16,80},{24,56},{32,96},{40,8},{48,112},{56,24},{64,... | collective-permute-start | bytes 196616 | tf_op jit(solution)/shard_map/ppermute | solution.py:452
  48.4 3.1 %collective-permute-start.12 = (f32[128,128]{1,0:T(8,128)S(1)}, f32[128,128]{1,0:T(8,128)S(1)}, u32[]{:S(2)}, u32[]{:S(2)}) collective-permute-start(f32[128,128]{1,0:T(8,128)S(1)} %get-tuple-element.48), channel_id=1, source_target_pairs={{0,64},{8,24},{16,80},{24,8},{32,96},{40,56},{48,112},{56,40},{64,... | collective-permute-start | bytes 196616 | tf_op jit(solution)/shard_map/ppermute | solution.py:452
  48.4 4.3 %collective-permute-start.11 = (f32[128,128]{1,0:T(8,128)S(1)}, f32[128,128]{1,0:T(8,128)S(1)}, u32[]{:S(2)}, u32[]{:S(2)}) collective-permute-start(f32[128,128]{1,0:T(8,128)S(1)} %get-tuple-element.47), channel_id=1, source_target_pairs={{0,64},{8,56},{16,80},{24,40},{32,96},{40,24},{48,112},{56,8},{64,... | collective-permute-start | bytes 196616 | tf_op jit(solution)/shard_map/ppermute | solution.py:452
  49.9 3.3 %collective-permute-start.14 = (f32[128,128]{1,0:T(8,128)S(1)}, f32[128,128]{1,0:T(8,128)S(1)}, u32[]{:S(2)}, u32[]{:S(2)}) collective-permute-start(f32[128,128]{1,0:T(8,128)S(1)} %get-tuple-element.50.after_ref.refs_8_), channel_id=1, source_target_pairs={{0,8},{8,0},{16,24},{24,16},{32,40},{40,32},{48,56},{56,48},{64,72... | collective-permute-start | bytes 196616 | tf_op jit(solution)/shard_map/ppermute | solution.py:531
  52.7 1.3 %collective-permute-start.17 = (f32[128,128]{1,0:T(8,128)S(1)}, f32[128,128]{1,0:T(8,128)S(1)}, u32[]{:S(2)}, u32[]{:S(2)}) collective-permute-start(f32[128,128]{1,0:T(8,128)S(1)} %collective-permute-done.11.refs_11_), channel_id=1, source_target_pairs={{0,8},{8,0},{16,24},{24,16},{32,40},{40,32},{48,56},{56,48},{64,72... | collective-permute-start | bytes 196616 | tf_op jit(solution)/shard_map/ppermute | solution.py:452
  52.7 1.4 %collective-permute-start.16 = (f32[128,128]{1,0:T(8,128)S(1)}, f32[128,128]{1,0:T(8,128)S(1)}, u32[]{:S(2)}, u32[]{:S(2)}) collective-permute-start(f32[128,128]{1,0:T(8,128)S(1)} %collective-permute-done.12.refs_10_), channel_id=1, source_target_pairs={{0,8},{8,0},{16,24},{24,16},{32,40},{40,32},{48,56},{56,48},{64,72... | collective-permute-start | bytes 196616 | tf_op jit(solution)/shard_map/ppermute | solution.py:452
  53.2 1.3 %collective-permute-start.15 = (f32[128,128]{1,0:T(8,128)S(1)}, f32[128,128]{1,0:T(8,128)S(1)}, u32[]{:S(2)}, u32[]{:S(2)}) collective-permute-start(f32[128,128]{1,0:T(8,128)S(1)} %collective-permute-done.13.refs_9_), channel_id=1, source_target_pairs={{0,8},{8,0},{16,24},{24,16},{32,40},{40,32},{48,56},{56,48},{64,72... | collective-permute-start | bytes 196616 | tf_op jit(solution)/shard_map/ppermute | solution.py:452

commit v14 on v12

--- a/solution.py
+++ b/solution.py
@@ -104,6 +104,7 @@
     row = iota2((BLK, BLK), 0)
     col = iota2((BLK, BLK), 1)
     eye = row == col
+    unit = jnp.where(eye, 1.0, 0.0).astype(bf16)
     pair = ((row >> 1) == (col >> 1)) & (row < col)
     chains = [(h, b) for h in range(HEADS) for b in range(nblk)]
     rs, rts, vts, uppers, invs, ccols, crows = [], [], [], [], [], [], []
@@ -111,8 +112,8 @@
         rows = pl.ds(h + HEADS * BLK * b, BLK, stride=HEADS)
         r = keys[rows, :].astype(bf16)
         r_ref[h, b * BLK : (b + 1) * BLK, :] = r
-        rt = r.T
-        gram = dot_nn(r, rt)
+        both = dot_nt(jnp.concatenate([r, unit], axis=0), r)
+        gram, rt = both[:BLK], both[BLK:].astype(bf16)
         diag = jnp.where(eye, gram, 0.0)
         ccol = lax.rsqrt(jnp.sum(diag, axis=1, keepdims=True) + 1e-06)
         crow = lax.rsqrt(jnp.sum(diag, axis=0, keepdims=True) + 1e-06)

time: 55.6 us -> 55.6 us (level)
  no operation moved by 1% of the time
where the time goes in v14:
time: 55.6 us; the launch traced here: 55.5 us
  starting transfers between devices  23.3 us (42%)
  Pallas kernels  17.4 us (31%)
  waiting for transfers between devices  14.5 us (26%)
    ppermute x15, starting transfers between devices, exchange(): out[k] = lax.ppermute(slots[k], axis, perms[k - 1])  15.4 us
    ppermute x15, waiting for transfers between devices, exchange(): out[k] = lax.ppermute(slots[k], axis, perms[k - 1])  11.2 us
    pallas_call x1, Pallas kernels, factor_call(): pl.pallas_call(factor_kernel, in_specs=[pl.BlockSpec(memory_space=pl.ANY)...  8.21 us
    pallas_call x4, Pallas kernels, reach_call(): pl.pallas_call(functools.partial(reach_kernel, head=head), grid=(1,), in_...  4.71 us
    ppermute x1, starting transfers between devices, per_device(): early = lax.ppermute(lead, ('seq', 'seg'), jump)  4.56 us
    ppermute x1, starting transfers between devices, per_device(): sib = lax.ppermute(pair, 'seq', swap)  3.33 us
    pallas_call x7, Pallas kernels, small_call(): pl.pallas_call(kernel, in_specs=whole(*arrays) + [pl.BlockSpec(memory_spa...  3.24 us
    ppermute x1, waiting for transfers between devices, per_device(): early = lax.ppermute(lead, ('seq', 'seg'), jump)  1.74 us
  transfers between devices with their start and end apart: 18, of which 14 were waited for; matrix products, arithmetic and copies ran while one was open for 0% of the time, Pallas kernels for 11%

profile of v14, /device:TPU:1, one launch (start us, length us, event | category | flops | bytes accessed | tf_op | source)
XLA Modules:
  0.0 55.5 jit_solution(9578750225596829838)
XLA Ops:
  0.0 8.2 %factor.1 = (f32[4,256,128]{2,1,0:T(8,128)S(1)}, f32[4,4,256,128]{3,2,1,0:T(8,128)S(1)}, bf16[4,512,128]{2,1,0:T(8,128)(2,1)S(1)}) custom-call(bf16[2048,128]{1,0:T(8,128)(2,1)} %bitcast.8, bf16[2048,128]{1,0:T(8,128)(2,1)} %bitcast.9), custom_call_target="tpu_custom_call" | custom-call | tf_op jit(solution)/shard_map/factor/pallas_call | solution.py:175
  8.2 3.3 %collective-permute-start = (f32[4,256,128]{2,1,0:T(8,128)S(1)}, f32[4,256,128]{2,1,0:T(8,128)S(1)}, u32[]{:S(2)}, u32[]{:S(2)}) collective-permute-start(f32[4,256,128]{2,1,0:T(8,128)S(1)} %get-tuple-element.34.own_ref), channel_id=1, source_target_pairs={{0,8},{8,0},{16,24},{24,16},{32,40},{40,32},{48,56},{56,48},{64,72... | collective-permute-start | bytes 1572872 | tf_op jit(solution)/shard_map/ppermute | solution.py:477
  11.5 1.5 %collective-permute-done.sib_ref = f32[4,256,128]{2,1,0:T(8,128)S(1)} collective-permute-done((f32[4,256,128]{2,1,0:T(8,128)S(1)}, f32[4,256,128]{2,1,0:T(8,128)S(1)}, u32[]{:S(2)}, u32[]{:S(2)}) %collective-permute-start) | collective-permute-done | bytes 524320 | tf_op jit(solution)/shard_map/ppermute | solution.py:477
  13.1 0.3 chip.1
  13.4 1.1 %collective-permute-start.1 = (f32[256,128]{1,0:T(8,128)S(1)}, f32[256,128]{1,0:T(8,128)S(1)}, u32[]{:S(2)}, u32[]{:S(2)}) collective-permute-start(f32[256,128]{1,0:T(8,128)S(1)} %get-tuple-element.38), channel_id=1, source_target_pairs={{0,64},{8,40},{16,80},{24,56},{32,96},{40,8},{48,112},{56,24},{64,... | collective-permute-start | bytes 393224 | tf_op jit(solution)/shard_map/ppermute | solution.py:453
  14.5 0.3 collective-permute-start.2
  14.8 1.9 %collective-permute-start.3 = (f32[256,128]{1,0:T(8,128)S(1)}, f32[256,128]{1,0:T(8,128)S(1)}, u32[]{:S(2)}, u32[]{:S(2)}) collective-permute-start(f32[256,128]{1,0:T(8,128)S(1)} %get-tuple-element.40), channel_id=1, source_target_pairs={{0,64},{8,56},{16,80},{24,40},{32,96},{40,24},{48,112},{56,8},{64,... | collective-permute-start | bytes 393224 | tf_op jit(solution)/shard_map/ppermute | solution.py:453
  16.7 1.2 %reach.4 = (bf16[256,256]{1,0:T(8,128)(2,1)S(1)}, f32[256,128]{1,0:T(8,128)S(1)}) custom-call(bf16[1024,128]{1,0:T(8,128)(2,1)S(1)} %bitcast.4, bf16[4,512,128]{2,1,0:T(8,128)(2,1)S(1)} %get-tuple-element.32.r_ref, f32[4,4,256,128]{3,2,1,0:T(8,128)S(1)} %get-tuple-element.33.z_ref, f32[4,256,128]{2,1,0:T(8,128)S(1)} %collective-permute-done.sib_ref, ...), custom_call_target="tpu_custom_call" | custom-call | flops 400000000 | bytes 3000000 | tf_op jit(solution)/shard_map/reach/pallas_call | solution.py:323
  17.9 0.9 %collective-permute-done.1.s2.refs_2_ = f32[256,128]{1,0:T(8,128)S(1)} collective-permute-done((f32[256,128]{1,0:T(8,128)S(1)}, f32[256,128]{1,0:T(8,128)S(1)}, u32[]{:S(2)}, u32[]{:S(2)}) %collective-permute-start.1) | collective-permute-done | bytes 131104 | tf_op jit(solution)/shard_map/ppermute | solution.py:453
  18.9 0.0 collective-permute-done.2.s1.refs_1_
  18.9 1.4 %collective-permute-done.3.s3.refs_3_ = f32[256,128]{1,0:T(8,128)S(1)} collective-permute-done((f32[256,128]{1,0:T(8,128)S(1)}, f32[256,128]{1,0:T(8,128)S(1)}, u32[]{:S(2)}, u32[]{:S(2)}) %collective-permute-start.3) | collective-permute-done | bytes 131104 | tf_op jit(solution)/shard_map/ppermute | solution.py:453
  20.2 0.5 row.1.after_ref.s0.refs_4_
  20.7 0.0 copy-start.1
  20.7 2.6 %collective-permute-start.6 = (f32[256,128]{1,0:T(8,128)S(1)}, f32[256,128]{1,0:T(8,128)S(1)}, u32[]{:S(2)}, u32[]{:S(2)}) collective-permute-start(f32[256,128]{1,0:T(8,128)S(1)} %row.1.after_ref.s0.refs_4_), channel_id=1, source_target_pairs={{0,16},{8,136},{16,0},{24,152},{32,48},{40,168},{48,32},{56,184},{... | collective-permute-start | bytes 393224 | tf_op jit(solution)/shard_map/ppermute | solution.py:453
  23.3 0.8 %collective-permute-start.5 = (f32[256,128]{1,0:T(8,128)S(1)}, f32[256,128]{1,0:T(8,128)S(1)}, u32[]{:S(2)}, u32[]{:S(2)}) collective-permute-start(f32[256,128]{1,0:T(8,128)S(1)} %row.1.after_ref.s0.refs_4_), channel_id=1, source_target_pairs={{0,16},{8,200},{16,0},{24,216},{32,48},{40,232},{48,32},{56,248},{... | collective-permute-start | bytes 393224 | tf_op jit(solution)/shard_map/ppermute | solution.py:453
  24.1 0.0 collective-permute-start.4
  24.1 1.2 %reach.5 = (bf16[256,256]{1,0:T(8,128)(2,1)S(1)}, f32[256,128]{1,0:T(8,128)S(1)}) custom-call(bf16[1024,128]{1,0:T(8,128)(2,1)S(1)} %bitcast.5, bf16[4,512,128]{2,1,0:T(8,128)(2,1)S(1)} %get-tuple-element.32.r_ref, f32[4,4,256,128]{3,2,1,0:T(8,128)S(1)} %get-tuple-element.33.z_ref, f32[4,256,128]{2,1,0:T(8,128)S(1)} %collective-permute-done.sib_ref, ...), custom_call_target="tpu_custom_call" | custom-call | flops 400000000 | bytes 3000000 | tf_op jit(solution)/shard_map/reach/pallas_call | solution.py:323
  25.3 0.8 %collective-permute-done.6.s2.refs_7_ = f32[256,128]{1,0:T(8,128)S(1)} collective-permute-done((f32[256,128]{1,0:T(8,128)S(1)}, f32[256,128]{1,0:T(8,128)S(1)}, u32[]{:S(2)}, u32[]{:S(2)}) %collective-permute-start.6) | collective-permute-done | bytes 131104 | tf_op jit(solution)/shard_map/ppermute | solution.py:453
  26.1 2.2 %collective-permute-done.5.s3.refs_6_ = f32[256,128]{1,0:T(8,128)S(1)} collective-permute-done((f32[256,128]{1,0:T(8,128)S(1)}, f32[256,128]{1,0:T(8,128)S(1)}, u32[]{:S(2)}, u32[]{:S(2)}) %collective-permute-start.5) | collective-permute-done | bytes 131104 | tf_op jit(solution)/shard_map/ppermute | solution.py:453
  28.4 0.0 collective-permute-done.4.s1.refs_5_
  28.4 0.5 column.1.refs_9_.s0
  28.8 4.4 %collective-permute-start.9 = (f32[256,128]{1,0:T(8,128)S(1)}, f32[256,128]{1,0:T(8,128)S(1)}, u32[]{:S(2)}, u32[]{:S(2)}) collective-permute-start(f32[256,128]{1,0:T(8,128)S(1)} %column.1.refs_9_.s0), channel_id=1, source_target_pairs={{0,16},{8,11},{1,17},{9,10},{2,18},{10,9},{3,19},{11,8},{4,20},{12... | collective-permute-start | bytes 393224 | tf_op jit(solution)/shard_map/ppermute | solution.py:453
  33.3 0.0 collective-permute-start.8
  33.3 0.4 collective-permute-start.7
  33.7 0.7 %path.1 = (f32[4,256,128]{2,1,0:T(8,128)S(1)}, f32[128,128]{1,0:T(8,128)S(1)}) custom-call(f32[256,128]{1,0:T(8,128)S(1)} %get-tuple-element.35.after_ref.s0.refs_0_, f32[256,128]{1,0:T(8,128)S(1)} %collective-permute-done.2.s1.refs_1_, f32[256,128]{1,0:T(8,128)S(1)} %collective-permute-done.1.s2.refs_2_, f32[256,128]{1,0:T(8,128)S(1)} %collective-permute-done.3.s3.refs_3_, ...), custom_call_target="tpu_custom_call" | custom-call | tf_op jit(solution)/shard_map/path/pallas_call | solution.py:410
  34.3 1.2 %reach.6 = (bf16[256,256]{1,0:T(8,128)(2,1)S(1)}, f32[256,128]{1,0:T(8,128)S(1)}) custom-call(bf16[1024,128]{1,0:T(8,128)(2,1)S(1)} %bitcast.6, bf16[4,512,128]{2,1,0:T(8,128)(2,1)S(1)} %get-tuple-element.32.r_ref, f32[4,4,256,128]{3,2,1,0:T(8,128)S(1)} %get-tuple-element.33.z_ref, f32[4,256,128]{2,1,0:T(8,128)S(1)} %collective-permute-done.sib_ref, ...), custom_call_target="tpu_custom_call" | custom-call | flops 400000000 | bytes 3000000 | tf_op jit(solution)/shard_map/reach/pallas_call | solution.py:323
  35.5 0.2 collective-permute-done.9.s3
  35.7 2.8 %collective-permute-done.8.s2 = f32[256,128]{1,0:T(8,128)S(1)} collective-permute-done((f32[256,128]{1,0:T(8,128)S(1)}, f32[256,128]{1,0:T(8,128)S(1)}, u32[]{:S(2)}, u32[]{:S(2)}) %collective-permute-start.8) | collective-permute-done | bytes 131104 | tf_op jit(solution)/shard_map/ppermute | solution.py:453
  38.5 0.0 collective-permute-done.7.s1
  38.5 0.5 lead.1.after_ref
  39.0 4.6 %collective-permute-start.10 = (f32[128,128]{1,0:T(8,128)S(1)}, f32[128,128]{1,0:T(8,128)S(1)}, u32[]{:S(2)}, u32[]{:S(2)}) collective-permute-start(f32[128,128]{1,0:T(8,128)S(1)} %lead.1.after_ref), channel_id=1, source_target_pairs={{0,16},{8,15},{1,17},{9,14},{2,18},{10,13},{3,19},{11,12},{4,20},{... | collective-permute-start | bytes 196616 | tf_op jit(solution)/shard_map/ppermute | solution.py:509
  43.5 0.6 %fuse.1.fuse_ref = f32[4,256,128]{2,1,0:T(8,128)S(1)} custom-call(f32[256,128]{1,0:T(8,128)S(1)} %column.1.refs_9_.s0, f32[256,128]{1,0:T(8,128)S(1)} %collective-permute-done.7.s1, f32[256,128]{1,0:T(8,128)S(1)} %collective-permute-done.8.s2, f32[256,128]{1,0:T(8,128)S(1)} %collective-permute-done.9.s3, ...), custom_call_target="tpu_custom_call" | custom-call | tf_op jit(solution)/shard_map/fuse/pallas_call | solution.py:410
  44.1 0.0 copy-start.2
  44.2 1.7 %collective-permute-done.10.early_ref = f32[128,128]{1,0:T(8,128)S(1)} collective-permute-done((f32[128,128]{1,0:T(8,128)S(1)}, f32[128,128]{1,0:T(8,128)S(1)}, u32[]{:S(2)}, u32[]{:S(2)}) %collective-permute-start.10) | collective-permute-done | bytes 65568 | tf_op jit(solution)/shard_map/ppermute | solution.py:509
  45.9 0.3 entry.1
  46.2 1.8 %collective-permute-start.13 = (f32[128,128]{1,0:T(8,128)S(1)}, f32[128,128]{1,0:T(8,128)S(1)}, u32[]{:S(2)}, u32[]{:S(2)}) collective-permute-start(f32[128,128]{1,0:T(8,128)S(1)} %get-tuple-element.49), channel_id=1, source_target_pairs={{0,64},{8,40},{16,80},{24,56},{32,96},{40,8},{48,112},{56,24},{64,... | collective-permute-start | bytes 196616 | tf_op jit(solution)/shard_map/ppermute | solution.py:453
  48.0 0.0 collective-permute-start.12
  48.0 1.5 %collective-permute-start.11 = (f32[128,128]{1,0:T(8,128)S(1)}, f32[128,128]{1,0:T(8,128)S(1)}, u32[]{:S(2)}, u32[]{:S(2)}) collective-permute-start(f32[128,128]{1,0:T(8,128)S(1)} %get-tuple-element.47), channel_id=1, source_target_pairs={{0,64},{8,56},{16,80},{24,40},{32,96},{40,24},{48,112},{56,8},{64,... | collective-permute-start | bytes 196616 | tf_op jit(solution)/shard_map/ppermute | solution.py:453
  49.5 1.2 %reach.7 = (bf16[256,256]{1,0:T(8,128)(2,1)S(1)}, f32[256,128]{1,0:T(8,128)S(1)}) custom-call(bf16[1024,128]{1,0:T(8,128)(2,1)S(1)} %bitcast.7, bf16[4,512,128]{2,1,0:T(8,128)(2,1)S(1)} %get-tuple-element.32.r_ref, f32[4,4,256,128]{3,2,1,0:T(8,128)S(1)} %get-tuple-element.33.z_ref, f32[4,256,128]{2,1,0:T(8,128)S(1)} %collective-permute-done.sib_ref, ...), custom_call_target="tpu_custom_call" | custom-call | flops 400000000 | bytes 3000000 | tf_op jit(solution)/shard_map/reach/pallas_call | solution.py:323
  50.7 0.2 collective-permute-done.13.refs_9_
  50.9 0.2 collective-permute-done.12.refs_10_
  51.1 1.2 %collective-permute-done.11.refs_11_ = f32[128,128]{1,0:T(8,128)S(1)} collective-permute-done((f32[128,128]{1,0:T(8,128)S(1)}, f32[128,128]{1,0:T(8,128)S(1)}, u32[]{:S(2)}, u32[]{:S(2)}) %collective-permute-start.11) | collective-permute-done | bytes 65568 | tf_op jit(solution)/shard_map/ppermute | solution.py:453
  52.3 0.5 collective-permute-start.16
  52.8 0.0 collective-permute-start.15
  52.8 0.7 %collective-permute-done.17.refs_15_ = f32[128,128]{1,0:T(8,128)S(1)} collective-permute-done((f32[128,128]{1,0:T(8,128)S(1)}, f32[128,128]{1,0:T(8,128)S(1)}, u32[]{:S(2)}, u32[]{:S(2)}) %collective-permute-start.17) | collective-permute-done | bytes 65568 | tf_op jit(solution)/shard_map/ppermute | solution.py:453
  53.6 0.2 collective-permute-done.16.refs_14_
  53.7 0.4 collective-permute-done.15.refs_13_
  54.1 1.3 %read.1 = bf16[1024,128]{1,0:T(8,128)(2,1)} custom-call(bf16[256,256]{1,0:T(8,128)(2,1)S(1)} %get-tuple-element.36.after_ref.refs_0_, f32[256,128]{1,0:T(8,128)S(1)} %get-tuple-element.37.refs_1_, bf16[256,256]{1,0:T(8,128)(2,1)S(1)} %get-tuple-element.41.after_ref.refs_2_, f32[256,128]{1,0:T(8,128)S(1)} %get-tuple-element.42.refs_3_, ...), custom_call_target="tpu_custom_call" | custom-call | tf_op jit(solution)/shard_map/read/pallas_call | solution.py:392
  (7 shorter events, 0.0 us)
Async XLA Ops:
  0.0 16.7 %copy-start = (bf16[1,256,4,128]{3,2,1,0:T(4,128)(2,1)S(1)}, bf16[1,256,4,128]{3,2,1,0:T(4,128)(2,1)}, u32[]{:S(2)}) copy-start(bf16[1,256,4,128]{3,2,1,0:T(4,128)(2,1)} %param.5) | copy-start | bytes 786436
  8.2 4.9 %collective-permute-start = (f32[4,256,128]{2,1,0:T(8,128)S(1)}, f32[4,256,128]{2,1,0:T(8,128)S(1)}, u32[]{:S(2)}, u32[]{:S(2)}) collective-permute-start(f32[4,256,128]{2,1,0:T(8,128)S(1)} %get-tuple-element.34.own_ref), channel_id=1, source_target_pairs={{0,8},{8,0},{16,24},{24,16},{32,40},{40,32},{48,56},{56,48},{64,72... | collective-permute-start | bytes 1572872 | tf_op jit(solution)/shard_map/ppermute | solution.py:477
  13.4 5.4 %collective-permute-start.1 = (f32[256,128]{1,0:T(8,128)S(1)}, f32[256,128]{1,0:T(8,128)S(1)}, u32[]{:S(2)}, u32[]{:S(2)}) collective-permute-start(f32[256,128]{1,0:T(8,128)S(1)} %get-tuple-element.38), channel_id=1, source_target_pairs={{0,64},{8,40},{16,80},{24,56},{32,96},{40,8},{48,112},{56,24},{64,... | collective-permute-start | bytes 393224 | tf_op jit(solution)/shard_map/ppermute | solution.py:453
  14.5 4.4 %collective-permute-start.2 = (f32[256,128]{1,0:T(8,128)S(1)}, f32[256,128]{1,0:T(8,128)S(1)}, u32[]{:S(2)}, u32[]{:S(2)}) collective-permute-start(f32[256,128]{1,0:T(8,128)S(1)} %get-tuple-element.39), channel_id=1, source_target_pairs={{0,64},{8,24},{16,80},{24,8},{32,96},{40,56},{48,112},{56,40},{64,... | collective-permute-start | bytes 393224 | tf_op jit(solution)/shard_map/ppermute | solution.py:453
  14.8 5.4 %collective-permute-start.3 = (f32[256,128]{1,0:T(8,128)S(1)}, f32[256,128]{1,0:T(8,128)S(1)}, u32[]{:S(2)}, u32[]{:S(2)}) collective-permute-start(f32[256,128]{1,0:T(8,128)S(1)} %get-tuple-element.40), channel_id=1, source_target_pairs={{0,64},{8,56},{16,80},{24,40},{32,96},{40,24},{48,112},{56,8},{64,... | collective-permute-start | bytes 393224 | tf_op jit(solution)/shard_map/ppermute | solution.py:453
  20.7 13.0 %copy-start.1 = (f32[4,128,128]{2,1,0:T(8,128)S(1)}, f32[4,128,128]{2,1,0:T(8,128)}, u32[]{:S(2)}) copy-start(f32[4,128,128]{2,1,0:T(8,128)} %refs_8_.1) | copy-start | bytes 786436
  20.7 5.4 %collective-permute-start.6 = (f32[256,128]{1,0:T(8,128)S(1)}, f32[256,128]{1,0:T(8,128)S(1)}, u32[]{:S(2)}, u32[]{:S(2)}) collective-permute-start(f32[256,128]{1,0:T(8,128)S(1)} %row.1.after_ref.s0.refs_4_), channel_id=1, source_target_pairs={{0,16},{8,136},{16,0},{24,152},{32,48},{40,168},{48,32},{56,184},{... | collective-permute-start | bytes 393224 | tf_op jit(solution)/shard_map/ppermute | solution.py:453
  23.3 5.0 %collective-permute-start.5 = (f32[256,128]{1,0:T(8,128)S(1)}, f32[256,128]{1,0:T(8,128)S(1)}, u32[]{:S(2)}, u32[]{:S(2)}) collective-permute-start(f32[256,128]{1,0:T(8,128)S(1)} %row.1.after_ref.s0.refs_4_), channel_id=1, source_target_pairs={{0,16},{8,200},{16,0},{24,216},{32,48},{40,232},{48,32},{56,248},{... | collective-permute-start | bytes 393224 | tf_op jit(solution)/shard_map/ppermute | solution.py:453
  24.1 4.2 %collective-permute-start.4 = (f32[256,128]{1,0:T(8,128)S(1)}, f32[256,128]{1,0:T(8,128)S(1)}, u32[]{:S(2)}, u32[]{:S(2)}) collective-permute-start(f32[256,128]{1,0:T(8,128)S(1)} %row.1.after_ref.s0.refs_4_), channel_id=1, source_target_pairs={{0,16},{8,72},{16,0},{24,88},{32,48},{40,104},{48,32},{56,120},{64... | collective-permute-start | bytes 393224 | tf_op jit(solution)/shard_map/ppermute | solution.py:453
  28.8 6.8 %collective-permute-start.9 = (f32[256,128]{1,0:T(8,128)S(1)}, f32[256,128]{1,0:T(8,128)S(1)}, u32[]{:S(2)}, u32[]{:S(2)}) collective-permute-start(f32[256,128]{1,0:T(8,128)S(1)} %column.1.refs_9_.s0), channel_id=1, source_target_pairs={{0,16},{8,11},{1,17},{9,10},{2,18},{10,9},{3,19},{11,8},{4,20},{12... | collective-permute-start | bytes 393224 | tf_op jit(solution)/shard_map/ppermute | solution.py:453
  33.3 5.2 %collective-permute-start.8 = (f32[256,128]{1,0:T(8,128)S(1)}, f32[256,128]{1,0:T(8,128)S(1)}, u32[]{:S(2)}, u32[]{:S(2)}) collective-permute-start(f32[256,128]{1,0:T(8,128)S(1)} %column.1.refs_9_.s0), channel_id=1, source_target_pairs={{0,16},{8,10},{1,17},{9,11},{2,18},{10,8},{3,19},{11,9},{4,20},{12... | collective-permute-start | bytes 393224 | tf_op jit(solution)/shard_map/ppermute | solution.py:453
  33.3 5.2 %collective-permute-start.7 = (f32[256,128]{1,0:T(8,128)S(1)}, f32[256,128]{1,0:T(8,128)S(1)}, u32[]{:S(2)}, u32[]{:S(2)}) collective-permute-start(f32[256,128]{1,0:T(8,128)S(1)} %column.1.refs_9_.s0), channel_id=1, source_target_pairs={{0,16},{8,9},{1,17},{9,8},{2,18},{10,11},{3,19},{11,10},{4,20},{12... | collective-permute-start | bytes 393224 | tf_op jit(solution)/shard_map/ppermute | solution.py:453
  39.0 6.9 %collective-permute-start.10 = (f32[128,128]{1,0:T(8,128)S(1)}, f32[128,128]{1,0:T(8,128)S(1)}, u32[]{:S(2)}, u32[]{:S(2)}) collective-permute-start(f32[128,128]{1,0:T(8,128)S(1)} %lead.1.after_ref), channel_id=1, source_target_pairs={{0,16},{8,15},{1,17},{9,14},{2,18},{10,13},{3,19},{11,12},{4,20},{... | collective-permute-start | bytes 196616 | tf_op jit(solution)/shard_map/ppermute | solution.py:509
  44.1 9.9 %copy-start.2 = (f32[4,128]{1,0:T(4,128)S(1)}, f32[4,128]{1,0:T(4,128)}, u32[]{:S(2)}) copy-start(f32[4,128]{1,0:T(4,128)} %refs_16_.1) | copy-start | bytes 6148
  46.2 4.7 %collective-permute-start.13 = (f32[128,128]{1,0:T(8,128)S(1)}, f32[128,128]{1,0:T(8,128)S(1)}, u32[]{:S(2)}, u32[]{:S(2)}) collective-permute-start(f32[128,128]{1,0:T(8,128)S(1)} %get-tuple-element.49), channel_id=1, source_target_pairs={{0,64},{8,40},{16,80},{24,56},{32,96},{40,8},{48,112},{56,24},{64,... | collective-permute-start | bytes 196616 | tf_op jit(solution)/shard_map/ppermute | solution.py:453
  48.0 3.1 %collective-permute-start.12 = (f32[128,128]{1,0:T(8,128)S(1)}, f32[128,128]{1,0:T(8,128)S(1)}, u32[]{:S(2)}, u32[]{:S(2)}) collective-permute-start(f32[128,128]{1,0:T(8,128)S(1)} %get-tuple-element.48), channel_id=1, source_target_pairs={{0,64},{8,24},{16,80},{24,8},{32,96},{40,56},{48,112},{56,40},{64,... | collective-permute-start | bytes 196616 | tf_op jit(solution)/shard_map/ppermute | solution.py:453
  48.0 4.3 %collective-permute-start.11 = (f32[128,128]{1,0:T(8,128)S(1)}, f32[128,128]{1,0:T(8,128)S(1)}, u32[]{:S(2)}, u32[]{:S(2)}) collective-permute-start(f32[128,128]{1,0:T(8,128)S(1)} %get-tuple-element.47), channel_id=1, source_target_pairs={{0,64},{8,56},{16,80},{24,40},{32,96},{40,24},{48,112},{56,8},{64,... | collective-permute-start | bytes 196616 | tf_op jit(solution)/shard_map/ppermute | solution.py:453
  49.5 3.3 %collective-permute-start.14 = (f32[128,128]{1,0:T(8,128)S(1)}, f32[128,128]{1,0:T(8,128)S(1)}, u32[]{:S(2)}, u32[]{:S(2)}) collective-permute-start(f32[128,128]{1,0:T(8,128)S(1)} %get-tuple-element.50.after_ref.refs_8_), channel_id=1, source_target_pairs={{0,8},{8,0},{16,24},{24,16},{32,40},{40,32},{48,56},{56,48},{64,72... | collective-permute-start | bytes 196616 | tf_op jit(solution)/shard_map/ppermute | solution.py:532
  52.3 1.3 %collective-permute-start.17 = (f32[128,128]{1,0:T(8,128)S(1)}, f32[128,128]{1,0:T(8,128)S(1)}, u32[]{:S(2)}, u32[]{:S(2)}) collective-permute-start(f32[128,128]{1,0:T(8,128)S(1)} %collective-permute-done.11.refs_11_), channel_id=1, source_target_pairs={{0,8},{8,0},{16,24},{24,16},{32,40},{40,32},{48,56},{56,48},{64,72... | collective-permute-start | bytes 196616 | tf_op jit(solution)/shard_map/ppermute | solution.py:453
  52.3 1.4 %collective-permute-start.16 = (f32[128,128]{1,0:T(8,128)S(1)}, f32[128,128]{1,0:T(8,128)S(1)}, u32[]{:S(2)}, u32[]{:S(2)}) collective-permute-start(f32[128,128]{1,0:T(8,128)S(1)} %collective-permute-done.12.refs_10_), channel_id=1, source_target_pairs={{0,8},{8,0},{16,24},{24,16},{32,40},{40,32},{48,56},{56,48},{64,72... | collective-permute-start | bytes 196616 | tf_op jit(solution)/shard_map/ppermute | solution.py:453
  52.8 1.3 %collective-permute-start.15 = (f32[128,128]{1,0:T(8,128)S(1)}, f32[128,128]{1,0:T(8,128)S(1)}, u32[]{:S(2)}, u32[]{:S(2)}) collective-permute-start(f32[128,128]{1,0:T(8,128)S(1)} %collective-permute-done.13.refs_9_), channel_id=1, source_target_pairs={{0,8},{8,0},{16,24},{24,16},{32,40},{40,32},{48,56},{56,48},{64,72... | collective-permute-start | bytes 196616 | tf_op jit(solution)/shard_map/ppermute | solution.py:453
